TPU v7x, 32 devices: a whole 2x2x4 slice. The times are simulated.
32 devices in a mesh: groups: 2 (over y), samples: 8 (over z, x), genome: 2 (over core).
Axes of the slice: x: 2, y: 2, z: 4, core: 2. Of those that a mesh axis runs over, the one named last changes fastest.
Arguments:
- genotypes: bfloat16 [16384, 1536], P(('groups', 'samples'), 'genome'), parts along dimension 0, may hold values from 0 to 2
- chromosome: int32 [3072], P('groups'), parts along dimension 0, may hold values from 1 to 3, as said below
- blocks: int32 [3072], P('groups'), parts along dimension 0, may hold values from 0 to 199, never falling along the last dimension, each value on 1 to 16 neighbouring positions
- annotation: int32 [97, 3072], P(None, 'groups'), parts along dimension 1, may hold values 0 or 1
- reach: int32 [3072], P('groups'), parts along dimension 0, may hold values from 384 to 768
Outputs:
- ld_scores: float32 [97, 3072], P(None, ('groups', 'genome')), parts along dimension 1
- block_sums: float32 [97, 400], P(None, 'groups'), parts along dimension 1
There are 2 independent parts, one for each index of `groups`. A program takes and returns all parts, laid end to end along the dimension named above; each array names one. Nothing has to cross between parts.
Inputs may be any that keep to these rules, and one draw needn't show every extreme that they name: chromosome ids never fall along the window and rise by one at each of 2 boundaries.
All inputs are finite; a program needn't handle non-finite values.
Results may differ from a plain program's by a relative error of at most 0.0015.
Values may be sent and summed in bfloat16 or wider, within the bound.
No kernel may reach another device: no remote copies, remote signals or barrier semaphores. Data moves between devices by JAX's collectives and lax.ppermute only.
A program may use at most 64 MiB of HBM per device.

v0:
```python
import jax
import jax.numpy as jnp
from jax import lax
from jax.sharding import PartitionSpec as P

BAND = 768
NBLK = 200


VAR_EPS = 1e-06


def shifted(block, axis, distance):
    devices = range(lax.axis_size(axis))
    route = [(i - distance, i) for i in devices if i - distance in devices]
    return lax.ppermute(block, axis, route)


def shear_band(product, band_len):
    rows_here, columns = product.shape
    flattened = jnp.pad(product.reshape(-1), (0, rows_here))
    return flattened.reshape(rows_here, columns + 1)[:, :band_len]


def unshear_band(gram_band):
    rows_here, band_len = gram_band.shape
    col_span = rows_here + band_len
    padded = jnp.pad(gram_band, ((0, 0), (1, rows_here)))
    return padded.reshape(-1)[: rows_here * col_span].reshape(rows_here, col_span)


def gram_rows(extended, row_start, row_count, band_len):
    left_cols = lax.dynamic_slice_in_dim(extended, row_start, row_count, 1)
    right_cols = lax.dynamic_slice_in_dim(extended, row_start + 1, row_count + band_len - 1, 1)
    product = lax.dot_general(
        left_cols, right_cols, (((0,), (0,)), ((), ())), preferred_element_type=jnp.float32
    )
    return shear_band(product, band_len)


def score_terms(
    gram_band,
    row_start,
    col_means,
    scales,
    chrom_ext,
    reach_own,
    annot_ext,
    first_col,
    snp_total,
    samples_all,
):
    row_count, band_len = gram_band.shape
    col_span = row_count + band_len
    dense_band = unshear_band(gram_band)
    mean_rows = lax.dynamic_slice_in_dim(col_means, row_start, row_count)
    scale_rows = lax.dynamic_slice_in_dim(scales, row_start, row_count)
    chrom_rows = lax.dynamic_slice_in_dim(chrom_ext, row_start, row_count)
    correl = (dense_band / samples_all - mean_rows[:, None] * col_means[None, :]) / (
        scale_rows[:, None] * scales[None, :]
    )
    squared = correl * correl
    unbiased = squared - (1.0 - squared) / (samples_all - 2.0)
    offsets = jnp.arange(col_span)[None, :] - jnp.arange(row_count)[:, None]
    col_index = first_col + row_start + jnp.arange(col_span)
    allowed = (
        (offsets >= 1)
        & (offsets <= reach_own[:, None])
        & (col_index[None, :] < snp_total)
        & (chrom_rows[:, None] == chrom_ext[None, :])
    )
    weights = jnp.where(allowed, unbiased, 0.0)
    annot_rows = lax.dynamic_slice_in_dim(annot_ext, row_start, row_count, 1)
    forward = lax.dot_general(
        annot_ext, weights, (((1,), (1,)), ((), ())), precision=lax.Precision.HIGHEST
    )
    backward = jnp.dot(annot_rows, weights, precision=lax.Precision.HIGHEST)
    empty_scores = jnp.zeros(annot_ext.shape, jnp.float32)
    placed_fore = lax.dynamic_update_slice_in_dim(empty_scores, forward, row_start, 1)
    return backward + placed_fore


def body(genotypes, chromosome, blocks, annotation, reach):
    slab_len = genotypes.shape[1]
    band_len = BAND
    snp_total = chromosome.shape[0]
    samples_all = float(genotypes.shape[0] * lax.axis_size("samples"))
    first_col = lax.axis_index("genome") * slab_len
    next_cols = shifted(genotypes, "genome", -1)
    extended = jnp.concatenate([genotypes, next_cols], axis=1)
    ext_values = extended.astype(jnp.float32)
    col_sums, squares = lax.psum(
        (jnp.sum(ext_values, 0), jnp.sum(ext_values * ext_values, 0)), "samples"
    )
    col_means = col_sums / samples_all
    variance = squares / samples_all - col_means * col_means + VAR_EPS
    scales = jnp.sqrt(variance)
    chrom_pad = jnp.pad(chromosome, (0, band_len), constant_values=-1)
    chrom_ext = lax.dynamic_slice_in_dim(chrom_pad, first_col, slab_len + band_len)
    reach_own = lax.dynamic_slice_in_dim(reach, first_col, slab_len)
    annot_pad = jnp.pad(annotation.astype(jnp.float32), ((0, 0), (0, band_len)))
    annot_ext = lax.dynamic_slice_in_dim(annot_pad, first_col, slab_len + band_len, 1)
    gram_band = lax.psum(gram_rows(extended, 0, slab_len, band_len), "samples")
    scores = score_terms(
        gram_band,
        0,
        col_means,
        scales,
        chrom_ext,
        reach_own,
        annot_ext,
        first_col,
        snp_total,
        samples_all,
    )
    carried = shifted(scores[:, slab_len:].astype(jnp.bfloat16), "genome", 1).astype(jnp.float32)
    ld_scores = annot_ext[:, :slab_len] + scores[:, :slab_len] + carried
    block_own = lax.dynamic_slice_in_dim(blocks, first_col, slab_len)
    onehot = (block_own[None, :] == jnp.arange(NBLK)[:, None]).astype(jnp.float32)
    block_part = lax.dot_general(
        ld_scores, onehot, (((1,), (1,)), ((), ())), precision=lax.Precision.HIGHEST
    )
    block_sums = lax.psum(block_part, "genome")
    return (ld_scores, block_sums)


def solution(mesh):
    placed = (
        P(("groups", "samples"), "genome"),
        P("groups"),
        P("groups"),
        P(None, "groups"),
        P("groups"),
    )
    return jax.shard_map(
        body,
        mesh=mesh,
        in_specs=placed,
        out_specs=(P(None, ("groups", "genome")), P(None, "groups")),
        check_vma=False,
    )
```

profile of v0, /device:TPU:0, one launch (start us, length us, event | category | flops | bytes accessed | tf_op | source)
XLA Modules:
  0.0 224.0 jit_solution(105049170321501688)
XLA Ops:
  7.2 0.0 copy-start.1
  7.2 0.0 all-reduce.9.cloned.1.call-start
  7.2 1.4 collective-permute-start
  8.7 1.5 constant_dynamic-update-slice_fusion.1
  10.2 2.7 %collective-permute-done = bf16[1024,768]{1,0:T(8,128)(2,1)S(1)} collective-permute-done((bf16[1024,768]{1,0:T(8,128)(2,1)}, bf16[1024,768]{1,0:T(8,128)(2,1)S(1)}, u32[]{:S(2)}, u32[]{:S(2)}) %collective-permute-start) | collective-permute-done | bytes 1572896 | tf_op jit(solution)/shard_map/ppermute | solution.py:16
  12.9 0.1 constant_dynamic-update-slice_fusion
  13.0 0.0 copy-start
  13.0 1.6 copy-done
  14.6 0.0 copy-done.1
  14.6 4.9 %convolution_bitcast_fusion = f32[768,1535]{0,1:T(8,128)} fusion(bf16[1024,768]{1,0:T(8,128)(2,1)S(1)} %copy-done.1, bf16[1024,1536]{1,0:T(8,128)(2,1)S(1)} %constant_dynamic-update-slice_fusion), kind=kOutput, calls=%fused_computation.11 | convolution fusion | flops 2414346240 | bytes 9434112 | tf_op jit(solution)/shard_map/dot_general | solution.py:35
  19.6 6.1 %copy.7 = f32[768,1535]{1,0:T(8,128)} copy(f32[768,1535]{0,1:T(8,128)} %convolution_bitcast_fusion) | data formatting | bytes 9431040 | tf_op jit(solution)/shard_map/dot_general | solution.py:35
  25.6 7.8 %reshape.30 = f32[1178880]{0:T(1024)} reshape(f32[768,1535]{1,0:T(8,128)} %copy.7) | data formatting | bytes 9431040 | tf_op jit(solution)/shard_map/reshape | solution.py:21
  33.5 4.1 %pad.19 = f32[1179648]{0:T(1024)} pad(f32[1178880]{0:T(1024)} %reshape.30, f32[]{:T(128)} %constant.12.clone.1), padding=0_768 | pad | bytes 9434116 | tf_op jit(solution)/shard_map/jit(_pad)/pad | solution.py:21
  37.6 5.8 %reshape.31 = f32[768,1536]{1,0:T(8,128)} reshape(f32[1179648]{0:T(1024)} %pad.19) | data formatting | bytes 9437184 | tf_op jit(solution)/shard_map/reshape | solution.py:22
  43.4 0.0 copy-start.3
  43.4 0.0 copy-start.5
  43.4 0.0 copy-start.4
  43.4 3.3 %slice.21 = f32[768,768]{1,0:T(8,128)} slice(f32[768,1536]{1,0:T(8,128)} %reshape.31), slice={[0:768], [0:768]} | slice | bytes 4718592 | tf_op jit(solution)/shard_map/slice | solution.py:22
  46.7 0.0 all-reduce.9.cloned.1.call-update
  46.7 0.0 all-reduce.11.cloned.1.call-start
  46.8 0.0 copy-done.3
  46.8 0.0 copy-done.5
  46.8 0.1 dynamic_slice.26
  46.9 0.0 copy-done.4
  46.9 0.1 pad_dynamic-slice_fusion.4
  47.0 0.1 pad_dynamic-slice_fusion.5
  47.1 2.8 %convert_reduce_fusion = (f32[1536]{0:T(1024)S(1)}, f32[1536]{0:T(1024)S(1)}) fusion(bf16[1024,1536]{1,0:T(8,128)(2,1)} %copy-done), kind=kLoop, calls=%fused_computation.1 | loop fusion | flops 6288384 | bytes 3158016 | tf_op jit(solution)/shard_map/reduce_sum | solution.py:93
  49.9 40.4 %all-reduce.5 = (f32[1536]{0:T(1024)S(1)}, f32[1536]{0:T(1024)S(1)}) all-reduce(f32[1536]{0:T(1024)S(1)} %get-tuple-element.3, f32[1536]{0:T(1024)S(1)} %get-tuple-element.2), channel_id=1, replica_groups=mesh['groups'=2,'samples'=8,'genome'=2] {'samples'}, use_global_device_ids=true, to_apply=%region_4.5 | all-reduce | flops 3072 | bytes 24576 | tf_op jit(solution)/shard_map/psum | solution.py:92
  90.2 68.6 %all-reduce.9.cloned.1.call-done = f32[768,768]{1,0:T(8,128)} async-done(((f32[768,768]{1,0:T(8,128)}), f32[768,768]{1,0:T(8,128)}) %all-reduce.9.cloned.1.call-update) | async-done | bytes 2359312 | tf_op jit(solution)/shard_map/psum | solution.py:103
  158.9 4.8 %pad.20 = f32[768,1537]{1,0:T(8,128)} pad(f32[768,768]{1,0:T(8,128)} %all-reduce.9.cloned.1.call-done, f32[]{:T(128)} %constant.12.clone.1), padding=0_0x1_768 | pad | bytes 7080964 | tf_op jit(solution)/shard_map/jit(_pad)/pad | solution.py:28
  163.7 8.1 %reshape.32 = f32[1180416]{0:T(1024)} reshape(f32[768,1537]{1,0:T(8,128)} %pad.20) | data formatting | bytes 9443328 | tf_op jit(solution)/shard_map/reshape | solution.py:29
  171.8 3.9 %slice_multiply_fusion = f32[1179648]{0:T(1024)} fusion(f32[1180416]{0:T(1024)} %reshape.32), kind=kLoop, calls=%fused_computation.3 | loop fusion | flops 1179648 | bytes 9437184 | tf_op jit(solution)/shard_map/div | solution.py:59
  175.8 5.8 %div.25 = f32[768,1536]{1,0:T(8,128)} reshape(f32[1179648]{0:T(1024)} %slice_multiply_fusion) | data formatting | bytes 9437184 | tf_op jit(solution)/shard_map/div | solution.py:59
  181.6 5.4 %subtract_select_fusion = f32[768,1536]{1,0:T(8,128)S(1)} fusion(f32[768,1536]{1,0:T(8,128)} %div.25, f32[1536]{0:T(1024)S(1)} %get-tuple-element.7, f32[768]{0:T(1024)S(1)} %dynamic_slice.35, f32[1536]{0:T(1024)S(1)} %get-tuple-element.6, f32[768]{0:T(1024)S(1)} %dynamic_slice.34, s32[1536]{0:T(1024)S(1)} %pad_dynamic-slice_fusion.5, ...), kind=kLoop, calls=%fused_computation.4 | loop fusion | flops 18874368 | bytes 9469440 | tf_op jit(solution)/shard_map/jit(_where)/select_n | solution.py:72
  187.0 4.7 %fusion.7 = f32[97,768]{1,0:T(8,128)S(1)} fusion(f32[768,1536]{1,0:T(8,128)S(1)} %subtract_select_fusion, s32[]{:T(128)S(6)} %select_n.12, f32[97,1536]{1,0:T(8,128)S(1)} %convert_element_type.17), kind=kOutput, calls=%fused_computation.16 | convolution fusion | flops 1373110272 | bytes 5612548 | tf_op jit(solution)/shard_map/dot_general | solution.py:74
  191.7 0.0 copy-start.6
  191.7 2.7 %convolution_add_fusion = f32[97,1536]{1,0:T(8,128)S(1)} fusion(f32[768,1536]{1,0:T(8,128)S(1)} %subtract_select_fusion, f32[97,768]{1,0:T(8,128)S(1)} %fusion.7, s32[]{:T(128)S(6)} %select_n.12, f32[97,1536]{1,0:T(8,128)S(1)} %convert_element_type.17), kind=kOutput, calls=%fused_computation.13 | convolution fusion | flops 1373259264 | bytes 6208516 | tf_op jit(solution)/shard_map/dot_general | solution.py:77
  194.5 1.3 collective-permute-start.1
  195.8 0.0 copy-done.6
  195.8 0.1 dynamic_slice.32
  195.9 0.9 collective-permute-done.1
  196.8 0.1 fusion.9
  196.9 0.0 copy-start.2
  196.9 1.1 fusion.8
  198.0 0.0 all-reduce.11.cloned.1.call-update
  198.0 17.6 %all-reduce.11.cloned.1.call-done = f32[97,200]{0,1:T(8,128)} async-done(((f32[97,200]{0,1:T(8,128)}), f32[97,200]{0,1:T(8,128)}) %all-reduce.11.cloned.1.call-update) | async-done | bytes 77616 | tf_op jit(solution)/shard_map/psum | solution.py:123
  215.6 1.5 copy.11
  217.1 0.0 copy-done.2
  (6 shorter events, 0.1 us)
Async XLA Ops:
  7.2 7.5 %copy-start.1 = (bf16[1024,768]{1,0:T(8,128)(2,1)S(1)}, bf16[1024,768]{1,0:T(8,128)(2,1)}, u32[]{:S(2)}) copy-start(bf16[1024,768]{1,0:T(8,128)(2,1)} %param.5) | copy-start | bytes 4718596
  7.2 151.7 %all-reduce.9.cloned.1.call-start = ((), (), s32[]{:S(2)}) async-start(), calls=%async_computation | async-start | bytes 4718592 | tf_op jit(solution)/shard_map/psum | solution.py:103
  7.2 5.6 %collective-permute-start = (bf16[1024,768]{1,0:T(8,128)(2,1)}, bf16[1024,768]{1,0:T(8,128)(2,1)S(1)}, u32[]{:S(2)}, u32[]{:S(2)}) collective-permute-start(bf16[1024,768]{1,0:T(8,128)(2,1)} %param.5), channel_id=1, source_target_pairs={{1,0},{3,2},{5,4},{7,6},{9,8},{11,10},{13,12},{15,14},{17,16},{19,... | collective-permute-start | bytes 4718600 | tf_op jit(solution)/shard_map/ppermute | solution.py:16
  13.0 1.6 copy-start
  43.4 3.4 %copy-start.3 = (s32[97,1536]{1,0:T(8,128)S(1)}, s32[97,1536]{1,0:T(8,128)}, u32[]{:S(2)}) copy-start(s32[97,1536]{1,0:T(8,128)} %param.8) | copy-start | bytes 1787908
  43.4 3.5 %copy-start.5 = (s32[1536]{0:T(1024)S(1)}, s32[1536]{0:T(1024)}, u32[]{:S(2)}) copy-start(s32[1536]{0:T(1024)} %param.9) | copy-start | bytes 18436
  43.4 3.6 %copy-start.4 = (s32[1536]{0:T(1024)S(1)}, s32[1536]{0:T(1024)}, u32[]{:S(2)}) copy-start(s32[1536]{0:T(1024)} %param.6) | copy-start | bytes 18436
  46.7 168.9 %all-reduce.11.cloned.1.call-start = ((), (), s32[]{:S(2)}) async-start(), calls=%async_computation.1 | async-start | bytes 204800 | tf_op jit(solution)/shard_map/psum | solution.py:123
  191.7 4.1 %copy-start.6 = (s32[1536]{0:T(1024)S(1)}, s32[1536]{0:T(1024)}, u32[]{:S(2)}) copy-start(s32[1536]{0:T(1024)} %param.7) | copy-start | bytes 18436
  194.5 2.3 %collective-permute-start.1 = (bf16[97,768]{1,0:T(8,128)(2,1)S(1)}, bf16[97,768]{1,0:T(8,128)(2,1)S(1)}, u32[]{:S(2)}, u32[]{:S(2)}) collective-permute-start(bf16[97,768]{1,0:T(8,128)(2,1)S(1)} %slice.30), channel_id=1, source_target_pairs={{0,1},{2,3},{4,5},{6,7},{8,9},{10,11},{12,13},{14,15},{16,17},{18,... | collective-permute-start | bytes 446984 | tf_op jit(solution)/shard_map/ppermute | solution.py:16
  196.9 20.3 %copy-start.2 = (f32[97,768]{1,0:T(8,128)}, f32[97,768]{1,0:T(8,128)S(1)}, u32[]{:S(2)}) copy-start(f32[97,768]{1,0:T(8,128)S(1)} %fusion.9) | copy-start | bytes 893956
Sparse Core Ops, SparseCore 0:
  46.8 112.0 all-reduce.8
  198.1 17.4 all-reduce.10
where the time goes:
time: 225 us; the launch traced here: 224 us
  waiting for transfers between devices  89.8 us (40%)
  local copies, waits for them, and re-layouts  51 us (23%)
  blocking collectives  40.4 us (18%)
  between operations  14.2 us (6%)
  matrix products  13.5 us (6%)
  other arithmetic  12.3 us (5%)
  starting transfers between devices  2.8 us (1%)
    psum x1, waiting for transfers between devices, body(): gram_band = lax.psum(gram_rows(extended, 0, slab_len, band_len), 'samples')  68.6 us
    psum x1, blocking collectives, body(): lax.psum((jnp.sum(ext_values, 0), jnp.sum(ext_values * ext_values, 0)), '...  40.4 us
    psum x1, waiting for transfers between devices, body(): block_sums = lax.psum(block_part, 'genome')  17.6 us
    reshape x1, local copies, waits for them, and re-layouts, unshear_band(): padded.reshape(-1)[:rows_here * col_span].reshape(rows_here, col_span)  8.14 us
    reshape x1, local copies, waits for them, and re-layouts, shear_band(): flattened = jnp.pad(product.reshape(-1), (0, rows_here))  7.84 us
    dot_general x1, local copies, waits for them, and re-layouts, gram_rows(): lax.dot_general(left_cols, right_cols, (((0,), (0,)), ((), ())), preferre...  6.05 us
    reshape x1, local copies, waits for them, and re-layouts, shear_band(): return flattened.reshape(rows_here, columns + 1)[:, :band_len]  5.81 us
    div x1, local copies, waits for them, and re-layouts, score_terms(): dense_band / samples_all - mean_rows[:, None] * col_means[None, :]  5.81 us
  transfers between devices with their start and end apart: 4, of which 4 were waited for; matrix products, arithmetic and copies ran while one was open for 2% of the time, Pallas kernels for 0%

commit v1 on v0

v1 whole, which is shorter than its diff:
```python
import functools
import math

import jax
import jax.numpy as jnp
from jax import lax
from jax.experimental import pallas as pl
from jax.experimental.pallas import tpu as pltpu
from jax.sharding import PartitionSpec as P

NBLK = 200
VAR_EPS = 1e-06
F32 = jnp.float32
BF16 = jnp.bfloat16
STAT_ROWS = 8
VMEM_LIMIT = 48 * 1024 * 1024


def pick(first, one, other):
    return jnp.where(first, one, other)


def col_parts(vec, first, half):
    left, right, there = vec[:, :half], vec[:, half : 2 * half], vec[:, 2 * half :]
    a_cols = pick(first, left, there)
    b_cols = pick(first, there, right)
    a_rolled = pltpu.roll(a_cols, half // 2, 1)
    b3_cols = pick(first, pltpu.roll(there, half // 2, 1), left)
    return left, right, b_cols, a_rolled, b3_cols


def row_parts(ref, core, start, count, half):
    def at(offset):
        rows = ref[pl.ds(pl.multiple_of(offset + start, 16), count), :]
        return jnp.concatenate([rows] * (half // 128), axis=1)

    left, right = at(0), at(half)
    a_rows = at(2 * half * core)
    a2_rows = at(half + half * core)
    b_rows = at(2 * half + half // 2 - half * core)
    return left, right, a_rows, a2_rows, b_rows


def index_parts(start, count, half):
    row = lax.broadcasted_iota(jnp.int32, (count, half), 0) + start
    col = lax.broadcasted_iota(jnp.int32, (count, half), 1)
    return row, col


def pair_products(rows, cols, row, col, half):
    left, right, a_rows, a2_rows, b_rows = rows
    c_left, c_right, c_b, c_a, c_b3 = cols
    fold = col < half // 2
    one = left * c_right
    two = jnp.where(row < col, left * c_left, jnp.where(row > col, right * c_right, a_rows * c_b))
    three = jnp.where(fold, jnp.where(row > col, a_rows * c_b, b_rows * c_a), a2_rows * c_b3)
    return one, two, three


def to_column(vec_row, ref, width):
    tall = jnp.broadcast_to(vec_row, (128, width))
    for k in range(width // 128):
        ref[k * 128 : (k + 1) * 128, :] = tall[:, k * 128 : (k + 1) * 128].T
    rest = ref.shape[0] - width
    ref[width:, :] = jnp.zeros((rest, 128), F32)


def coded(stats):
    high = stats.astype(BF16)
    left = stats - high.astype(F32)
    middle = left.astype(BF16)
    low = (left - middle.astype(F32)).astype(BF16)
    return jnp.concatenate([high[:2], middle[:2], low[:2], high[:2]], axis=0)


def decoded(rows):
    parts = rows.astype(F32)
    return parts[0:2] + parts[2:4] + parts[4:6]


def dot_tt(left, right):
    return lax.dot_general(left, right, (((0,), (0,)), ((), ())), preferred_element_type=F32)


def gram_kernel(pos_ref, own_ref, there_ref, keep_ref, send_ref, stats_ref, full_ref, col_ref):
    half = own_ref.shape[1] // 2
    count = own_ref.shape[0]
    width = 3 * half
    core = pos_ref[0]
    first = core == 0
    left, right, there = own_ref[:, :half], own_ref[:, half:], there_ref[...]
    ones = jnp.ones((8, count), BF16)
    sums = jnp.concatenate(
        [
            lax.dot_general(ones, x, (((1,), (0,)), ((), ())), preferred_element_type=F32)[:1]
            for x in (left, right, there)
        ],
        axis=1,
    )
    squares = []
    for ref, lo in ((own_ref, 0), (own_ref, half), (there_ref, 0)):
        total = jnp.zeros((8, half), F32)
        for k in range(0, count, 64):
            part = ref[k : k + 64, lo : lo + half].astype(F32)
            total = total + jnp.sum((part * part).reshape(8, 8, half), axis=0)
        squares.append(jnp.sum(total, axis=0, keepdims=True))
    squares = jnp.concatenate(squares, axis=1)
    shift = sums * (1.0 / math.sqrt(count))
    stats = jnp.concatenate([sums, squares - shift * shift], axis=0)
    stats_ref[...] = jnp.concatenate([stats] * 4, axis=0)
    to_column(shift, col_ref, width)
    full_ref[:, :half] = dot_tt(left, right)
    row, col = index_parts(0, half, half)
    full_ref[:, half : 2 * half] = jnp.where(row < col, dot_tt(left, left), dot_tt(right, right))

    def cross(a_cols, b_cols, a2_cols, b3_cols, turn):
        straight = dot_tt(a_cols, b_cols)
        full_ref[:, half : 2 * half] = jnp.where(row == col, straight, full_ref[:, half : 2 * half])
        folded = pltpu.roll(dot_tt(b_cols[:, half // 2 :], a_cols), half // 2, 1)
        folded = jnp.concatenate([folded, folded], axis=0)
        apart = dot_tt(a2_cols, b3_cols)
        if turn:
            apart = pltpu.roll(apart, half // 2, 1)
        full_ref[:, 2 * half :] = jnp.where(
            col < half // 2, jnp.where(row > col, straight, folded), apart
        )

    @pl.when(first)
    def _():
        cross(left, there, right, there, True)

    @pl.when(jnp.logical_not(first))
    def _():
        cross(there, right, there, left, False)

    cols = col_parts(jnp.broadcast_to(shift, (8, width)), first, half)
    cols = tuple(x[:1] for x in cols)
    step = 48
    bit = pos_ref[1]

    def centred(start):
        rows = row_parts(col_ref, core, start, step, half)
        products = pair_products(rows, cols, *index_parts(start, step, half), half)
        return full_ref[pl.ds(start, step), :] - jnp.concatenate(products, axis=1)

    part = keep_ref.shape[0]
    for k in range(0, part, step):
        keep_ref[k : k + step, :] = centred(pl.multiple_of(bit * part + k, 16))
        send_ref[k : k + step, :] = centred(pl.multiple_of((1 - bit) * part + k, 16)).astype(BF16)
    send_ref[part:, :] = coded(stats)


def merged_stats(msg_ref, stats_ref, rows, samples):
    theirs = decoded(msg_ref[rows:, :])
    mine = stats_ref[:2, :]
    shift = (mine[:1] - theirs[:1]) * (1.0 / math.sqrt(2.0 * samples))
    total = mine + theirs
    total = jnp.concatenate([total[:1], total[1:] + shift * shift], axis=0)
    return shift, total


def merge_kernel(pos_ref, kept_ref, msg_ref, stats_ref, keep_ref, send_ref, out_ref, col_ref, *, samples, split):
    rows, width = kept_ref.shape
    half = width // 3
    core = pos_ref[0]
    shift, total = merged_stats(msg_ref, stats_ref, rows, samples)
    out_ref[...] = jnp.concatenate([total] * 4, axis=0)
    to_column(shift, col_ref, width)
    cols = col_parts(jnp.broadcast_to(shift, (8, width)), core == 0, half)
    cols = tuple(x[:1] for x in cols)
    base, bit = pos_ref[2], pos_ref[1]
    step = 48

    def added(offset):
        start = base + offset
        part = row_parts(col_ref, core, start, step, half)
        products = pair_products(part, cols, *index_parts(start, step, half), half)
        here = pl.ds(offset, step)
        return kept_ref[here, :] + msg_ref[here, :].astype(F32) + jnp.concatenate(products, axis=1)

    out_rows = keep_ref.shape[0]
    for k in range(0, out_rows, step):
        if split:
            keep_ref[k : k + step, :] = added(pl.multiple_of(bit * out_rows + k, 16))
            send_ref[k : k + step, :] = added(pl.multiple_of((1 - bit) * out_rows + k, 16)).astype(BF16)
        else:
            rounded = added(k).astype(BF16)
            keep_ref[k : k + step, :] = rounded.astype(F32)
            send_ref[k : k + step, :] = rounded
    send_ref[out_rows:, :] = coded(total)


def weight_kernel(pos_ref, kept_ref, msg_ref, stats_ref, limit_ref, out_ref, col_ref, scale_ref, lim_ref, *, samples):
    rows, width = kept_ref.shape
    half = width // 3
    core = pos_ref[0]
    first = core == 0
    everyone = 2.0 * samples
    shift, total = merged_stats(msg_ref, stats_ref, rows, samples)
    scale = 1.0 / jnp.sqrt(total[1:] * (1.0 / everyone) + VAR_EPS)
    limit = limit_ref[:1, :]
    to_column(shift, col_ref, width)
    to_column(scale * (1.0 / everyone), scale_ref, width)
    to_column(limit, lim_ref, width)

    def cols_of(vec):
        return tuple(x[:1] for x in col_parts(jnp.broadcast_to(vec, (8, width)), first, half))

    cols, scales, limits = cols_of(shift), cols_of(scale), cols_of(limit)
    base = pos_ref[2]
    step = 48
    for k in range(0, rows, step):
        start = base + k
        row, col = index_parts(start, step, half)
        fold = col < half // 2
        products = pair_products(row_parts(col_ref, core, start, step, half), cols, row, col, half)
        norms = pair_products(row_parts(scale_ref, core, start, step, half), scales, row, col, half)
        l_left, _, l_a, l_a2, _ = row_parts(lim_ref, core, start, step, half)
        apart = jnp.abs(row - col)
        two_lim = jnp.where(row < col, l_left, jnp.where(row > col, limits[1], l_a))
        three_lim = jnp.where(fold, jnp.where(row > col, l_a, limits[3]), l_a2)
        two_gap = jnp.where(row == col, 2 * half, apart)
        three_gap = jnp.where(
            fold,
            jnp.where(row == col, 4 * half, 2 * half - apart),
            half - half // 2 + (half // 2) * core + col - row,
        )
        gaps = (half + col - row, two_gap, three_gap)
        lims = (l_left, two_lim, three_lim)
        for s in range(3):
            here = slice(s * half, (s + 1) * half)
            value = kept_ref[k : k + step, here] + msg_ref[k : k + step, here].astype(F32) + products[s]
            correl = value * norms[s]
            squared = correl * correl
            unbiased = squared - (1.0 - squared) * (1.0 / (everyone - 2.0))
            out_ref[k : k + step, here] = jnp.where(gaps[s].astype(F32) <= lims[s], unbiased, 0.0).astype(BF16)


def dot_n(left, right):
    return lax.dot_general(left, right, (((1,), (0,)), ((), ())), preferred_element_type=F32)


def dot_t(left, right):
    return lax.dot_general(left, right, (((1,), (1,)), ((), ())), preferred_element_type=F32)


def onehot_sums(scores, onehot):
    high = scores.astype(BF16)
    left = scores - high.astype(F32)
    middle = left.astype(BF16)
    low = (left - middle.astype(F32)).astype(BF16)
    return dot_n(high, onehot) + dot_n(middle, onehot) + dot_n(low, onehot)


def score_kernel(pos_ref, mine_ref, theirs_ref, annot_ref, hot_ref, own_ref, msg_ref, w_ref):
    part, width = mine_ref.shape
    half = width // 3
    quarter = half // 2
    core = pos_ref[0]
    bit = pos_ref[1]
    w_ref[pl.ds(pl.multiple_of(bit * part, 16), part), :] = mine_ref[...]
    w_ref[pl.ds(pl.multiple_of((1 - bit) * part, 16), part), :] = theirs_ref[...]
    row, col = index_parts(0, half, half)
    zero = jnp.zeros((half, half), BF16)
    one = w_ref[:, :half]
    two = w_ref[:, half : 2 * half]
    three = w_ref[:, 2 * half :]
    a_left, a_right, a_there = annot_ref[:, :half], annot_ref[:, half : 2 * half], annot_ref[:, 2 * half :]
    upper = jnp.where(row < col, two, zero)
    lower = jnp.where(row > col, two, zero)
    diag = jnp.sum(jnp.where(row == col, two, zero).astype(F32), axis=0, keepdims=True)
    fold = col < quarter
    straight = jnp.where(fold & (row > col), three, zero)
    folded = jnp.where(fold & (row < col), three, zero)[:quarter]
    apart = jnp.where(fold, zero, three)
    out_left = dot_t(a_right, one) + dot_n(a_left, upper) + dot_t(a_left, upper) + a_left.astype(F32)
    out_right = dot_n(a_left, one) + dot_n(a_right, lower) + dot_t(a_right, lower) + a_right.astype(F32)
    wide = jnp.zeros((annot_ref.shape[0], half), BF16)
    lane = lax.broadcasted_iota(jnp.int32, wide.shape, 1)

    def turned(x):
        return pltpu.roll(x, quarter, 1)

    def cross(a_cols, b_cols, a2_cols, b3_cols):
        late_b = turned(b_cols.astype(F32)).astype(BF16)[:, :quarter]
        late_a = turned(jnp.where(lane < quarter, 0.0, a_cols.astype(F32))).astype(BF16)
        out_a = dot_t(b_cols, straight) + turned(dot_n(late_b, folded)) + b_cols.astype(F32) * diag
        back = jnp.concatenate([dot_t(late_a, folded), jnp.zeros((wide.shape[0], quarter), F32)], axis=1)
        out_b = dot_n(a_cols, straight) + turned(back) + a_cols.astype(F32) * diag
        out_a2 = dot_t(b3_cols, apart)
        out_b3 = dot_n(a2_cols, apart)
        return out_a, out_b, out_a2, out_b3

    def finish(own_left, own_right, other):
        own_ref[:, :half] = own_left
        own_ref[:, half:] = own_right
        msg_ref[:, :half] = other
        msg_ref[:, half:] = (
            onehot_sums(own_left, hot_ref[:half, :])
            + onehot_sums(own_right, hot_ref[half : 2 * half, :])
            + onehot_sums(other, hot_ref[2 * half :, :])
        )

    @pl.when(core == 0)
    def _():
        b3_cols = turned(a_there.astype(F32)).astype(BF16)
        out_a, out_b, out_a2, out_b3 = cross(a_left, a_there, a_right, b3_cols)
        finish(out_left + out_a, out_right + out_a2, out_b + turned(out_b3))

    @pl.when(core != 0)
    def _():
        out_a, out_b, out_a2, out_b3 = cross(a_there, a_right, a_there, a_left)
        finish(out_left + out_b3, out_right + out_b, out_a + out_a2)


def call(kernel, inputs, outputs, scratch, flops, moved):
    vmem = pl.BlockSpec(memory_space=pltpu.VMEM)
    smem = pl.BlockSpec(memory_space=pltpu.SMEM)
    return pl.pallas_call(
        kernel,
        out_shape=outputs,
        in_specs=[smem] + [vmem] * (len(inputs) - 1),
        out_specs=jax.tree.map(lambda _: vmem, outputs),
        scratch_shapes=scratch,
        compiler_params=pltpu.CompilerParams(vmem_limit_bytes=VMEM_LIMIT),
        cost_estimate=pl.CostEstimate(flops=flops, bytes_accessed=moved, transcendentals=0),
    )(*inputs)


def body(genotypes, chromosome, blocks, annotation, reach):
    count, slab = genotypes.shape
    half = slab // 2
    width = 3 * half
    snps = chromosome.shape[0]
    parts = lax.axis_size("samples")
    bits = parts.bit_length() - 1
    core = lax.axis_index("genome")
    place = lax.axis_index("samples")
    order = [list(range(bits)) for _ in range(2)]
    if bits > 1:
        order[1][0], order[1][1] = 1, 0
    splits = min(bits, 3)
    bit_at = [(place >> jnp.where(core == 0, order[0][t], order[1][t])) & 1 for t in range(bits)]

    def exchange(x, t):
        route = []
        for s in range(parts):
            for g in range(2):
                route.append((s * 2 + g, (s ^ (1 << order[g][t])) * 2 + g))
        return lax.ppermute(x, ("samples", "genome"), route)

    def across(x):
        return lax.ppermute(x, "genome", [(0, 1), (1, 0)])

    def scalars(*values):
        return jnp.stack([jnp.asarray(v, jnp.int32) for v in values])

    def shape(rows, cols, dtype):
        return jax.ShapeDtypeStruct((rows, cols), dtype)

    there = across(lax.dynamic_slice_in_dim(genotypes, (1 - core) * half, half, 1))

    first_col = core * slab
    there_col = (1 - core) * slab + core * half

    def local(x):
        axis = x.ndim - 1
        return jnp.concatenate(
            [
                lax.dynamic_slice_in_dim(x, first_col, slab, axis),
                lax.dynamic_slice_in_dim(x, there_col, half, axis),
            ],
            axis=axis,
        )

    ends = jnp.sum((chromosome[None, :] <= jnp.arange(1, 4)[:, None]).astype(jnp.int32), axis=1)
    last = jnp.where(chromosome == 1, ends[0], jnp.where(chromosome == 2, ends[1], ends[2]))
    limit = local(jnp.minimum(reach, last - 1 - jnp.arange(snps))).astype(F32)
    limit = jnp.broadcast_to(limit[None, :], (8, width))
    annot = annotation.shape[0]
    annot_rows = -(-annot // 16) * 16
    flags = jnp.pad(local(annotation).astype(BF16), ((0, annot_rows - annot), (0, 0)))
    hot_cols = -(-NBLK // 128) * 128
    hot = (local(blocks)[:, None] == jnp.arange(hot_cols)[None, :]).astype(BF16)

    columns = pltpu.VMEM((width + half // 2, 128), F32)
    rows = half // 2
    keep, send, stats = call(
        gram_kernel,
        (scalars(core, bit_at[0]), genotypes, there),
        (shape(rows, width, F32), shape(rows + STAT_ROWS, width, BF16), shape(8, width, F32)),
        [pltpu.VMEM((half, width), F32), columns],
        2 * count * half * half * 6,
        count * width * 2,
    )
    base = bit_at[0] * rows
    samples = count
    for t in range(1, bits):
        msg = exchange(send, t - 1)
        split = t < splits
        new_rows = rows // 2 if split else rows
        keep, send, stats = call(
            functools.partial(merge_kernel, samples=float(samples), split=split),
            (scalars(core, bit_at[t], base), keep, msg, stats),
            (shape(new_rows, width, F32), shape(new_rows + STAT_ROWS, width, BF16), shape(8, width, F32)),
            [columns],
            rows * width * 8,
            rows * width * 12,
        )
        if split:
            base = base + bit_at[t] * new_rows
        rows = new_rows
        samples = 2 * samples
    msg = exchange(send, bits - 1)
    weights = call(
        functools.partial(weight_kernel, samples=float(samples)),
        (scalars(core, 0, base), keep, msg, stats, limit),
        shape(rows, width, BF16),
        [columns, columns, columns],
        rows * width * 30,
        rows * width * 8,
    )
    for t in range(splits - 1, 0, -1):
        other = exchange(weights, t)
        weights = jnp.where(
            bit_at[t] == 0,
            jnp.concatenate([weights, other], axis=0),
            jnp.concatenate([other, weights], axis=0),
        )
    other = exchange(weights, 0)
    own, msg = call(
        score_kernel,
        (scalars(core, bit_at[0]), weights, other, flags, hot),
        (shape(annot_rows, slab, F32), shape(annot_rows, half + hot_cols, F32)),
        [pltpu.VMEM((half, width), BF16)],
        2 * annot_rows * half * half * 12,
        half * width * 2,
    )
    carried = across(msg)
    arrived = carried[:annot, :half]
    nothing = jnp.zeros_like(arrived)
    ld_scores = own[:annot] + jnp.where(
        core == 0,
        jnp.concatenate([nothing, arrived], axis=1),
        jnp.concatenate([arrived, nothing], axis=1),
    )
    block_sums = msg[:annot, half : half + NBLK] + carried[:annot, half : half + NBLK]
    return (ld_scores, block_sums)


def solution(mesh):
    placed = (
        P(("groups", "samples"), "genome"),
        P("groups"),
        P("groups"),
        P(None, "groups"),
        P("groups"),
    )
    return jax.shard_map(
        body,
        mesh=mesh,
        in_specs=placed,
        out_specs=(P(None, ("groups", "genome")), P(None, "groups")),
        check_vma=False,
    )
```

time: 225 us -> 64.7 us (0.29)
  waiting for transfers between devices: 89.8 us -> 34.6 us
  local copies, waits for them, and re-layouts: 51 us -> 3.07 us
  blocking collectives: 40.4 us -> 0 us
  matrix products: 13.5 us -> 0 us
  between operations: 14.2 us -> 0.75 us
  Pallas kernels: 0 us -> 10.6 us
  starting transfers between devices: 2.8 us -> 12.1 us
  other arithmetic: 12.3 us -> 3.42 us
    psum x2 -> x0, waiting for transfers between devices: 86.2 us -> none  [the longest x1 68.6 us: body(): gram_band = lax.psum(gram_rows(extended, 0, slab_len, band_len), 'samples')]
    psum x1 -> x0, blocking collectives: 40.4 us -> none  [body(): lax.psum((jnp.sum(ext_values, 0), jnp.sum(ext_values * ext_values, 0)), '...]
    ppermute x2 -> x8, waiting for transfers between devices: 3.59 us -> 34.6 us  [the longest x6 31.2 us: exchange(): return lax.ppermute(x, ('samples', 'genome'), route)]
    reshape x3 -> x0, local copies, waits for them, and re-layouts: 21.8 us -> none  [the longest x1 8.14 us: unshear_band(): padded.reshape(-1)[:rows_here * col_span].reshape(rows_here, col_span)]
    dot_general x4 -> x0, matrix products: 13.5 us -> none  [the longest x1 4.95 us: gram_rows(): lax.dot_general(left_cols, right_cols, (((0,), (0,)), ((), ())), preferre...]
    pallas_call x0 -> x5, Pallas kernels: none -> 10.6 us  [call(): pl.pallas_call(kernel, out_shape=outputs, in_specs=[smem] + [vmem] * (len...]
    ppermute x2 -> x8, starting transfers between devices: 2.72 us -> 12.1 us  [the longest x6 11.5 us: exchange(): return lax.ppermute(x, ('samples', 'genome'), route)]
    pad x2 -> x0, local copies, waits for them, and re-layouts: 8.9 us -> none  [the longest x1 4.8 us: unshear_band(): padded = jnp.pad(gram_band, ((0, 0), (1, rows_here)))]
  transfers between devices with their start and end apart: 4 -> 8, of which waited for: 4 -> 8; matrix products, arithmetic and copies ran while one was open for 2% -> 5% of each run, Pallas kernels for 0% -> 0%
where the time goes in v1:
time: 64.7 us; the launch traced here: 64.5 us
  waiting for transfers between devices  34.6 us (53%)
  starting transfers between devices  12.1 us (19%)
  Pallas kernels  10.6 us (16%)
  other arithmetic  3.42 us (5%)
  local copies, waits for them, and re-layouts  3.07 us (5%)
  between operations  0.75 us (1%)
    ppermute x6, waiting for transfers between devices, exchange(): return lax.ppermute(x, ('samples', 'genome'), route)  31.2 us
    ppermute x6, starting transfers between devices, exchange(): return lax.ppermute(x, ('samples', 'genome'), route)  11.5 us
    pallas_call x5, Pallas kernels, call(): pl.pallas_call(kernel, out_shape=outputs, in_specs=[smem] + [vmem] * (len...  10.6 us
    ppermute x2, waiting for transfers between devices, across(): return lax.ppermute(x, 'genome', [(0, 1), (1, 0)])  3.39 us
    min x1, other arithmetic, body(): limit = local(jnp.minimum(reach, last - 1 - jnp.arange(snps))).astype(F32)  1.73 us
    dynamic_slice x1, local copies, waits for them, and re-layouts, body(): lax.dynamic_slice_in_dim(genotypes, (1 - core) * half, half, 1)  1.33 us
  transfers between devices with their start and end apart: 8, of which 8 were waited for; matrix products, arithmetic and copies ran while one was open for 5% of the time, Pallas kernels for 0%

profile of v1, /device:TPU:0, one launch (start us, length us, event | category | flops | bytes accessed | tf_op | source)
XLA Modules:
  0.0 64.5 jit_solution(16134180461408056162)
XLA Ops:
  0.6 0.0 copy-start
  0.6 1.3 %constant_dynamic-slice_fusion = bf16[1024,384]{1,0:T(8,128)(2,1)S(1)} fusion(bf16[1024,768]{1,0:T(8,128)(2,1)} %own_ref.1, s32[]{:T(128)S(6)} %select_n.57), kind=kLoop, calls=%fused_computation.16 | loop fusion | bytes 1572868 | tf_op jit(solution)/shard_map/dynamic_slice | solution.py:361
  2.0 0.5 collective-permute-start
  2.5 0.1 pad_add_fusion.1.pos_ref
  2.6 0.0 copy-start.2
  2.6 0.0 copy-start.3
  2.6 1.8 %collective-permute-done.there_ref = bf16[1024,384]{1,0:T(8,128)(2,1)S(1)} collective-permute-done((bf16[1024,384]{1,0:T(8,128)(2,1)S(1)}, bf16[1024,384]{1,0:T(8,128)(2,1)S(1)}, u32[]{:S(2)}, u32[]{:S(2)}) %collective-permute-start) | collective-permute-done | bytes 786464 | tf_op jit(solution)/shard_map/ppermute | solution.py:353
  4.4 0.0 copy-done
  4.4 4.9 %shard_map.68 = (f32[192,1152]{1,0:T(8,128)S(1)}, bf16[200,1152]{1,0:T(8,128)(2,1)}, f32[8,1152]{1,0:T(8,128)S(1)}) custom-call(s32[2]{0:T(128)S(1)} %pad_add_fusion.1.pos_ref, bf16[1024,768]{1,0:T(8,128)(2,1)S(1)} %copy-done, bf16[1024,384]{1,0:T(8,128)(2,1)S(1)} %collective-permute-done.there_ref), custom_call_target="tpu_custom_call" | custom-call | flops 1811939328 | bytes 2359296 | tf_op jit(solution)/shard_map/pallas_call | solution.py:319
  9.3 0.0 copy-start.1
  9.3 0.0 copy-start.4
  9.3 2.9 %collective-permute-start.1 = (bf16[200,1152]{1,0:T(8,128)(2,1)}, bf16[200,1152]{1,0:T(8,128)(2,1)S(1)}, u32[]{:S(2)}, u32[]{:S(2)}) collective-permute-start(bf16[200,1152]{1,0:T(8,128)(2,1)} %get-tuple-element.14), channel_id=1, source_target_pairs={{0,2},{1,5},{2,0},{3,7},{4,6},{5,1},{6,4},{7,3},{8,10},{9,13},{10,... | collective-permute-start | bytes 1382408 | tf_op jit(solution)/shard_map/ppermute | solution.py:350
  12.2 0.1 pad_add_fusion.4.pos_ref
  12.2 0.0 copy-done.2
  12.3 0.2 convert_reduce_fusion
  12.4 0.7 %fusion.4 = (s32[1]{0:T(128)}, s32[1]{0:T(128)}, s32[1]{0:T(128)}) fusion(s32[3]{0:T(128)S(1)} %convert_reduce_fusion), kind=kLoop, calls=%fused_computation.22 | loop fusion | bytes 24 | tf_op jit(solution)/shard_map/slice | solution.py:377
  13.1 0.0 copy-done.3
  13.1 1.7 %subtract_minimum_fusion = s32[1536]{0:T(1024)S(1)} fusion(s32[1536]{0:T(1024)S(1)} %copy-done.3, s32[1536]{0:T(1024)S(1)} %copy-done.2, s32[]{:T(128)} %bitcast.9, s32[]{:T(128)} %bitcast.8, s32[]{:T(128)} %bitcast.7), kind=kLoop, calls=%fused_computation.15 | loop fusion | flops 10752 | bytes 18444 | tf_op jit(solution)/shard_map/min | solution.py:378
  14.8 4.0 %collective-permute-done.1.msg_ref = bf16[200,1152]{1,0:T(8,128)(2,1)S(1)} collective-permute-done((bf16[200,1152]{1,0:T(8,128)(2,1)}, bf16[200,1152]{1,0:T(8,128)(2,1)S(1)}, u32[]{:S(2)}, u32[]{:S(2)}) %collective-permute-start.1) | collective-permute-done | bytes 460832 | tf_op jit(solution)/shard_map/ppermute | solution.py:350
  18.9 1.0 %shard_map.69 = (f32[96,1152]{1,0:T(8,128)S(1)}, bf16[104,1152]{1,0:T(8,128)(2,1)S(1)}, f32[8,1152]{1,0:T(8,128)S(1)}) custom-call(s32[3]{0:T(128)S(1)} %pad_add_fusion.4.pos_ref, f32[192,1152]{1,0:T(8,128)S(1)} %get-tuple-element.13.kept_ref, bf16[200,1152]{1,0:T(8,128)(2,1)S(1)} %collective-permute-done.1.msg_ref, f32[8,1152]{1,0:T(8,128)S(1)} %get-tuple-element.15.stats_ref), custom_call_target="tpu_custom_call" | custom-call | flops 1769472 | bytes 2654208 | tf_op jit(solution)/shard_map/pallas_call | solution.py:319
  19.9 2.2 %collective-permute-start.2 = (bf16[104,1152]{1,0:T(8,128)(2,1)S(1)}, bf16[104,1152]{1,0:T(8,128)(2,1)S(1)}, u32[]{:S(2)}, u32[]{:S(2)}) collective-permute-start(bf16[104,1152]{1,0:T(8,128)(2,1)S(1)} %get-tuple-element.17), channel_id=1, source_target_pairs={{0,4},{1,3},{2,6},{3,1},{4,0},{5,7},{6,2},{7,5},{8,12},{9,11},{10,... | collective-permute-start | bytes 718856 | tf_op jit(solution)/shard_map/ppermute | solution.py:350
  22.0 0.1 pad_add_fusion.3.pos_ref
  22.1 0.1 dynamic_slice.23
  22.2 0.1 dynamic_slice.22
  22.3 0.0 copy-done.1
  22.3 3.8 %collective-permute-done.2.msg_ref = bf16[104,1152]{1,0:T(8,128)(2,1)S(1)} collective-permute-done((bf16[104,1152]{1,0:T(8,128)(2,1)S(1)}, bf16[104,1152]{1,0:T(8,128)(2,1)S(1)}, u32[]{:S(2)}, u32[]{:S(2)}) %collective-permute-start.2) | collective-permute-done | bytes 239648 | tf_op jit(solution)/shard_map/ppermute | solution.py:350
  26.2 0.9 %shard_map.70 = (f32[48,1152]{1,0:T(8,128)S(1)}, bf16[56,1152]{1,0:T(8,128)(2,1)S(1)}, f32[8,1152]{1,0:T(8,128)S(1)}) custom-call(s32[3]{0:T(128)S(1)} %pad_add_fusion.3.pos_ref, f32[96,1152]{1,0:T(8,128)S(1)} %get-tuple-element.16.kept_ref, bf16[104,1152]{1,0:T(8,128)(2,1)S(1)} %collective-permute-done.2.msg_ref, f32[8,1152]{1,0:T(8,128)S(1)} %get-tuple-element.18.stats_ref), custom_call_target="tpu_custom_call" | custom-call | flops 884736 | bytes 1327104 | tf_op jit(solution)/shard_map/pallas_call | solution.py:319
  27.1 3.1 %collective-permute-start.3 = (bf16[56,1152]{1,0:T(8,128)(2,1)S(1)}, bf16[56,1152]{1,0:T(8,128)(2,1)S(1)}, u32[]{:S(2)}, u32[]{:S(2)}) collective-permute-start(bf16[56,1152]{1,0:T(8,128)(2,1)S(1)} %get-tuple-element.20), channel_id=1, source_target_pairs={{0,8},{1,9},{2,10},{3,11},{4,12},{5,13},{6,14},{7,15},{8,0},{9,1},... | collective-permute-start | bytes 387080 | tf_op jit(solution)/shard_map/ppermute | solution.py:350
  30.2 0.1 pad_add_fusion.2.pos_ref
  30.2 0.0 copy-done.4
  30.2 0.1 dynamic_slice.27
  30.3 0.1 dynamic_slice.26
  30.4 4.6 %collective-permute-done.3.msg_ref = bf16[56,1152]{1,0:T(8,128)(2,1)S(1)} collective-permute-done((bf16[56,1152]{1,0:T(8,128)(2,1)S(1)}, bf16[56,1152]{1,0:T(8,128)(2,1)S(1)}, u32[]{:S(2)}, u32[]{:S(2)}) %collective-permute-start.3) | collective-permute-done | bytes 129056 | tf_op jit(solution)/shard_map/ppermute | solution.py:350
  35.0 1.2 %shard_map.71 = bf16[48,1152]{1,0:T(8,128)(2,1)S(1)} custom-call(s32[3]{0:T(128)S(1)} %pad_add_fusion.2.pos_ref, f32[48,1152]{1,0:T(8,128)S(1)} %get-tuple-element.19.kept_ref, bf16[56,1152]{1,0:T(8,128)(2,1)S(1)} %collective-permute-done.3.msg_ref, f32[8,1152]{1,0:T(8,128)S(1)} %get-tuple-element.21.stats_ref, f32[8,1152]{1,0:T(8,128)S(1)} %broadcast_in_dim.26.limit_ref), custom_call_target="tpu_custom_call" | custom-call | flops 1658880 | bytes 442368 | tf_op jit(solution)/shard_map/pallas_call | solution.py:319
  36.3 1.1 %collective-permute-start.4 = (bf16[48,1152]{1,0:T(8,128)(2,1)S(1)}, bf16[48,1152]{1,0:T(8,128)(2,1)S(1)}, u32[]{:S(2)}, u32[]{:S(2)}) collective-permute-start(bf16[48,1152]{1,0:T(8,128)(2,1)S(1)} %shard_map.71), channel_id=1, source_target_pairs={{0,8},{1,9},{2,10},{3,11},{4,12},{5,13},{6,14},{7,15},{8,0},{9,1},... | collective-permute-start | bytes 331784 | tf_op jit(solution)/shard_map/ppermute | solution.py:350
  37.4 5.8 %collective-permute-done.4 = bf16[48,1152]{1,0:T(8,128)(2,1)S(1)} collective-permute-done((bf16[48,1152]{1,0:T(8,128)(2,1)S(1)}, bf16[48,1152]{1,0:T(8,128)(2,1)S(1)}, u32[]{:S(2)}, u32[]{:S(2)}) %collective-permute-start.4) | collective-permute-done | bytes 110624 | tf_op jit(solution)/shard_map/ppermute | solution.py:350
  43.2 0.2 collective-permute-start.5
  43.4 6.9 %collective-permute-done.5 = bf16[96,1152]{1,0:T(8,128)(2,1)S(1)} collective-permute-done((bf16[96,1152]{1,0:T(8,128)(2,1)S(1)}, bf16[96,1152]{1,0:T(8,128)(2,1)S(1)}, u32[]{:S(2)}, u32[]{:S(2)}) %collective-permute-start.5) | collective-permute-done | bytes 221216 | tf_op jit(solution)/shard_map/ppermute | solution.py:350
  50.3 0.1 maximum_select_fusion.mine_ref
  50.4 2.0 %collective-permute-start.6 = (bf16[192,1152]{1,0:T(8,128)(2,1)S(1)}, bf16[192,1152]{1,0:T(8,128)(2,1)S(1)}, u32[]{:S(2)}, u32[]{:S(2)}) collective-permute-start(bf16[192,1152]{1,0:T(8,128)(2,1)S(1)} %maximum_select_fusion.mine_ref), channel_id=1, source_target_pairs={{0,2},{1,5},{2,0},{3,7},{4,6},{5,1},{6,4},{7,3},{8,10},{9,13},{10,... | collective-permute-start | bytes 1327112 | tf_op jit(solution)/shard_map/ppermute | solution.py:350
  52.4 0.2 fusion.hot_ref
  52.6 6.1 %collective-permute-done.6.theirs_ref = bf16[192,1152]{1,0:T(8,128)(2,1)S(1)} collective-permute-done((bf16[192,1152]{1,0:T(8,128)(2,1)S(1)}, bf16[192,1152]{1,0:T(8,128)(2,1)S(1)}, u32[]{:S(2)}, u32[]{:S(2)}) %collective-permute-start.6) | collective-permute-done | bytes 442400 | tf_op jit(solution)/shard_map/ppermute | solution.py:350
  58.8 2.6 %shard_map.72 = (f32[112,768]{1,0:T(8,128)S(1)}, f32[112,640]{1,0:T(8,128)S(1)}) custom-call(s32[2]{0:T(128)S(1)} %pad_add_fusion.1.pos_ref, bf16[192,1152]{1,0:T(8,128)(2,1)S(1)} %maximum_select_fusion.mine_ref, bf16[192,1152]{1,0:T(8,128)(2,1)S(1)} %collective-permute-done.6.theirs_ref, bf16[112,1152]{1,0:T(8,128)(2,1)S(1)} %fusion.3.annot_ref, ...), custom_call_target="tpu_custom_call" | custom-call | flops 396361728 | bytes 884736 | tf_op jit(solution)/shard_map/pallas_call | solution.py:319
  61.3 0.1 collective-permute-start.7
  61.4 1.6 %collective-permute-done.7 = f32[112,640]{1,0:T(8,128)S(1)} collective-permute-done((f32[112,640]{1,0:T(8,128)S(1)}, f32[112,640]{1,0:T(8,128)S(1)}, u32[]{:S(2)}, u32[]{:S(2)}) %collective-permute-start.7) | collective-permute-done | bytes 286752 | tf_op jit(solution)/shard_map/ppermute | solution.py:353
  63.0 0.7 %copy.8 = f32[97,200]{0,1:T(8,128)} copy(f32[97,200]{1,0:T(8,128)S(1)} %slice_add_fusion) | data formatting | bytes 155200
  63.8 0.8 %select_add_fusion = f32[97,768]{1,0:T(8,128)} fusion(f32[97,384]{1,0:T(8,128)S(1)} %slice.28, f32[112,768]{1,0:T(8,128)S(1)} %get-tuple-element.22, pred[]{:T(512)S(6)} %eq.34), kind=kLoop, calls=%fused_computation.6 | loop fusion | flops 148992 | bytes 744961 | tf_op jit(solution)/shard_map/add | solution.py:442
  (10 shorter events, 0.2 us)
Async XLA Ops:
  0.6 3.8 %copy-start = (bf16[1024,768]{1,0:T(8,128)(2,1)S(1)}, bf16[1024,768]{1,0:T(8,128)(2,1)}, u32[]{:S(2)}) copy-start(bf16[1024,768]{1,0:T(8,128)(2,1)} %own_ref.1) | copy-start | bytes 4718596
  2.0 2.4 %collective-permute-start = (bf16[1024,384]{1,0:T(8,128)(2,1)S(1)}, bf16[1024,384]{1,0:T(8,128)(2,1)S(1)}, u32[]{:S(2)}, u32[]{:S(2)}) collective-permute-start(bf16[1024,384]{1,0:T(8,128)(2,1)S(1)} %constant_dynamic-slice_fusion), channel_id=1, source_target_pairs={{0,1},{1,0},{2,3},{3,2},{4,5},{5,4},{6,7},{7,6},{8,9},{9,8},{10,11... | collective-permute-start | bytes 2359304 | tf_op jit(solution)/shard_map/ppermute | solution.py:353
  2.6 9.7 %copy-start.2 = (s32[1536]{0:T(1024)S(1)}, s32[1536]{0:T(1024)}, u32[]{:S(2)}) copy-start(s32[1536]{0:T(1024)} %param.6) | copy-start | bytes 18436
  2.6 10.5 %copy-start.3 = (s32[1536]{0:T(1024)S(1)}, s32[1536]{0:T(1024)}, u32[]{:S(2)}) copy-start(s32[1536]{0:T(1024)} %param.9) | copy-start | bytes 18436
  9.3 13.0 %copy-start.1 = (s32[97,1536]{1,0:T(8,128)S(1)}, s32[97,1536]{1,0:T(8,128)}, u32[]{:S(2)}) copy-start(s32[97,1536]{1,0:T(8,128)} %param.8) | copy-start | bytes 1787908
  9.3 20.9 %copy-start.4 = (s32[1536]{0:T(1024)S(1)}, s32[1536]{0:T(1024)}, u32[]{:S(2)}) copy-start(s32[1536]{0:T(1024)} %param.7) | copy-start | bytes 18436
  9.3 9.6 %collective-permute-start.1 = (bf16[200,1152]{1,0:T(8,128)(2,1)}, bf16[200,1152]{1,0:T(8,128)(2,1)S(1)}, u32[]{:S(2)}, u32[]{:S(2)}) collective-permute-start(bf16[200,1152]{1,0:T(8,128)(2,1)} %get-tuple-element.14), channel_id=1, source_target_pairs={{0,2},{1,5},{2,0},{3,7},{4,6},{5,1},{6,4},{7,3},{8,10},{9,13},{10,... | collective-permute-start | bytes 1382408 | tf_op jit(solution)/shard_map/ppermute | solution.py:350
  19.9 6.3 %collective-permute-start.2 = (bf16[104,1152]{1,0:T(8,128)(2,1)S(1)}, bf16[104,1152]{1,0:T(8,128)(2,1)S(1)}, u32[]{:S(2)}, u32[]{:S(2)}) collective-permute-start(bf16[104,1152]{1,0:T(8,128)(2,1)S(1)} %get-tuple-element.17), channel_id=1, source_target_pairs={{0,4},{1,3},{2,6},{3,1},{4,0},{5,7},{6,2},{7,5},{8,12},{9,11},{10,... | collective-permute-start | bytes 718856 | tf_op jit(solution)/shard_map/ppermute | solution.py:350
  27.1 8.0 %collective-permute-start.3 = (bf16[56,1152]{1,0:T(8,128)(2,1)S(1)}, bf16[56,1152]{1,0:T(8,128)(2,1)S(1)}, u32[]{:S(2)}, u32[]{:S(2)}) collective-permute-start(bf16[56,1152]{1,0:T(8,128)(2,1)S(1)} %get-tuple-element.20), channel_id=1, source_target_pairs={{0,8},{1,9},{2,10},{3,11},{4,12},{5,13},{6,14},{7,15},{8,0},{9,1},... | collective-permute-start | bytes 387080 | tf_op jit(solution)/shard_map/ppermute | solution.py:350
  36.3 6.9 %collective-permute-start.4 = (bf16[48,1152]{1,0:T(8,128)(2,1)S(1)}, bf16[48,1152]{1,0:T(8,128)(2,1)S(1)}, u32[]{:S(2)}, u32[]{:S(2)}) collective-permute-start(bf16[48,1152]{1,0:T(8,128)(2,1)S(1)} %shard_map.71), channel_id=1, source_target_pairs={{0,8},{1,9},{2,10},{3,11},{4,12},{5,13},{6,14},{7,15},{8,0},{9,1},... | collective-permute-start | bytes 331784 | tf_op jit(solution)/shard_map/ppermute | solution.py:350
  43.2 7.1 %collective-permute-start.5 = (bf16[96,1152]{1,0:T(8,128)(2,1)S(1)}, bf16[96,1152]{1,0:T(8,128)(2,1)S(1)}, u32[]{:S(2)}, u32[]{:S(2)}) collective-permute-start(bf16[96,1152]{1,0:T(8,128)(2,1)S(1)} %maximum_select_fusion.1), channel_id=1, source_target_pairs={{0,4},{1,3},{2,6},{3,1},{4,0},{5,7},{6,2},{7,5},{8,12},{9,11},{10,... | collective-permute-start | bytes 663560 | tf_op jit(solution)/shard_map/ppermute | solution.py:350
  50.4 8.4 %collective-permute-start.6 = (bf16[192,1152]{1,0:T(8,128)(2,1)S(1)}, bf16[192,1152]{1,0:T(8,128)(2,1)S(1)}, u32[]{:S(2)}, u32[]{:S(2)}) collective-permute-start(bf16[192,1152]{1,0:T(8,128)(2,1)S(1)} %maximum_select_fusion.mine_ref), channel_id=1, source_target_pairs={{0,2},{1,5},{2,0},{3,7},{4,6},{5,1},{6,4},{7,3},{8,10},{9,13},{10,... | collective-permute-start | bytes 1327112 | tf_op jit(solution)/shard_map/ppermute | solution.py:350
  61.3 1.6 %collective-permute-start.7 = (f32[112,640]{1,0:T(8,128)S(1)}, f32[112,640]{1,0:T(8,128)S(1)}, u32[]{:S(2)}, u32[]{:S(2)}) collective-permute-start(f32[112,640]{1,0:T(8,128)S(1)} %get-tuple-element.23), channel_id=1, source_target_pairs={{0,1},{1,0},{2,3},{3,2},{4,5},{5,4},{6,7},{7,6},{8,9},{9,8},{10,11... | collective-permute-start | bytes 860168 | tf_op jit(solution)/shard_map/ppermute | solution.py:353

commit v2 on v0

v2 whole, which is shorter than its diff:
```python
import functools
import math

import jax
import jax.numpy as jnp
from jax import lax
from jax.experimental import pallas as pl
from jax.experimental.pallas import tpu as pltpu
from jax.sharding import PartitionSpec as P

NBLK = 200
VAR_EPS = 1e-06
F32 = jnp.float32
BF16 = jnp.bfloat16
CORE_ONE_ORDER = [1, 2, 0]
VMEM_LIMIT = 48 * 1024 * 1024


STEP = 48


def pick(first, one, other):
    return jnp.where(first, one, other)


def wide_rows(ref, offset, count, half):
    rows = ref[pl.ds(pl.multiple_of(offset, 16), count), :]
    return jnp.concatenate([rows] * (half // 128), axis=1)


def index_parts(start, count, half):
    row = lax.broadcasted_iota(jnp.int32, (count, half), 0) + start
    col = lax.broadcasted_iota(jnp.int32, (count, half), 1)
    return row, col


def to_column(vec_row, ref):
    width = vec_row.shape[1]
    tall = jnp.broadcast_to(vec_row, (128, width))
    for k in range(width // 128):
        ref[k * 128 : (k + 1) * 128, :] = tall[:, k * 128 : (k + 1) * 128].T
    rest = ref.shape[0] - width
    if rest:
        ref[width:, :] = jnp.zeros((rest, 128), F32)


def coded(stats):
    high = stats.astype(BF16)
    left = stats - high.astype(F32)
    middle = left.astype(BF16)
    low = (left - middle.astype(F32)).astype(BF16)
    blank = jnp.zeros((stats.shape[0] * 8 // 2 - 3 * stats.shape[0], stats.shape[1]), BF16)
    return jnp.concatenate([high, middle, low, blank], axis=0)


def decoded(rows, count):
    parts = rows.astype(F32)
    return parts[:count] + parts[count : 2 * count] + parts[2 * count : 3 * count]


def own_cols(vec, half):
    return vec[:, :half], vec[:, half : 2 * half]


def own_products(ref, cols, start, row, col):
    count, half = row.shape
    left, right = cols
    l_rows = wide_rows(ref, start, count, half)
    r_rows = wide_rows(ref, start + half, count, half)
    return l_rows * right, jnp.where(row < col, l_rows * left, r_rows * right)


def cross_halves(vec, first, half):
    left, right, there = vec[:, :half], vec[:, half : 2 * half], vec[:, 2 * half :]
    return pick(first, left, there), pick(first, there, right)


def cross_cols(vec, first, half):
    vec = jnp.broadcast_to(vec, (8, vec.shape[1]))
    a_cols, b_cols = cross_halves(vec, first, half)
    a_turned = pltpu.roll(a_cols, half // 2, 1)
    b3_cols = pick(first, pltpu.roll(vec[:, 2 * half :], half // 2, 1), vec[:, :half])
    return b_cols[:1], a_turned[:1], b3_cols[:1]


def cross_products(ref, cols, core, start, row, col):
    count, half = row.shape
    c_b, c_a, c_b3 = cols
    a_rows = wide_rows(ref, start + 2 * half * core, count, half)
    a2_rows = wide_rows(ref, start + half + half * core, count, half)
    b_rows = wide_rows(ref, start + 2 * half + half // 2 - half * core, count, half)
    return jnp.where(
        col < half // 2, jnp.where(row > col, a_rows * c_b, b_rows * c_a), a2_rows * c_b3
    )


def dot_tt(left, right):
    return lax.dot_general(left, right, (((0,), (0,)), ((), ())), preferred_element_type=F32)


def dot_n(left, right):
    return lax.dot_general(left, right, (((1,), (0,)), ((), ())), preferred_element_type=F32)


def dot_t(left, right):
    return lax.dot_general(left, right, (((1,), (1,)), ((), ())), preferred_element_type=F32)


def moments(ref):
    count, width = ref.shape
    sums = dot_n(jnp.ones((8, count), BF16), ref[...])[:1]
    total = jnp.zeros((8, width), F32)
    for k in range(0, count, 64):
        part = ref[k : k + 64, :].astype(F32)
        total = total + jnp.sum((part * part).reshape(8, 8, width), axis=0)
    shift = sums * (1.0 / math.sqrt(count))
    return sums, jnp.sum(total, axis=0, keepdims=True) - shift * shift, shift


def eight(*rows):
    return jnp.concatenate(list(rows) + [rows[-1]] * (8 - len(rows)), axis=0)


def halved(pos_ref, keep_ref, send_ref, value):
    part = keep_ref.shape[0]
    bit = pos_ref[1]
    for k in range(0, part, STEP):
        send_ref[k : k + STEP, :] = value(pl.multiple_of((1 - bit) * part + k, 16)).astype(BF16)
        keep_ref[k : k + STEP, :] = value(pl.multiple_of(bit * part + k, 16))


def own_gram_kernel(pos_ref, own_ref, keep_ref, send_ref, stats_ref, full_ref, col_ref):
    half = own_ref.shape[1] // 2
    left, right = own_ref[:, :half], own_ref[:, half:]
    sums, squares, shift = moments(own_ref)
    stats_ref[...] = eight(sums, squares, shift)
    to_column(shift, col_ref)
    full_ref[:, :half] = dot_tt(left, right)
    row, col = index_parts(0, half, half)
    full_ref[:, half:] = jnp.where(row < col, dot_tt(left, left), dot_tt(right, right))
    cols = own_cols(shift, half)

    def value(start):
        products = own_products(col_ref, cols, start, *index_parts(start, STEP, half))
        return full_ref[pl.ds(start, STEP), :] - jnp.concatenate(products, axis=1)

    halved(pos_ref, keep_ref, send_ref, value)
    send_ref[keep_ref.shape[0] :, :] = coded(jnp.concatenate([sums, squares], axis=0))


def cross_gram_kernel(pos_ref, own_ref, there_ref, own_stats_ref, keep_ref, send_ref, stats_ref, full_ref, col_ref):
    half = there_ref.shape[1]
    core = pos_ref[0]
    first = core == 0
    left, right, there = own_ref[:, :half], own_ref[:, half:], there_ref[...]
    sums, squares, shift = moments(there_ref)
    shift = jnp.concatenate([own_stats_ref[2:3, :], shift], axis=1)
    to_column(shift, col_ref)
    row, col = index_parts(0, half, half)
    a_shift, b_shift = cross_halves(shift, first, half)

    def cross(a_cols, b_cols, a2_cols, b3_cols, turn):
        straight = dot_tt(a_cols, b_cols)
        level = jnp.sum(jnp.where(row == col, straight, 0.0), axis=0, keepdims=True)
        stats = jnp.concatenate([sums, squares, level - a_shift * b_shift], axis=0)
        stats_ref[...] = eight(stats[0:1], stats[1:2], stats[2:3])
        send_ref[keep_ref.shape[0] :, :] = coded(jnp.concatenate([stats, stats[2:3]], axis=0))
        folded = pltpu.roll(dot_tt(b_cols[:, half // 2 :], a_cols), half // 2, 1)
        folded = jnp.concatenate([folded, folded], axis=0)
        apart = dot_tt(a2_cols, b3_cols)
        if turn:
            apart = pltpu.roll(apart, half // 2, 1)
        full_ref[...] = jnp.where(col < half // 2, jnp.where(row > col, straight, folded), apart)

    @pl.when(first)
    def _():
        cross(left, there, right, there, True)

    @pl.when(jnp.logical_not(first))
    def _():
        cross(there, right, there, left, False)

    cols = cross_cols(shift, first, half)

    def value(start):
        products = cross_products(col_ref, cols, core, start, *index_parts(start, STEP, half))
        return full_ref[pl.ds(start, STEP), :] - products

    halved(pos_ref, keep_ref, send_ref, value)


def own_merged(msg_ref, stats_ref, rows, samples):
    theirs = decoded(msg_ref[rows:, :], 2)
    sums, squares = stats_ref[:1, :], stats_ref[1:2, :]
    shift = (sums - theirs[:1]) * (1.0 / math.sqrt(2.0 * samples))
    return sums + theirs[:1], squares + theirs[1:2] + shift * shift, shift


def cross_merged(msg_ref, stats_ref, own_shift, rows, samples, first):
    half = stats_ref.shape[1]
    theirs = decoded(msg_ref[rows:, :], 4)
    sums, squares, level = stats_ref[:1, :], stats_ref[1:2, :], stats_ref[2:3, :]
    shift = (sums - theirs[:1]) * (1.0 / math.sqrt(2.0 * samples))
    both = jnp.concatenate([own_shift, shift], axis=1)
    a_shift, b_shift = cross_halves(both, first, half)
    return (
        sums + theirs[:1],
        squares + theirs[1:2] + shift * shift,
        (level + theirs[2:3]) + a_shift * b_shift,
        both,
    )


def passed_on(pos_ref, keep_ref, send_ref, value, split):
    if split:
        halved(pos_ref, keep_ref, send_ref, value)
        return keep_ref.shape[0]
    rows = send_ref.shape[0] // STEP * STEP
    for k in range(0, rows, STEP):
        send_ref[k : k + STEP, :] = value(k).astype(BF16)
    return rows


def own_merge_kernel(pos_ref, kept_ref, msg_ref, stats_ref, *refs, samples, split):
    keep_ref = refs[0] if split else None
    send_ref, out_ref, col_ref = refs[-3:]
    rows = kept_ref.shape[0] // STEP * STEP
    half = kept_ref.shape[1] // 2
    sums, squares, shift = own_merged(msg_ref, stats_ref, rows, samples)
    out_ref[...] = eight(sums, squares, shift)
    to_column(shift, col_ref)
    cols = own_cols(shift, half)
    base = pos_ref[2]

    def value(offset):
        start = base + offset
        products = own_products(col_ref, cols, start, *index_parts(start, STEP, half))
        here = pl.ds(offset, STEP)
        both = kept_ref[here, :].astype(F32) + msg_ref[here, :].astype(F32)
        return both + jnp.concatenate(products, axis=1)

    done = passed_on(pos_ref, keep_ref, send_ref, value, split)
    send_ref[done:, :] = coded(jnp.concatenate([sums, squares], axis=0))


def cross_merge_kernel(pos_ref, kept_ref, msg_ref, stats_ref, own_ref, *refs, samples, split):
    keep_ref = refs[0] if split else None
    send_ref, out_ref, col_ref = refs[-3:]
    rows = kept_ref.shape[0] // STEP * STEP
    half = kept_ref.shape[1]
    core = pos_ref[0]
    first = core == 0
    sums, squares, level, shift = cross_merged(msg_ref, stats_ref, own_ref[2:3, :], rows, samples, first)
    out_ref[...] = eight(sums, squares, level)
    to_column(shift, col_ref)
    cols = cross_cols(shift, first, half)
    base = pos_ref[2]

    def value(offset):
        start = base + offset
        products = cross_products(col_ref, cols, core, start, *index_parts(start, STEP, half))
        here = pl.ds(offset, STEP)
        return kept_ref[here, :].astype(F32) + msg_ref[here, :].astype(F32) + products

    done = passed_on(pos_ref, keep_ref, send_ref, value, split)
    send_ref[done:, :] = coded(jnp.concatenate([sums, squares, level, level], axis=0))


def unbiased(correl, everyone):
    squared = correl * correl
    return squared - (1.0 - squared) * (1.0 / (everyone - 2.0))


def placed_at(rows_part, offset, half):
    blank = jnp.zeros((rows_part.shape[0], half - rows_part.shape[1]), F32)
    return pltpu.roll(jnp.concatenate([rows_part, blank], axis=1), offset, 1)


def own_score_kernel(
    pos_ref, kept_ref, msg_ref, stats_ref, limit_ref, flag_ref, sub_ref,
    out_ref, vec_ref, col_ref, scale_ref, lim_ref, one_ref, two_ref, *, samples,
):
    rows = one_ref.shape[0]
    half = kept_ref.shape[1] // 2
    everyone = 2.0 * samples
    _, squares, shift = own_merged(msg_ref, stats_ref, rows, samples)
    scale = 1.0 / jnp.sqrt(squares * (1.0 / everyone) + VAR_EPS)
    vec_ref[...] = eight(shift, scale)
    to_column(shift, col_ref)
    to_column(scale * (1.0 / everyone), scale_ref)
    to_column(limit_ref[:1, : 2 * half], lim_ref)
    cols, scales = own_cols(shift, half), own_cols(scale, half)
    right_lim = limit_ref[:1, half : 2 * half]
    base = pos_ref[2]
    for k in range(0, rows, STEP):
        start = base + k
        row, col = index_parts(start, STEP, half)
        products = own_products(col_ref, cols, start, row, col)
        norms = own_products(scale_ref, scales, start, row, col)
        left_lim = wide_rows(lim_ref, start, STEP, half)
        gaps = (half + col - row, jnp.where(row == col, 8 * half, jnp.abs(row - col)))
        lims = (left_lim, jnp.where(row < col, left_lim, right_lim))
        for s, ref in ((0, one_ref), (1, two_ref)):
            here = slice(s * half, (s + 1) * half)
            value = kept_ref[k : k + STEP, here].astype(F32) + msg_ref[k : k + STEP, here].astype(F32)
            weight = unbiased((value + products[s]) * norms[s], everyone)
            ref[k : k + STEP, :] = jnp.where(gaps[s].astype(F32) <= lims[s], weight, 0.0).astype(BF16)
    row, col = index_parts(base, rows, half)
    one, two = one_ref[...], two_ref[...]
    zero = jnp.zeros_like(two)
    upper, lower = jnp.where(row < col, two, zero), jnp.where(row > col, two, zero)
    f_left, f_right = flag_ref[:, :half], flag_ref[:, half : 2 * half]
    s_left, s_right = sub_ref[:, :rows], sub_ref[:, 128 : 128 + rows]
    out_ref[:, :half] = dot_n(s_left, upper) + placed_at(dot_t(f_right, one) + dot_t(f_left, upper), base, half)
    out_ref[:, half:] = dot_n(s_left, one) + dot_n(s_right, lower) + placed_at(dot_t(f_right, lower), base, half)


def cross_score_kernel(
    pos_ref, kept_ref, msg_ref, stats_ref, vec_ref, limit_ref, flag_ref, sub_ref, own_ref,
    out_ref, col_ref, scale_ref, lim_ref, three_ref, *, samples,
):
    rows = three_ref.shape[0]
    half = kept_ref.shape[1]
    quarter = half // 2
    core = pos_ref[0]
    first = core == 0
    everyone = 2.0 * samples
    _, squares, level, shift = cross_merged(msg_ref, stats_ref, vec_ref[:1, :], rows, samples, first)
    scale = 1.0 / jnp.sqrt(squares * (1.0 / everyone) + VAR_EPS)
    scale = jnp.concatenate([vec_ref[1:2, :], scale], axis=1)
    limit = limit_ref[:1, :]
    to_column(shift, col_ref)
    to_column(scale * (1.0 / everyone), scale_ref)
    to_column(limit, lim_ref)
    cols, scales = cross_cols(shift, first, half), cross_cols(scale, first, half)
    _, late_lim, _ = cross_cols(limit, first, half)
    base = pos_ref[2]
    for k in range(0, rows, STEP):
        start = base + k
        row, col = index_parts(start, STEP, half)
        fold = col < quarter
        products = cross_products(col_ref, cols, core, start, row, col)
        norms = cross_products(scale_ref, scales, core, start, row, col)
        a_lim = wide_rows(lim_ref, start + 2 * half * core, STEP, half)
        a2_lim = wide_rows(lim_ref, start + half + half * core, STEP, half)
        lims = jnp.where(fold, jnp.where(row > col, a_lim, late_lim), a2_lim)
        near = jnp.where(row == col, 8 * half, 2 * half - jnp.abs(row - col))
        gaps = jnp.where(fold, near, quarter + quarter * core + col - row)
        value = kept_ref[k : k + STEP, :].astype(F32) + msg_ref[k : k + STEP, :].astype(F32)
        weight = unbiased((value + products) * norms, everyone)
        three_ref[k : k + STEP, :] = jnp.where(gaps.astype(F32) <= lims, weight, 0.0).astype(BF16)
    a_scale, b_scale = cross_halves(scale, first, half)
    a_limit, _ = cross_halves(limit, first, half)
    lane = lax.broadcasted_iota(jnp.int32, (1, half), 1)
    level = unbiased(level * (1.0 / everyone) * a_scale * b_scale, everyone)
    mine = (lane >= base) & (lane < base + rows) & (a_limit >= 2.0 * half)
    level = jnp.where(mine, level, 0.0)
    row, col = index_parts(base, rows, half)
    three = three_ref[...]
    zero = jnp.zeros_like(three)
    fold = col < quarter
    straight = jnp.where(fold & (row > col), three, zero)
    folded = jnp.where(fold & (row < col), three, zero)
    apart = jnp.where(fold, zero, three)
    f_a, f_b = flag_ref[:, :half], flag_ref[:, half : 2 * half]
    f_late, f_b3 = flag_ref[:, 2 * half : 3 * half], flag_ref[:, 3 * half :]
    s_a, s_a2, s_late = sub_ref[:, 256 : 256 + rows], sub_ref[:, 384 : 384 + rows], sub_ref[:, 512 : 512 + rows]
    out_a = placed_at(dot_t(f_b, straight), base, half) + pltpu.roll(dot_n(s_late, folded), quarter, 1)
    out_b = dot_n(s_a, straight) + placed_at(dot_t(f_late, folded), lax.rem(base + quarter, half), half)
    out_a = out_a + f_b.astype(F32) * level
    out_b = out_b + f_a.astype(F32) * level
    out_a2 = placed_at(dot_t(f_b3, apart), base, half)
    out_b3 = dot_n(s_a2, apart)
    out_ref[:, :half] = own_ref[:, :half] + pick(first, out_a, out_b3)
    out_ref[:, half : 2 * half] = own_ref[:, half:] + pick(first, out_a2, out_b)
    out_ref[:, 2 * half :] = pick(first, out_b + pltpu.roll(out_b3, quarter, 1), out_a + out_a2)


def block_kernel(pos_ref, score_ref, flag_ref, hot_ref, own_ref, msg_ref, sum_ref):
    slab = own_ref.shape[1]
    own = score_ref[:, :slab] + flag_ref[:, :slab].astype(F32)
    other = score_ref[:, slab:]
    own_ref[...] = own
    msg_ref[...] = other
    scores = jnp.concatenate([own, other], axis=1)
    high = scores.astype(BF16)
    left = scores - high.astype(F32)
    middle = left.astype(BF16)
    low = (left - middle.astype(F32)).astype(BF16)
    hot = hot_ref[...]
    sum_ref[...] = dot_t(hot, high) + dot_t(hot, middle) + dot_t(hot, low)


def call(kernel, inputs, outputs, scratch, flops, moved):
    vmem = pl.BlockSpec(memory_space=pltpu.VMEM)
    smem = pl.BlockSpec(memory_space=pltpu.SMEM)
    return pl.pallas_call(
        kernel,
        out_shape=outputs,
        in_specs=[smem] + [vmem] * (len(inputs) - 1),
        out_specs=jax.tree.map(lambda _: vmem, outputs),
        scratch_shapes=scratch,
        compiler_params=pltpu.CompilerParams(vmem_limit_bytes=VMEM_LIMIT),
        cost_estimate=pl.CostEstimate(flops=flops, bytes_accessed=moved, transcendentals=0),
    )(*inputs)


def body(genotypes, chromosome, blocks, annotation, reach):
    count, slab = genotypes.shape
    half = slab // 2
    quarter = half // 2
    width = 3 * half
    snps = chromosome.shape[0]
    parts = lax.axis_size("samples")
    bits = parts.bit_length() - 1
    core = lax.axis_index("genome")
    place = lax.axis_index("samples")
    order = [list(range(bits)), CORE_ONE_ORDER + list(range(3, bits))]
    bit_at = [(place >> jnp.where(core == 0, order[0][t], order[1][t])) & 1 for t in range(bits)]

    def exchange(x, t):
        route = []
        for s in range(parts):
            for g in range(2):
                route.append((s * 2 + g, (s ^ (1 << order[g][t])) * 2 + g))
        return lax.ppermute(x, ("samples", "genome"), route)

    def across(x):
        return lax.ppermute(x, "genome", [(0, 1), (1, 0)])

    def scalars(*values):
        return jnp.stack([jnp.asarray(v, jnp.int32) for v in values])

    def shape(rows, cols, dtype):
        return jax.ShapeDtypeStruct((rows, cols), dtype)

    there = across(lax.dynamic_slice_in_dim(genotypes, (1 - core) * half, half, 1))
    base = bit_at[0] * quarter + bit_at[1] * (quarter // 2)
    rows = quarter // 2

    own_at = core * slab
    there_at = (1 - core) * slab + core * half
    a_at, b_at = core * half, slab + core * half
    b3_at = slab + core * quarter

    def local(x):
        axis = x.ndim - 1
        parts_of = [(own_at, slab), (there_at, half)]
        return jnp.concatenate([lax.dynamic_slice_in_dim(x, at, n, axis) for at, n in parts_of], axis=axis)

    ends = jnp.sum((chromosome[None, :] <= jnp.arange(1, 4)[:, None]).astype(jnp.int32), axis=1)
    last = jnp.where(chromosome == 1, ends[0], jnp.where(chromosome == 2, ends[1], ends[2]))
    limit = local(jnp.minimum(reach, last - 1 - jnp.arange(snps))).astype(F32)
    limit = jnp.broadcast_to(limit[None, :], (8, width))
    annot = annotation.shape[0]
    annot_rows = -(-annot // 16) * 16
    flags_all = jnp.pad(annotation.astype(BF16), ((0, annot_rows - annot), (0, 0)))

    def columns_of(at, n):
        return lax.dynamic_slice_in_dim(flags_all, at, n, 1)

    none = jnp.zeros((annot_rows, quarter), BF16)
    flags = local(flags_all)
    flags_cross = jnp.concatenate(
        [columns_of(a_at, half), columns_of(b_at, half), columns_of(a_at + quarter, quarter), none, none, columns_of(b3_at, quarter)],
        axis=1,
    )
    padded = jnp.pad(flags_all, ((0, 0), (0, slab)))
    starts = (own_at, own_at + half, a_at, half, b_at + quarter)
    subs = jnp.concatenate([lax.dynamic_slice_in_dim(padded, at + base, 128, 1) for at in starts], axis=1)
    hot_rows = -(-NBLK // 8) * 8
    hot = (jnp.arange(hot_rows)[:, None] == local(blocks)[None, :]).astype(BF16)

    own_column = pltpu.VMEM((slab, 128), F32)
    column = pltpu.VMEM((width + quarter, 128), F32)

    def outputs(kept, sent, cols, stat_rows):
        kept_shape = (shape(kept, cols, F32),) if kept else ()
        return kept_shape + (shape(sent + stat_rows, cols, BF16), shape(8, cols, F32))

    where = scalars(core, bit_at[0], 0)
    keep_a, send_a, stats_a = call(
        own_gram_kernel,
        (where, genotypes),
        outputs(quarter, quarter, slab, 8),
        [pltpu.VMEM((half, slab), F32), own_column],
        2 * count * half * half * 3,
        count * slab * 2,
    )
    msg_a = exchange(send_a, 0)
    keep_b, send_b, stats_b = call(
        cross_gram_kernel,
        (where, genotypes, there, stats_a),
        outputs(quarter, quarter, half, 16),
        [pltpu.VMEM((half, half), F32), column],
        2 * count * half * half * 3,
        count * slab * 2,
    )
    msg_b = exchange(send_b, 0)
    samples = float(count)
    for t in range(1, bits):
        split = t == 1
        where = scalars(core, bit_at[t], bit_at[0] * quarter if split else base)
        *kept_a, send_a, stats_a = call(
            functools.partial(own_merge_kernel, samples=samples, split=split),
            (where, keep_a, msg_a, stats_a),
            outputs(rows if split else 0, rows, slab, 8),
            [own_column],
            rows * slab * 8,
            rows * slab * 20,
        )
        msg_a = exchange(send_a, t)
        *kept_b, send_b, stats_b = call(
            functools.partial(cross_merge_kernel, samples=samples, split=split),
            (where, keep_b, msg_b, stats_b, stats_a),
            outputs(rows if split else 0, rows, half, 16),
            [column],
            rows * half * 8,
            rows * half * 20,
        )
        msg_b = exchange(send_b, t)
        keep_a = kept_a[0] if split else send_a
        keep_b = kept_b[0] if split else send_b
        samples = 2 * samples
    where = scalars(core, 0, base)
    scores_a, vectors = call(
        functools.partial(own_score_kernel, samples=samples),
        (where, keep_a, msg_a, stats_a, limit, flags, subs),
        (shape(annot_rows, slab, F32), shape(8, slab, F32)),
        [own_column] * 3 + [pltpu.VMEM((rows, half), BF16)] * 2,
        2 * annot_rows * half * rows * 8,
        rows * slab * 20,
    )
    partial = call(
        functools.partial(cross_score_kernel, samples=samples),
        (where, keep_b, msg_b, stats_b, vectors, limit, flags_cross, subs, scores_a),
        shape(annot_rows, width, F32),
        [column] * 3 + [pltpu.VMEM((rows, half), BF16)],
        2 * annot_rows * half * rows * 8,
        rows * slab * 20,
    )
    partial = partial[:annot]
    for t in (1, 0):
        rounded = partial.astype(jnp.float16)
        partial = rounded.astype(F32) + exchange(rounded, t).astype(F32)
    own, other, sums = call(
        block_kernel,
        (where, partial, flags[:annot], hot),
        (shape(annot, slab, F32), shape(annot, half, F32), shape(hot_rows, annot, F32)),
        [],
        2 * annot * width * hot_rows * 3,
        annot * width * 8,
    )
    arrived, sums_there = across(other), across(sums)
    nothing = jnp.zeros_like(arrived)
    ld_scores = own + jnp.where(
        core == 0,
        jnp.concatenate([nothing, arrived], axis=1),
        jnp.concatenate([arrived, nothing], axis=1),
    )
    return (ld_scores, (sums + sums_there)[:NBLK].T)


def solution(mesh):
    placed = (
        P(("groups", "samples"), "genome"),
        P("groups"),
        P("groups"),
        P(None, "groups"),
        P("groups"),
    )
    return jax.shard_map(
        body,
        mesh=mesh,
        in_specs=placed,
        out_specs=(P(None, ("groups", "genome")), P(None, "groups")),
        check_vma=False,
    )
```

time: 225 us -> 61.7 us (0.27)
  waiting for transfers between devices: 89.8 us -> 13.3 us
  local copies, waits for them, and re-layouts: 51 us -> 9.05 us
  blocking collectives: 40.4 us -> 0 us
  starting transfers between devices: 2.8 us -> 20.2 us
  matrix products: 13.5 us -> 0 us
  between operations: 14.2 us -> 0.89 us
  Pallas kernels: 0 us -> 13.1 us
  other arithmetic: 12.3 us -> 4.83 us
    psum x2 -> x0, waiting for transfers between devices: 86.2 us -> none  [the longest x1 68.6 us: body(): gram_band = lax.psum(gram_rows(extended, 0, slab_len, band_len), 'samples')]
    psum x1 -> x0, blocking collectives: 40.4 us -> none  [body(): lax.psum((jnp.sum(ext_values, 0), jnp.sum(ext_values * ext_values, 0)), '...]
    reshape x3 -> x0, local copies, waits for them, and re-layouts: 21.8 us -> none  [the longest x1 8.14 us: unshear_band(): padded.reshape(-1)[:rows_here * col_span].reshape(rows_here, col_span)]
    ppermute x2 -> x11, starting transfers between devices: 2.72 us -> 20.2 us  [the longest x8 19.2 us: exchange(): return lax.ppermute(x, ('samples', 'genome'), route)]
    dot_general x4 -> x0, matrix products: 13.5 us -> none  [the longest x1 4.95 us: gram_rows(): lax.dot_general(left_cols, right_cols, (((0,), (0,)), ((), ())), preferre...]
    pallas_call x0 -> x9, Pallas kernels: none -> 13.1 us  [call(): pl.pallas_call(kernel, out_shape=outputs, in_specs=[smem] + [vmem] * (len...]
    ppermute x2 -> x11, waiting for transfers between devices: 3.59 us -> 13.3 us  [the longest x8 12.5 us: exchange(): return lax.ppermute(x, ('samples', 'genome'), route)]
    pad x2 -> x1, local copies, waits for them, and re-layouts: 8.9 us -> 0.99 us  [body(): jnp.pad(annotation.astype(BF16), ((0, annot_rows - annot), (0, 0)))]
  transfers between devices with their start and end apart: 4 -> 11, of which waited for: 4 -> 5; matrix products, arithmetic and copies ran while one was open for 2% -> 17% of each run, Pallas kernels for 0% -> 17%
where the time goes in v2:
time: 61.7 us; the launch traced here: 61.3 us
  starting transfers between devices  20.2 us (33%)
  waiting for transfers between devices  13.3 us (22%)
  Pallas kernels  13.1 us (21%)
  local copies, waits for them, and re-layouts  9.05 us (15%)
  other arithmetic  4.83 us (8%)
  between operations  0.89 us (1%)
    ppermute x8, starting transfers between devices, exchange(): return lax.ppermute(x, ('samples', 'genome'), route)  19.2 us
    pallas_call x9, Pallas kernels, call(): pl.pallas_call(kernel, out_shape=outputs, in_specs=[smem] + [vmem] * (len...  13.1 us
    ppermute x8, waiting for transfers between devices, exchange(): return lax.ppermute(x, ('samples', 'genome'), route)  12.5 us
    dynamic_slice x2, local copies, waits for them, and re-layouts, columns_of(): return lax.dynamic_slice_in_dim(flags_all, at, n, 1)  2.74 us
    dynamic_slice x1, local copies, waits for them, and re-layouts, body(): lax.dynamic_slice_in_dim(genotypes, (1 - core) * half, half, 1)  2.24 us
    min x1, other arithmetic, body(): limit = local(jnp.minimum(reach, last - 1 - jnp.arange(snps))).astype(F32)  1.86 us
    dynamic_slice x5, local copies, waits for them, and re-layouts, local(): lax.dynamic_slice_in_dim(x, at, n, axis)  1.24 us
  transfers between devices with their start and end apart: 11, of which 5 were waited for; matrix products, arithmetic and copies ran while one was open for 17% of the time, Pallas kernels for 17%

profile of v2, /device:TPU:0, one launch (start us, length us, event | category | flops | bytes accessed | tf_op | source)
XLA Modules:
  0.0 61.3 jit_solution(16646655305337563824)
XLA Ops:
  0.6 2.2 %constant_dynamic-slice_fusion.6 = bf16[1024,384]{1,0:T(8,128)(2,1)} fusion(bf16[1024,768]{1,0:T(8,128)(2,1)} %own_ref.3, s32[]{:T(128)S(6)} %select_n.69), kind=kLoop, calls=%fused_computation.31 | loop fusion | bytes 1572868 | tf_op jit(solution)/shard_map/dynamic_slice | solution.py:437
  2.9 0.5 collective-permute-start
  3.3 0.1 pad_add_fusion.2.pos_ref
  3.4 2.3 %shard_map.68 = (f32[192,768]{1,0:T(8,128)S(1)}, bf16[200,768]{1,0:T(8,128)(2,1)S(1)}, f32[8,768]{1,0:T(8,128)S(1)}) custom-call(s32[3]{0:T(128)S(1)} %pad_add_fusion.2.pos_ref, bf16[1024,768]{1,0:T(8,128)(2,1)S(1)} %copy-done), custom_call_target="tpu_custom_call" | custom-call | flops 905969664 | bytes 1572864 | tf_op jit(solution)/shard_map/pallas_call | solution.py:397
  5.8 2.6 %collective-permute-start.2 = (bf16[200,768]{1,0:T(8,128)(2,1)S(1)}, bf16[200,768]{1,0:T(8,128)(2,1)S(1)}, u32[]{:S(2)}, u32[]{:S(2)}) collective-permute-start(bf16[200,768]{1,0:T(8,128)(2,1)S(1)} %get-tuple-element.28), channel_id=1, source_target_pairs={{0,2},{1,5},{2,0},{3,7},{4,6},{5,1},{6,4},{7,3},{8,10},{9,13},{10,... | collective-permute-start | bytes 921608 | tf_op jit(solution)/shard_map/ppermute | solution.py:426
  8.3 0.2 convert_reduce_fusion
  8.5 0.6 fusion.7
  9.1 1.9 %subtract_minimum_fusion = s32[1536]{0:T(1024)S(1)} fusion(s32[1536]{0:T(1024)S(1)} %copy-done.9, s32[1536]{0:T(1024)S(1)} %copy-done.8, s32[]{:T(128)} %bitcast.8, s32[]{:T(128)} %bitcast.7, s32[]{:T(128)} %bitcast.6), kind=kLoop, calls=%fused_computation.24 | loop fusion | flops 10752 | bytes 18444 | tf_op jit(solution)/shard_map/min | solution.py:453
  11.0 0.1 dynamic_slice.50
  11.1 0.1 dynamic_slice.49
  11.1 0.8 %convert_element_type.38 = bf16[97,1536]{1,0:T(8,128)(2,1)} convert(s32[97,1536]{1,0:T(8,128)S(1)} %copy-done.5) | non-fusion elementwise | flops 148992 | bytes 893952 | tf_op jit(solution)/shard_map/convert_element_type | solution.py:457
  11.9 1.0 %pad.10 = bf16[112,1536]{1,0:T(8,128)(2,1)S(1)} pad(bf16[97,1536]{1,0:T(8,128)(2,1)} %convert_element_type.38, bf16[]{:T(256)} %constant.40.clone.1), padding=0_15x0_0 | pad | bytes 642050 | tf_op jit(solution)/shard_map/jit(_pad)/pad | solution.py:457
  12.9 0.1 fusion.2
  13.0 0.1 fusion.3
  13.1 0.1 fusion.4
  13.2 0.1 fusion.5
  13.3 0.1 fusion.6.sub_ref
  13.4 0.9 %constant_dynamic-slice_fusion.5 = bf16[112,768]{1,0:T(8,128)(2,1)S(1)} fusion(s32[]{:T(128)S(6)} %select_n.72, bf16[97,1536]{1,0:T(8,128)(2,1)} %convert_element_type.38), kind=kLoop, calls=%fused_computation.30 | loop fusion | bytes 470020 | tf_op jit(solution)/shard_map/dynamic_slice | solution.py:449
  14.4 1.7 %constant_dynamic-slice_fusion.2 = (bf16[112,384]{1,0:T(8,128)(2,1)}, bf16[112,384]{1,0:T(8,128)(2,1)S(1)}, bf16[112,384]{1,0:T(8,128)(2,1)}) fusion(s32[]{:T(128)S(6)} %select_n.80, bf16[97,1536]{1,0:T(8,128)(2,1)} %convert_element_type.38, s32[]{:T(128)S(6)} %select_n.73, s32[]{:T(128)S(6)} %select_n.79), kind=kLoop, calls=%fused_computation.27 | loop fusion | bytes 556044 | tf_op jit(solution)/shard_map/dynamic_slice | solution.py:460
  16.1 0.1 pad_add_fusion.1.pos_ref
  16.2 0.5 copy-done.3
  16.7 0.8 %shard_map.70 = (f32[96,768]{1,0:T(8,128)S(1)}, bf16[104,768]{1,0:T(8,128)(2,1)S(1)}, f32[8,768]{1,0:T(8,128)S(1)}) custom-call(s32[3]{0:T(128)S(1)} %pad_add_fusion.1.pos_ref, f32[192,768]{1,0:T(8,128)S(1)} %get-tuple-element.27.kept_ref, bf16[200,768]{1,0:T(8,128)(2,1)S(1)} %collective-permute-done.2.msg_ref, ...), custom_call_target="tpu_custom_call" | custom-call | flops 589824 | bytes 1474560 | tf_op jit(solution)/shard_map/pallas_call | solution.py:397
  17.6 1.6 %collective-permute-start.4 = (bf16[104,768]{1,0:T(8,128)(2,1)S(1)}, bf16[104,768]{1,0:T(8,128)(2,1)S(1)}, u32[]{:S(2)}, u32[]{:S(2)}) collective-permute-start(bf16[104,768]{1,0:T(8,128)(2,1)S(1)} %get-tuple-element.34), channel_id=1, source_target_pairs={{0,4},{1,9},{2,6},{3,11},{4,0},{5,13},{6,2},{7,15},{8,12},{9,1},{1... | collective-permute-start | bytes 479240 | tf_op jit(solution)/shard_map/ppermute | solution.py:426
  19.2 3.3 %shard_map.69 = (f32[192,384]{1,0:T(8,128)S(1)}, bf16[208,384]{1,0:T(8,128)(2,1)S(1)}, f32[8,384]{1,0:T(8,128)S(1)}) custom-call(s32[3]{0:T(128)S(1)} %pad_add_fusion.2.pos_ref, bf16[1024,768]{1,0:T(8,128)(2,1)S(1)} %copy-done, bf16[1024,384]{1,0:T(8,128)(2,1)} %collective-permute-done.there_ref, f32[8,768]{1,0:T(8,128)S(1)} %get-tuple-element.23.own_stats_ref.stats_ref), custom_call_target="tpu_custom_call" | custom-call | flops 905969664 | bytes 1572864 | tf_op jit(solution)/shard_map/pallas_call | solution.py:397
  22.6 0.6 collective-permute-start.1
  23.4 1.0 %constant_dynamic-slice_fusion = (bf16[112,192]{1,0:T(8,128)(2,1)S(1)}, bf16[112,192]{1,0:T(8,128)(2,1)S(1)}) fusion(s32[]{:T(128)S(6)} %select_n.82, bf16[97,1536]{1,0:T(8,128)(2,1)} %convert_element_type.38, s32[]{:T(128)S(6)} %select_n.81), kind=kLoop, calls=%fused_computation.25 | loop fusion | bytes 384008 | tf_op jit(solution)/shard_map/dynamic_slice | solution.py:460
  24.4 0.8 %shard_map.72 = (bf16[104,768]{1,0:T(8,128)(2,1)S(1)}, f32[8,768]{1,0:T(8,128)S(1)}) custom-call(s32[3]{0:T(128)S(1)} %add_add_fusion.1.pos_ref, f32[96,768]{1,0:T(8,128)S(1)} %get-tuple-element.33.kept_ref, bf16[104,768]{1,0:T(8,128)(2,1)S(1)} %collective-permute-done.4.msg_ref, f32[8,768]{1,0:T(8,128)S(1)} %get-tuple-element.29.own_ref.stats_ref), custom_call_target="tpu_custom_call" | custom-call | flops 589824 | bytes 1474560 | tf_op jit(solution)/shard_map/pallas_call | solution.py:397
  25.2 2.7 %collective-permute-start.6 = (bf16[104,768]{1,0:T(8,128)(2,1)S(1)}, bf16[104,768]{1,0:T(8,128)(2,1)S(1)}, u32[]{:S(2)}, u32[]{:S(2)}) collective-permute-start(bf16[104,768]{1,0:T(8,128)(2,1)S(1)} %get-tuple-element.38.kept_ref), channel_id=1, source_target_pairs={{0,8},{1,3},{2,10},{3,1},{4,12},{5,7},{6,14},{7,5},{8,0},{9,11},{1... | collective-permute-start | bytes 479240 | tf_op jit(solution)/shard_map/ppermute | solution.py:426
  27.9 0.8 %shard_map.71 = (f32[96,384]{1,0:T(8,128)S(1)}, bf16[112,384]{1,0:T(8,128)(2,1)S(1)}, f32[8,384]{1,0:T(8,128)S(1)}) custom-call(s32[3]{0:T(128)S(1)} %pad_add_fusion.1.pos_ref, f32[192,384]{1,0:T(8,128)S(1)} %get-tuple-element.24.kept_ref, bf16[208,384]{1,0:T(8,128)(2,1)S(1)} %collective-permute-done.1.msg_ref, f32[8,384]{1,0:T(8,128)S(1)} %get-tuple-element.26.stats_ref, ...), custom_call_target="tpu_custom_call" | custom-call | flops 294912 | bytes 737280 | tf_op jit(solution)/shard_map/pallas_call | solution.py:397
  28.8 1.8 %collective-permute-start.3 = (bf16[112,384]{1,0:T(8,128)(2,1)S(1)}, bf16[112,384]{1,0:T(8,128)(2,1)S(1)}, u32[]{:S(2)}, u32[]{:S(2)}) collective-permute-start(bf16[112,384]{1,0:T(8,128)(2,1)S(1)} %get-tuple-element.31), channel_id=1, source_target_pairs={{0,4},{1,9},{2,6},{3,11},{4,0},{5,13},{6,2},{7,15},{8,12},{9,1},{1... | collective-permute-start | bytes 258056 | tf_op jit(solution)/shard_map/ppermute | solution.py:426
  30.6 0.2 concatenate.32.flag_ref
  30.8 2.5 %collective-permute-done.3.msg_ref = bf16[112,384]{1,0:T(8,128)(2,1)S(1)} collective-permute-done((bf16[112,384]{1,0:T(8,128)(2,1)S(1)}, bf16[112,384]{1,0:T(8,128)(2,1)S(1)}, u32[]{:S(2)}, u32[]{:S(2)}) %collective-permute-start.3) | collective-permute-done | bytes 86048 | tf_op jit(solution)/shard_map/ppermute | solution.py:426
  33.3 0.8 %shard_map.73 = (bf16[112,384]{1,0:T(8,128)(2,1)S(1)}, f32[8,384]{1,0:T(8,128)S(1)}) custom-call(s32[3]{0:T(128)S(1)} %add_add_fusion.1.pos_ref, f32[96,384]{1,0:T(8,128)S(1)} %get-tuple-element.30.kept_ref, bf16[112,384]{1,0:T(8,128)(2,1)S(1)} %collective-permute-done.3.msg_ref, f32[8,384]{1,0:T(8,128)S(1)} %get-tuple-element.32.stats_ref, ...), custom_call_target="tpu_custom_call" | custom-call | flops 294912 | bytes 737280 | tf_op jit(solution)/shard_map/pallas_call | solution.py:397
  34.1 2.7 %collective-permute-start.5 = (bf16[112,384]{1,0:T(8,128)(2,1)S(1)}, bf16[112,384]{1,0:T(8,128)(2,1)S(1)}, u32[]{:S(2)}, u32[]{:S(2)}) collective-permute-start(bf16[112,384]{1,0:T(8,128)(2,1)S(1)} %get-tuple-element.36.kept_ref), channel_id=1, source_target_pairs={{0,8},{1,3},{2,10},{3,1},{4,12},{5,7},{6,14},{7,5},{8,0},{9,11},{1... | collective-permute-start | bytes 258056 | tf_op jit(solution)/shard_map/ppermute | solution.py:426
  36.9 1.4 %shard_map.74 = (f32[112,768]{1,0:T(8,128)S(1)}, f32[8,768]{1,0:T(8,128)S(1)}) custom-call(s32[3]{0:T(128)S(1)} %add_add_fusion.pos_ref, bf16[104,768]{1,0:T(8,128)(2,1)S(1)} %get-tuple-element.38.kept_ref, bf16[104,768]{1,0:T(8,128)(2,1)S(1)} %collective-permute-done.6.msg_ref, f32[8,768]{1,0:T(8,128)S(1)} %get-tuple-element.35.own_ref.stats_ref, ...), custom_call_target="tpu_custom_call" | custom-call | flops 66060288 | bytes 1474560 | tf_op jit(solution)/shard_map/pallas_call | solution.py:397
  38.3 1.2 %collective-permute-done.5.msg_ref = bf16[112,384]{1,0:T(8,128)(2,1)S(1)} collective-permute-done((bf16[112,384]{1,0:T(8,128)(2,1)S(1)}, bf16[112,384]{1,0:T(8,128)(2,1)S(1)}, u32[]{:S(2)}, u32[]{:S(2)}) %collective-permute-start.5) | collective-permute-done | bytes 86048 | tf_op jit(solution)/shard_map/ppermute | solution.py:426
  39.6 1.6 %shard_map.75 = f32[112,1152]{1,0:T(8,128)S(1)} custom-call(s32[3]{0:T(128)S(1)} %add_add_fusion.pos_ref, bf16[112,384]{1,0:T(8,128)(2,1)S(1)} %get-tuple-element.36.kept_ref, bf16[112,384]{1,0:T(8,128)(2,1)S(1)} %collective-permute-done.5.msg_ref, f32[8,384]{1,0:T(8,128)S(1)} %get-tuple-element.37.stats_ref, f32[8,768]{1,0:T(8,128)S(1)} %get-tuple-element.39.vec_ref, ...), custom_call_target="tpu_custom_call" | custom-call | flops 66060288 | bytes 1474560 | tf_op jit(solution)/shard_map/pallas_call | solution.py:397
  41.3 1.8 %collective-permute-start.7 = (f16[97,1152]{1,0:T(8,128)(2,1)S(1)}, f16[97,1152]{1,0:T(8,128)(2,1)S(1)}, u32[]{:S(2)}, u32[]{:S(2)}) collective-permute-start(f16[97,1152]{1,0:T(8,128)(2,1)S(1)} %slice_convert_fusion), channel_id=1, source_target_pairs={{0,4},{1,9},{2,6},{3,11},{4,0},{5,13},{6,2},{7,15},{8,12},{9,1},{1... | collective-permute-start | bytes 670472 | tf_op jit(solution)/shard_map/ppermute | solution.py:426
  43.1 0.1 fusion.hot_ref
  43.2 4.6 %collective-permute-done.7 = f16[97,1152]{1,0:T(8,128)(2,1)S(1)} collective-permute-done((f16[97,1152]{1,0:T(8,128)(2,1)S(1)}, f16[97,1152]{1,0:T(8,128)(2,1)S(1)}, u32[]{:S(2)}, u32[]{:S(2)}) %collective-permute-start.7) | collective-permute-done | bytes 223520 | tf_op jit(solution)/shard_map/ppermute | solution.py:426
  47.8 0.1 add_convert_fusion
  47.9 5.3 %collective-permute-start.8 = (f16[97,1152]{1,0:T(8,128)(2,1)S(1)}, f16[97,1152]{1,0:T(8,128)(2,1)S(1)}, u32[]{:S(2)}, u32[]{:S(2)}) collective-permute-start(f16[97,1152]{1,0:T(8,128)(2,1)S(1)} %add_convert_fusion), channel_id=1, source_target_pairs={{0,2},{1,5},{2,0},{3,7},{4,6},{5,1},{6,4},{7,3},{8,10},{9,13},{10,... | collective-permute-start | bytes 670472 | tf_op jit(solution)/shard_map/ppermute | solution.py:426
  53.2 4.1 %collective-permute-done.8 = f16[97,1152]{1,0:T(8,128)(2,1)S(1)} collective-permute-done((f16[97,1152]{1,0:T(8,128)(2,1)S(1)}, f16[97,1152]{1,0:T(8,128)(2,1)S(1)}, u32[]{:S(2)}, u32[]{:S(2)}) %collective-permute-start.8) | collective-permute-done | bytes 223520 | tf_op jit(solution)/shard_map/ppermute | solution.py:426
  57.4 1.1 %shard_map.76 = (f32[97,768]{1,0:T(8,128)S(1)}, f32[97,384]{1,0:T(8,128)S(1)}, f32[200,97]{1,0:T(8,128)S(1)}) custom-call(s32[3]{0:T(128)S(1)} %add_add_fusion.pos_ref, f32[97,1152]{1,0:T(8,128)S(1)} %convert_add_fusion.score_ref, bf16[97,1152]{1,0:T(8,128)(2,1)S(1)} %fusion.1.flag_ref, bf16[200,1152]{1,0:T(8,128)(2,1)S(1)} %fusion.hot_ref), custom_call_target="tpu_custom_call" | custom-call | flops 134092800 | bytes 893952 | tf_op jit(solution)/shard_map/pallas_call | solution.py:397
  58.6 0.5 collective-permute-start.9
  59.1 0.8 %collective-permute-done.10 = f32[200,97]{1,0:T(8,128)S(1)} collective-permute-done((f32[200,97]{1,0:T(8,128)S(1)}, f32[200,97]{1,0:T(8,128)S(1)}, u32[]{:S(2)}, u32[]{:S(2)}) %collective-permute-start.10) | collective-permute-done | bytes 77632 | tf_op jit(solution)/shard_map/ppermute | solution.py:429
  59.9 0.7 %add_bitcast_fusion = f32[97,200]{0,1:T(8,128)} fusion(f32[200,97]{1,0:T(8,128)S(1)} %get-tuple-element.43, f32[200,97]{1,0:T(8,128)S(1)} %collective-permute-done.10), kind=kLoop, calls=%fused_computation.15 | loop fusion | flops 19400 | bytes 232800 | tf_op jit(solution)/shard_map/transpose | solution.py:561
  60.6 0.8 %select_add_fusion = f32[97,768]{1,0:T(8,128)} fusion(f32[97,768]{1,0:T(8,128)S(1)} %get-tuple-element.41, f32[97,384]{1,0:T(8,128)S(1)} %collective-permute-done.9, pred[]{:T(512)S(6)} %eq.28), kind=kLoop, calls=%fused_computation.10 | loop fusion | flops 148992 | bytes 744961 | tf_op jit(solution)/shard_map/add | solution.py:556
  (41 shorter events, 0.6 us)
Async XLA Ops:
  0.6 2.8 %copy-start = (bf16[1024,768]{1,0:T(8,128)(2,1)S(1)}, bf16[1024,768]{1,0:T(8,128)(2,1)}, u32[]{:S(2)}) copy-start(bf16[1024,768]{1,0:T(8,128)(2,1)} %own_ref.3) | copy-start | bytes 4718596
  2.9 16.4 %collective-permute-start = (bf16[1024,384]{1,0:T(8,128)(2,1)}, bf16[1024,384]{1,0:T(8,128)(2,1)}, u32[]{:S(2)}, u32[]{:S(2)}) collective-permute-start(bf16[1024,384]{1,0:T(8,128)(2,1)} %constant_dynamic-slice_fusion.6), channel_id=1, source_target_pairs={{0,1},{1,0},{2,3},{3,2},{4,5},{5,4},{6,7},{7,6},{8,9},{9,8},{10,11... | collective-permute-start | bytes 2359304 | tf_op jit(solution)/shard_map/ppermute | solution.py:429
  3.4 4.9 %copy-start.8 = (s32[1536]{0:T(1024)S(1)}, s32[1536]{0:T(1024)}, u32[]{:S(2)}) copy-start(s32[1536]{0:T(1024)} %param.6) | copy-start | bytes 18436
  3.4 5.7 %copy-start.9 = (s32[1536]{0:T(1024)S(1)}, s32[1536]{0:T(1024)}, u32[]{:S(2)}) copy-start(s32[1536]{0:T(1024)} %param.9) | copy-start | bytes 18436
  3.4 7.7 %copy-start.5 = (s32[97,1536]{1,0:T(8,128)S(1)}, s32[97,1536]{1,0:T(8,128)}, u32[]{:S(2)}) copy-start(s32[97,1536]{1,0:T(8,128)} %param.8) | copy-start | bytes 1787908
  5.8 10.4 %collective-permute-start.2 = (bf16[200,768]{1,0:T(8,128)(2,1)S(1)}, bf16[200,768]{1,0:T(8,128)(2,1)S(1)}, u32[]{:S(2)}, u32[]{:S(2)}) collective-permute-start(bf16[200,768]{1,0:T(8,128)(2,1)S(1)} %get-tuple-element.28), channel_id=1, source_target_pairs={{0,2},{1,5},{2,0},{3,7},{4,6},{5,1},{6,4},{7,3},{8,10},{9,13},{10,... | collective-permute-start | bytes 921608 | tf_op jit(solution)/shard_map/ppermute | solution.py:426
  14.4 1.8 %copy-start.1 = (bf16[112,768]{1,0:T(8,128)(2,1)}, bf16[112,768]{1,0:T(8,128)(2,1)S(1)}, u32[]{:S(2)}) copy-start(bf16[112,768]{1,0:T(8,128)(2,1)S(1)} %constant_dynamic-slice_fusion.5) | copy-start | bytes 516100
  16.1 0.6 %copy-start.3 = (bf16[112,384]{1,0:T(8,128)(2,1)}, bf16[112,384]{1,0:T(8,128)(2,1)S(1)}, u32[]{:S(2)}) copy-start(bf16[112,384]{1,0:T(8,128)(2,1)S(1)} %get-tuple-element.47) | copy-start | bytes 258052
  17.6 5.7 %copy-start.10 = (s32[1536]{0:T(1024)S(1)}, s32[1536]{0:T(1024)}, u32[]{:S(2)}) copy-start(s32[1536]{0:T(1024)} %param.7) | copy-start | bytes 18436
  17.6 6.8 %collective-permute-start.4 = (bf16[104,768]{1,0:T(8,128)(2,1)S(1)}, bf16[104,768]{1,0:T(8,128)(2,1)S(1)}, u32[]{:S(2)}, u32[]{:S(2)}) collective-permute-start(bf16[104,768]{1,0:T(8,128)(2,1)S(1)} %get-tuple-element.34), channel_id=1, source_target_pairs={{0,4},{1,9},{2,6},{3,11},{4,0},{5,13},{6,2},{7,15},{8,12},{9,1},{1... | collective-permute-start | bytes 479240 | tf_op jit(solution)/shard_map/ppermute | solution.py:426
  22.6 8.1 %copy-start.6 = (bf16[112,384]{1,0:T(8,128)(2,1)S(1)}, bf16[112,384]{1,0:T(8,128)(2,1)}, u32[]{:S(2)}) copy-start(bf16[112,384]{1,0:T(8,128)(2,1)} %get-tuple-element.46) | copy-start | bytes 258052
  22.6 8.1 %copy-start.7 = (bf16[112,384]{1,0:T(8,128)(2,1)S(1)}, bf16[112,384]{1,0:T(8,128)(2,1)}, u32[]{:S(2)}) copy-start(bf16[112,384]{1,0:T(8,128)(2,1)} %get-tuple-element.48) | copy-start | bytes 258052
  22.6 5.3 %collective-permute-start.1 = (bf16[208,384]{1,0:T(8,128)(2,1)S(1)}, bf16[208,384]{1,0:T(8,128)(2,1)S(1)}, u32[]{:S(2)}, u32[]{:S(2)}) collective-permute-start(bf16[208,384]{1,0:T(8,128)(2,1)S(1)} %get-tuple-element.25), channel_id=1, source_target_pairs={{0,2},{1,5},{2,0},{3,7},{4,6},{5,1},{6,4},{7,3},{8,10},{9,13},{10,... | collective-permute-start | bytes 479240 | tf_op jit(solution)/shard_map/ppermute | solution.py:426
  25.2 11.7 %collective-permute-start.6 = (bf16[104,768]{1,0:T(8,128)(2,1)S(1)}, bf16[104,768]{1,0:T(8,128)(2,1)S(1)}, u32[]{:S(2)}, u32[]{:S(2)}) collective-permute-start(bf16[104,768]{1,0:T(8,128)(2,1)S(1)} %get-tuple-element.38.kept_ref), channel_id=1, source_target_pairs={{0,8},{1,3},{2,10},{3,1},{4,12},{5,7},{6,14},{7,5},{8,0},{9,11},{1... | collective-permute-start | bytes 479240 | tf_op jit(solution)/shard_map/ppermute | solution.py:426
  28.8 4.6 %collective-permute-start.3 = (bf16[112,384]{1,0:T(8,128)(2,1)S(1)}, bf16[112,384]{1,0:T(8,128)(2,1)S(1)}, u32[]{:S(2)}, u32[]{:S(2)}) collective-permute-start(bf16[112,384]{1,0:T(8,128)(2,1)S(1)} %get-tuple-element.31), channel_id=1, source_target_pairs={{0,4},{1,9},{2,6},{3,11},{4,0},{5,13},{6,2},{7,15},{8,12},{9,1},{1... | collective-permute-start | bytes 258056 | tf_op jit(solution)/shard_map/ppermute | solution.py:426
  34.1 5.4 %collective-permute-start.5 = (bf16[112,384]{1,0:T(8,128)(2,1)S(1)}, bf16[112,384]{1,0:T(8,128)(2,1)S(1)}, u32[]{:S(2)}, u32[]{:S(2)}) collective-permute-start(bf16[112,384]{1,0:T(8,128)(2,1)S(1)} %get-tuple-element.36.kept_ref), channel_id=1, source_target_pairs={{0,8},{1,3},{2,10},{3,1},{4,12},{5,7},{6,14},{7,5},{8,0},{9,11},{1... | collective-permute-start | bytes 258056 | tf_op jit(solution)/shard_map/ppermute | solution.py:426
  39.6 13.6 %copy-start.2 = (bf16[112,768]{1,0:T(8,128)(2,1)S(1)}, bf16[112,768]{1,0:T(8,128)(2,1)}, u32[]{:S(2)}) copy-start(bf16[112,768]{1,0:T(8,128)(2,1)} %copy-done.1) | copy-start | bytes 516100
  39.6 13.6 %copy-start.4 = (bf16[112,384]{1,0:T(8,128)(2,1)S(1)}, bf16[112,384]{1,0:T(8,128)(2,1)}, u32[]{:S(2)}) copy-start(bf16[112,384]{1,0:T(8,128)(2,1)} %copy-done.3) | copy-start | bytes 258052
  41.3 6.5 %collective-permute-start.7 = (f16[97,1152]{1,0:T(8,128)(2,1)S(1)}, f16[97,1152]{1,0:T(8,128)(2,1)S(1)}, u32[]{:S(2)}, u32[]{:S(2)}) collective-permute-start(f16[97,1152]{1,0:T(8,128)(2,1)S(1)} %slice_convert_fusion), channel_id=1, source_target_pairs={{0,4},{1,9},{2,6},{3,11},{4,0},{5,13},{6,2},{7,15},{8,12},{9,1},{1... | collective-permute-start | bytes 670472 | tf_op jit(solution)/shard_map/ppermute | solution.py:426
  47.9 9.5 %collective-permute-start.8 = (f16[97,1152]{1,0:T(8,128)(2,1)S(1)}, f16[97,1152]{1,0:T(8,128)(2,1)S(1)}, u32[]{:S(2)}, u32[]{:S(2)}) collective-permute-start(f16[97,1152]{1,0:T(8,128)(2,1)S(1)} %add_convert_fusion), channel_id=1, source_target_pairs={{0,2},{1,5},{2,0},{3,7},{4,6},{5,1},{6,4},{7,3},{8,10},{9,13},{10,... | collective-permute-start | bytes 670472 | tf_op jit(solution)/shard_map/ppermute | solution.py:426
  58.5 1.4 %collective-permute-start.10 = (f32[200,97]{1,0:T(8,128)S(1)}, f32[200,97]{1,0:T(8,128)S(1)}, u32[]{:S(2)}, u32[]{:S(2)}) collective-permute-start(f32[200,97]{1,0:T(8,128)S(1)} %get-tuple-element.43), channel_id=1, source_target_pairs={{0,1},{1,0},{2,3},{3,2},{4,5},{5,4},{6,7},{7,6},{8,9},{9,8},{10,11... | collective-permute-start | bytes 232808 | tf_op jit(solution)/shard_map/ppermute | solution.py:429
  58.6 2.0 %collective-permute-start.9 = (f32[97,384]{1,0:T(8,128)S(1)}, f32[97,384]{1,0:T(8,128)S(1)}, u32[]{:S(2)}, u32[]{:S(2)}) collective-permute-start(f32[97,384]{1,0:T(8,128)S(1)} %get-tuple-element.42), channel_id=1, source_target_pairs={{0,1},{1,0},{2,3},{3,2},{4,5},{5,4},{6,7},{7,6},{8,9},{9,8},{10,11... | collective-permute-start | bytes 446984 | tf_op jit(solution)/shard_map/ppermute | solution.py:429

commit v3 on v2

--- a/solution.py
+++ b/solution.py
@@ -13,7 +13,7 @@
 F32 = jnp.float32
 BF16 = jnp.bfloat16
 CORE_ONE_ORDER = [1, 2, 0]
-VMEM_LIMIT = 48 * 1024 * 1024
+VMEM_LIMIT = 20 * 1024 * 1024
 
 
 STEP = 48
@@ -92,10 +92,6 @@
     return jnp.where(
         col < half // 2, jnp.where(row > col, a_rows * c_b, b_rows * c_a), a2_rows * c_b3
     )
-
-
-def dot_tt(left, right):
-    return lax.dot_general(left, right, (((0,), (0,)), ((), ())), preferred_element_type=F32)
 
 
 def dot_n(left, right):
@@ -121,72 +117,81 @@
     return jnp.concatenate(list(rows) + [rows[-1]] * (8 - len(rows)), axis=0)
 
 
-def halved(pos_ref, keep_ref, send_ref, value):
+def halved(bit, keep_ref, send_ref, value):
     part = keep_ref.shape[0]
-    bit = pos_ref[1]
     for k in range(0, part, STEP):
         send_ref[k : k + STEP, :] = value(pl.multiple_of((1 - bit) * part + k, 16)).astype(BF16)
         keep_ref[k : k + STEP, :] = value(pl.multiple_of(bit * part + k, 16))
 
 
-def own_gram_kernel(pos_ref, own_ref, keep_ref, send_ref, stats_ref, full_ref, col_ref):
+def own_gram_kernel(pos_ref, own_ref, keep_ref, send_ref, stats_ref, turned_ref, piece_ref, full_ref, col_ref):
     half = own_ref.shape[1] // 2
-    left, right = own_ref[:, :half], own_ref[:, half:]
+
+    @pl.when(pos_ref[0] == 0)
+    def _():
+        piece_ref[...] = own_ref[:, half:]
+
+    @pl.when(pos_ref[0] != 0)
+    def _():
+        piece_ref[...] = own_ref[:, :half]
+
+    turned_ref[...] = own_ref[...].T
     sums, squares, shift = moments(own_ref)
     stats_ref[...] = eight(sums, squares, shift)
     to_column(shift, col_ref)
-    full_ref[:, :half] = dot_tt(left, right)
+    left, right = turned_ref[:half, :], turned_ref[half:, :]
+    full_ref[:, :half] = dot_n(left, own_ref[:, half:])
     row, col = index_parts(0, half, half)
-    full_ref[:, half:] = jnp.where(row < col, dot_tt(left, left), dot_tt(right, right))
+    full_ref[:, half:] = jnp.where(row < col, dot_n(left, own_ref[:, :half]), dot_n(right, own_ref[:, half:]))
     cols = own_cols(shift, half)
 
     def value(start):
         products = own_products(col_ref, cols, start, *index_parts(start, STEP, half))
         return full_ref[pl.ds(start, STEP), :] - jnp.concatenate(products, axis=1)
 
-    halved(pos_ref, keep_ref, send_ref, value)
+    halved(pos_ref[1], keep_ref, send_ref, value)
     send_ref[keep_ref.shape[0] :, :] = coded(jnp.concatenate([sums, squares], axis=0))
 
 
-def cross_gram_kernel(pos_ref, own_ref, there_ref, own_stats_ref, keep_ref, send_ref, stats_ref, full_ref, col_ref):
+def cross_gram_kernel(pos_ref, turned_ref, there_ref, own_stats_ref, keep_ref, send_ref, stats_ref, full_ref, col_ref, side_ref):
     half = there_ref.shape[1]
+    quarter = half // 2
     core = pos_ref[0]
     first = core == 0
-    left, right, there = own_ref[:, :half], own_ref[:, half:], there_ref[...]
+    row, col = index_parts(0, half, half)
+
+    @pl.when(first)
+    def _():
+        full_ref[:, :half] = dot_n(turned_ref[:half, :], there_ref[...])
+        full_ref[:, half:] = pltpu.roll(dot_n(turned_ref[half:, :], there_ref[...]), quarter, 1)
+
+    @pl.when(jnp.logical_not(first))
+    def _():
+        side_ref[...] = there_ref[...].T
+        full_ref[:, :half] = dot_t(side_ref[...], turned_ref[half:, :])
+        full_ref[:, half:] = dot_t(side_ref[...], turned_ref[:half, :])
+
     sums, squares, shift = moments(there_ref)
     shift = jnp.concatenate([own_stats_ref[2:3, :], shift], axis=1)
     to_column(shift, col_ref)
-    row, col = index_parts(0, half, half)
     a_shift, b_shift = cross_halves(shift, first, half)
-
-    def cross(a_cols, b_cols, a2_cols, b3_cols, turn):
-        straight = dot_tt(a_cols, b_cols)
-        level = jnp.sum(jnp.where(row == col, straight, 0.0), axis=0, keepdims=True)
-        stats = jnp.concatenate([sums, squares, level - a_shift * b_shift], axis=0)
-        stats_ref[...] = eight(stats[0:1], stats[1:2], stats[2:3])
-        send_ref[keep_ref.shape[0] :, :] = coded(jnp.concatenate([stats, stats[2:3]], axis=0))
-        folded = pltpu.roll(dot_tt(b_cols[:, half // 2 :], a_cols), half // 2, 1)
-        folded = jnp.concatenate([folded, folded], axis=0)
-        apart = dot_tt(a2_cols, b3_cols)
-        if turn:
-            apart = pltpu.roll(apart, half // 2, 1)
-        full_ref[...] = jnp.where(col < half // 2, jnp.where(row > col, straight, folded), apart)
-
-    @pl.when(first)
-    def _():
-        cross(left, there, right, there, True)
-
-    @pl.when(jnp.logical_not(first))
-    def _():
-        cross(there, right, there, left, False)
-
+    straight = full_ref[:, :half]
+    level = jnp.sum(jnp.where(row == col, straight, 0.0), axis=0, keepdims=True) - a_shift * b_shift
+    stats_ref[...] = eight(sums, squares, level)
+    send_ref[keep_ref.shape[0] :, :] = coded(jnp.concatenate([sums, squares, level, level], axis=0))
+    corner = full_ref[half - 256 : half, half - 256 : half].T[256 - quarter :, :]
+    corner = pltpu.roll(corner, quarter, 1)[:, :quarter]
+    corner = jnp.concatenate([corner, corner], axis=0)
+    folded = jnp.concatenate([corner, jnp.zeros((half, half - quarter), F32)], axis=1)
+    apart = full_ref[:, half:]
+    full_ref[:, :half] = jnp.where(col < quarter, jnp.where(row > col, straight, folded), apart)
     cols = cross_cols(shift, first, half)
 
     def value(start):
         products = cross_products(col_ref, cols, core, start, *index_parts(start, STEP, half))
-        return full_ref[pl.ds(start, STEP), :] - products
-
-    halved(pos_ref, keep_ref, send_ref, value)
+        return full_ref[pl.ds(start, STEP), :half] - products
+
+    halved(pos_ref[1], keep_ref, send_ref, value)
 
 
 def own_merged(msg_ref, stats_ref, rows, samples):
@@ -213,7 +218,7 @@
 
 def passed_on(pos_ref, keep_ref, send_ref, value, split):
     if split:
-        halved(pos_ref, keep_ref, send_ref, value)
+        halved(pos_ref[2], keep_ref, send_ref, value)
         return keep_ref.shape[0]
     rows = send_ref.shape[0] // STEP * STEP
     for k in range(0, rows, STEP):
@@ -230,7 +235,7 @@
     out_ref[...] = eight(sums, squares, shift)
     to_column(shift, col_ref)
     cols = own_cols(shift, half)
-    base = pos_ref[2]
+    base = pos_ref[3] if split else pos_ref[4]
 
     def value(offset):
         start = base + offset
@@ -254,7 +259,7 @@
     out_ref[...] = eight(sums, squares, level)
     to_column(shift, col_ref)
     cols = cross_cols(shift, first, half)
-    base = pos_ref[2]
+    base = pos_ref[3] if split else pos_ref[4]
 
     def value(offset):
         start = base + offset
@@ -291,7 +296,7 @@
     to_column(limit_ref[:1, : 2 * half], lim_ref)
     cols, scales = own_cols(shift, half), own_cols(scale, half)
     right_lim = limit_ref[:1, half : 2 * half]
-    base = pos_ref[2]
+    base = pos_ref[4]
     for k in range(0, rows, STEP):
         start = base + k
         row, col = index_parts(start, STEP, half)
@@ -334,7 +339,7 @@
     to_column(limit, lim_ref)
     cols, scales = cross_cols(shift, first, half), cross_cols(scale, first, half)
     _, late_lim, _ = cross_cols(limit, first, half)
-    base = pos_ref[2]
+    base = pos_ref[4]
     for k in range(0, rows, STEP):
         start = base + k
         row, col = index_parts(start, STEP, half)
@@ -376,8 +381,59 @@
     out_ref[:, 2 * half :] = pick(first, out_b + pltpu.roll(out_b3, quarter, 1), out_a + out_a2)
 
 
-def block_kernel(pos_ref, score_ref, flag_ref, hot_ref, own_ref, msg_ref, sum_ref):
+def local_kernel(pos_ref, annot_ref, chrom_ref, reach_ref, ids_ref, flag_ref, cross_ref, sub_ref, limit_ref, block_ref):
+    half = annot_ref.shape[1] // 4
+    first = pos_ref[0] == 0
+    base = pos_ref[4]
+    flags = annot_ref[...].astype(F32)
+
+    def quarters(x):
+        return [x[:, k * half : (k + 1) * half] for k in range(4)]
+
+    def local(x):
+        one, two, three, four = quarters(x)
+        return pick(first, one, three), pick(first, two, four), pick(first, three, two)
+
+    left, right, there = local(flags)
+    for k, x in enumerate((left, right, there)):
+        flag_ref[:, k * half : (k + 1) * half] = x.astype(BF16)
+    a_cols, b_cols, a2_cols = pick(first, left, there), pick(first, there, right), pick(first, right, there)
+    b3_cols = pick(first, pltpu.roll(there, half // 2, 1), left)
+    for k, x in enumerate((a_cols, b_cols, pltpu.roll(a_cols, half // 2, 1), b3_cols)):
+        cross_ref[:, k * half : (k + 1) * half] = x.astype(BF16)
+    back = lax.rem(half - base, half)
+    late = lax.rem(half + half // 2 - base, half)
+    for k, (x, turn) in enumerate(((left, back), (right, back), (a_cols, back), (a2_cols, back), (b_cols, late))):
+        sub_ref[:, k * 128 : (k + 1) * 128] = pltpu.roll(x, turn, 1)[:, :128].astype(BF16)
+
+    def line(ref):
+        return jnp.concatenate([ref[k : k + 1, :] for k in range(ref.shape[0])], axis=1).astype(F32)
+
+    chrom, reach = line(chrom_ref), line(reach_ref)
+    ends = [jnp.sum((chrom <= k).astype(F32), axis=1, keepdims=True) for k in (1, 2, 3)]
+    last = jnp.where(chrom == 1, ends[0], jnp.where(chrom == 2, ends[1], ends[2]))
+    place = lax.broadcasted_iota(jnp.int32, chrom.shape, 1).astype(F32)
+    limit = jnp.concatenate(local(jnp.minimum(reach, last - 1.0 - place)), axis=1)
+    limit_ref[...] = jnp.broadcast_to(limit, limit_ref.shape)
+    block = jnp.concatenate(local(line(ids_ref)), axis=1)
+    block_ref[...] = jnp.broadcast_to(block, block_ref.shape)
+
+
+def join_kernel(pos_ref, own_ref, other_ref, sums_ref, there_ref, score_ref, out_ref):
+    half = other_ref.shape[1]
+    first = pos_ref[0] == 0
+    nothing = jnp.zeros(other_ref.shape, F32)
+    other = other_ref[...]
+    score_ref[:, :half] = own_ref[:, :half] + pick(first, nothing, other)
+    score_ref[:, half:] = own_ref[:, half:] + pick(first, other, nothing)
+    out_ref[...] = sums_ref[...] + there_ref[...]
+
+
+def block_kernel(pos_ref, score_ref, flag_ref, block_ref, own_ref, msg_ref, sum_ref):
     slab = own_ref.shape[1]
+    blocks = block_ref[:1, :]
+    number = lax.broadcasted_iota(jnp.int32, (sum_ref.shape[0], blocks.shape[1]), 0).astype(F32)
+    hot = jnp.where(number == blocks, 1.0, 0.0).astype(BF16)
     own = score_ref[:, :slab] + flag_ref[:, :slab].astype(F32)
     other = score_ref[:, slab:]
     own_ref[...] = own
@@ -387,7 +443,6 @@
     left = scores - high.astype(F32)
     middle = left.astype(BF16)
     low = (left - middle.astype(F32)).astype(BF16)
-    hot = hot_ref[...]
     sum_ref[...] = dot_t(hot, high) + dot_t(hot, middle) + dot_t(hot, low)
 
 
@@ -428,48 +483,33 @@
     def across(x):
         return lax.ppermute(x, "genome", [(0, 1), (1, 0)])
 
-    def scalars(*values):
-        return jnp.stack([jnp.asarray(v, jnp.int32) for v in values])
-
     def shape(rows, cols, dtype):
         return jax.ShapeDtypeStruct((rows, cols), dtype)
 
-    there = across(lax.dynamic_slice_in_dim(genotypes, (1 - core) * half, half, 1))
     base = bit_at[0] * quarter + bit_at[1] * (quarter // 2)
     rows = quarter // 2
 
-    own_at = core * slab
-    there_at = (1 - core) * slab + core * half
-    a_at, b_at = core * half, slab + core * half
-    b3_at = slab + core * quarter
-
-    def local(x):
-        axis = x.ndim - 1
-        parts_of = [(own_at, slab), (there_at, half)]
-        return jnp.concatenate([lax.dynamic_slice_in_dim(x, at, n, axis) for at, n in parts_of], axis=axis)
-
-    ends = jnp.sum((chromosome[None, :] <= jnp.arange(1, 4)[:, None]).astype(jnp.int32), axis=1)
-    last = jnp.where(chromosome == 1, ends[0], jnp.where(chromosome == 2, ends[1], ends[2]))
-    limit = local(jnp.minimum(reach, last - 1 - jnp.arange(snps))).astype(F32)
-    limit = jnp.broadcast_to(limit[None, :], (8, width))
+    where = jnp.stack([core, bit_at[0], bit_at[1], bit_at[0] * quarter, base]).astype(jnp.int32)
     annot = annotation.shape[0]
-    annot_rows = -(-annot // 16) * 16
-    flags_all = jnp.pad(annotation.astype(BF16), ((0, annot_rows - annot), (0, 0)))
-
-    def columns_of(at, n):
-        return lax.dynamic_slice_in_dim(flags_all, at, n, 1)
-
-    none = jnp.zeros((annot_rows, quarter), BF16)
-    flags = local(flags_all)
-    flags_cross = jnp.concatenate(
-        [columns_of(a_at, half), columns_of(b_at, half), columns_of(a_at + quarter, quarter), none, none, columns_of(b3_at, quarter)],
-        axis=1,
-    )
-    padded = jnp.pad(flags_all, ((0, 0), (0, slab)))
-    starts = (own_at, own_at + half, a_at, half, b_at + quarter)
-    subs = jnp.concatenate([lax.dynamic_slice_in_dim(padded, at + base, 128, 1) for at in starts], axis=1)
+
+    def tiles(x):
+        return x.reshape(-1, 128)
+
+    flags, flags_cross, subs, limit, ids = call(
+        local_kernel,
+        (where, annotation, tiles(chromosome), tiles(reach), tiles(blocks)),
+        (
+            shape(annot, width, BF16),
+            shape(annot, 4 * half, BF16),
+            shape(annot, 5 * 128, BF16),
+            shape(8, width, F32),
+            shape(8, width, F32),
+        ),
+        [],
+        annot * snps * 10,
+        annot * snps * 8,
+    )
     hot_rows = -(-NBLK // 8) * 8
-    hot = (jnp.arange(hot_rows)[:, None] == local(blocks)[None, :]).astype(BF16)
 
     own_column = pltpu.VMEM((slab, 128), F32)
     column = pltpu.VMEM((width + quarter, 128), F32)
@@ -478,21 +518,21 @@
         kept_shape = (shape(kept, cols, F32),) if kept else ()
         return kept_shape + (shape(sent + stat_rows, cols, BF16), shape(8, cols, F32))
 
-    where = scalars(core, bit_at[0], 0)
-    keep_a, send_a, stats_a = call(
+    keep_a, send_a, stats_a, turned, piece = call(
         own_gram_kernel,
         (where, genotypes),
-        outputs(quarter, quarter, slab, 8),
+        outputs(quarter, quarter, slab, 8) + (shape(slab, count, BF16), shape(count, half, BF16)),
         [pltpu.VMEM((half, slab), F32), own_column],
         2 * count * half * half * 3,
         count * slab * 2,
     )
+    there = across(piece)
     msg_a = exchange(send_a, 0)
     keep_b, send_b, stats_b = call(
         cross_gram_kernel,
-        (where, genotypes, there, stats_a),
+        (where, turned, there, stats_a),
         outputs(quarter, quarter, half, 16),
-        [pltpu.VMEM((half, half), F32), column],
+        [pltpu.VMEM((half, slab), F32), column, pltpu.VMEM((half, count), BF16)],
         2 * count * half * half * 3,
         count * slab * 2,
     )
@@ -500,7 +540,7 @@
     samples = float(count)
     for t in range(1, bits):
         split = t == 1
-        where = scalars(core, bit_at[t], bit_at[0] * quarter if split else base)
+        msg_a, send_b = lax.optimization_barrier((msg_a, send_b)) if split else (msg_a, send_b)
         *kept_a, send_a, stats_a = call(
             functools.partial(own_merge_kernel, samples=samples, split=split),
             (where, keep_a, msg_a, stats_a),
@@ -522,43 +562,42 @@
         keep_a = kept_a[0] if split else send_a
         keep_b = kept_b[0] if split else send_b
         samples = 2 * samples
-    where = scalars(core, 0, base)
     scores_a, vectors = call(
         functools.partial(own_score_kernel, samples=samples),
         (where, keep_a, msg_a, stats_a, limit, flags, subs),
-        (shape(annot_rows, slab, F32), shape(8, slab, F32)),
+        (shape(annot, slab, F32), shape(8, slab, F32)),
         [own_column] * 3 + [pltpu.VMEM((rows, half), BF16)] * 2,
-        2 * annot_rows * half * rows * 8,
+        2 * annot * half * rows * 8,
         rows * slab * 20,
     )
     partial = call(
         functools.partial(cross_score_kernel, samples=samples),
         (where, keep_b, msg_b, stats_b, vectors, limit, flags_cross, subs, scores_a),
-        shape(annot_rows, width, F32),
+        shape(annot, width, F32),
         [column] * 3 + [pltpu.VMEM((rows, half), BF16)],
-        2 * annot_rows * half * rows * 8,
+        2 * annot * half * rows * 8,
         rows * slab * 20,
     )
-    partial = partial[:annot]
     for t in (1, 0):
         rounded = partial.astype(jnp.float16)
         partial = rounded.astype(F32) + exchange(rounded, t).astype(F32)
     own, other, sums = call(
         block_kernel,
-        (where, partial, flags[:annot], hot),
+        (where, partial, flags, ids),
         (shape(annot, slab, F32), shape(annot, half, F32), shape(hot_rows, annot, F32)),
         [],
         2 * annot * width * hot_rows * 3,
         annot * width * 8,
     )
-    arrived, sums_there = across(other), across(sums)
-    nothing = jnp.zeros_like(arrived)
-    ld_scores = own + jnp.where(
-        core == 0,
-        jnp.concatenate([nothing, arrived], axis=1),
-        jnp.concatenate([arrived, nothing], axis=1),
-    )
-    return (ld_scores, (sums + sums_there)[:NBLK].T)
+    ld_scores, block_sums = call(
+        join_kernel,
+        (where, own, across(other), sums, across(sums)),
+        (shape(annot, slab, F32), shape(hot_rows, annot, F32)),
+        [],
+        annot * width,
+        annot * width * 8,
+    )
+    return (ld_scores, block_sums[:NBLK].T)
 
 
 def solution(mesh):

time: 61.7 us -> 50.1 us (0.81)
  local copies, waits for them, and re-layouts: 9.05 us -> 1.52 us
  other arithmetic: 4.83 us -> 0.17 us
  starting transfers between devices: 20.2 us -> 18.1 us
  waiting for transfers between devices: 13.3 us -> 15 us
  Pallas kernels: 13.1 us -> 14.3 us
    dynamic_slice x8 -> x0, local copies, waits for them, and re-layouts: 6.22 us -> none  [the longest x2 2.74 us: columns_of(): return lax.dynamic_slice_in_dim(flags_all, at, n, 1)]
    ppermute x8, starting transfers between devices: 19.2 us -> 17 us  [exchange(): return lax.ppermute(x, ('samples', 'genome'), route)]
    min x1 -> x0, other arithmetic: 1.86 us -> none  [body(): limit = local(jnp.minimum(reach, last - 1 - jnp.arange(snps))).astype(F32)]
    ppermute x8, waiting for transfers between devices: 12.5 us -> 14 us  [exchange(): return lax.ppermute(x, ('samples', 'genome'), route)]
    pallas_call x9 -> x11, Pallas kernels: 13.1 us -> 14.3 us  [call(): pl.pallas_call(kernel, out_shape=outputs, in_specs=[smem] + [vmem] * (len...]
    pad x1 -> x0, local copies, waits for them, and re-layouts: 0.99 us -> none  [body(): jnp.pad(annotation.astype(BF16), ((0, annot_rows - annot), (0, 0)))]
    convert_element_type x3 -> x0, other arithmetic: 0.85 us -> none  [the longest x1 0.76 us: body(): annotation.astype(BF16)]
    add x2 -> x0, other arithmetic: 0.76 us -> none  [the longest x1 0.76 us: body(): own + jnp.where(core == 0, jnp.concatenate([nothing, arrived], axis=1), j...]
  transfers between devices with their start and end apart: 11 -> 11, of which waited for: 5 -> 7; matrix products, arithmetic and copies ran while one was open for 17% -> 0% of each run, Pallas kernels for 17% -> 16%
where the time goes in v3:
time: 50.1 us; the launch traced here: 49.9 us
  starting transfers between devices  18.1 us (36%)
  waiting for transfers between devices  15 us (30%)
  Pallas kernels  14.3 us (29%)
  local copies, waits for them, and re-layouts  1.52 us (3%)
  between operations  0.79 us (2%)
    ppermute x8, starting transfers between devices, exchange(): return lax.ppermute(x, ('samples', 'genome'), route)  17 us
    pallas_call x11, Pallas kernels, call(): pl.pallas_call(kernel, out_shape=outputs, in_specs=[smem] + [vmem] * (len...  14.3 us
    ppermute x8, waiting for transfers between devices, exchange(): return lax.ppermute(x, ('samples', 'genome'), route)  14 us
    unnamed x10, local copies, waits for them, and re-layouts  1.43 us
    ppermute x3, starting transfers between devices, across(): return lax.ppermute(x, 'genome', [(0, 1), (1, 0)])  1.09 us
    ppermute x3, waiting for transfers between devices, across(): return lax.ppermute(x, 'genome', [(0, 1), (1, 0)])  1.03 us
  transfers between devices with their start and end apart: 11, of which 7 were waited for; matrix products, arithmetic and copies ran while one was open for 0% of the time, Pallas kernels for 16%

profile of v3, /device:TPU:0, one launch (start us, length us, event | category | flops | bytes accessed | tf_op | source)
XLA Modules:
  0.0 49.9 jit_solution(14252961839271871183)
XLA Ops:
  0.6 0.1 stack.23.pos_ref
  0.7 0.0 copy-start.4
  0.7 1.4 %copy-done.4 = bf16[1024,768]{1,0:T(8,128)(2,1)S(1)} copy-done((bf16[1024,768]{1,0:T(8,128)(2,1)S(1)}, bf16[1024,768]{1,0:T(8,128)(2,1)}, u32[]{:S(2)}) %copy-start.4) | copy-done | bytes 1572888
  2.1 2.5 %shard_map.68 = (f32[192,768]{1,0:T(8,128)S(1)}, bf16[200,768]{1,0:T(8,128)(2,1)S(1)}, f32[8,768]{1,0:T(8,128)S(1)}, bf16[768,1024]{1,0:T(8,128)(2,1)S(1)}, bf16[1024,384]{1,0:T(8,128)(2,1)S(1)}) custom-call(s32[5]{0:T(128)S(1)} %stack.23.pos_ref, bf16[1024,768]{1,0:T(8,128)(2,1)S(1)} %copy-done.4), custom_call_target="tpu_custom_call" | custom-call | flops 905969664 | bytes 1572864 | tf_op jit(solution)/shard_map/pallas_call | solution.py:452
  4.6 0.5 %collective-permute-start = (bf16[1024,384]{1,0:T(8,128)(2,1)S(1)}, bf16[1024,384]{1,0:T(8,128)(2,1)S(1)}, u32[]{:S(2)}, u32[]{:S(2)}) collective-permute-start(bf16[1024,384]{1,0:T(8,128)(2,1)S(1)} %get-tuple-element.34), channel_id=1, source_target_pairs={{0,1},{1,0},{2,3},{3,2},{4,5},{5,4},{6,7},{7,6},{8,9},{9,8},{10,11... | collective-permute-start | bytes 2359304 | tf_op jit(solution)/shard_map/ppermute | solution.py:484
  5.1 2.6 %collective-permute-start.2 = (bf16[200,768]{1,0:T(8,128)(2,1)S(1)}, bf16[200,768]{1,0:T(8,128)(2,1)S(1)}, u32[]{:S(2)}, u32[]{:S(2)}) collective-permute-start(bf16[200,768]{1,0:T(8,128)(2,1)S(1)} %get-tuple-element.40), channel_id=1, source_target_pairs={{0,2},{1,5},{2,0},{3,7},{4,6},{5,1},{6,4},{7,3},{8,10},{9,13},{10,... | collective-permute-start | bytes 921608 | tf_op jit(solution)/shard_map/ppermute | solution.py:481
  7.7 0.0 collective-permute-done.there_ref
  7.7 2.2 %shard_map.69 = (f32[192,384]{1,0:T(8,128)S(1)}, bf16[208,384]{1,0:T(8,128)(2,1)S(1)}, f32[8,384]{1,0:T(8,128)S(1)}) custom-call(s32[5]{0:T(128)S(1)} %stack.23.pos_ref, bf16[768,1024]{1,0:T(8,128)(2,1)S(1)} %get-tuple-element.33.turned_ref, bf16[1024,384]{1,0:T(8,128)(2,1)S(1)} %collective-permute-done.there_ref, ...), custom_call_target="tpu_custom_call" | custom-call | flops 905969664 | bytes 1572864 | tf_op jit(solution)/shard_map/pallas_call | solution.py:452
  9.9 0.0 copy-start
  9.9 0.0 copy-start.1
  9.9 0.0 copy-start.2
  9.9 0.0 copy-start.3
  10.0 2.3 %collective-permute-start.1 = (bf16[208,384]{1,0:T(8,128)(2,1)S(1)}, bf16[208,384]{1,0:T(8,128)(2,1)S(1)}, u32[]{:S(2)}, u32[]{:S(2)}) collective-permute-start(bf16[208,384]{1,0:T(8,128)(2,1)S(1)} %get-tuple-element.37), channel_id=1, source_target_pairs={{0,2},{1,5},{2,0},{3,7},{4,6},{5,1},{6,4},{7,3},{8,10},{9,13},{10,... | collective-permute-start | bytes 479240 | tf_op jit(solution)/shard_map/ppermute | solution.py:481
  12.2 0.3 collective-permute-done.2.msg_ref
  12.5 0.8 %shard_map.70 = (f32[96,768]{1,0:T(8,128)S(1)}, bf16[104,768]{1,0:T(8,128)(2,1)S(1)}, f32[8,768]{1,0:T(8,128)S(1)}) custom-call(s32[5]{0:T(128)S(1)} %stack.23.pos_ref, f32[192,768]{1,0:T(8,128)S(1)} %get-tuple-element.39.kept_ref, bf16[200,768]{1,0:T(8,128)(2,1)S(1)} %collective-permute-done.2.msg_ref, f32[8,768]{1,0:T(8,128)S(1)} %get-tuple-element.35.own_stats_ref.stats_ref), custom_call_target="tpu_custom_call" | custom-call | flops 589824 | bytes 1474560 | tf_op jit(solution)/shard_map/pallas_call | solution.py:452
  13.4 2.2 %collective-permute-start.4 = (bf16[104,768]{1,0:T(8,128)(2,1)S(1)}, bf16[104,768]{1,0:T(8,128)(2,1)S(1)}, u32[]{:S(2)}, u32[]{:S(2)}) collective-permute-start(bf16[104,768]{1,0:T(8,128)(2,1)S(1)} %get-tuple-element.47), channel_id=1, source_target_pairs={{0,4},{1,9},{2,6},{3,11},{4,0},{5,13},{6,2},{7,15},{8,12},{9,1},{1... | collective-permute-start | bytes 479240 | tf_op jit(solution)/shard_map/ppermute | solution.py:481
  15.5 0.0 collective-permute-done.1.msg_ref
  15.5 0.8 %shard_map.71 = (f32[96,384]{1,0:T(8,128)S(1)}, bf16[112,384]{1,0:T(8,128)(2,1)S(1)}, f32[8,384]{1,0:T(8,128)S(1)}) custom-call(s32[5]{0:T(128)S(1)} %stack.23.pos_ref, f32[192,384]{1,0:T(8,128)S(1)} %get-tuple-element.36.kept_ref, bf16[208,384]{1,0:T(8,128)(2,1)S(1)} %collective-permute-done.1.msg_ref, f32[8,384]{1,0:T(8,128)S(1)} %get-tuple-element.38.stats_ref, ...), custom_call_target="tpu_custom_call" | custom-call | flops 294912 | bytes 737280 | tf_op jit(solution)/shard_map/pallas_call | solution.py:452
  16.4 2.1 %collective-permute-start.3 = (bf16[112,384]{1,0:T(8,128)(2,1)S(1)}, bf16[112,384]{1,0:T(8,128)(2,1)S(1)}, u32[]{:S(2)}, u32[]{:S(2)}) collective-permute-start(bf16[112,384]{1,0:T(8,128)(2,1)S(1)} %get-tuple-element.44), channel_id=1, source_target_pairs={{0,4},{1,9},{2,6},{3,11},{4,0},{5,13},{6,2},{7,15},{8,12},{9,1},{1... | collective-permute-start | bytes 258056 | tf_op jit(solution)/shard_map/ppermute | solution.py:481
  18.5 1.5 %collective-permute-done.4.msg_ref = bf16[104,768]{1,0:T(8,128)(2,1)S(1)} collective-permute-done((bf16[104,768]{1,0:T(8,128)(2,1)S(1)}, bf16[104,768]{1,0:T(8,128)(2,1)S(1)}, u32[]{:S(2)}, u32[]{:S(2)}) %collective-permute-start.4) | collective-permute-done | bytes 159776 | tf_op jit(solution)/shard_map/ppermute | solution.py:481
  20.0 0.8 %shard_map.72 = (bf16[104,768]{1,0:T(8,128)(2,1)S(1)}, f32[8,768]{1,0:T(8,128)S(1)}) custom-call(s32[5]{0:T(128)S(1)} %stack.23.pos_ref, f32[96,768]{1,0:T(8,128)S(1)} %get-tuple-element.46.kept_ref, bf16[104,768]{1,0:T(8,128)(2,1)S(1)} %collective-permute-done.4.msg_ref, f32[8,768]{1,0:T(8,128)S(1)} %get-tuple-element.42.own_ref.stats_ref), custom_call_target="tpu_custom_call" | custom-call | flops 589824 | bytes 1474560 | tf_op jit(solution)/shard_map/pallas_call | solution.py:452
  20.8 2.6 %collective-permute-start.6 = (bf16[104,768]{1,0:T(8,128)(2,1)S(1)}, bf16[104,768]{1,0:T(8,128)(2,1)S(1)}, u32[]{:S(2)}, u32[]{:S(2)}) collective-permute-start(bf16[104,768]{1,0:T(8,128)(2,1)S(1)} %get-tuple-element.51.kept_ref), channel_id=1, source_target_pairs={{0,8},{1,3},{2,10},{3,1},{4,12},{5,7},{6,14},{7,5},{8,0},{9,11},{1... | collective-permute-start | bytes 479240 | tf_op jit(solution)/shard_map/ppermute | solution.py:481
  23.3 0.0 collective-permute-done.3.msg_ref
  23.3 0.8 %shard_map.73 = (bf16[112,384]{1,0:T(8,128)(2,1)S(1)}, f32[8,384]{1,0:T(8,128)S(1)}) custom-call(s32[5]{0:T(128)S(1)} %stack.23.pos_ref, f32[96,384]{1,0:T(8,128)S(1)} %get-tuple-element.43.kept_ref, bf16[112,384]{1,0:T(8,128)(2,1)S(1)} %collective-permute-done.3.msg_ref, f32[8,384]{1,0:T(8,128)S(1)} %get-tuple-element.45.stats_ref, ...), custom_call_target="tpu_custom_call" | custom-call | flops 294912 | bytes 737280 | tf_op jit(solution)/shard_map/pallas_call | solution.py:452
  24.2 1.1 %collective-permute-start.5 = (bf16[112,384]{1,0:T(8,128)(2,1)S(1)}, bf16[112,384]{1,0:T(8,128)(2,1)S(1)}, u32[]{:S(2)}, u32[]{:S(2)}) collective-permute-start(bf16[112,384]{1,0:T(8,128)(2,1)S(1)} %get-tuple-element.49.kept_ref), channel_id=1, source_target_pairs={{0,8},{1,3},{2,10},{3,1},{4,12},{5,7},{6,14},{7,5},{8,0},{9,11},{1... | collective-permute-start | bytes 258056 | tf_op jit(solution)/shard_map/ppermute | solution.py:481
  25.2 0.0 copy-done
  25.2 0.0 copy-done.1
  25.2 0.0 copy-done.2
  25.2 0.0 copy-done.3
  25.3 0.9 %shard_map.74 = (bf16[97,1152]{1,0:T(8,128)(2,1)S(1)}, bf16[97,1536]{1,0:T(8,128)(2,1)S(1)}, bf16[97,640]{1,0:T(8,128)(2,1)S(1)}, f32[8,1152]{1,0:T(8,128)S(1)}, f32[8,1152]{1,0:T(8,128)S(1)}) custom-call(s32[5]{0:T(128)S(1)} %stack.23.pos_ref, s32[97,1536]{1,0:T(8,128)S(1)} %copy-done, s32[12,128]{1,0:T(8,128)S(1)} %bitcast.9, s32[12,128]{1,0:T(8,128)S(1)} %bitcast.10, ...), custom_call_target="tpu_custom_call" | custom-call | flops 1489920 | bytes 1191936 | tf_op jit(solution)/shard_map/pallas_call | solution.py:452
  26.1 0.9 %collective-permute-done.6.msg_ref = bf16[104,768]{1,0:T(8,128)(2,1)S(1)} collective-permute-done((bf16[104,768]{1,0:T(8,128)(2,1)S(1)}, bf16[104,768]{1,0:T(8,128)(2,1)S(1)}, u32[]{:S(2)}, u32[]{:S(2)}) %collective-permute-start.6) | collective-permute-done | bytes 159776 | tf_op jit(solution)/shard_map/ppermute | solution.py:481
  27.0 1.4 %shard_map.75 = (f32[97,768]{1,0:T(8,128)S(1)}, f32[8,768]{1,0:T(8,128)S(1)}) custom-call(s32[5]{0:T(128)S(1)} %stack.23.pos_ref, bf16[104,768]{1,0:T(8,128)(2,1)S(1)} %get-tuple-element.51.kept_ref, bf16[104,768]{1,0:T(8,128)(2,1)S(1)} %collective-permute-done.6.msg_ref, f32[8,768]{1,0:T(8,128)S(1)} %get-tuple-element.48.own_ref.stats_ref, ...), custom_call_target="tpu_custom_call" | custom-call | flops 57212928 | bytes 1474560 | tf_op jit(solution)/shard_map/pallas_call | solution.py:452
  28.4 1.4 %collective-permute-done.5.msg_ref = bf16[112,384]{1,0:T(8,128)(2,1)S(1)} collective-permute-done((bf16[112,384]{1,0:T(8,128)(2,1)S(1)}, bf16[112,384]{1,0:T(8,128)(2,1)S(1)}, u32[]{:S(2)}, u32[]{:S(2)}) %collective-permute-start.5) | collective-permute-done | bytes 86048 | tf_op jit(solution)/shard_map/ppermute | solution.py:481
  29.8 1.6 %shard_map.76 = f32[97,1152]{1,0:T(8,128)S(1)} custom-call(s32[5]{0:T(128)S(1)} %stack.23.pos_ref, bf16[112,384]{1,0:T(8,128)(2,1)S(1)} %get-tuple-element.49.kept_ref, bf16[112,384]{1,0:T(8,128)(2,1)S(1)} %collective-permute-done.5.msg_ref, f32[8,384]{1,0:T(8,128)S(1)} %get-tuple-element.50.stats_ref, f32[8,768]{1,0:T(8,128)S(1)} %get-tuple-element.55.vec_ref, ...), custom_call_target="tpu_custom_call" | custom-call | flops 57212928 | bytes 1474560 | tf_op jit(solution)/shard_map/pallas_call | solution.py:452
  31.5 2.5 %collective-permute-start.7 = (f16[97,1152]{1,0:T(8,128)(2,1)S(1)}, f16[97,1152]{1,0:T(8,128)(2,1)S(1)}, u32[]{:S(2)}, u32[]{:S(2)}) collective-permute-start(f16[97,1152]{1,0:T(8,128)(2,1)S(1)} %convert_element_type.18), channel_id=1, source_target_pairs={{0,4},{1,9},{2,6},{3,11},{4,0},{5,13},{6,2},{7,15},{8,12},{9,1},{1... | collective-permute-start | bytes 670472 | tf_op jit(solution)/shard_map/ppermute | solution.py:481
  34.0 5.5 %collective-permute-done.7 = f16[97,1152]{1,0:T(8,128)(2,1)S(1)} collective-permute-done((f16[97,1152]{1,0:T(8,128)(2,1)S(1)}, f16[97,1152]{1,0:T(8,128)(2,1)S(1)}, u32[]{:S(2)}, u32[]{:S(2)}) %collective-permute-start.7) | collective-permute-done | bytes 223520 | tf_op jit(solution)/shard_map/ppermute | solution.py:481
  39.5 0.1 add_convert_fusion
  39.6 1.8 %collective-permute-start.8 = (f16[97,1152]{1,0:T(8,128)(2,1)S(1)}, f16[97,1152]{1,0:T(8,128)(2,1)S(1)}, u32[]{:S(2)}, u32[]{:S(2)}) collective-permute-start(f16[97,1152]{1,0:T(8,128)(2,1)S(1)} %add_convert_fusion), channel_id=1, source_target_pairs={{0,2},{1,5},{2,0},{3,7},{4,6},{5,1},{6,4},{7,3},{8,10},{9,13},{10,... | collective-permute-start | bytes 670472 | tf_op jit(solution)/shard_map/ppermute | solution.py:481
  41.4 4.4 %collective-permute-done.8 = f16[97,1152]{1,0:T(8,128)(2,1)S(1)} collective-permute-done((f16[97,1152]{1,0:T(8,128)(2,1)S(1)}, f16[97,1152]{1,0:T(8,128)(2,1)S(1)}, u32[]{:S(2)}, u32[]{:S(2)}) %collective-permute-start.8) | collective-permute-done | bytes 223520 | tf_op jit(solution)/shard_map/ppermute | solution.py:481
  45.8 0.1 convert_add_fusion.score_ref
  45.8 1.1 %shard_map.77 = (f32[97,768]{1,0:T(8,128)S(1)}, f32[97,384]{1,0:T(8,128)S(1)}, f32[200,97]{1,0:T(8,128)S(1)}) custom-call(s32[5]{0:T(128)S(1)} %stack.23.pos_ref, f32[97,1152]{1,0:T(8,128)S(1)} %convert_add_fusion.score_ref, bf16[97,1152]{1,0:T(8,128)(2,1)S(1)} %get-tuple-element.53.flag_ref, f32[8,1152]{1,0:T(8,128)S(1)} %get-tuple-element.58.block_ref), custom_call_target="tpu_custom_call" | custom-call | flops 134092800 | bytes 893952 | tf_op jit(solution)/shard_map/pallas_call | solution.py:452
  47.0 0.1 collective-permute-start.9
  47.1 0.5 collective-permute-start.10
  47.6 1.0 %collective-permute-done.10.there_ref = f32[200,97]{1,0:T(8,128)S(1)} collective-permute-done((f32[200,97]{1,0:T(8,128)S(1)}, f32[200,97]{1,0:T(8,128)S(1)}, u32[]{:S(2)}, u32[]{:S(2)}) %collective-permute-start.10) | collective-permute-done | bytes 77632 | tf_op jit(solution)/shard_map/ppermute | solution.py:484
  48.6 0.0 collective-permute-done.9.other_ref
  48.6 1.3 %shard_map.78 = (f32[97,768]{1,0:T(8,128)}, f32[200,97]{1,0:T(8,128)}) custom-call(s32[5]{0:T(128)S(1)} %stack.23.pos_ref, f32[97,768]{1,0:T(8,128)S(1)} %get-tuple-element.59.own_ref, f32[97,384]{1,0:T(8,128)S(1)} %collective-permute-done.9.other_ref, f32[200,97]{1,0:T(8,128)S(1)} %get-tuple-element.61.sums_ref, f32[200,97]{1,0:T(8,128)S(1)} %collective-permute-done.10.there_ref), custom_call_target="tpu_custom_call" | custom-call | flops 111744 | bytes 893952 | tf_op jit(solution)/shard_map/pallas_call | solution.py:452
  (1 shorter events, 0.0 us)
Async XLA Ops:
  0.7 1.4 %copy-start.4 = (bf16[1024,768]{1,0:T(8,128)(2,1)S(1)}, bf16[1024,768]{1,0:T(8,128)(2,1)}, u32[]{:S(2)}) copy-start(bf16[1024,768]{1,0:T(8,128)(2,1)} %own_ref.1) | copy-start | bytes 4718596
  4.6 3.1 %collective-permute-start = (bf16[1024,384]{1,0:T(8,128)(2,1)S(1)}, bf16[1024,384]{1,0:T(8,128)(2,1)S(1)}, u32[]{:S(2)}, u32[]{:S(2)}) collective-permute-start(bf16[1024,384]{1,0:T(8,128)(2,1)S(1)} %get-tuple-element.34), channel_id=1, source_target_pairs={{0,1},{1,0},{2,3},{3,2},{4,5},{5,4},{6,7},{7,6},{8,9},{9,8},{10,11... | collective-permute-start | bytes 2359304 | tf_op jit(solution)/shard_map/ppermute | solution.py:484
  5.1 7.4 %collective-permute-start.2 = (bf16[200,768]{1,0:T(8,128)(2,1)S(1)}, bf16[200,768]{1,0:T(8,128)(2,1)S(1)}, u32[]{:S(2)}, u32[]{:S(2)}) collective-permute-start(bf16[200,768]{1,0:T(8,128)(2,1)S(1)} %get-tuple-element.40), channel_id=1, source_target_pairs={{0,2},{1,5},{2,0},{3,7},{4,6},{5,1},{6,4},{7,3},{8,10},{9,13},{10,... | collective-permute-start | bytes 921608 | tf_op jit(solution)/shard_map/ppermute | solution.py:481
  9.9 15.3 %copy-start = (s32[97,1536]{1,0:T(8,128)S(1)}, s32[97,1536]{1,0:T(8,128)}, u32[]{:S(2)}) copy-start(s32[97,1536]{1,0:T(8,128)} %annot_ref.1) | copy-start | bytes 1787908
  9.9 15.3 %copy-start.1 = (s32[1536]{0:T(1024)S(1)}, s32[1536]{0:T(1024)}, u32[]{:S(2)}) copy-start(s32[1536]{0:T(1024)} %param.6) | copy-start | bytes 18436
  9.9 15.3 %copy-start.2 = (s32[1536]{0:T(1024)S(1)}, s32[1536]{0:T(1024)}, u32[]{:S(2)}) copy-start(s32[1536]{0:T(1024)} %param.9) | copy-start | bytes 18436
  9.9 15.3 %copy-start.3 = (s32[1536]{0:T(1024)S(1)}, s32[1536]{0:T(1024)}, u32[]{:S(2)}) copy-start(s32[1536]{0:T(1024)} %param.7) | copy-start | bytes 18436
  10.0 5.6 %collective-permute-start.1 = (bf16[208,384]{1,0:T(8,128)(2,1)S(1)}, bf16[208,384]{1,0:T(8,128)(2,1)S(1)}, u32[]{:S(2)}, u32[]{:S(2)}) collective-permute-start(bf16[208,384]{1,0:T(8,128)(2,1)S(1)} %get-tuple-element.37), channel_id=1, source_target_pairs={{0,2},{1,5},{2,0},{3,7},{4,6},{5,1},{6,4},{7,3},{8,10},{9,13},{10,... | collective-permute-start | bytes 479240 | tf_op jit(solution)/shard_map/ppermute | solution.py:481
  13.4 6.6 %collective-permute-start.4 = (bf16[104,768]{1,0:T(8,128)(2,1)S(1)}, bf16[104,768]{1,0:T(8,128)(2,1)S(1)}, u32[]{:S(2)}, u32[]{:S(2)}) collective-permute-start(bf16[104,768]{1,0:T(8,128)(2,1)S(1)} %get-tuple-element.47), channel_id=1, source_target_pairs={{0,4},{1,9},{2,6},{3,11},{4,0},{5,13},{6,2},{7,15},{8,12},{9,1},{1... | collective-permute-start | bytes 479240 | tf_op jit(solution)/shard_map/ppermute | solution.py:481
  16.4 6.9 %collective-permute-start.3 = (bf16[112,384]{1,0:T(8,128)(2,1)S(1)}, bf16[112,384]{1,0:T(8,128)(2,1)S(1)}, u32[]{:S(2)}, u32[]{:S(2)}) collective-permute-start(bf16[112,384]{1,0:T(8,128)(2,1)S(1)} %get-tuple-element.44), channel_id=1, source_target_pairs={{0,4},{1,9},{2,6},{3,11},{4,0},{5,13},{6,2},{7,15},{8,12},{9,1},{1... | collective-permute-start | bytes 258056 | tf_op jit(solution)/shard_map/ppermute | solution.py:481
  20.8 6.2 %collective-permute-start.6 = (bf16[104,768]{1,0:T(8,128)(2,1)S(1)}, bf16[104,768]{1,0:T(8,128)(2,1)S(1)}, u32[]{:S(2)}, u32[]{:S(2)}) collective-permute-start(bf16[104,768]{1,0:T(8,128)(2,1)S(1)} %get-tuple-element.51.kept_ref), channel_id=1, source_target_pairs={{0,8},{1,3},{2,10},{3,1},{4,12},{5,7},{6,14},{7,5},{8,0},{9,11},{1... | collective-permute-start | bytes 479240 | tf_op jit(solution)/shard_map/ppermute | solution.py:481
  24.2 5.7 %collective-permute-start.5 = (bf16[112,384]{1,0:T(8,128)(2,1)S(1)}, bf16[112,384]{1,0:T(8,128)(2,1)S(1)}, u32[]{:S(2)}, u32[]{:S(2)}) collective-permute-start(bf16[112,384]{1,0:T(8,128)(2,1)S(1)} %get-tuple-element.49.kept_ref), channel_id=1, source_target_pairs={{0,8},{1,3},{2,10},{3,1},{4,12},{5,7},{6,14},{7,5},{8,0},{9,11},{1... | collective-permute-start | bytes 258056 | tf_op jit(solution)/shard_map/ppermute | solution.py:481
  31.5 8.0 %collective-permute-start.7 = (f16[97,1152]{1,0:T(8,128)(2,1)S(1)}, f16[97,1152]{1,0:T(8,128)(2,1)S(1)}, u32[]{:S(2)}, u32[]{:S(2)}) collective-permute-start(f16[97,1152]{1,0:T(8,128)(2,1)S(1)} %convert_element_type.18), channel_id=1, source_target_pairs={{0,4},{1,9},{2,6},{3,11},{4,0},{5,13},{6,2},{7,15},{8,12},{9,1},{1... | collective-permute-start | bytes 670472 | tf_op jit(solution)/shard_map/ppermute | solution.py:481
  39.6 6.2 %collective-permute-start.8 = (f16[97,1152]{1,0:T(8,128)(2,1)S(1)}, f16[97,1152]{1,0:T(8,128)(2,1)S(1)}, u32[]{:S(2)}, u32[]{:S(2)}) collective-permute-start(f16[97,1152]{1,0:T(8,128)(2,1)S(1)} %add_convert_fusion), channel_id=1, source_target_pairs={{0,2},{1,5},{2,0},{3,7},{4,6},{5,1},{6,4},{7,3},{8,10},{9,13},{10,... | collective-permute-start | bytes 670472 | tf_op jit(solution)/shard_map/ppermute | solution.py:481
  47.0 1.6 %collective-permute-start.9 = (f32[97,384]{1,0:T(8,128)S(1)}, f32[97,384]{1,0:T(8,128)S(1)}, u32[]{:S(2)}, u32[]{:S(2)}) collective-permute-start(f32[97,384]{1,0:T(8,128)S(1)} %get-tuple-element.60), channel_id=1, source_target_pairs={{0,1},{1,0},{2,3},{3,2},{4,5},{5,4},{6,7},{7,6},{8,9},{9,8},{10,11... | collective-permute-start | bytes 446984 | tf_op jit(solution)/shard_map/ppermute | solution.py:484
  47.1 1.5 %collective-permute-start.10 = (f32[200,97]{1,0:T(8,128)S(1)}, f32[200,97]{1,0:T(8,128)S(1)}, u32[]{:S(2)}, u32[]{:S(2)}) collective-permute-start(f32[200,97]{1,0:T(8,128)S(1)} %get-tuple-element.61.sums_ref), channel_id=1, source_target_pairs={{0,1},{1,0},{2,3},{3,2},{4,5},{5,4},{6,7},{7,6},{8,9},{9,8},{10,11... | collective-permute-start | bytes 232808 | tf_op jit(solution)/shard_map/ppermute | solution.py:484

commit v4 on v3

--- a/solution.py
+++ b/solution.py
@@ -14,6 +14,7 @@
 BF16 = jnp.bfloat16
 CORE_ONE_ORDER = [1, 2, 0]
 VMEM_LIMIT = 20 * 1024 * 1024
+COPY_LIMIT = 50 * 1024 * 1024
 
 
 STEP = 48
@@ -21,11 +22,6 @@
 
 def pick(first, one, other):
     return jnp.where(first, one, other)
-
-
-def wide_rows(ref, offset, count, half):
-    rows = ref[pl.ds(pl.multiple_of(offset, 16), count), :]
-    return jnp.concatenate([rows] * (half // 128), axis=1)
 
 
 def index_parts(start, count, half):
@@ -34,14 +30,18 @@
     return row, col
 
 
-def to_column(vec_row, ref):
-    width = vec_row.shape[1]
-    tall = jnp.broadcast_to(vec_row, (128, width))
-    for k in range(width // 128):
-        ref[k * 128 : (k + 1) * 128, :] = tall[:, k * 128 : (k + 1) * 128].T
-    rest = ref.shape[0] - width
-    if rest:
-        ref[width:, :] = jnp.zeros((rest, 128), F32)
+def column_table(vectors, start, ref):
+    table = eight(*vectors)
+    half = table.shape[1]
+    if start is not None:
+        table = pltpu.roll(table, lax.rem(half - start, half), 1)
+    for k in range(ref.shape[0] // 128):
+        ref[k * 128 : (k + 1) * 128, :8] = table[:, k * 128 : (k + 1) * 128].T
+
+
+def table_rows(ref, offset, columns, count=STEP):
+    rows = ref[pl.ds(pl.multiple_of(offset, 16), count), :8]
+    return tuple(rows[:, k : k + 1] for k in columns)
 
 
 def coded(stats):
@@ -62,11 +62,8 @@
     return vec[:, :half], vec[:, half : 2 * half]
 
 
-def own_products(ref, cols, start, row, col):
-    count, half = row.shape
-    left, right = cols
-    l_rows = wide_rows(ref, start, count, half)
-    r_rows = wide_rows(ref, start + half, count, half)
+def own_products(rows, cols, row, col):
+    (l_rows, r_rows), (left, right) = rows, cols
     return l_rows * right, jnp.where(row < col, l_rows * left, r_rows * right)
 
 
@@ -83,12 +80,16 @@
     return b_cols[:1], a_turned[:1], b3_cols[:1]
 
 
-def cross_products(ref, cols, core, start, row, col):
-    count, half = row.shape
-    c_b, c_a, c_b3 = cols
-    a_rows = wide_rows(ref, start + 2 * half * core, count, half)
-    a2_rows = wide_rows(ref, start + half + half * core, count, half)
-    b_rows = wide_rows(ref, start + 2 * half + half // 2 - half * core, count, half)
+def cross_vectors(vec, first, half):
+    a_cols, b_cols = cross_halves(vec, first, half)
+    a2_cols = pick(first, vec[:, half : 2 * half], vec[:, 2 * half :])
+    b_late = pltpu.roll(jnp.broadcast_to(b_cols, (8, half)), half // 2, 1)[:1]
+    return a_cols, a2_cols, b_late
+
+
+def cross_products(rows, cols, row, col):
+    (a_rows, a2_rows, b_rows), (c_b, c_a, c_b3) = rows, cols
+    half = row.shape[1]
     return jnp.where(
         col < half // 2, jnp.where(row > col, a_rows * c_b, b_rows * c_a), a2_rows * c_b3
     )
@@ -102,13 +103,18 @@
     return lax.dot_general(left, right, (((1,), (1,)), ((), ())), preferred_element_type=F32)
 
 
-def moments(ref):
-    count, width = ref.shape
-    sums = dot_n(jnp.ones((8, count), BF16), ref[...])[:1]
+def squared_sums(ref, start, stop):
+    width = ref.shape[1]
     total = jnp.zeros((8, width), F32)
-    for k in range(0, count, 64):
+    for k in range(start, stop, 64):
         part = ref[k : k + 64, :].astype(F32)
         total = total + jnp.sum((part * part).reshape(8, 8, width), axis=0)
+    return total
+
+
+def moments(ref, total):
+    count = ref.shape[0]
+    sums = dot_n(jnp.ones((8, count), BF16), ref[...])[:1]
     shift = sums * (1.0 / math.sqrt(count))
     return sums, jnp.sum(total, axis=0, keepdims=True) - shift * shift, shift
 
@@ -124,8 +130,24 @@
         keep_ref[k : k + STEP, :] = value(pl.multiple_of(bit * part + k, 16))
 
 
-def own_gram_kernel(pos_ref, own_ref, keep_ref, send_ref, stats_ref, turned_ref, piece_ref, full_ref, col_ref):
-    half = own_ref.shape[1] // 2
+def own_gram_kernel(
+    pos_ref, slab_ref, keep_ref, send_ref, stats_ref, turned_ref, piece_ref, full_ref, col_ref, own_ref, sems,
+):
+    count, slab = slab_ref.shape
+    half = slab // 2
+    pieces = sems.shape[0]
+    size = count // pieces
+    copies = []
+    for k in range(pieces):
+        here = pl.ds(k * size, size)
+        copies.append(pltpu.make_async_copy(slab_ref.at[here, :], own_ref.at[here, :], sems.at[k]))
+        copies[k].start()
+    total = jnp.zeros((8, slab), F32)
+    for k in range(pieces):
+        copies[k].wait()
+        here = slice(k * size, (k + 1) * size)
+        turned_ref[:, here] = own_ref[here, :].T
+        total = total + squared_sums(own_ref, k * size, (k + 1) * size)
 
     @pl.when(pos_ref[0] == 0)
     def _():
@@ -135,10 +157,9 @@
     def _():
         piece_ref[...] = own_ref[:, :half]
 
-    turned_ref[...] = own_ref[...].T
-    sums, squares, shift = moments(own_ref)
+    sums, squares, shift = moments(own_ref, total)
     stats_ref[...] = eight(sums, squares, shift)
-    to_column(shift, col_ref)
+    column_table(own_cols(shift, half), None, col_ref)
     left, right = turned_ref[:half, :], turned_ref[half:, :]
     full_ref[:, :half] = dot_n(left, own_ref[:, half:])
     row, col = index_parts(0, half, half)
@@ -146,7 +167,8 @@
     cols = own_cols(shift, half)
 
     def value(start):
-        products = own_products(col_ref, cols, start, *index_parts(start, STEP, half))
+        rows = table_rows(col_ref, start, (0, 1))
+        products = own_products(rows, cols, *index_parts(start, STEP, half))
         return full_ref[pl.ds(start, STEP), :] - jnp.concatenate(products, axis=1)
 
     halved(pos_ref[1], keep_ref, send_ref, value)
@@ -171,9 +193,9 @@
         full_ref[:, :half] = dot_t(side_ref[...], turned_ref[half:, :])
         full_ref[:, half:] = dot_t(side_ref[...], turned_ref[:half, :])
 
-    sums, squares, shift = moments(there_ref)
+    sums, squares, shift = moments(there_ref, squared_sums(there_ref, 0, there_ref.shape[0]))
     shift = jnp.concatenate([own_stats_ref[2:3, :], shift], axis=1)
-    to_column(shift, col_ref)
+    column_table(cross_vectors(shift, first, half), None, col_ref)
     a_shift, b_shift = cross_halves(shift, first, half)
     straight = full_ref[:, :half]
     level = jnp.sum(jnp.where(row == col, straight, 0.0), axis=0, keepdims=True) - a_shift * b_shift
@@ -188,7 +210,8 @@
     cols = cross_cols(shift, first, half)
 
     def value(start):
-        products = cross_products(col_ref, cols, core, start, *index_parts(start, STEP, half))
+        rows = table_rows(col_ref, start, (0, 1, 2))
+        products = cross_products(rows, cols, *index_parts(start, STEP, half))
         return full_ref[pl.ds(start, STEP), :half] - products
 
     halved(pos_ref[1], keep_ref, send_ref, value)
@@ -233,13 +256,13 @@
     half = kept_ref.shape[1] // 2
     sums, squares, shift = own_merged(msg_ref, stats_ref, rows, samples)
     out_ref[...] = eight(sums, squares, shift)
-    to_column(shift, col_ref)
     cols = own_cols(shift, half)
     base = pos_ref[3] if split else pos_ref[4]
+    column_table(cols, base, col_ref)
 
     def value(offset):
-        start = base + offset
-        products = own_products(col_ref, cols, start, *index_parts(start, STEP, half))
+        factors = table_rows(col_ref, offset, (0, 1))
+        products = own_products(factors, cols, *index_parts(base + offset, STEP, half))
         here = pl.ds(offset, STEP)
         both = kept_ref[here, :].astype(F32) + msg_ref[here, :].astype(F32)
         return both + jnp.concatenate(products, axis=1)
@@ -257,13 +280,13 @@
     first = core == 0
     sums, squares, level, shift = cross_merged(msg_ref, stats_ref, own_ref[2:3, :], rows, samples, first)
     out_ref[...] = eight(sums, squares, level)
-    to_column(shift, col_ref)
     cols = cross_cols(shift, first, half)
     base = pos_ref[3] if split else pos_ref[4]
+    column_table(cross_vectors(shift, first, half), base, col_ref)
 
     def value(offset):
-        start = base + offset
-        products = cross_products(col_ref, cols, core, start, *index_parts(start, STEP, half))
+        factors = table_rows(col_ref, offset, (0, 1, 2))
+        products = cross_products(factors, cols, *index_parts(base + offset, STEP, half))
         here = pl.ds(offset, STEP)
         return kept_ref[here, :].astype(F32) + msg_ref[here, :].astype(F32) + products
 
@@ -283,7 +306,7 @@
 
 def own_score_kernel(
     pos_ref, kept_ref, msg_ref, stats_ref, limit_ref, flag_ref, sub_ref,
-    out_ref, vec_ref, col_ref, scale_ref, lim_ref, one_ref, two_ref, *, samples,
+    out_ref, vec_ref, col_ref, one_ref, two_ref, *, samples,
 ):
     rows = one_ref.shape[0]
     half = kept_ref.shape[1] // 2
@@ -291,18 +314,17 @@
     _, squares, shift = own_merged(msg_ref, stats_ref, rows, samples)
     scale = 1.0 / jnp.sqrt(squares * (1.0 / everyone) + VAR_EPS)
     vec_ref[...] = eight(shift, scale)
-    to_column(shift, col_ref)
-    to_column(scale * (1.0 / everyone), scale_ref)
-    to_column(limit_ref[:1, : 2 * half], lim_ref)
     cols, scales = own_cols(shift, half), own_cols(scale, half)
+    factors = cols + own_cols(scale * (1.0 / everyone), half) + (limit_ref[:1, :half],)
+    column_table(factors, pos_ref[4], col_ref)
     right_lim = limit_ref[:1, half : 2 * half]
     base = pos_ref[4]
     for k in range(0, rows, STEP):
         start = base + k
         row, col = index_parts(start, STEP, half)
-        products = own_products(col_ref, cols, start, row, col)
-        norms = own_products(scale_ref, scales, start, row, col)
-        left_lim = wide_rows(lim_ref, start, STEP, half)
+        l_shift, r_shift, l_scale, r_scale, left_lim = table_rows(col_ref, k, range(5))
+        products = own_products((l_shift, r_shift), cols, row, col)
+        norms = own_products((l_scale, r_scale), scales, row, col)
         gaps = (half + col - row, jnp.where(row == col, 8 * half, jnp.abs(row - col)))
         lims = (left_lim, jnp.where(row < col, left_lim, right_lim))
         for s, ref in ((0, one_ref), (1, two_ref)):
@@ -322,7 +344,7 @@
 
 def cross_score_kernel(
     pos_ref, kept_ref, msg_ref, stats_ref, vec_ref, limit_ref, flag_ref, sub_ref, own_ref,
-    out_ref, col_ref, scale_ref, lim_ref, three_ref, *, samples,
+    out_ref, col_ref, three_ref, *, samples,
 ):
     rows = three_ref.shape[0]
     half = kept_ref.shape[1]
@@ -334,9 +356,9 @@
     scale = 1.0 / jnp.sqrt(squares * (1.0 / everyone) + VAR_EPS)
     scale = jnp.concatenate([vec_ref[1:2, :], scale], axis=1)
     limit = limit_ref[:1, :]
-    to_column(shift, col_ref)
-    to_column(scale * (1.0 / everyone), scale_ref)
-    to_column(limit, lim_ref)
+    factors = cross_vectors(shift, first, half)
+    factors = factors + cross_vectors(scale * (1.0 / everyone), first, half)
+    column_table(factors + cross_vectors(limit, first, half)[:2], pos_ref[4], col_ref)
     cols, scales = cross_cols(shift, first, half), cross_cols(scale, first, half)
     _, late_lim, _ = cross_cols(limit, first, half)
     base = pos_ref[4]
@@ -344,10 +366,10 @@
         start = base + k
         row, col = index_parts(start, STEP, half)
         fold = col < quarter
-        products = cross_products(col_ref, cols, core, start, row, col)
-        norms = cross_products(scale_ref, scales, core, start, row, col)
-        a_lim = wide_rows(lim_ref, start + 2 * half * core, STEP, half)
-        a2_lim = wide_rows(lim_ref, start + half + half * core, STEP, half)
+        parts = table_rows(col_ref, k, range(8))
+        a_lim, a2_lim = parts[6:]
+        products = cross_products(parts[:3], cols, row, col)
+        norms = cross_products(parts[3:6], scales, row, col)
         lims = jnp.where(fold, jnp.where(row > col, a_lim, late_lim), a2_lim)
         near = jnp.where(row == col, 8 * half, 2 * half - jnp.abs(row - col))
         gaps = jnp.where(fold, near, quarter + quarter * core + col - row)
@@ -446,16 +468,17 @@
     sum_ref[...] = dot_t(hot, high) + dot_t(hot, middle) + dot_t(hot, low)
 
 
-def call(kernel, inputs, outputs, scratch, flops, moved):
+def call(kernel, inputs, outputs, scratch, flops, moved, space=pltpu.VMEM, limit=VMEM_LIMIT):
     vmem = pl.BlockSpec(memory_space=pltpu.VMEM)
+    source = pl.BlockSpec(memory_space=space)
     smem = pl.BlockSpec(memory_space=pltpu.SMEM)
     return pl.pallas_call(
         kernel,
         out_shape=outputs,
-        in_specs=[smem] + [vmem] * (len(inputs) - 1),
+        in_specs=[smem] + [source] * (len(inputs) - 1),
         out_specs=jax.tree.map(lambda _: vmem, outputs),
         scratch_shapes=scratch,
-        compiler_params=pltpu.CompilerParams(vmem_limit_bytes=VMEM_LIMIT),
+        compiler_params=pltpu.CompilerParams(vmem_limit_bytes=limit),
         cost_estimate=pl.CostEstimate(flops=flops, bytes_accessed=moved, transcendentals=0),
     )(*inputs)
 
@@ -511,8 +534,10 @@
     )
     hot_rows = -(-NBLK // 8) * 8
 
-    own_column = pltpu.VMEM((slab, 128), F32)
-    column = pltpu.VMEM((width + quarter, 128), F32)
+    def table_of(count):
+        return pltpu.VMEM((-(-count // 128) * 128, 128), F32)
+
+    table = table_of(rows)
 
     def outputs(kept, sent, cols, stat_rows):
         kept_shape = (shape(kept, cols, F32),) if kept else ()
@@ -522,9 +547,11 @@
         own_gram_kernel,
         (where, genotypes),
         outputs(quarter, quarter, slab, 8) + (shape(slab, count, BF16), shape(count, half, BF16)),
-        [pltpu.VMEM((half, slab), F32), own_column],
+        [pltpu.VMEM((half, slab), F32), table_of(half), pltpu.VMEM((count, slab), BF16), pltpu.SemaphoreType.DMA((8,))],
         2 * count * half * half * 3,
         count * slab * 2,
+        pltpu.HBM,
+        COPY_LIMIT,
     )
     there = across(piece)
     msg_a = exchange(send_a, 0)
@@ -532,7 +559,7 @@
         cross_gram_kernel,
         (where, turned, there, stats_a),
         outputs(quarter, quarter, half, 16),
-        [pltpu.VMEM((half, slab), F32), column, pltpu.VMEM((half, count), BF16)],
+        [pltpu.VMEM((half, slab), F32), table_of(half), pltpu.VMEM((half, count), BF16)],
         2 * count * half * half * 3,
         count * slab * 2,
     )
@@ -545,7 +572,7 @@
             functools.partial(own_merge_kernel, samples=samples, split=split),
             (where, keep_a, msg_a, stats_a),
             outputs(rows if split else 0, rows, slab, 8),
-            [own_column],
+            [table_of(quarter) if split else table],
             rows * slab * 8,
             rows * slab * 20,
         )
@@ -554,7 +581,7 @@
             functools.partial(cross_merge_kernel, samples=samples, split=split),
             (where, keep_b, msg_b, stats_b, stats_a),
             outputs(rows if split else 0, rows, half, 16),
-            [column],
+            [table_of(quarter) if split else table],
             rows * half * 8,
             rows * half * 20,
         )
@@ -566,7 +593,7 @@
         functools.partial(own_score_kernel, samples=samples),
         (where, keep_a, msg_a, stats_a, limit, flags, subs),
         (shape(annot, slab, F32), shape(8, slab, F32)),
-        [own_column] * 3 + [pltpu.VMEM((rows, half), BF16)] * 2,
+        [table] + [pltpu.VMEM((rows, half), BF16)] * 2,
         2 * annot * half * rows * 8,
         rows * slab * 20,
     )
@@ -574,7 +601,7 @@
         functools.partial(cross_score_kernel, samples=samples),
         (where, keep_b, msg_b, stats_b, vectors, limit, flags_cross, subs, scores_a),
         shape(annot, width, F32),
-        [column] * 3 + [pltpu.VMEM((rows, half), BF16)],
+        [table] + [pltpu.VMEM((rows, half), BF16)],
         2 * annot * half * rows * 8,
         rows * slab * 20,
     )

time: 50.1 us -> 50.6 us (level)
  Pallas kernels: 14.3 us -> 16.7 us
  local copies, waits for them, and re-layouts: 1.52 us -> 0.11 us
  waiting for transfers between devices: 15 us -> 14.4 us
    pallas_call x11, Pallas kernels: 14.3 us -> 16.7 us  [call(): pl.pallas_call(kernel, out_shape=outputs, in_specs=[smem] + [source] * (l...]
    unnamed x10 -> x8, local copies, waits for them, and re-layouts: 1.43 us -> 0.03 us
    ppermute x8, waiting for transfers between devices: 14 us -> 13.4 us  [exchange(): return lax.ppermute(x, ('samples', 'genome'), route)]
  transfers between devices with their start and end apart: 11 -> 11, of which waited for: 7 -> 8; matrix products, arithmetic and copies ran while one was open for 0% -> 0% of each run, Pallas kernels for 16% -> 17%
where the time goes in v4:
time: 50.6 us; the launch traced here: 50.4 us
  starting transfers between devices  18.3 us (36%)
  Pallas kernels  16.7 us (33%)
  waiting for transfers between devices  14.4 us (28%)
  between operations  0.79 us (2%)
    ppermute x8, starting transfers between devices, exchange(): return lax.ppermute(x, ('samples', 'genome'), route)  17.2 us
    pallas_call x11, Pallas kernels, call(): pl.pallas_call(kernel, out_shape=outputs, in_specs=[smem] + [source] * (l...  16.7 us
    ppermute x8, waiting for transfers between devices, exchange(): return lax.ppermute(x, ('samples', 'genome'), route)  13.4 us
    ppermute x3, starting transfers between devices, across(): return lax.ppermute(x, 'genome', [(0, 1), (1, 0)])  1.08 us
    ppermute x3, waiting for transfers between devices, across(): return lax.ppermute(x, 'genome', [(0, 1), (1, 0)])  1.03 us
  transfers between devices with their start and end apart: 11, of which 8 were waited for; matrix products, arithmetic and copies ran while one was open for 0% of the time, Pallas kernels for 17%

profile of v4, /device:TPU:0, one launch (start us, length us, event | category | flops | bytes accessed | tf_op | source)
XLA Modules:
  0.0 50.4 jit_solution(8959886082676867610)
XLA Ops:
  0.6 0.1 stack.23.pos_ref
  0.7 4.4 %shard_map.68 = (f32[192,768]{1,0:T(8,128)S(1)}, bf16[200,768]{1,0:T(8,128)(2,1)S(1)}, f32[8,768]{1,0:T(8,128)S(1)}, bf16[768,1024]{1,0:T(8,128)(2,1)S(1)}, bf16[1024,384]{1,0:T(8,128)(2,1)S(1)}) custom-call(s32[5]{0:T(128)S(1)} %stack.23.pos_ref, bf16[1024,768]{1,0:T(8,128)(2,1)} %slab_ref.1), custom_call_target="tpu_custom_call" | custom-call | flops 905969664 | bytes 1572864 | tf_op jit(solution)/shard_map/pallas_call | solution.py:475
  5.1 0.5 %collective-permute-start = (bf16[1024,384]{1,0:T(8,128)(2,1)S(1)}, bf16[1024,384]{1,0:T(8,128)(2,1)S(1)}, u32[]{:S(2)}, u32[]{:S(2)}) collective-permute-start(bf16[1024,384]{1,0:T(8,128)(2,1)S(1)} %get-tuple-element.34), channel_id=1, source_target_pairs={{0,1},{1,0},{2,3},{3,2},{4,5},{5,4},{6,7},{7,6},{8,9},{9,8},{10,11... | collective-permute-start | bytes 2359304 | tf_op jit(solution)/shard_map/ppermute | solution.py:507
  5.6 2.6 %collective-permute-start.2 = (bf16[200,768]{1,0:T(8,128)(2,1)S(1)}, bf16[200,768]{1,0:T(8,128)(2,1)S(1)}, u32[]{:S(2)}, u32[]{:S(2)}) collective-permute-start(bf16[200,768]{1,0:T(8,128)(2,1)S(1)} %get-tuple-element.40), channel_id=1, source_target_pairs={{0,2},{1,5},{2,0},{3,7},{4,6},{5,1},{6,4},{7,3},{8,10},{9,13},{10,... | collective-permute-start | bytes 921608 | tf_op jit(solution)/shard_map/ppermute | solution.py:504
  8.2 0.0 collective-permute-done.there_ref
  8.2 2.4 %shard_map.69 = (f32[192,384]{1,0:T(8,128)S(1)}, bf16[208,384]{1,0:T(8,128)(2,1)S(1)}, f32[8,384]{1,0:T(8,128)S(1)}) custom-call(s32[5]{0:T(128)S(1)} %stack.23.pos_ref, bf16[768,1024]{1,0:T(8,128)(2,1)S(1)} %get-tuple-element.33.turned_ref, bf16[1024,384]{1,0:T(8,128)(2,1)S(1)} %collective-permute-done.there_ref, ...), custom_call_target="tpu_custom_call" | custom-call | flops 905969664 | bytes 1572864 | tf_op jit(solution)/shard_map/pallas_call | solution.py:475
  10.6 0.0 copy-start
  10.6 0.0 copy-start.1
  10.6 0.0 copy-start.2
  10.7 0.0 copy-start.3
  10.7 2.3 %collective-permute-start.1 = (bf16[208,384]{1,0:T(8,128)(2,1)S(1)}, bf16[208,384]{1,0:T(8,128)(2,1)S(1)}, u32[]{:S(2)}, u32[]{:S(2)}) collective-permute-start(bf16[208,384]{1,0:T(8,128)(2,1)S(1)} %get-tuple-element.37), channel_id=1, source_target_pairs={{0,2},{1,5},{2,0},{3,7},{4,6},{5,1},{6,4},{7,3},{8,10},{9,13},{10,... | collective-permute-start | bytes 479240 | tf_op jit(solution)/shard_map/ppermute | solution.py:504
  12.9 0.1 collective-permute-done.2.msg_ref
  13.0 0.9 %shard_map.70 = (f32[96,768]{1,0:T(8,128)S(1)}, bf16[104,768]{1,0:T(8,128)(2,1)S(1)}, f32[8,768]{1,0:T(8,128)S(1)}) custom-call(s32[5]{0:T(128)S(1)} %stack.23.pos_ref, f32[192,768]{1,0:T(8,128)S(1)} %get-tuple-element.39.kept_ref, bf16[200,768]{1,0:T(8,128)(2,1)S(1)} %collective-permute-done.2.msg_ref, f32[8,768]{1,0:T(8,128)S(1)} %get-tuple-element.35.own_stats_ref.stats_ref), custom_call_target="tpu_custom_call" | custom-call | flops 589824 | bytes 1474560 | tf_op jit(solution)/shard_map/pallas_call | solution.py:475
  13.9 2.2 %collective-permute-start.4 = (bf16[104,768]{1,0:T(8,128)(2,1)S(1)}, bf16[104,768]{1,0:T(8,128)(2,1)S(1)}, u32[]{:S(2)}, u32[]{:S(2)}) collective-permute-start(bf16[104,768]{1,0:T(8,128)(2,1)S(1)} %get-tuple-element.47), channel_id=1, source_target_pairs={{0,4},{1,9},{2,6},{3,11},{4,0},{5,13},{6,2},{7,15},{8,12},{9,1},{1... | collective-permute-start | bytes 479240 | tf_op jit(solution)/shard_map/ppermute | solution.py:504
  16.1 0.1 collective-permute-done.1.msg_ref
  16.2 1.0 %shard_map.71 = (f32[96,384]{1,0:T(8,128)S(1)}, bf16[112,384]{1,0:T(8,128)(2,1)S(1)}, f32[8,384]{1,0:T(8,128)S(1)}) custom-call(s32[5]{0:T(128)S(1)} %stack.23.pos_ref, f32[192,384]{1,0:T(8,128)S(1)} %get-tuple-element.36.kept_ref, bf16[208,384]{1,0:T(8,128)(2,1)S(1)} %collective-permute-done.1.msg_ref, f32[8,384]{1,0:T(8,128)S(1)} %get-tuple-element.38.stats_ref, ...), custom_call_target="tpu_custom_call" | custom-call | flops 294912 | bytes 737280 | tf_op jit(solution)/shard_map/pallas_call | solution.py:475
  17.2 2.2 %collective-permute-start.3 = (bf16[112,384]{1,0:T(8,128)(2,1)S(1)}, bf16[112,384]{1,0:T(8,128)(2,1)S(1)}, u32[]{:S(2)}, u32[]{:S(2)}) collective-permute-start(bf16[112,384]{1,0:T(8,128)(2,1)S(1)} %get-tuple-element.44), channel_id=1, source_target_pairs={{0,4},{1,9},{2,6},{3,11},{4,0},{5,13},{6,2},{7,15},{8,12},{9,1},{1... | collective-permute-start | bytes 258056 | tf_op jit(solution)/shard_map/ppermute | solution.py:504
  19.3 1.2 %collective-permute-done.4.msg_ref = bf16[104,768]{1,0:T(8,128)(2,1)S(1)} collective-permute-done((bf16[104,768]{1,0:T(8,128)(2,1)S(1)}, bf16[104,768]{1,0:T(8,128)(2,1)S(1)}, u32[]{:S(2)}, u32[]{:S(2)}) %collective-permute-start.4) | collective-permute-done | bytes 159776 | tf_op jit(solution)/shard_map/ppermute | solution.py:504
  20.6 0.9 %shard_map.72 = (bf16[104,768]{1,0:T(8,128)(2,1)S(1)}, f32[8,768]{1,0:T(8,128)S(1)}) custom-call(s32[5]{0:T(128)S(1)} %stack.23.pos_ref, f32[96,768]{1,0:T(8,128)S(1)} %get-tuple-element.46.kept_ref, bf16[104,768]{1,0:T(8,128)(2,1)S(1)} %collective-permute-done.4.msg_ref, f32[8,768]{1,0:T(8,128)S(1)} %get-tuple-element.42.own_ref.stats_ref), custom_call_target="tpu_custom_call" | custom-call | flops 589824 | bytes 1474560 | tf_op jit(solution)/shard_map/pallas_call | solution.py:475
  21.4 2.6 %collective-permute-start.6 = (bf16[104,768]{1,0:T(8,128)(2,1)S(1)}, bf16[104,768]{1,0:T(8,128)(2,1)S(1)}, u32[]{:S(2)}, u32[]{:S(2)}) collective-permute-start(bf16[104,768]{1,0:T(8,128)(2,1)S(1)} %get-tuple-element.51.kept_ref), channel_id=1, source_target_pairs={{0,8},{1,3},{2,10},{3,1},{4,12},{5,7},{6,14},{7,5},{8,0},{9,11},{1... | collective-permute-start | bytes 479240 | tf_op jit(solution)/shard_map/ppermute | solution.py:504
  24.0 0.0 collective-permute-done.3.msg_ref
  24.0 0.9 %shard_map.73 = (bf16[112,384]{1,0:T(8,128)(2,1)S(1)}, f32[8,384]{1,0:T(8,128)S(1)}) custom-call(s32[5]{0:T(128)S(1)} %stack.23.pos_ref, f32[96,384]{1,0:T(8,128)S(1)} %get-tuple-element.43.kept_ref, bf16[112,384]{1,0:T(8,128)(2,1)S(1)} %collective-permute-done.3.msg_ref, f32[8,384]{1,0:T(8,128)S(1)} %get-tuple-element.45.stats_ref, ...), custom_call_target="tpu_custom_call" | custom-call | flops 294912 | bytes 737280 | tf_op jit(solution)/shard_map/pallas_call | solution.py:475
  24.9 1.0 %collective-permute-start.5 = (bf16[112,384]{1,0:T(8,128)(2,1)S(1)}, bf16[112,384]{1,0:T(8,128)(2,1)S(1)}, u32[]{:S(2)}, u32[]{:S(2)}) collective-permute-start(bf16[112,384]{1,0:T(8,128)(2,1)S(1)} %get-tuple-element.49.kept_ref), channel_id=1, source_target_pairs={{0,8},{1,3},{2,10},{3,1},{4,12},{5,7},{6,14},{7,5},{8,0},{9,11},{1... | collective-permute-start | bytes 258056 | tf_op jit(solution)/shard_map/ppermute | solution.py:504
  25.9 0.0 copy-done
  25.9 0.0 copy-done.1
  25.9 0.0 copy-done.2
  25.9 0.0 copy-done.3
  25.9 0.9 %shard_map.74 = (bf16[97,1152]{1,0:T(8,128)(2,1)S(1)}, bf16[97,1536]{1,0:T(8,128)(2,1)S(1)}, bf16[97,640]{1,0:T(8,128)(2,1)S(1)}, f32[8,1152]{1,0:T(8,128)S(1)}, f32[8,1152]{1,0:T(8,128)S(1)}) custom-call(s32[5]{0:T(128)S(1)} %stack.23.pos_ref, s32[97,1536]{1,0:T(8,128)S(1)} %copy-done, s32[12,128]{1,0:T(8,128)S(1)} %bitcast.9, s32[12,128]{1,0:T(8,128)S(1)} %bitcast.10, ...), custom_call_target="tpu_custom_call" | custom-call | flops 1489920 | bytes 1191936 | tf_op jit(solution)/shard_map/pallas_call | solution.py:475
  26.8 0.8 %collective-permute-done.6.msg_ref = bf16[104,768]{1,0:T(8,128)(2,1)S(1)} collective-permute-done((bf16[104,768]{1,0:T(8,128)(2,1)S(1)}, bf16[104,768]{1,0:T(8,128)(2,1)S(1)}, u32[]{:S(2)}, u32[]{:S(2)}) %collective-permute-start.6) | collective-permute-done | bytes 159776 | tf_op jit(solution)/shard_map/ppermute | solution.py:504
  27.7 1.4 %shard_map.75 = (f32[97,768]{1,0:T(8,128)S(1)}, f32[8,768]{1,0:T(8,128)S(1)}) custom-call(s32[5]{0:T(128)S(1)} %stack.23.pos_ref, bf16[104,768]{1,0:T(8,128)(2,1)S(1)} %get-tuple-element.51.kept_ref, bf16[104,768]{1,0:T(8,128)(2,1)S(1)} %collective-permute-done.6.msg_ref, f32[8,768]{1,0:T(8,128)S(1)} %get-tuple-element.48.own_ref.stats_ref, ...), custom_call_target="tpu_custom_call" | custom-call | flops 57212928 | bytes 1474560 | tf_op jit(solution)/shard_map/pallas_call | solution.py:475
  29.1 1.4 %collective-permute-done.5.msg_ref = bf16[112,384]{1,0:T(8,128)(2,1)S(1)} collective-permute-done((bf16[112,384]{1,0:T(8,128)(2,1)S(1)}, bf16[112,384]{1,0:T(8,128)(2,1)S(1)}, u32[]{:S(2)}, u32[]{:S(2)}) %collective-permute-start.5) | collective-permute-done | bytes 86048 | tf_op jit(solution)/shard_map/ppermute | solution.py:504
  30.5 1.4 %shard_map.76 = f32[97,1152]{1,0:T(8,128)S(1)} custom-call(s32[5]{0:T(128)S(1)} %stack.23.pos_ref, bf16[112,384]{1,0:T(8,128)(2,1)S(1)} %get-tuple-element.49.kept_ref, bf16[112,384]{1,0:T(8,128)(2,1)S(1)} %collective-permute-done.5.msg_ref, f32[8,384]{1,0:T(8,128)S(1)} %get-tuple-element.50.stats_ref, f32[8,768]{1,0:T(8,128)S(1)} %get-tuple-element.55.vec_ref, ...), custom_call_target="tpu_custom_call" | custom-call | flops 57212928 | bytes 1474560 | tf_op jit(solution)/shard_map/pallas_call | solution.py:475
  32.0 2.6 %collective-permute-start.7 = (f16[97,1152]{1,0:T(8,128)(2,1)S(1)}, f16[97,1152]{1,0:T(8,128)(2,1)S(1)}, u32[]{:S(2)}, u32[]{:S(2)}) collective-permute-start(f16[97,1152]{1,0:T(8,128)(2,1)S(1)} %convert_element_type.18), channel_id=1, source_target_pairs={{0,4},{1,9},{2,6},{3,11},{4,0},{5,13},{6,2},{7,15},{8,12},{9,1},{1... | collective-permute-start | bytes 670472 | tf_op jit(solution)/shard_map/ppermute | solution.py:504
  34.6 5.4 %collective-permute-done.7 = f16[97,1152]{1,0:T(8,128)(2,1)S(1)} collective-permute-done((f16[97,1152]{1,0:T(8,128)(2,1)S(1)}, f16[97,1152]{1,0:T(8,128)(2,1)S(1)}, u32[]{:S(2)}, u32[]{:S(2)}) %collective-permute-start.7) | collective-permute-done | bytes 223520 | tf_op jit(solution)/shard_map/ppermute | solution.py:504
  40.0 0.1 add_convert_fusion
  40.1 1.9 %collective-permute-start.8 = (f16[97,1152]{1,0:T(8,128)(2,1)S(1)}, f16[97,1152]{1,0:T(8,128)(2,1)S(1)}, u32[]{:S(2)}, u32[]{:S(2)}) collective-permute-start(f16[97,1152]{1,0:T(8,128)(2,1)S(1)} %add_convert_fusion), channel_id=1, source_target_pairs={{0,2},{1,5},{2,0},{3,7},{4,6},{5,1},{6,4},{7,3},{8,10},{9,13},{10,... | collective-permute-start | bytes 670472 | tf_op jit(solution)/shard_map/ppermute | solution.py:504
  41.9 4.3 %collective-permute-done.8 = f16[97,1152]{1,0:T(8,128)(2,1)S(1)} collective-permute-done((f16[97,1152]{1,0:T(8,128)(2,1)S(1)}, f16[97,1152]{1,0:T(8,128)(2,1)S(1)}, u32[]{:S(2)}, u32[]{:S(2)}) %collective-permute-start.8) | collective-permute-done | bytes 223520 | tf_op jit(solution)/shard_map/ppermute | solution.py:504
  46.3 0.1 convert_add_fusion.score_ref
  46.3 1.1 %shard_map.77 = (f32[97,768]{1,0:T(8,128)S(1)}, f32[97,384]{1,0:T(8,128)S(1)}, f32[200,97]{1,0:T(8,128)S(1)}) custom-call(s32[5]{0:T(128)S(1)} %stack.23.pos_ref, f32[97,1152]{1,0:T(8,128)S(1)} %convert_add_fusion.score_ref, bf16[97,1152]{1,0:T(8,128)(2,1)S(1)} %get-tuple-element.53.flag_ref, f32[8,1152]{1,0:T(8,128)S(1)} %get-tuple-element.58.block_ref), custom_call_target="tpu_custom_call" | custom-call | flops 134092800 | bytes 893952 | tf_op jit(solution)/shard_map/pallas_call | solution.py:475
  47.5 0.1 collective-permute-start.9
  47.6 0.5 collective-permute-start.10
  48.1 1.0 %collective-permute-done.10.there_ref = f32[200,97]{1,0:T(8,128)S(1)} collective-permute-done((f32[200,97]{1,0:T(8,128)S(1)}, f32[200,97]{1,0:T(8,128)S(1)}, u32[]{:S(2)}, u32[]{:S(2)}) %collective-permute-start.10) | collective-permute-done | bytes 77632 | tf_op jit(solution)/shard_map/ppermute | solution.py:507
  49.1 0.0 collective-permute-done.9.other_ref
  49.1 1.3 %shard_map.78 = (f32[97,768]{1,0:T(8,128)}, f32[200,97]{1,0:T(8,128)}) custom-call(s32[5]{0:T(128)S(1)} %stack.23.pos_ref, f32[97,768]{1,0:T(8,128)S(1)} %get-tuple-element.59.own_ref, f32[97,384]{1,0:T(8,128)S(1)} %collective-permute-done.9.other_ref, f32[200,97]{1,0:T(8,128)S(1)} %get-tuple-element.61.sums_ref, f32[200,97]{1,0:T(8,128)S(1)} %collective-permute-done.10.there_ref), custom_call_target="tpu_custom_call" | custom-call | flops 111744 | bytes 893952 | tf_op jit(solution)/shard_map/pallas_call | solution.py:475
  (1 shorter events, 0.0 us)
Async XLA Ops:
  5.1 3.1 %collective-permute-start = (bf16[1024,384]{1,0:T(8,128)(2,1)S(1)}, bf16[1024,384]{1,0:T(8,128)(2,1)S(1)}, u32[]{:S(2)}, u32[]{:S(2)}) collective-permute-start(bf16[1024,384]{1,0:T(8,128)(2,1)S(1)} %get-tuple-element.34), channel_id=1, source_target_pairs={{0,1},{1,0},{2,3},{3,2},{4,5},{5,4},{6,7},{7,6},{8,9},{9,8},{10,11... | collective-permute-start | bytes 2359304 | tf_op jit(solution)/shard_map/ppermute | solution.py:507
  5.6 7.4 %collective-permute-start.2 = (bf16[200,768]{1,0:T(8,128)(2,1)S(1)}, bf16[200,768]{1,0:T(8,128)(2,1)S(1)}, u32[]{:S(2)}, u32[]{:S(2)}) collective-permute-start(bf16[200,768]{1,0:T(8,128)(2,1)S(1)} %get-tuple-element.40), channel_id=1, source_target_pairs={{0,2},{1,5},{2,0},{3,7},{4,6},{5,1},{6,4},{7,3},{8,10},{9,13},{10,... | collective-permute-start | bytes 921608 | tf_op jit(solution)/shard_map/ppermute | solution.py:504
  10.6 15.3 %copy-start = (s32[97,1536]{1,0:T(8,128)S(1)}, s32[97,1536]{1,0:T(8,128)}, u32[]{:S(2)}) copy-start(s32[97,1536]{1,0:T(8,128)} %annot_ref.1) | copy-start | bytes 1787908
  10.6 15.3 %copy-start.1 = (s32[1536]{0:T(1024)S(1)}, s32[1536]{0:T(1024)}, u32[]{:S(2)}) copy-start(s32[1536]{0:T(1024)} %param.6) | copy-start | bytes 18436
  10.6 15.3 %copy-start.2 = (s32[1536]{0:T(1024)S(1)}, s32[1536]{0:T(1024)}, u32[]{:S(2)}) copy-start(s32[1536]{0:T(1024)} %param.9) | copy-start | bytes 18436
  10.7 15.3 %copy-start.3 = (s32[1536]{0:T(1024)S(1)}, s32[1536]{0:T(1024)}, u32[]{:S(2)}) copy-start(s32[1536]{0:T(1024)} %param.7) | copy-start | bytes 18436
  10.7 5.5 %collective-permute-start.1 = (bf16[208,384]{1,0:T(8,128)(2,1)S(1)}, bf16[208,384]{1,0:T(8,128)(2,1)S(1)}, u32[]{:S(2)}, u32[]{:S(2)}) collective-permute-start(bf16[208,384]{1,0:T(8,128)(2,1)S(1)} %get-tuple-element.37), channel_id=1, source_target_pairs={{0,2},{1,5},{2,0},{3,7},{4,6},{5,1},{6,4},{7,3},{8,10},{9,13},{10,... | collective-permute-start | bytes 479240 | tf_op jit(solution)/shard_map/ppermute | solution.py:504
  13.9 6.6 %collective-permute-start.4 = (bf16[104,768]{1,0:T(8,128)(2,1)S(1)}, bf16[104,768]{1,0:T(8,128)(2,1)S(1)}, u32[]{:S(2)}, u32[]{:S(2)}) collective-permute-start(bf16[104,768]{1,0:T(8,128)(2,1)S(1)} %get-tuple-element.47), channel_id=1, source_target_pairs={{0,4},{1,9},{2,6},{3,11},{4,0},{5,13},{6,2},{7,15},{8,12},{9,1},{1... | collective-permute-start | bytes 479240 | tf_op jit(solution)/shard_map/ppermute | solution.py:504
  17.2 6.8 %collective-permute-start.3 = (bf16[112,384]{1,0:T(8,128)(2,1)S(1)}, bf16[112,384]{1,0:T(8,128)(2,1)S(1)}, u32[]{:S(2)}, u32[]{:S(2)}) collective-permute-start(bf16[112,384]{1,0:T(8,128)(2,1)S(1)} %get-tuple-element.44), channel_id=1, source_target_pairs={{0,4},{1,9},{2,6},{3,11},{4,0},{5,13},{6,2},{7,15},{8,12},{9,1},{1... | collective-permute-start | bytes 258056 | tf_op jit(solution)/shard_map/ppermute | solution.py:504
  21.4 6.2 %collective-permute-start.6 = (bf16[104,768]{1,0:T(8,128)(2,1)S(1)}, bf16[104,768]{1,0:T(8,128)(2,1)S(1)}, u32[]{:S(2)}, u32[]{:S(2)}) collective-permute-start(bf16[104,768]{1,0:T(8,128)(2,1)S(1)} %get-tuple-element.51.kept_ref), channel_id=1, source_target_pairs={{0,8},{1,3},{2,10},{3,1},{4,12},{5,7},{6,14},{7,5},{8,0},{9,11},{1... | collective-permute-start | bytes 479240 | tf_op jit(solution)/shard_map/ppermute | solution.py:504
  24.9 5.5 %collective-permute-start.5 = (bf16[112,384]{1,0:T(8,128)(2,1)S(1)}, bf16[112,384]{1,0:T(8,128)(2,1)S(1)}, u32[]{:S(2)}, u32[]{:S(2)}) collective-permute-start(bf16[112,384]{1,0:T(8,128)(2,1)S(1)} %get-tuple-element.49.kept_ref), channel_id=1, source_target_pairs={{0,8},{1,3},{2,10},{3,1},{4,12},{5,7},{6,14},{7,5},{8,0},{9,11},{1... | collective-permute-start | bytes 258056 | tf_op jit(solution)/shard_map/ppermute | solution.py:504
  32.0 8.0 %collective-permute-start.7 = (f16[97,1152]{1,0:T(8,128)(2,1)S(1)}, f16[97,1152]{1,0:T(8,128)(2,1)S(1)}, u32[]{:S(2)}, u32[]{:S(2)}) collective-permute-start(f16[97,1152]{1,0:T(8,128)(2,1)S(1)} %convert_element_type.18), channel_id=1, source_target_pairs={{0,4},{1,9},{2,6},{3,11},{4,0},{5,13},{6,2},{7,15},{8,12},{9,1},{1... | collective-permute-start | bytes 670472 | tf_op jit(solution)/shard_map/ppermute | solution.py:504
  40.1 6.2 %collective-permute-start.8 = (f16[97,1152]{1,0:T(8,128)(2,1)S(1)}, f16[97,1152]{1,0:T(8,128)(2,1)S(1)}, u32[]{:S(2)}, u32[]{:S(2)}) collective-permute-start(f16[97,1152]{1,0:T(8,128)(2,1)S(1)} %add_convert_fusion), channel_id=1, source_target_pairs={{0,2},{1,5},{2,0},{3,7},{4,6},{5,1},{6,4},{7,3},{8,10},{9,13},{10,... | collective-permute-start | bytes 670472 | tf_op jit(solution)/shard_map/ppermute | solution.py:504
  47.5 1.6 %collective-permute-start.9 = (f32[97,384]{1,0:T(8,128)S(1)}, f32[97,384]{1,0:T(8,128)S(1)}, u32[]{:S(2)}, u32[]{:S(2)}) collective-permute-start(f32[97,384]{1,0:T(8,128)S(1)} %get-tuple-element.60), channel_id=1, source_target_pairs={{0,1},{1,0},{2,3},{3,2},{4,5},{5,4},{6,7},{7,6},{8,9},{9,8},{10,11... | collective-permute-start | bytes 446984 | tf_op jit(solution)/shard_map/ppermute | solution.py:507
  47.6 1.5 %collective-permute-start.10 = (f32[200,97]{1,0:T(8,128)S(1)}, f32[200,97]{1,0:T(8,128)S(1)}, u32[]{:S(2)}, u32[]{:S(2)}) collective-permute-start(f32[200,97]{1,0:T(8,128)S(1)} %get-tuple-element.61.sums_ref), channel_id=1, source_target_pairs={{0,1},{1,0},{2,3},{3,2},{4,5},{5,4},{6,7},{7,6},{8,9},{9,8},{10,11... | collective-permute-start | bytes 232808 | tf_op jit(solution)/shard_map/ppermute | solution.py:507

commit v5 on v4

v5 whole, which is shorter than its diff:
```python
import functools
import math

import jax
import jax.numpy as jnp
from jax import lax
from jax.experimental import pallas as pl
from jax.experimental.pallas import tpu as pltpu
from jax.sharding import PartitionSpec as P

NBLK = 200
VAR_EPS = 1e-06
F32 = jnp.float32
BF16 = jnp.bfloat16
ORDERS = [[0, 1, 2], [1, 2, 0]]
ROUNDS = [[0, 1], [2, 1]]
VMEM_LIMIT = 20 * 1024 * 1024


STEP = 48


def pick(first, one, other):
    return jnp.where(first, one, other)


def index_parts(start, count, half):
    row = lax.broadcasted_iota(jnp.int32, (count, half), 0) + start
    col = lax.broadcasted_iota(jnp.int32, (count, half), 1)
    return row, col


def column_table(vectors, start, ref):
    table = eight(*vectors)
    half = table.shape[1]
    if start is not None:
        table = pltpu.roll(table, lax.rem(half - start, half), 1)
    for n in range(len(vectors)):
        for k in range(ref.shape[1] // 128):
            here = slice(k * 128, (k + 1) * 128)
            ref[n, here, :] = jnp.broadcast_to(table[n : n + 1, here], (128, 128)).T


def table_rows(ref, offset, columns, half):
    here = pl.ds(pl.multiple_of(offset, 16), STEP)
    return tuple(jnp.concatenate([ref[n, here, :]] * (half // 128), axis=1) for n in columns)


def high_low(values):
    high = values.astype(BF16)
    return high, (values - high.astype(F32)).astype(BF16)


def coded(sums, exact):
    high, low = high_low(sums)
    first, left = high_low(exact)
    third = (exact - first.astype(F32) - left.astype(F32)).astype(BF16)
    rows = coded_rows(sums.shape[0], exact.shape[0])
    gap = rows - 2 * sums.shape[0] - 3 * exact.shape[0]
    blank = [jnp.zeros((gap, sums.shape[1]), BF16)] if gap else []
    return jnp.concatenate([high, low, first, left, third] + blank, axis=0)


def coded_rows(many, exact):
    return -(-(2 * many + 3 * exact) // (24 * exact - 16)) * (24 * exact - 16)


def decoded(rows, many, exact):
    parts = rows.astype(F32)
    sums = parts[:many] + parts[many : 2 * many]
    at = 2 * many
    return sums, parts[at : at + exact] + parts[at + exact : at + 2 * exact] + parts[at + 2 * exact : at + 3 * exact]


def list_rows(many):
    return -(-many // 8) * 8


def put_stats(ref, sums, exact):
    many, width = sums.shape
    gap = list_rows(many) - many
    rows = [sums] + ([jnp.zeros((gap, width), F32)] if gap else [])
    rows = rows + [exact, jnp.zeros((8 - exact.shape[0], width), F32)]
    ref[...] = jnp.concatenate(rows, axis=0)


def merged(bit, msg_ref, stats_ref, rows, many, exact):
    theirs, added = decoded(msg_ref[rows:, :], many, exact)
    mine = stats_ref[:many, :]
    place = list_rows(many)
    both = pick(
        bit == 0, jnp.concatenate([mine, theirs], axis=0), jnp.concatenate([theirs, mine], axis=0)
    )
    return both, stats_ref[place : place + exact, :] + added


def two_parts(values):
    high, low = high_low(values)
    return high.astype(F32) + low.astype(F32)


def own_cols(vec, half):
    return vec[:, :half], vec[:, half : 2 * half]


def own_products(rows, cols, row, col):
    (l_rows, r_rows), (left, right) = rows, cols
    return l_rows * right, jnp.where(row < col, l_rows * left, r_rows * right)


def cross_halves(vec, first, half):
    left, right, there = vec[:, :half], vec[:, half : 2 * half], vec[:, 2 * half :]
    return pick(first, left, there), pick(first, there, right)


def cross_cols(vec, first, half):
    vec = jnp.broadcast_to(vec, (8, vec.shape[1]))
    a_cols, b_cols = cross_halves(vec, first, half)
    a_turned = pltpu.roll(a_cols, half // 2, 1)
    b3_cols = pick(first, pltpu.roll(vec[:, 2 * half :], half // 2, 1), vec[:, :half])
    return b_cols[:1], a_turned[:1], b3_cols[:1]


def cross_vectors(vec, first, half):
    a_cols, b_cols = cross_halves(vec, first, half)
    a2_cols = pick(first, vec[:, half : 2 * half], vec[:, 2 * half :])
    b_late = pltpu.roll(jnp.broadcast_to(b_cols, (8, half)), half // 2, 1)[:1]
    return a_cols, a2_cols, b_late


def cross_products(rows, cols, row, col):
    (a_rows, a2_rows, b_rows), (c_b, c_a, c_b3) = rows, cols
    half = row.shape[1]
    return jnp.where(
        col < half // 2, jnp.where(row > col, a_rows * c_b, b_rows * c_a), a2_rows * c_b3
    )


def dot_n(left, right):
    return lax.dot_general(left, right, (((1,), (0,)), ((), ())), preferred_element_type=F32)


def dot_t(left, right):
    return lax.dot_general(left, right, (((1,), (1,)), ((), ())), preferred_element_type=F32)


def squared_sums(ref, start, stop):
    width = ref.shape[1]
    total = jnp.zeros((8, width), F32)
    for k in range(start, stop, 64):
        part = ref[k : k + 64, :].astype(F32)
        total = total + jnp.sum((part * part).reshape(8, 8, width), axis=0)
    return total


def moments(ref, total):
    count = ref.shape[0]
    sums = dot_n(jnp.ones((8, count), BF16), ref[...])[:1]
    shift = sums * (1.0 / math.sqrt(count))
    return sums, jnp.sum(total, axis=0, keepdims=True) - shift * shift, shift


def eight(*rows):
    return jnp.concatenate(list(rows) + [rows[-1]] * (8 - len(rows)), axis=0)


def halved(bit, keep_ref, send_ref, value):
    part = keep_ref.shape[0]
    for k in range(0, part, STEP):
        send_ref[k : k + STEP, :] = value(pl.multiple_of((1 - bit) * part + k, 16)).astype(BF16)
        keep_ref[k : k + STEP, :] = value(pl.multiple_of(bit * part + k, 16))


def own_gram_kernel(pos_ref, own_ref, keep_ref, send_ref, stats_ref, turned_ref, piece_ref, full_ref, col_ref):
    count, slab = own_ref.shape
    half = slab // 2

    @pl.when(pos_ref[0] == 0)
    def _():
        piece_ref[...] = own_ref[:, half:]

    @pl.when(pos_ref[0] != 0)
    def _():
        piece_ref[...] = own_ref[:, :half]

    turned_ref[...] = own_ref[...].T
    sums, squares, shift = moments(own_ref, squared_sums(own_ref, 0, count))
    sums = two_parts(sums)
    put_stats(stats_ref, sums, jnp.concatenate([squares, shift], axis=0))
    column_table(own_cols(shift, half), None, col_ref)
    left, right = turned_ref[:half, :], turned_ref[half:, :]
    full_ref[:, :half] = dot_n(left, own_ref[:, half:])
    row, col = index_parts(0, half, half)
    full_ref[:, half:] = jnp.where(row < col, dot_n(left, own_ref[:, :half]), dot_n(right, own_ref[:, half:]))
    cols = own_cols(shift, half)

    def value(start):
        rows = table_rows(col_ref, start, (0, 1), half)
        products = own_products(rows, cols, *index_parts(start, STEP, half))
        return full_ref[pl.ds(start, STEP), :] - jnp.concatenate(products, axis=1)

    halved(pos_ref[3], keep_ref, send_ref, value)
    send_ref[keep_ref.shape[0] :, :] = coded(sums, squares)


def cross_gram_kernel(pos_ref, turned_ref, there_ref, own_stats_ref, keep_ref, send_ref, stats_ref, full_ref, col_ref, side_ref):
    half = there_ref.shape[1]
    quarter = half // 2
    core = pos_ref[0]
    first = core == 0
    row, col = index_parts(0, half, half)

    @pl.when(first)
    def _():
        full_ref[:, :half] = dot_n(turned_ref[:half, :], there_ref[...])
        full_ref[:, half:] = pltpu.roll(dot_n(turned_ref[half:, :], there_ref[...]), quarter, 1)

    @pl.when(jnp.logical_not(first))
    def _():
        side_ref[...] = there_ref[...].T
        full_ref[:, :half] = dot_t(side_ref[...], turned_ref[half:, :])
        full_ref[:, half:] = dot_t(side_ref[...], turned_ref[:half, :])

    sums, squares, shift = moments(there_ref, squared_sums(there_ref, 0, there_ref.shape[0]))
    shift = jnp.concatenate([own_stats_ref[list_rows(1) + 1 : list_rows(1) + 2, :], shift], axis=1)
    column_table(cross_vectors(shift, first, half), None, col_ref)
    a_shift, b_shift = cross_halves(shift, first, half)
    straight = full_ref[:, :half]
    level = jnp.sum(jnp.where(row == col, straight, 0.0), axis=0, keepdims=True) - a_shift * b_shift
    sums = two_parts(sums)
    exact = jnp.concatenate([squares, level], axis=0)
    put_stats(stats_ref, sums, exact)
    send_ref[keep_ref.shape[0] :, :] = coded(sums, exact)
    corner = full_ref[half - 256 : half, half - 256 : half].T[256 - quarter :, :]
    corner = pltpu.roll(corner, quarter, 1)[:, :quarter]
    corner = jnp.concatenate([corner, corner], axis=0)
    folded = jnp.concatenate([corner, jnp.zeros((half, half - quarter), F32)], axis=1)
    apart = full_ref[:, half:]
    full_ref[:, :half] = jnp.where(col < quarter, jnp.where(row > col, straight, folded), apart)
    cols = cross_cols(shift, first, half)

    def value(start):
        rows = table_rows(col_ref, start, (0, 1, 2), half)
        products = cross_products(rows, cols, *index_parts(start, STEP, half))
        return full_ref[pl.ds(start, STEP), :half] - products

    halved(pos_ref[3], keep_ref, send_ref, value)


def merge_kernel(pos_ref, kept_ref, msg_ref, stats_ref, *refs, rows_in, bits, many, exact, split):
    keep_ref = refs[-3] if split else None
    send_ref, out_ref = refs[-2:]
    rows = rows_in

    def value(offset):
        here = pl.ds(offset, STEP)
        return kept_ref[here, :].astype(F32) + msg_ref[here, :].astype(F32)

    if split:
        halved(pos_ref[bits[1]], keep_ref, send_ref, value)
        done = keep_ref.shape[0]
    else:
        done = rows
        for k in range(0, rows, STEP):
            send_ref[k : k + STEP, :] = value(k).astype(BF16)
    sums, more = merged(pos_ref[bits[0]], msg_ref, stats_ref, rows, many, exact)
    put_stats(out_ref, sums, more)
    send_ref[done:, :] = coded(sums, more)


def deviations(sums, samples):
    mean = jnp.sum(sums, axis=0, keepdims=True) * (1.0 / sums.shape[0])
    return (sums - mean) * (1.0 / math.sqrt(samples))


def outer_sums(left, right):
    (l_high, l_low), (r_high, r_low) = high_low(left), high_low(right)
    left = jnp.concatenate([l_high, l_high, l_low], axis=0)
    right = jnp.concatenate([r_high, r_low, r_high], axis=0)
    return lax.dot_general(left, right, (((0,), (0,)), ((), ())), preferred_element_type=F32)


def from_row(vec, start):
    half = vec.shape[1]
    return pltpu.roll(vec, lax.rem(half - start, half), 1)[:, :128]


def unbiased(correl, everyone):
    squared = correl * correl
    return squared - (1.0 - squared) * (1.0 / (everyone - 2.0))


def placed_at(rows_part, offset, half):
    blank = jnp.zeros((rows_part.shape[0], half - rows_part.shape[1]), F32)
    return pltpu.roll(jnp.concatenate([rows_part, blank], axis=1), offset, 1)


def own_score_kernel(
    pos_ref, kept_ref, msg_ref, stats_ref, limit_ref, flag_ref, sub_ref,
    out_ref, vec_ref, col_ref, one_ref, two_ref, *, bit, many, samples,
):
    rows = one_ref.shape[0]
    half = kept_ref.shape[1] // 2
    everyone = 2.0 * many * samples
    base = pos_ref[2]
    sums, squares = merged(pos_ref[bit], msg_ref, stats_ref, rows, many, 1)
    apart = deviations(sums, samples)
    squares = squares + jnp.sum(apart * apart, axis=0, keepdims=True)
    scale = 1.0 / jnp.sqrt(squares * (1.0 / everyone) + VAR_EPS)
    put_stats(vec_ref, apart, scale)
    scales = own_cols(scale, half)
    factors = own_cols(scale * (1.0 / everyone), half) + (limit_ref[:1, :half],)
    column_table(factors, base, col_ref)
    left, right = own_cols(apart, half)
    l_rows = from_row(left, base)
    products = outer_sums(l_rows, right), outer_sums(l_rows, left), outer_sums(from_row(right, base), right)
    right_lim = limit_ref[:1, half : 2 * half]
    for k in range(0, rows, STEP):
        start = base + k
        row, col = index_parts(start, STEP, half)
        l_scale, r_scale, left_lim = table_rows(col_ref, k, range(3), half)
        one, upper, lower = (x[k : k + STEP] for x in products)
        shifts = one, jnp.where(row < col, upper, lower)
        norms = own_products((l_scale, r_scale), scales, row, col)
        gaps = (half + col - row, jnp.where(row == col, 8 * half, jnp.abs(row - col)))
        lims = (left_lim, jnp.where(row < col, left_lim, right_lim))
        for s, ref in ((0, one_ref), (1, two_ref)):
            here = slice(s * half, (s + 1) * half)
            value = kept_ref[k : k + STEP, here].astype(F32) + msg_ref[k : k + STEP, here].astype(F32)
            weight = unbiased((value + shifts[s]) * norms[s], everyone)
            ref[k : k + STEP, :] = jnp.where(gaps[s].astype(F32) <= lims[s], weight, 0.0).astype(BF16)
    row, col = index_parts(base, rows, half)
    one, two = one_ref[...], two_ref[...]
    zero = jnp.zeros_like(two)
    upper, lower = jnp.where(row < col, two, zero), jnp.where(row > col, two, zero)
    f_left, f_right = flag_ref[:, :half], flag_ref[:, half : 2 * half]
    s_left, s_right = sub_ref[:, :rows], sub_ref[:, 128 : 128 + rows]
    out_ref[:, :half] = dot_n(s_left, upper) + placed_at(dot_t(f_right, one) + dot_t(f_left, upper), base, half)
    out_ref[:, half:] = dot_n(s_left, one) + dot_n(s_right, lower) + placed_at(dot_t(f_right, lower), base, half)


def cross_score_kernel(
    pos_ref, kept_ref, msg_ref, stats_ref, vec_ref, limit_ref, flag_ref, sub_ref, own_ref,
    out_ref, col_ref, three_ref, *, bit, many, samples,
):
    rows = three_ref.shape[0]
    half = kept_ref.shape[1]
    quarter = half // 2
    core = pos_ref[0]
    first = core == 0
    everyone = 2.0 * many * samples
    base = pos_ref[2]
    sums, exact = merged(pos_ref[bit], msg_ref, stats_ref, rows, many, 2)
    apart = deviations(sums, samples)
    squares = exact[:1] + jnp.sum(apart * apart, axis=0, keepdims=True)
    place = list_rows(2 * many)
    apart = jnp.concatenate([vec_ref[: 2 * many, :], apart], axis=1)
    a_apart, b_apart = cross_halves(apart, first, half)
    level = exact[1:2] + jnp.sum(a_apart * b_apart, axis=0, keepdims=True)
    scale = 1.0 / jnp.sqrt(squares * (1.0 / everyone) + VAR_EPS)
    scale = jnp.concatenate([vec_ref[place : place + 1, :], scale], axis=1)
    limit = limit_ref[:1, :]
    factors = cross_vectors(scale * (1.0 / everyone), first, half)
    column_table(factors + cross_vectors(limit, first, half)[:2], base, col_ref)
    scales = cross_cols(scale, first, half)
    there = apart[:, 2 * half :]
    a2_apart = pick(first, apart[:, half : 2 * half], there)
    b3_apart = pick(first, pltpu.roll(there, quarter, 1), apart[:, :half])
    late_a, late_b = pltpu.roll(a_apart, quarter, 1), pltpu.roll(b_apart, quarter, 1)
    shifts = (
        outer_sums(from_row(a_apart, base), b_apart),
        outer_sums(from_row(late_b, base), late_a),
        outer_sums(from_row(a2_apart, base), b3_apart),
    )
    _, late_lim, _ = cross_cols(limit, first, half)
    for k in range(0, rows, STEP):
        start = base + k
        row, col = index_parts(start, STEP, half)
        fold = col < quarter
        parts = table_rows(col_ref, k, range(5), half)
        a_lim, a2_lim = parts[3:]
        straight, late, apart = (x[k : k + STEP] for x in shifts)
        products = jnp.where(fold, jnp.where(row > col, straight, late), apart)
        norms = cross_products(parts[:3], scales, row, col)
        lims = jnp.where(fold, jnp.where(row > col, a_lim, late_lim), a2_lim)
        near = jnp.where(row == col, 8 * half, 2 * half - jnp.abs(row - col))
        gaps = jnp.where(fold, near, quarter + quarter * core + col - row)
        value = kept_ref[k : k + STEP, :].astype(F32) + msg_ref[k : k + STEP, :].astype(F32)
        weight = unbiased((value + products) * norms, everyone)
        three_ref[k : k + STEP, :] = jnp.where(gaps.astype(F32) <= lims, weight, 0.0).astype(BF16)
    a_scale, b_scale = cross_halves(scale, first, half)
    a_limit, _ = cross_halves(limit, first, half)
    lane = lax.broadcasted_iota(jnp.int32, (1, half), 1)
    level = unbiased(level * (1.0 / everyone) * a_scale * b_scale, everyone)
    mine = (lane >= base) & (lane < base + rows) & (a_limit >= 2.0 * half)
    level = jnp.where(mine, level, 0.0)
    row, col = index_parts(base, rows, half)
    three = three_ref[...]
    zero = jnp.zeros_like(three)
    fold = col < quarter
    straight = jnp.where(fold & (row > col), three, zero)
    folded = jnp.where(fold & (row < col), three, zero)
    apart = jnp.where(fold, zero, three)
    f_a, f_b = flag_ref[:, :half], flag_ref[:, half : 2 * half]
    f_late, f_b3 = flag_ref[:, 2 * half : 3 * half], flag_ref[:, 3 * half :]
    s_a, s_a2, s_late = sub_ref[:, 256 : 256 + rows], sub_ref[:, 384 : 384 + rows], sub_ref[:, 512 : 512 + rows]
    out_a = placed_at(dot_t(f_b, straight), base, half) + pltpu.roll(dot_n(s_late, folded), quarter, 1)
    out_b = dot_n(s_a, straight) + placed_at(dot_t(f_late, folded), lax.rem(base + quarter, half), half)
    out_a = out_a + f_b.astype(F32) * level
    out_b = out_b + f_a.astype(F32) * level
    out_a2 = placed_at(dot_t(f_b3, apart), base, half)
    out_b3 = dot_n(s_a2, apart)
    out_ref[:, :half] = own_ref[:, :half] + pick(first, out_a, out_b3)
    out_ref[:, half : 2 * half] = own_ref[:, half:] + pick(first, out_a2, out_b)
    out_ref[:, 2 * half :] = pick(first, out_b + pltpu.roll(out_b3, quarter, 1), out_a + out_a2)


def local_kernel(pos_ref, annot_ref, chrom_ref, reach_ref, ids_ref, flag_ref, cross_ref, sub_ref, limit_ref, hot_ref):
    half = annot_ref.shape[1] // 4
    first = pos_ref[0] == 0
    base = pos_ref[2]
    flags = annot_ref[...].astype(F32)

    def quarters(x):
        return [x[:, k * half : (k + 1) * half] for k in range(4)]

    def local(x):
        one, two, three, four = quarters(x)
        return pick(first, one, three), pick(first, two, four), pick(first, three, two)

    left, right, there = local(flags)
    for k, x in enumerate((left, right, there)):
        flag_ref[:, k * half : (k + 1) * half] = x.astype(BF16)
    a_cols, b_cols, a2_cols = pick(first, left, there), pick(first, there, right), pick(first, right, there)
    b3_cols = pick(first, pltpu.roll(there, half // 2, 1), left)
    for k, x in enumerate((a_cols, b_cols, pltpu.roll(a_cols, half // 2, 1), b3_cols)):
        cross_ref[:, k * half : (k + 1) * half] = x.astype(BF16)
    back = lax.rem(half - base, half)
    late = lax.rem(half + half // 2 - base, half)
    for k, (x, turn) in enumerate(((left, back), (right, back), (a_cols, back), (a2_cols, back), (b_cols, late))):
        sub_ref[:, k * 128 : (k + 1) * 128] = pltpu.roll(x, turn, 1)[:, :128].astype(BF16)

    def line(ref):
        return jnp.concatenate([ref[k : k + 1, :] for k in range(ref.shape[0])], axis=1).astype(F32)

    chrom, reach = line(chrom_ref), line(reach_ref)
    ends = [jnp.sum((chrom <= k).astype(F32), axis=1, keepdims=True) for k in (1, 2, 3)]
    last = jnp.where(chrom == 1, ends[0], jnp.where(chrom == 2, ends[1], ends[2]))
    place = lax.broadcasted_iota(jnp.int32, chrom.shape, 1).astype(F32)
    limit = jnp.concatenate(local(jnp.minimum(reach, last - 1.0 - place)), axis=1)
    limit_ref[...] = jnp.broadcast_to(limit, limit_ref.shape)
    block = jnp.concatenate(local(line(ids_ref)), axis=1)
    tall = jnp.broadcast_to(block, (128, block.shape[1]))
    for k in range(block.shape[1] // 128):
        rows = tall[:, k * 128 : (k + 1) * 128].T
        for n in range(hot_ref.shape[1] // 128):
            number = (lax.broadcasted_iota(jnp.int32, rows.shape, 1) + n * 128).astype(F32)
            hot_ref[k * 128 : (k + 1) * 128, n * 128 : (n + 1) * 128] = jnp.where(number == rows, 1.0, 0.0).astype(BF16)


def block_kernel(pos_ref, score_ref, flag_ref, hot_ref, sum_ref):
    slab = flag_ref.shape[1] // 3 * 2
    hot = hot_ref[...]
    own = score_ref[:, :slab] + flag_ref[:, :slab].astype(F32)
    scores = jnp.concatenate([own, score_ref[:, slab:]], axis=1)
    high = scores.astype(BF16)
    left = scores - high.astype(F32)
    sum_ref[...] = (dot_n(high, hot) + dot_n(left.astype(BF16), hot)).T[: sum_ref.shape[0], :]


def call(kernel, inputs, outputs, scratch, flops, moved):
    vmem = pl.BlockSpec(memory_space=pltpu.VMEM)
    smem = pl.BlockSpec(memory_space=pltpu.SMEM)
    return pl.pallas_call(
        kernel,
        out_shape=outputs,
        in_specs=[smem] + [vmem] * (len(inputs) - 1),
        out_specs=jax.tree.map(lambda _: vmem, outputs),
        scratch_shapes=scratch,
        compiler_params=pltpu.CompilerParams(vmem_limit_bytes=VMEM_LIMIT),
        cost_estimate=pl.CostEstimate(flops=flops, bytes_accessed=moved, transcendentals=0),
    )(*inputs)


def body(genotypes, chromosome, blocks, annotation, reach):
    count, slab = genotypes.shape
    half = slab // 2
    quarter = half // 2
    width = 3 * half
    snps = chromosome.shape[0]
    parts = lax.axis_size("samples")
    bits = parts.bit_length() - 1
    core = lax.axis_index("genome")
    place = lax.axis_index("samples")
    order = [first + list(range(3, bits)) for first in ORDERS]
    bit_at = [(place >> jnp.where(core == 0, order[0][t], order[1][t])) & 1 for t in range(bits)]

    def exchange(x, t, order=order):
        route = []
        for s in range(parts):
            for g in range(2):
                route.append((s * 2 + g, (s ^ (1 << order[g][t])) * 2 + g))
        return lax.ppermute(x, ("samples", "genome"), route)

    def across(x):
        return lax.ppermute(x, "genome", [(0, 1), (1, 0)])

    def shape(rows, cols, dtype):
        return jax.ShapeDtypeStruct((rows, cols), dtype)

    base = bit_at[0] * quarter + bit_at[1] * (quarter // 2)
    rows = quarter // 2

    where = jnp.stack([core, place, base] + bit_at).astype(jnp.int32)
    annot = annotation.shape[0]

    hot_rows = -(-NBLK // 8) * 8

    def tiles(x):
        return x.reshape(-1, 128)

    flags, flags_cross, subs, limit, hot = call(
        local_kernel,
        (where, annotation, tiles(chromosome), tiles(reach), tiles(blocks)),
        (
            shape(annot, width, BF16),
            shape(annot, 4 * half, BF16),
            shape(annot, 5 * 128, BF16),
            shape(8, width, F32),
            shape(width, -(-hot_rows // 128) * 128, BF16),
        ),
        [],
        annot * snps * 10,
        annot * snps * 8,
    )
    def table_of(vectors, count):
        return pltpu.VMEM((vectors, -(-count // 128) * 128, 128), F32)

    def outputs(kept, sent, cols, many, exact):
        kept_shape = (shape(kept, cols, F32),) if kept else ()
        coded_shape = shape(sent + coded_rows(many, exact), cols, BF16)
        return kept_shape + (coded_shape, shape(list_rows(many) + 8, cols, F32))

    keep_a, send_a, stats_a, turned, piece = call(
        own_gram_kernel,
        (where, genotypes),
        outputs(quarter, quarter, slab, 1, 1)
        + (shape(slab, count, BF16), shape(count, half, BF16)),
        [pltpu.VMEM((half, slab), F32), table_of(2, half)],
        2 * count * half * half * 3,
        count * slab * 2,
    )
    there = across(piece)
    msg_a = exchange(send_a, 0)
    keep_b, send_b, stats_b = call(
        cross_gram_kernel,
        (where, turned, there, stats_a),
        outputs(quarter, quarter, half, 1, 2),
        [pltpu.VMEM((half, slab), F32), table_of(3, half), pltpu.VMEM((half, count), BF16)],
        2 * count * half * half * 3,
        count * slab * 2,
    )
    msg_b = exchange(send_b, 0)

    def merge(keep, msg, stats, cols, t, exact, *after):
        split = t == 1
        *kept, send, stats = call(
            functools.partial(merge_kernel, rows_in=quarter if split else rows, bits=(2 + t, 3 + t), many=1 << (t - 1), exact=exact, split=split),
            (where, keep, msg, stats) + after,
            outputs(rows if split else 0, rows, cols, 1 << t, exact),
            [],
            rows * cols * 8,
            rows * cols * 20,
        )
        return (kept[0] if split else send), send, stats

    for t in range(1, bits):
        if t == 1:
            msg_a, send_b = lax.optimization_barrier((msg_a, send_b))
        keep_a, send_a, stats_a = merge(keep_a, msg_a, stats_a, slab, t, 1)
        msg_a = exchange(send_a, t)
        keep_b, send_b, stats_b = merge(keep_b, msg_b, stats_b, half, t, 2, stats_a)
        msg_b = exchange(send_b, t)
    last = {"bit": 2 + bits, "many": parts // 2, "samples": float(count)}
    scores_a, vectors = call(
        functools.partial(own_score_kernel, **last),
        (where, keep_a, msg_a, stats_a, limit, flags, subs),
        (shape(annot, slab, F32), shape(list_rows(parts) + 8, slab, F32)),
        [table_of(3, rows)] + [pltpu.VMEM((rows, half), BF16)] * 2,
        2 * annot * half * rows * 8,
        rows * slab * 20,
    )
    partial = call(
        functools.partial(cross_score_kernel, **last),
        (where, keep_b, msg_b, stats_b, vectors, limit, flags_cross, subs, scores_a),
        shape(annot, width, F32),
        [table_of(5, rows)] + [pltpu.VMEM((rows, half), BF16)],
        2 * annot * half * rows * 8,
        rows * slab * 20,
    )
    for t in range(2):
        rounded = partial.astype(jnp.float16)
        partial = rounded.astype(F32) + exchange(rounded, t, ROUNDS).astype(F32)
    arrived = across(partial[:, slab:])
    sums = call(
        block_kernel,
        (where, partial, flags, hot),
        shape(hot_rows, annot, F32),
        [],
        2 * annot * width * hot_rows * 2,
        annot * width * 8,
    )
    nothing = jnp.zeros_like(arrived)
    ld_scores = (partial[:, :slab] + flags[:, :slab].astype(F32)) + jnp.where(
        core == 0,
        jnp.concatenate([nothing, arrived], axis=1),
        jnp.concatenate([arrived, nothing], axis=1),
    )
    sums_there = across(sums)
    sums, ld_scores = lax.optimization_barrier((sums, ld_scores))
    return (ld_scores, (sums + sums_there)[:NBLK].T)


def solution(mesh):
    placed = (
        P(("groups", "samples"), "genome"),
        P("groups"),
        P("groups"),
        P(None, "groups"),
        P("groups"),
    )
    return jax.shard_map(
        body,
        mesh=mesh,
        in_specs=placed,
        out_specs=(P(None, ("groups", "genome")), P(None, "groups")),
        check_vma=False,
    )
```

time: 50.6 us -> 48 us (0.949)
  Pallas kernels: 16.7 us -> 12.1 us
  other arithmetic: 0.17 us -> 1.59 us
  local copies, waits for them, and re-layouts: 0.11 us -> 1.53 us
    pallas_call x11 -> x10, Pallas kernels: 16.7 us -> 12.1 us  [call(): pl.pallas_call(kernel, out_shape=outputs, in_specs=[smem] + [vmem] * (len...]
    unnamed x8 -> x10, local copies, waits for them, and re-layouts: 0.03 us -> 1.44 us
    ppermute x3, waiting for transfers between devices: 1.03 us -> 0.18 us  [across(): return lax.ppermute(x, 'genome', [(0, 1), (1, 0)])]
    add x1 -> x2, other arithmetic: 0.06 us -> 0.82 us  [the longest x1 0.77 us: body(): partial[:, :slab] + flags[:, :slab].astype(F32) + jnp.where(core == 0, jn...]
    transpose x0 -> x1, other arithmetic: none -> 0.65 us  [body(): return (ld_scores, (sums + sums_there)[:NBLK].T)]
  transfers between devices with their start and end apart: 11 -> 11, of which waited for: 8 -> 8; matrix products, arithmetic and copies ran while one was open for 0% -> 2% of each run, Pallas kernels for 17% -> 17%
where the time goes in v5:
time: 48 us; the launch traced here: 47.9 us
  starting transfers between devices  18.1 us (38%)
  waiting for transfers between devices  13.9 us (29%)
  Pallas kernels  12.1 us (25%)
  other arithmetic  1.59 us (3%)
  local copies, waits for them, and re-layouts  1.53 us (3%)
  between operations  0.78 us (2%)
    ppermute x8, starting transfers between devices, exchange(): return lax.ppermute(x, ('samples', 'genome'), route)  16.9 us
    ppermute x8, waiting for transfers between devices, exchange(): return lax.ppermute(x, ('samples', 'genome'), route)  13.7 us
    pallas_call x10, Pallas kernels, call(): pl.pallas_call(kernel, out_shape=outputs, in_specs=[smem] + [vmem] * (len...  12.1 us
    unnamed x10, local copies, waits for them, and re-layouts  1.44 us
    ppermute x3, starting transfers between devices, across(): return lax.ppermute(x, 'genome', [(0, 1), (1, 0)])  1.15 us
  transfers between devices with their start and end apart: 11, of which 8 were waited for; matrix products, arithmetic and copies ran while one was open for 2% of the time, Pallas kernels for 17%

profile of v5, /device:TPU:0, one launch (start us, length us, event | category | flops | bytes accessed | tf_op | source)
XLA Modules:
  0.0 47.9 jit_solution(6041082543197445127)
XLA Ops:
  0.6 0.1 stack.27.pos_ref
  0.7 0.0 copy-start.4
  0.7 1.4 %copy-done.4 = bf16[1024,768]{1,0:T(8,128)(2,1)S(1)} copy-done((bf16[1024,768]{1,0:T(8,128)(2,1)S(1)}, bf16[1024,768]{1,0:T(8,128)(2,1)}, u32[]{:S(2)}) %copy-start.4) | copy-done | bytes 1572888
  2.1 2.4 %shard_map.68 = (f32[192,768]{1,0:T(8,128)S(1)}, bf16[200,768]{1,0:T(8,128)(2,1)S(1)}, f32[16,768]{1,0:T(8,128)S(1)}, bf16[768,1024]{1,0:T(8,128)(2,1)S(1)}, bf16[1024,384]{1,0:T(8,128)(2,1)S(1)}) custom-call(s32[6]{0:T(128)S(1)} %stack.27.pos_ref, bf16[1024,768]{1,0:T(8,128)(2,1)S(1)} %copy-done.4), custom_call_target="tpu_custom_call" | custom-call | flops 905969664 | bytes 1572864 | tf_op jit(solution)/shard_map/pallas_call | solution.py:474
  4.6 0.5 %collective-permute-start = (bf16[1024,384]{1,0:T(8,128)(2,1)S(1)}, bf16[1024,384]{1,0:T(8,128)(2,1)S(1)}, u32[]{:S(2)}, u32[]{:S(2)}) collective-permute-start(bf16[1024,384]{1,0:T(8,128)(2,1)S(1)} %get-tuple-element.31), channel_id=1, source_target_pairs={{0,1},{1,0},{2,3},{3,2},{4,5},{5,4},{6,7},{7,6},{8,9},{9,8},{10,11... | collective-permute-start | bytes 2359304 | tf_op jit(solution)/shard_map/ppermute | solution.py:506
  5.1 2.6 %collective-permute-start.2 = (bf16[200,768]{1,0:T(8,128)(2,1)S(1)}, bf16[200,768]{1,0:T(8,128)(2,1)S(1)}, u32[]{:S(2)}, u32[]{:S(2)}) collective-permute-start(bf16[200,768]{1,0:T(8,128)(2,1)S(1)} %get-tuple-element.37), channel_id=1, source_target_pairs={{0,2},{1,5},{2,0},{3,7},{4,6},{5,1},{6,4},{7,3},{8,10},{9,13},{10,... | collective-permute-start | bytes 921608 | tf_op jit(solution)/shard_map/ppermute | solution.py:503
  7.7 0.0 collective-permute-done.there_ref
  7.7 2.3 %shard_map.69 = (f32[192,384]{1,0:T(8,128)S(1)}, bf16[224,384]{1,0:T(8,128)(2,1)S(1)}, f32[16,384]{1,0:T(8,128)S(1)}) custom-call(s32[6]{0:T(128)S(1)} %stack.27.pos_ref, bf16[768,1024]{1,0:T(8,128)(2,1)S(1)} %get-tuple-element.30.turned_ref, bf16[1024,384]{1,0:T(8,128)(2,1)S(1)} %collective-permute-done.there_ref, ...), custom_call_target="tpu_custom_call" | custom-call | flops 905969664 | bytes 1572864 | tf_op jit(solution)/shard_map/pallas_call | solution.py:474
  10.0 0.0 copy-start
  10.0 0.0 copy-start.1
  10.0 0.0 copy-start.2
  10.0 0.0 copy-start.3
  10.0 2.3 %collective-permute-start.1 = (bf16[224,384]{1,0:T(8,128)(2,1)S(1)}, bf16[224,384]{1,0:T(8,128)(2,1)S(1)}, u32[]{:S(2)}, u32[]{:S(2)}) collective-permute-start(bf16[224,384]{1,0:T(8,128)(2,1)S(1)} %get-tuple-element.34), channel_id=1, source_target_pairs={{0,2},{1,5},{2,0},{3,7},{4,6},{5,1},{6,4},{7,3},{8,10},{9,13},{10,... | collective-permute-start | bytes 516104 | tf_op jit(solution)/shard_map/ppermute | solution.py:503
  12.3 0.2 collective-permute-done.2.msg_ref
  12.5 0.6 %shard_map.70 = (f32[96,768]{1,0:T(8,128)S(1)}, bf16[104,768]{1,0:T(8,128)(2,1)S(1)}, f32[16,768]{1,0:T(8,128)S(1)}) custom-call(s32[6]{0:T(128)S(1)} %stack.27.pos_ref, f32[192,768]{1,0:T(8,128)S(1)} %get-tuple-element.36.kept_ref, bf16[200,768]{1,0:T(8,128)(2,1)S(1)} %collective-permute-done.2.msg_ref, f32[16,768]{1,0:T(8,128)S(1)} %get-tuple-element.32.own_stats_ref.stats_ref), custom_call_target="tpu_custom_call" | custom-call | flops 589824 | bytes 1474560 | tf_op jit(solution)/shard_map/pallas_call | solution.py:474
  13.1 2.2 %collective-permute-start.4 = (bf16[104,768]{1,0:T(8,128)(2,1)S(1)}, bf16[104,768]{1,0:T(8,128)(2,1)S(1)}, u32[]{:S(2)}, u32[]{:S(2)}) collective-permute-start(bf16[104,768]{1,0:T(8,128)(2,1)S(1)} %get-tuple-element.44), channel_id=1, source_target_pairs={{0,4},{1,9},{2,6},{3,11},{4,0},{5,13},{6,2},{7,15},{8,12},{9,1},{1... | collective-permute-start | bytes 479240 | tf_op jit(solution)/shard_map/ppermute | solution.py:503
  15.3 0.4 collective-permute-done.1.msg_ref
  15.7 0.6 %shard_map.71 = (f32[96,384]{1,0:T(8,128)S(1)}, bf16[128,384]{1,0:T(8,128)(2,1)S(1)}, f32[16,384]{1,0:T(8,128)S(1)}) custom-call(s32[6]{0:T(128)S(1)} %stack.27.pos_ref, f32[192,384]{1,0:T(8,128)S(1)} %get-tuple-element.33.kept_ref, bf16[224,384]{1,0:T(8,128)(2,1)S(1)} %collective-permute-done.1.msg_ref, f32[16,384]{1,0:T(8,128)S(1)} %get-tuple-element.35.stats_ref, ...), custom_call_target="tpu_custom_call" | custom-call | flops 294912 | bytes 737280 | tf_op jit(solution)/shard_map/pallas_call | solution.py:474
  16.3 2.2 %collective-permute-start.3 = (bf16[128,384]{1,0:T(8,128)(2,1)S(1)}, bf16[128,384]{1,0:T(8,128)(2,1)S(1)}, u32[]{:S(2)}, u32[]{:S(2)}) collective-permute-start(bf16[128,384]{1,0:T(8,128)(2,1)S(1)} %get-tuple-element.41), channel_id=1, source_target_pairs={{0,4},{1,9},{2,6},{3,11},{4,0},{5,13},{6,2},{7,15},{8,12},{9,1},{1... | collective-permute-start | bytes 294920 | tf_op jit(solution)/shard_map/ppermute | solution.py:503
  18.4 1.3 %collective-permute-done.4.msg_ref = bf16[104,768]{1,0:T(8,128)(2,1)S(1)} collective-permute-done((bf16[104,768]{1,0:T(8,128)(2,1)S(1)}, bf16[104,768]{1,0:T(8,128)(2,1)S(1)}, u32[]{:S(2)}, u32[]{:S(2)}) %collective-permute-start.4) | collective-permute-done | bytes 159776 | tf_op jit(solution)/shard_map/ppermute | solution.py:503
  19.8 0.6 %shard_map.72 = (bf16[112,768]{1,0:T(8,128)(2,1)S(1)}, f32[16,768]{1,0:T(8,128)S(1)}) custom-call(s32[6]{0:T(128)S(1)} %stack.27.pos_ref, f32[96,768]{1,0:T(8,128)S(1)} %get-tuple-element.43.kept_ref, bf16[104,768]{1,0:T(8,128)(2,1)S(1)} %collective-permute-done.4.msg_ref, f32[16,768]{1,0:T(8,128)S(1)} %get-tuple-element.39.refs_0_.stats_ref), custom_call_target="tpu_custom_call" | custom-call | flops 589824 | bytes 1474560 | tf_op jit(solution)/shard_map/pallas_call | solution.py:474
  20.4 2.6 %collective-permute-start.6 = (bf16[112,768]{1,0:T(8,128)(2,1)S(1)}, bf16[112,768]{1,0:T(8,128)(2,1)S(1)}, u32[]{:S(2)}, u32[]{:S(2)}) collective-permute-start(bf16[112,768]{1,0:T(8,128)(2,1)S(1)} %get-tuple-element.48.kept_ref), channel_id=1, source_target_pairs={{0,8},{1,3},{2,10},{3,1},{4,12},{5,7},{6,14},{7,5},{8,0},{9,11},{1... | collective-permute-start | bytes 516104 | tf_op jit(solution)/shard_map/ppermute | solution.py:503
  23.0 0.0 collective-permute-done.3.msg_ref
  23.0 0.6 %shard_map.73 = (bf16[128,384]{1,0:T(8,128)(2,1)S(1)}, f32[16,384]{1,0:T(8,128)S(1)}) custom-call(s32[6]{0:T(128)S(1)} %stack.27.pos_ref, f32[96,384]{1,0:T(8,128)S(1)} %get-tuple-element.40.kept_ref, bf16[128,384]{1,0:T(8,128)(2,1)S(1)} %collective-permute-done.3.msg_ref, f32[16,384]{1,0:T(8,128)S(1)} %get-tuple-element.42.stats_ref, ...), custom_call_target="tpu_custom_call" | custom-call | flops 294912 | bytes 737280 | tf_op jit(solution)/shard_map/pallas_call | solution.py:474
  23.5 1.5 %collective-permute-start.5 = (bf16[128,384]{1,0:T(8,128)(2,1)S(1)}, bf16[128,384]{1,0:T(8,128)(2,1)S(1)}, u32[]{:S(2)}, u32[]{:S(2)}) collective-permute-start(bf16[128,384]{1,0:T(8,128)(2,1)S(1)} %get-tuple-element.46.kept_ref), channel_id=1, source_target_pairs={{0,8},{1,3},{2,10},{3,1},{4,12},{5,7},{6,14},{7,5},{8,0},{9,11},{1... | collective-permute-start | bytes 294920 | tf_op jit(solution)/shard_map/ppermute | solution.py:503
  25.0 0.0 copy-done
  25.0 0.0 copy-done.1
  25.0 0.0 copy-done.2
  25.0 0.0 copy-done.3
  25.0 1.0 %shard_map.74 = (bf16[97,1152]{1,0:T(8,128)(2,1)S(1)}, bf16[97,1536]{1,0:T(8,128)(2,1)S(1)}, bf16[97,640]{1,0:T(8,128)(2,1)S(1)}, f32[8,1152]{1,0:T(8,128)S(1)}, bf16[1152,256]{1,0:T(8,128)(2,1)S(1)}) custom-call(s32[6]{0:T(128)S(1)} %stack.27.pos_ref, s32[97,1536]{1,0:T(8,128)S(1)} %copy-done, s32[12,128]{1,0:T(8,128)S(1)} %bitcast.11, ...), custom_call_target="tpu_custom_call" | custom-call | flops 1489920 | bytes 1191936 | tf_op jit(solution)/shard_map/pallas_call | solution.py:474
  26.1 0.6 %collective-permute-done.6.msg_ref = bf16[112,768]{1,0:T(8,128)(2,1)S(1)} collective-permute-done((bf16[112,768]{1,0:T(8,128)(2,1)S(1)}, bf16[112,768]{1,0:T(8,128)(2,1)S(1)}, u32[]{:S(2)}, u32[]{:S(2)}) %collective-permute-start.6) | collective-permute-done | bytes 172064 | tf_op jit(solution)/shard_map/ppermute | solution.py:503
  26.7 1.4 %shard_map.75 = (f32[97,768]{1,0:T(8,128)S(1)}, f32[16,768]{1,0:T(8,128)S(1)}) custom-call(s32[6]{0:T(128)S(1)} %stack.27.pos_ref, bf16[112,768]{1,0:T(8,128)(2,1)S(1)} %get-tuple-element.48.kept_ref, bf16[112,768]{1,0:T(8,128)(2,1)S(1)} %collective-permute-done.6.msg_ref, f32[16,768]{1,0:T(8,128)S(1)} %get-tuple-element.45.refs_0_.stats_ref, ...), custom_call_target="tpu_custom_call" | custom-call | flops 57212928 | bytes 1474560 | tf_op jit(solution)/shard_map/pallas_call | solution.py:474
  28.2 1.5 %collective-permute-done.5.msg_ref = bf16[128,384]{1,0:T(8,128)(2,1)S(1)} collective-permute-done((bf16[128,384]{1,0:T(8,128)(2,1)S(1)}, bf16[128,384]{1,0:T(8,128)(2,1)S(1)}, u32[]{:S(2)}, u32[]{:S(2)}) %collective-permute-start.5) | collective-permute-done | bytes 98336 | tf_op jit(solution)/shard_map/ppermute | solution.py:503
  29.7 1.5 %shard_map.76 = f32[97,1152]{1,0:T(8,128)S(1)} custom-call(s32[6]{0:T(128)S(1)} %stack.27.pos_ref, bf16[128,384]{1,0:T(8,128)(2,1)S(1)} %get-tuple-element.46.kept_ref, bf16[128,384]{1,0:T(8,128)(2,1)S(1)} %collective-permute-done.5.msg_ref, f32[16,384]{1,0:T(8,128)S(1)} %get-tuple-element.47.stats_ref, f32[16,768]{1,0:T(8,128)S(1)} %get-tuple-element.52.vec_ref, ...), custom_call_target="tpu_custom_call" | custom-call | flops 57212928 | bytes 1474560 | tf_op jit(solution)/shard_map/pallas_call | solution.py:474
  31.2 1.6 %collective-permute-start.7 = (f16[97,1152]{1,0:T(8,128)(2,1)S(1)}, f16[97,1152]{1,0:T(8,128)(2,1)S(1)}, u32[]{:S(2)}, u32[]{:S(2)}) collective-permute-start(f16[97,1152]{1,0:T(8,128)(2,1)S(1)} %convert_element_type.21), channel_id=1, source_target_pairs={{0,2},{1,9},{2,0},{3,11},{4,6},{5,13},{6,4},{7,15},{8,10},{9,1},{1... | collective-permute-start | bytes 670472 | tf_op jit(solution)/shard_map/ppermute | solution.py:503
  32.8 4.6 %collective-permute-done.7 = f16[97,1152]{1,0:T(8,128)(2,1)S(1)} collective-permute-done((f16[97,1152]{1,0:T(8,128)(2,1)S(1)}, f16[97,1152]{1,0:T(8,128)(2,1)S(1)}, u32[]{:S(2)}, u32[]{:S(2)}) %collective-permute-start.7) | collective-permute-done | bytes 223520 | tf_op jit(solution)/shard_map/ppermute | solution.py:503
  37.4 0.1 add_convert_fusion
  37.5 2.1 %collective-permute-start.8 = (f16[97,1152]{1,0:T(8,128)(2,1)S(1)}, f16[97,1152]{1,0:T(8,128)(2,1)S(1)}, u32[]{:S(2)}, u32[]{:S(2)}) collective-permute-start(f16[97,1152]{1,0:T(8,128)(2,1)S(1)} %add_convert_fusion), channel_id=1, source_target_pairs={{0,4},{1,5},{2,6},{3,7},{4,0},{5,1},{6,2},{7,3},{8,12},{9,13},{10,... | collective-permute-start | bytes 670472 | tf_op jit(solution)/shard_map/ppermute | solution.py:503
  39.6 5.0 %collective-permute-done.8 = f16[97,1152]{1,0:T(8,128)(2,1)S(1)} collective-permute-done((f16[97,1152]{1,0:T(8,128)(2,1)S(1)}, f16[97,1152]{1,0:T(8,128)(2,1)S(1)}, u32[]{:S(2)}, u32[]{:S(2)}) %collective-permute-start.8) | collective-permute-done | bytes 223520 | tf_op jit(solution)/shard_map/ppermute | solution.py:503
  44.6 0.1 convert_add_fusion.score_ref
  44.7 0.1 collective-permute-start.9
  44.8 0.9 %shard_map.77 = f32[200,97]{1,0:T(8,128)S(1)} custom-call(s32[6]{0:T(128)S(1)} %stack.27.pos_ref, f32[97,1152]{1,0:T(8,128)S(1)} %convert_add_fusion.score_ref, bf16[97,1152]{1,0:T(8,128)(2,1)S(1)} %get-tuple-element.50.flag_ref, bf16[1152,256]{1,0:T(8,128)(2,1)S(1)} %get-tuple-element.55.hot_ref), custom_call_target="tpu_custom_call" | custom-call | flops 89395200 | bytes 893952 | tf_op jit(solution)/shard_map/pallas_call | solution.py:474
  45.7 0.6 %collective-permute-start.10 = (f32[200,97]{1,0:T(8,128)S(1)}, f32[200,97]{1,0:T(8,128)S(1)}, u32[]{:S(2)}, u32[]{:S(2)}) collective-permute-start(f32[200,97]{1,0:T(8,128)S(1)} %shard_map.77), channel_id=1, source_target_pairs={{0,1},{1,0},{2,3},{3,2},{4,5},{5,4},{6,7},{7,6},{8,9},{9,8},{10,11... | collective-permute-start | bytes 232808 | tf_op jit(solution)/shard_map/ppermute | solution.py:506
  46.3 0.0 collective-permute-done.9
  46.3 0.8 %fusion = f32[97,768]{1,0:T(8,128)} fusion(f32[97,1152]{1,0:T(8,128)S(1)} %convert_add_fusion.score_ref, f32[97,384]{1,0:T(8,128)S(1)} %collective-permute-done.9, bf16[97,1152]{1,0:T(8,128)(2,1)S(1)} %get-tuple-element.50.flag_ref, pred[]{:T(512)S(6)} %eq.2), kind=kLoop, calls=%fused_computation.3 | loop fusion | flops 297984 | bytes 893953 | tf_op jit(solution)/shard_map/add | solution.py:614
  47.1 0.2 collective-permute-done.10
  47.2 0.7 %add_bitcast_fusion = f32[97,200]{0,1:T(8,128)} fusion(f32[200,97]{1,0:T(8,128)S(1)} %shard_map.77, f32[200,97]{1,0:T(8,128)S(1)} %collective-permute-done.10), kind=kLoop, calls=%fused_computation.4 | loop fusion | flops 19400 | bytes 232800 | tf_op jit(solution)/shard_map/transpose | solution.py:621
  (2 shorter events, 0.0 us)
Async XLA Ops:
  0.7 1.4 %copy-start.4 = (bf16[1024,768]{1,0:T(8,128)(2,1)S(1)}, bf16[1024,768]{1,0:T(8,128)(2,1)}, u32[]{:S(2)}) copy-start(bf16[1024,768]{1,0:T(8,128)(2,1)} %own_ref.1) | copy-start | bytes 4718596
  4.6 3.1 %collective-permute-start = (bf16[1024,384]{1,0:T(8,128)(2,1)S(1)}, bf16[1024,384]{1,0:T(8,128)(2,1)S(1)}, u32[]{:S(2)}, u32[]{:S(2)}) collective-permute-start(bf16[1024,384]{1,0:T(8,128)(2,1)S(1)} %get-tuple-element.31), channel_id=1, source_target_pairs={{0,1},{1,0},{2,3},{3,2},{4,5},{5,4},{6,7},{7,6},{8,9},{9,8},{10,11... | collective-permute-start | bytes 2359304 | tf_op jit(solution)/shard_map/ppermute | solution.py:506
  5.1 7.4 %collective-permute-start.2 = (bf16[200,768]{1,0:T(8,128)(2,1)S(1)}, bf16[200,768]{1,0:T(8,128)(2,1)S(1)}, u32[]{:S(2)}, u32[]{:S(2)}) collective-permute-start(bf16[200,768]{1,0:T(8,128)(2,1)S(1)} %get-tuple-element.37), channel_id=1, source_target_pairs={{0,2},{1,5},{2,0},{3,7},{4,6},{5,1},{6,4},{7,3},{8,10},{9,13},{10,... | collective-permute-start | bytes 921608 | tf_op jit(solution)/shard_map/ppermute | solution.py:503
  10.0 15.1 %copy-start = (s32[97,1536]{1,0:T(8,128)S(1)}, s32[97,1536]{1,0:T(8,128)}, u32[]{:S(2)}) copy-start(s32[97,1536]{1,0:T(8,128)} %annot_ref.1) | copy-start | bytes 1787908
  10.0 15.0 %copy-start.1 = (s32[1536]{0:T(1024)S(1)}, s32[1536]{0:T(1024)}, u32[]{:S(2)}) copy-start(s32[1536]{0:T(1024)} %param.6) | copy-start | bytes 18436
  10.0 15.0 %copy-start.2 = (s32[1536]{0:T(1024)S(1)}, s32[1536]{0:T(1024)}, u32[]{:S(2)}) copy-start(s32[1536]{0:T(1024)} %param.9) | copy-start | bytes 18436
  10.0 15.0 %copy-start.3 = (s32[1536]{0:T(1024)S(1)}, s32[1536]{0:T(1024)}, u32[]{:S(2)}) copy-start(s32[1536]{0:T(1024)} %param.7) | copy-start | bytes 18436
  10.0 5.7 %collective-permute-start.1 = (bf16[224,384]{1,0:T(8,128)(2,1)S(1)}, bf16[224,384]{1,0:T(8,128)(2,1)S(1)}, u32[]{:S(2)}, u32[]{:S(2)}) collective-permute-start(bf16[224,384]{1,0:T(8,128)(2,1)S(1)} %get-tuple-element.34), channel_id=1, source_target_pairs={{0,2},{1,5},{2,0},{3,7},{4,6},{5,1},{6,4},{7,3},{8,10},{9,13},{10,... | collective-permute-start | bytes 516104 | tf_op jit(solution)/shard_map/ppermute | solution.py:503
  13.1 6.6 %collective-permute-start.4 = (bf16[104,768]{1,0:T(8,128)(2,1)S(1)}, bf16[104,768]{1,0:T(8,128)(2,1)S(1)}, u32[]{:S(2)}, u32[]{:S(2)}) collective-permute-start(bf16[104,768]{1,0:T(8,128)(2,1)S(1)} %get-tuple-element.44), channel_id=1, source_target_pairs={{0,4},{1,9},{2,6},{3,11},{4,0},{5,13},{6,2},{7,15},{8,12},{9,1},{1... | collective-permute-start | bytes 479240 | tf_op jit(solution)/shard_map/ppermute | solution.py:503
  16.3 6.7 %collective-permute-start.3 = (bf16[128,384]{1,0:T(8,128)(2,1)S(1)}, bf16[128,384]{1,0:T(8,128)(2,1)S(1)}, u32[]{:S(2)}, u32[]{:S(2)}) collective-permute-start(bf16[128,384]{1,0:T(8,128)(2,1)S(1)} %get-tuple-element.41), channel_id=1, source_target_pairs={{0,4},{1,9},{2,6},{3,11},{4,0},{5,13},{6,2},{7,15},{8,12},{9,1},{1... | collective-permute-start | bytes 294920 | tf_op jit(solution)/shard_map/ppermute | solution.py:503
  20.4 6.4 %collective-permute-start.6 = (bf16[112,768]{1,0:T(8,128)(2,1)S(1)}, bf16[112,768]{1,0:T(8,128)(2,1)S(1)}, u32[]{:S(2)}, u32[]{:S(2)}) collective-permute-start(bf16[112,768]{1,0:T(8,128)(2,1)S(1)} %get-tuple-element.48.kept_ref), channel_id=1, source_target_pairs={{0,8},{1,3},{2,10},{3,1},{4,12},{5,7},{6,14},{7,5},{8,0},{9,11},{1... | collective-permute-start | bytes 516104 | tf_op jit(solution)/shard_map/ppermute | solution.py:503
  23.5 6.1 %collective-permute-start.5 = (bf16[128,384]{1,0:T(8,128)(2,1)S(1)}, bf16[128,384]{1,0:T(8,128)(2,1)S(1)}, u32[]{:S(2)}, u32[]{:S(2)}) collective-permute-start(bf16[128,384]{1,0:T(8,128)(2,1)S(1)} %get-tuple-element.46.kept_ref), channel_id=1, source_target_pairs={{0,8},{1,3},{2,10},{3,1},{4,12},{5,7},{6,14},{7,5},{8,0},{9,11},{1... | collective-permute-start | bytes 294920 | tf_op jit(solution)/shard_map/ppermute | solution.py:503
  31.2 6.2 %collective-permute-start.7 = (f16[97,1152]{1,0:T(8,128)(2,1)S(1)}, f16[97,1152]{1,0:T(8,128)(2,1)S(1)}, u32[]{:S(2)}, u32[]{:S(2)}) collective-permute-start(f16[97,1152]{1,0:T(8,128)(2,1)S(1)} %convert_element_type.21), channel_id=1, source_target_pairs={{0,2},{1,9},{2,0},{3,11},{4,6},{5,13},{6,4},{7,15},{8,10},{9,1},{1... | collective-permute-start | bytes 670472 | tf_op jit(solution)/shard_map/ppermute | solution.py:503
  37.5 7.1 %collective-permute-start.8 = (f16[97,1152]{1,0:T(8,128)(2,1)S(1)}, f16[97,1152]{1,0:T(8,128)(2,1)S(1)}, u32[]{:S(2)}, u32[]{:S(2)}) collective-permute-start(f16[97,1152]{1,0:T(8,128)(2,1)S(1)} %add_convert_fusion), channel_id=1, source_target_pairs={{0,4},{1,5},{2,6},{3,7},{4,0},{5,1},{6,2},{7,3},{8,12},{9,13},{10,... | collective-permute-start | bytes 670472 | tf_op jit(solution)/shard_map/ppermute | solution.py:503
  44.7 1.6 %collective-permute-start.9 = (f32[97,384]{1,0:T(8,128)S(1)}, f32[97,384]{1,0:T(8,128)S(1)}, u32[]{:S(2)}, u32[]{:S(2)}) collective-permute-start(f32[97,384]{1,0:T(8,128)S(1)} %slice.13), channel_id=1, source_target_pairs={{0,1},{1,0},{2,3},{3,2},{4,5},{5,4},{6,7},{7,6},{8,9},{9,8},{10,11... | collective-permute-start | bytes 446984 | tf_op jit(solution)/shard_map/ppermute | solution.py:506
  45.7 1.5 %collective-permute-start.10 = (f32[200,97]{1,0:T(8,128)S(1)}, f32[200,97]{1,0:T(8,128)S(1)}, u32[]{:S(2)}, u32[]{:S(2)}) collective-permute-start(f32[200,97]{1,0:T(8,128)S(1)} %shard_map.77), channel_id=1, source_target_pairs={{0,1},{1,0},{2,3},{3,2},{4,5},{5,4},{6,7},{7,6},{8,9},{9,8},{10,11... | collective-permute-start | bytes 232808 | tf_op jit(solution)/shard_map/ppermute | solution.py:506

commit v6 on v5

--- a/solution.py
+++ b/solution.py
@@ -450,12 +450,8 @@
     limit = jnp.concatenate(local(jnp.minimum(reach, last - 1.0 - place)), axis=1)
     limit_ref[...] = jnp.broadcast_to(limit, limit_ref.shape)
     block = jnp.concatenate(local(line(ids_ref)), axis=1)
-    tall = jnp.broadcast_to(block, (128, block.shape[1]))
-    for k in range(block.shape[1] // 128):
-        rows = tall[:, k * 128 : (k + 1) * 128].T
-        for n in range(hot_ref.shape[1] // 128):
-            number = (lax.broadcasted_iota(jnp.int32, rows.shape, 1) + n * 128).astype(F32)
-            hot_ref[k * 128 : (k + 1) * 128, n * 128 : (n + 1) * 128] = jnp.where(number == rows, 1.0, 0.0).astype(BF16)
+    number = lax.broadcasted_iota(jnp.int32, hot_ref.shape, 0).astype(F32)
+    hot_ref[...] = jnp.where(number == block, 1.0, 0.0).astype(BF16)
 
 
 def block_kernel(pos_ref, score_ref, flag_ref, hot_ref, sum_ref):
@@ -464,8 +460,10 @@
     own = score_ref[:, :slab] + flag_ref[:, :slab].astype(F32)
     scores = jnp.concatenate([own, score_ref[:, slab:]], axis=1)
     high = scores.astype(BF16)
-    left = scores - high.astype(F32)
-    sum_ref[...] = (dot_n(high, hot) + dot_n(left.astype(BF16), hot)).T[: sum_ref.shape[0], :]
+    left = (scores - high.astype(F32)).astype(BF16)
+    gap = jnp.zeros((128 - scores.shape[0], scores.shape[1]), BF16)
+    both = dot_t(hot, jnp.concatenate([high, gap, left, gap], axis=0))
+    sum_ref[...] = (both[:, :128] + both[:, 128:])[:, : sum_ref.shape[1]]
 
 
 def call(kernel, inputs, outputs, scratch, flops, moved):
@@ -527,7 +525,7 @@
             shape(annot, 4 * half, BF16),
             shape(annot, 5 * 128, BF16),
             shape(8, width, F32),
-            shape(width, -(-hot_rows // 128) * 128, BF16),
+            shape(hot_rows, width, BF16),
         ),
         [],
         annot * snps * 10,
@@ -598,9 +596,12 @@
         2 * annot * half * rows * 8,
         rows * slab * 20,
     )
+    cut = -(-width // 256) * 128
+    pieces = [partial[:, :cut], partial[:, cut:]]
     for t in range(2):
-        rounded = partial.astype(jnp.float16)
-        partial = rounded.astype(F32) + exchange(rounded, t, ROUNDS).astype(F32)
+        rounded = [x.astype(jnp.float16) for x in pieces]
+        pieces = [x.astype(F32) + exchange(x, t, ROUNDS).astype(F32) for x in rounded]
+    partial = jnp.concatenate(pieces, axis=1)
     arrived = across(partial[:, slab:])
     sums = call(
         block_kernel,

time: 48 us -> 46.7 us (0.973)
  waiting for transfers between devices: 13.9 us -> 10.5 us
  starting transfers between devices: 18.1 us -> 20 us
    ppermute x8 -> x10, waiting for transfers between devices: 13.7 us -> 9.98 us  [exchange(): return lax.ppermute(x, ('samples', 'genome'), route)]
    ppermute x8 -> x10, starting transfers between devices: 16.9 us -> 19.3 us  [exchange(): return lax.ppermute(x, ('samples', 'genome'), route)]
    ppermute x3, starting transfers between devices: 1.15 us -> 0.66 us  [across(): return lax.ppermute(x, 'genome', [(0, 1), (1, 0)])]
  transfers between devices with their start and end apart: 11 -> 13, of which waited for: 8 -> 9; matrix products, arithmetic and copies ran while one was open for 2% -> 2% of each run, Pallas kernels for 17% -> 17%
where the time goes in v6:
time: 46.7 us; the launch traced here: 46.5 us
  starting transfers between devices  20 us (43%)
  Pallas kernels  12 us (26%)
  waiting for transfers between devices  10.5 us (22%)
  other arithmetic  1.63 us (3%)
  local copies, waits for them, and re-layouts  1.58 us (3%)
  between operations  0.82 us (2%)
    ppermute x10, starting transfers between devices, exchange(): return lax.ppermute(x, ('samples', 'genome'), route)  19.3 us
    pallas_call x10, Pallas kernels, call(): pl.pallas_call(kernel, out_shape=outputs, in_specs=[smem] + [vmem] * (len...  12 us
    ppermute x10, waiting for transfers between devices, exchange(): return lax.ppermute(x, ('samples', 'genome'), route)  9.98 us
    unnamed x10, local copies, waits for them, and re-layouts  1.44 us
  transfers between devices with their start and end apart: 13, of which 9 were waited for; matrix products, arithmetic and copies ran while one was open for 2% of the time, Pallas kernels for 17%

profile of v6, /device:TPU:0, one launch (start us, length us, event | category | flops | bytes accessed | tf_op | source)
XLA Modules:
  0.0 46.5 jit_solution(11585261757252573821)
XLA Ops:
  0.6 0.1 stack.27.pos_ref
  0.7 1.4 %copy-done.4 = bf16[1024,768]{1,0:T(8,128)(2,1)S(1)} copy-done((bf16[1024,768]{1,0:T(8,128)(2,1)S(1)}, bf16[1024,768]{1,0:T(8,128)(2,1)}, u32[]{:S(2)}) %copy-start.4) | copy-done | bytes 1572888
  2.1 2.4 %shard_map.68 = (f32[192,768]{1,0:T(8,128)S(1)}, bf16[200,768]{1,0:T(8,128)(2,1)S(1)}, f32[16,768]{1,0:T(8,128)S(1)}, bf16[768,1024]{1,0:T(8,128)(2,1)S(1)}, bf16[1024,384]{1,0:T(8,128)(2,1)S(1)}) custom-call(s32[6]{0:T(128)S(1)} %stack.27.pos_ref, bf16[1024,768]{1,0:T(8,128)(2,1)S(1)} %copy-done.4), custom_call_target="tpu_custom_call" | custom-call | flops 905969664 | bytes 1572864 | tf_op jit(solution)/shard_map/pallas_call | solution.py:472
  4.6 0.5 %collective-permute-start = (bf16[1024,384]{1,0:T(8,128)(2,1)S(1)}, bf16[1024,384]{1,0:T(8,128)(2,1)S(1)}, u32[]{:S(2)}, u32[]{:S(2)}) collective-permute-start(bf16[1024,384]{1,0:T(8,128)(2,1)S(1)} %get-tuple-element.31), channel_id=1, source_target_pairs={{0,1},{1,0},{2,3},{3,2},{4,5},{5,4},{6,7},{7,6},{8,9},{9,8},{10,11... | collective-permute-start | bytes 2359304 | tf_op jit(solution)/shard_map/ppermute | solution.py:504
  5.1 2.6 %collective-permute-start.2 = (bf16[200,768]{1,0:T(8,128)(2,1)S(1)}, bf16[200,768]{1,0:T(8,128)(2,1)S(1)}, u32[]{:S(2)}, u32[]{:S(2)}) collective-permute-start(bf16[200,768]{1,0:T(8,128)(2,1)S(1)} %get-tuple-element.37), channel_id=1, source_target_pairs={{0,2},{1,5},{2,0},{3,7},{4,6},{5,1},{6,4},{7,3},{8,10},{9,13},{10,... | collective-permute-start | bytes 921608 | tf_op jit(solution)/shard_map/ppermute | solution.py:501
  7.7 0.0 collective-permute-done.there_ref
  7.7 2.3 %shard_map.69 = (f32[192,384]{1,0:T(8,128)S(1)}, bf16[224,384]{1,0:T(8,128)(2,1)S(1)}, f32[16,384]{1,0:T(8,128)S(1)}) custom-call(s32[6]{0:T(128)S(1)} %stack.27.pos_ref, bf16[768,1024]{1,0:T(8,128)(2,1)S(1)} %get-tuple-element.30.turned_ref, bf16[1024,384]{1,0:T(8,128)(2,1)S(1)} %collective-permute-done.there_ref, ...), custom_call_target="tpu_custom_call" | custom-call | flops 905969664 | bytes 1572864 | tf_op jit(solution)/shard_map/pallas_call | solution.py:472
  10.0 0.0 copy-start
  10.0 0.0 copy-start.1
  10.0 0.0 copy-start.2
  10.0 0.0 copy-start.3
  10.0 2.3 %collective-permute-start.1 = (bf16[224,384]{1,0:T(8,128)(2,1)S(1)}, bf16[224,384]{1,0:T(8,128)(2,1)S(1)}, u32[]{:S(2)}, u32[]{:S(2)}) collective-permute-start(bf16[224,384]{1,0:T(8,128)(2,1)S(1)} %get-tuple-element.34), channel_id=1, source_target_pairs={{0,2},{1,5},{2,0},{3,7},{4,6},{5,1},{6,4},{7,3},{8,10},{9,13},{10,... | collective-permute-start | bytes 516104 | tf_op jit(solution)/shard_map/ppermute | solution.py:501
  12.3 0.2 collective-permute-done.2.msg_ref
  12.5 0.6 %shard_map.70 = (f32[96,768]{1,0:T(8,128)S(1)}, bf16[104,768]{1,0:T(8,128)(2,1)S(1)}, f32[16,768]{1,0:T(8,128)S(1)}) custom-call(s32[6]{0:T(128)S(1)} %stack.27.pos_ref, f32[192,768]{1,0:T(8,128)S(1)} %get-tuple-element.36.kept_ref, bf16[200,768]{1,0:T(8,128)(2,1)S(1)} %collective-permute-done.2.msg_ref, f32[16,768]{1,0:T(8,128)S(1)} %get-tuple-element.32.own_stats_ref.stats_ref), custom_call_target="tpu_custom_call" | custom-call | flops 589824 | bytes 1474560 | tf_op jit(solution)/shard_map/pallas_call | solution.py:472
  13.1 2.2 %collective-permute-start.4 = (bf16[104,768]{1,0:T(8,128)(2,1)S(1)}, bf16[104,768]{1,0:T(8,128)(2,1)S(1)}, u32[]{:S(2)}, u32[]{:S(2)}) collective-permute-start(bf16[104,768]{1,0:T(8,128)(2,1)S(1)} %get-tuple-element.44), channel_id=1, source_target_pairs={{0,4},{1,9},{2,6},{3,11},{4,0},{5,13},{6,2},{7,15},{8,12},{9,1},{1... | collective-permute-start | bytes 479240 | tf_op jit(solution)/shard_map/ppermute | solution.py:501
  15.3 0.4 collective-permute-done.1.msg_ref
  15.7 0.6 %shard_map.71 = (f32[96,384]{1,0:T(8,128)S(1)}, bf16[128,384]{1,0:T(8,128)(2,1)S(1)}, f32[16,384]{1,0:T(8,128)S(1)}) custom-call(s32[6]{0:T(128)S(1)} %stack.27.pos_ref, f32[192,384]{1,0:T(8,128)S(1)} %get-tuple-element.33.kept_ref, bf16[224,384]{1,0:T(8,128)(2,1)S(1)} %collective-permute-done.1.msg_ref, f32[16,384]{1,0:T(8,128)S(1)} %get-tuple-element.35.stats_ref, ...), custom_call_target="tpu_custom_call" | custom-call | flops 294912 | bytes 737280 | tf_op jit(solution)/shard_map/pallas_call | solution.py:472
  16.3 2.2 %collective-permute-start.3 = (bf16[128,384]{1,0:T(8,128)(2,1)S(1)}, bf16[128,384]{1,0:T(8,128)(2,1)S(1)}, u32[]{:S(2)}, u32[]{:S(2)}) collective-permute-start(bf16[128,384]{1,0:T(8,128)(2,1)S(1)} %get-tuple-element.41), channel_id=1, source_target_pairs={{0,4},{1,9},{2,6},{3,11},{4,0},{5,13},{6,2},{7,15},{8,12},{9,1},{1... | collective-permute-start | bytes 294920 | tf_op jit(solution)/shard_map/ppermute | solution.py:501
  18.4 1.3 %collective-permute-done.4.msg_ref = bf16[104,768]{1,0:T(8,128)(2,1)S(1)} collective-permute-done((bf16[104,768]{1,0:T(8,128)(2,1)S(1)}, bf16[104,768]{1,0:T(8,128)(2,1)S(1)}, u32[]{:S(2)}, u32[]{:S(2)}) %collective-permute-start.4) | collective-permute-done | bytes 159776 | tf_op jit(solution)/shard_map/ppermute | solution.py:501
  19.8 0.6 %shard_map.72 = (bf16[112,768]{1,0:T(8,128)(2,1)S(1)}, f32[16,768]{1,0:T(8,128)S(1)}) custom-call(s32[6]{0:T(128)S(1)} %stack.27.pos_ref, f32[96,768]{1,0:T(8,128)S(1)} %get-tuple-element.43.kept_ref, bf16[104,768]{1,0:T(8,128)(2,1)S(1)} %collective-permute-done.4.msg_ref, f32[16,768]{1,0:T(8,128)S(1)} %get-tuple-element.39.refs_0_.stats_ref), custom_call_target="tpu_custom_call" | custom-call | flops 589824 | bytes 1474560 | tf_op jit(solution)/shard_map/pallas_call | solution.py:472
  20.4 2.6 %collective-permute-start.6 = (bf16[112,768]{1,0:T(8,128)(2,1)S(1)}, bf16[112,768]{1,0:T(8,128)(2,1)S(1)}, u32[]{:S(2)}, u32[]{:S(2)}) collective-permute-start(bf16[112,768]{1,0:T(8,128)(2,1)S(1)} %get-tuple-element.48.kept_ref), channel_id=1, source_target_pairs={{0,8},{1,3},{2,10},{3,1},{4,12},{5,7},{6,14},{7,5},{8,0},{9,11},{1... | collective-permute-start | bytes 516104 | tf_op jit(solution)/shard_map/ppermute | solution.py:501
  23.0 0.0 collective-permute-done.3.msg_ref
  23.0 0.6 %shard_map.73 = (bf16[128,384]{1,0:T(8,128)(2,1)S(1)}, f32[16,384]{1,0:T(8,128)S(1)}) custom-call(s32[6]{0:T(128)S(1)} %stack.27.pos_ref, f32[96,384]{1,0:T(8,128)S(1)} %get-tuple-element.40.kept_ref, bf16[128,384]{1,0:T(8,128)(2,1)S(1)} %collective-permute-done.3.msg_ref, f32[16,384]{1,0:T(8,128)S(1)} %get-tuple-element.42.stats_ref, ...), custom_call_target="tpu_custom_call" | custom-call | flops 294912 | bytes 737280 | tf_op jit(solution)/shard_map/pallas_call | solution.py:472
  23.5 1.5 %collective-permute-start.5 = (bf16[128,384]{1,0:T(8,128)(2,1)S(1)}, bf16[128,384]{1,0:T(8,128)(2,1)S(1)}, u32[]{:S(2)}, u32[]{:S(2)}) collective-permute-start(bf16[128,384]{1,0:T(8,128)(2,1)S(1)} %get-tuple-element.46.kept_ref), channel_id=1, source_target_pairs={{0,8},{1,3},{2,10},{3,1},{4,12},{5,7},{6,14},{7,5},{8,0},{9,11},{1... | collective-permute-start | bytes 294920 | tf_op jit(solution)/shard_map/ppermute | solution.py:501
  25.0 0.0 copy-done
  25.0 0.0 copy-done.1
  25.0 0.0 copy-done.2
  25.0 0.0 copy-done.3
  25.0 1.0 %shard_map.74 = (bf16[97,1152]{1,0:T(8,128)(2,1)S(1)}, bf16[97,1536]{1,0:T(8,128)(2,1)S(1)}, bf16[97,640]{1,0:T(8,128)(2,1)S(1)}, f32[8,1152]{1,0:T(8,128)S(1)}, bf16[200,1152]{1,0:T(8,128)(2,1)S(1)}) custom-call(s32[6]{0:T(128)S(1)} %stack.27.pos_ref, s32[97,1536]{1,0:T(8,128)S(1)} %copy-done, s32[12,128]{1,0:T(8,128)S(1)} %bitcast.11, ...), custom_call_target="tpu_custom_call" | custom-call | flops 1489920 | bytes 1191936 | tf_op jit(solution)/shard_map/pallas_call | solution.py:472
  26.0 0.7 %collective-permute-done.6.msg_ref = bf16[112,768]{1,0:T(8,128)(2,1)S(1)} collective-permute-done((bf16[112,768]{1,0:T(8,128)(2,1)S(1)}, bf16[112,768]{1,0:T(8,128)(2,1)S(1)}, u32[]{:S(2)}, u32[]{:S(2)}) %collective-permute-start.6) | collective-permute-done | bytes 172064 | tf_op jit(solution)/shard_map/ppermute | solution.py:501
  26.7 1.4 %shard_map.75 = (f32[97,768]{1,0:T(8,128)S(1)}, f32[16,768]{1,0:T(8,128)S(1)}) custom-call(s32[6]{0:T(128)S(1)} %stack.27.pos_ref, bf16[112,768]{1,0:T(8,128)(2,1)S(1)} %get-tuple-element.48.kept_ref, bf16[112,768]{1,0:T(8,128)(2,1)S(1)} %collective-permute-done.6.msg_ref, f32[16,768]{1,0:T(8,128)S(1)} %get-tuple-element.45.refs_0_.stats_ref, ...), custom_call_target="tpu_custom_call" | custom-call | flops 57212928 | bytes 1474560 | tf_op jit(solution)/shard_map/pallas_call | solution.py:472
  28.2 1.5 %collective-permute-done.5.msg_ref = bf16[128,384]{1,0:T(8,128)(2,1)S(1)} collective-permute-done((bf16[128,384]{1,0:T(8,128)(2,1)S(1)}, bf16[128,384]{1,0:T(8,128)(2,1)S(1)}, u32[]{:S(2)}, u32[]{:S(2)}) %collective-permute-start.5) | collective-permute-done | bytes 98336 | tf_op jit(solution)/shard_map/ppermute | solution.py:501
  29.7 1.5 %shard_map.76 = f32[97,1152]{1,0:T(8,128)S(1)} custom-call(s32[6]{0:T(128)S(1)} %stack.27.pos_ref, bf16[128,384]{1,0:T(8,128)(2,1)S(1)} %get-tuple-element.46.kept_ref, bf16[128,384]{1,0:T(8,128)(2,1)S(1)} %collective-permute-done.5.msg_ref, f32[16,384]{1,0:T(8,128)S(1)} %get-tuple-element.47.stats_ref, f32[16,768]{1,0:T(8,128)S(1)} %get-tuple-element.52.vec_ref, ...), custom_call_target="tpu_custom_call" | custom-call | flops 57212928 | bytes 1474560 | tf_op jit(solution)/shard_map/pallas_call | solution.py:472
  31.2 1.6 %collective-permute-start.9 = (f16[97,512]{1,0:T(8,128)(2,1)S(1)}, f16[97,512]{1,0:T(8,128)(2,1)S(1)}, u32[]{:S(2)}, u32[]{:S(2)}) collective-permute-start(f16[97,512]{1,0:T(8,128)(2,1)S(1)} %slice.23), channel_id=1, source_target_pairs={{0,2},{1,9},{2,0},{3,11},{4,6},{5,13},{6,4},{7,15},{8,10},{9,1},{1... | collective-permute-start | bytes 297992 | tf_op jit(solution)/shard_map/ppermute | solution.py:501
  32.8 0.6 %collective-permute-start.7 = (f16[97,640]{1,0:T(8,128)(2,1)S(1)}, f16[97,640]{1,0:T(8,128)(2,1)S(1)}, u32[]{:S(2)}, u32[]{:S(2)}) collective-permute-start(f16[97,640]{1,0:T(8,128)(2,1)S(1)} %slice.22), channel_id=1, source_target_pairs={{0,2},{1,9},{2,0},{3,11},{4,6},{5,13},{6,4},{7,15},{8,10},{9,1},{1... | collective-permute-start | bytes 372488 | tf_op jit(solution)/shard_map/ppermute | solution.py:501
  33.4 2.6 %collective-permute-done.9 = f16[97,512]{1,0:T(8,128)(2,1)S(1)} collective-permute-done((f16[97,512]{1,0:T(8,128)(2,1)S(1)}, f16[97,512]{1,0:T(8,128)(2,1)S(1)}, u32[]{:S(2)}, u32[]{:S(2)}) %collective-permute-start.9) | collective-permute-done | bytes 99360 | tf_op jit(solution)/shard_map/ppermute | solution.py:501
  36.0 2.1 %collective-permute-start.10 = (f16[97,512]{1,0:T(8,128)(2,1)S(1)}, f16[97,512]{1,0:T(8,128)(2,1)S(1)}, u32[]{:S(2)}, u32[]{:S(2)}) collective-permute-start(f16[97,512]{1,0:T(8,128)(2,1)S(1)} %add_convert_fusion.1), channel_id=1, source_target_pairs={{0,4},{1,5},{2,6},{3,7},{4,0},{5,1},{6,2},{7,3},{8,12},{9,13},{10,... | collective-permute-start | bytes 297992 | tf_op jit(solution)/shard_map/ppermute | solution.py:501
  38.2 0.0 collective-permute-done.7
  38.2 1.8 %collective-permute-start.8 = (f16[97,640]{1,0:T(8,128)(2,1)S(1)}, f16[97,640]{1,0:T(8,128)(2,1)S(1)}, u32[]{:S(2)}, u32[]{:S(2)}) collective-permute-start(f16[97,640]{1,0:T(8,128)(2,1)S(1)} %add_convert_fusion), channel_id=1, source_target_pairs={{0,4},{1,5},{2,6},{3,7},{4,0},{5,1},{6,2},{7,3},{8,12},{9,13},{10,... | collective-permute-start | bytes 372488 | tf_op jit(solution)/shard_map/ppermute | solution.py:501
  40.0 1.9 %collective-permute-done.10 = f16[97,512]{1,0:T(8,128)(2,1)S(1)} collective-permute-done((f16[97,512]{1,0:T(8,128)(2,1)S(1)}, f16[97,512]{1,0:T(8,128)(2,1)S(1)}, u32[]{:S(2)}, u32[]{:S(2)}) %collective-permute-start.10) | collective-permute-done | bytes 99360 | tf_op jit(solution)/shard_map/ppermute | solution.py:501
  42.0 0.1 collective-permute-start.11
  42.1 1.3 %collective-permute-done.8 = f16[97,640]{1,0:T(8,128)(2,1)S(1)} collective-permute-done((f16[97,640]{1,0:T(8,128)(2,1)S(1)}, f16[97,640]{1,0:T(8,128)(2,1)S(1)}, u32[]{:S(2)}, u32[]{:S(2)}) %collective-permute-start.8) | collective-permute-done | bytes 124192 | tf_op jit(solution)/shard_map/ppermute | solution.py:501
  43.5 0.9 %shard_map.77 = f32[200,97]{1,0:T(8,128)S(1)} custom-call(s32[6]{0:T(128)S(1)} %stack.27.pos_ref, f32[97,1152]{1,0:T(8,128)S(1)} %pad_maximum_fusion.score_ref, bf16[97,1152]{1,0:T(8,128)(2,1)S(1)} %get-tuple-element.50.flag_ref, bf16[200,1152]{1,0:T(8,128)(2,1)S(1)} %get-tuple-element.55.hot_ref), custom_call_target="tpu_custom_call" | custom-call | flops 89395200 | bytes 893952 | tf_op jit(solution)/shard_map/pallas_call | solution.py:472
  44.5 0.1 collective-permute-start.12
  44.6 0.0 collective-permute-done.11
  44.6 0.8 %fusion.2 = f32[97,768]{1,0:T(8,128)} fusion(f32[97,640]{1,0:T(8,128)S(1)} %convert_add_fusion, f32[97,512]{1,0:T(8,128)S(1)} %convert_add_fusion.1, f32[97,384]{1,0:T(8,128)S(1)} %collective-permute-done.11, bf16[97,1152]{1,0:T(8,128)(2,1)S(1)} %get-tuple-element.50.flag_ref, pred[]{:T(512)S(6)} %eq.2), kind=kLoop, calls=%fused_computation.5 | loop fusion | flops 372480 | bytes 1042945 | tf_op jit(solution)/shard_map/add | solution.py:615
  45.3 0.5 %collective-permute-done.12 = f32[200,97]{1,0:T(8,128)S(1)} collective-permute-done((f32[200,97]{1,0:T(8,128)S(1)}, f32[200,97]{1,0:T(8,128)S(1)}, u32[]{:S(2)}, u32[]{:S(2)}) %collective-permute-start.12) | collective-permute-done | bytes 77632 | tf_op jit(solution)/shard_map/ppermute | solution.py:504
  45.8 0.7 %add_bitcast_fusion = f32[97,200]{0,1:T(8,128)} fusion(f32[200,97]{1,0:T(8,128)S(1)} %shard_map.77, f32[200,97]{1,0:T(8,128)S(1)} %collective-permute-done.12), kind=kLoop, calls=%fused_computation.10 | loop fusion | flops 19400 | bytes 232800 | tf_op jit(solution)/shard_map/transpose | solution.py:622
  (10 shorter events, 0.3 us)
Async XLA Ops:
  0.7 1.4 %copy-start.4 = (bf16[1024,768]{1,0:T(8,128)(2,1)S(1)}, bf16[1024,768]{1,0:T(8,128)(2,1)}, u32[]{:S(2)}) copy-start(bf16[1024,768]{1,0:T(8,128)(2,1)} %own_ref.1) | copy-start | bytes 4718596
  4.6 3.1 %collective-permute-start = (bf16[1024,384]{1,0:T(8,128)(2,1)S(1)}, bf16[1024,384]{1,0:T(8,128)(2,1)S(1)}, u32[]{:S(2)}, u32[]{:S(2)}) collective-permute-start(bf16[1024,384]{1,0:T(8,128)(2,1)S(1)} %get-tuple-element.31), channel_id=1, source_target_pairs={{0,1},{1,0},{2,3},{3,2},{4,5},{5,4},{6,7},{7,6},{8,9},{9,8},{10,11... | collective-permute-start | bytes 2359304 | tf_op jit(solution)/shard_map/ppermute | solution.py:504
  5.1 7.4 %collective-permute-start.2 = (bf16[200,768]{1,0:T(8,128)(2,1)S(1)}, bf16[200,768]{1,0:T(8,128)(2,1)S(1)}, u32[]{:S(2)}, u32[]{:S(2)}) collective-permute-start(bf16[200,768]{1,0:T(8,128)(2,1)S(1)} %get-tuple-element.37), channel_id=1, source_target_pairs={{0,2},{1,5},{2,0},{3,7},{4,6},{5,1},{6,4},{7,3},{8,10},{9,13},{10,... | collective-permute-start | bytes 921608 | tf_op jit(solution)/shard_map/ppermute | solution.py:501
  10.0 15.1 %copy-start = (s32[97,1536]{1,0:T(8,128)S(1)}, s32[97,1536]{1,0:T(8,128)}, u32[]{:S(2)}) copy-start(s32[97,1536]{1,0:T(8,128)} %annot_ref.1) | copy-start | bytes 1787908
  10.0 15.0 %copy-start.1 = (s32[1536]{0:T(1024)S(1)}, s32[1536]{0:T(1024)}, u32[]{:S(2)}) copy-start(s32[1536]{0:T(1024)} %param.6) | copy-start | bytes 18436
  10.0 15.0 %copy-start.2 = (s32[1536]{0:T(1024)S(1)}, s32[1536]{0:T(1024)}, u32[]{:S(2)}) copy-start(s32[1536]{0:T(1024)} %param.9) | copy-start | bytes 18436
  10.0 15.0 %copy-start.3 = (s32[1536]{0:T(1024)S(1)}, s32[1536]{0:T(1024)}, u32[]{:S(2)}) copy-start(s32[1536]{0:T(1024)} %param.7) | copy-start | bytes 18436
  10.0 5.7 %collective-permute-start.1 = (bf16[224,384]{1,0:T(8,128)(2,1)S(1)}, bf16[224,384]{1,0:T(8,128)(2,1)S(1)}, u32[]{:S(2)}, u32[]{:S(2)}) collective-permute-start(bf16[224,384]{1,0:T(8,128)(2,1)S(1)} %get-tuple-element.34), channel_id=1, source_target_pairs={{0,2},{1,5},{2,0},{3,7},{4,6},{5,1},{6,4},{7,3},{8,10},{9,13},{10,... | collective-permute-start | bytes 516104 | tf_op jit(solution)/shard_map/ppermute | solution.py:501
  13.1 6.6 %collective-permute-start.4 = (bf16[104,768]{1,0:T(8,128)(2,1)S(1)}, bf16[104,768]{1,0:T(8,128)(2,1)S(1)}, u32[]{:S(2)}, u32[]{:S(2)}) collective-permute-start(bf16[104,768]{1,0:T(8,128)(2,1)S(1)} %get-tuple-element.44), channel_id=1, source_target_pairs={{0,4},{1,9},{2,6},{3,11},{4,0},{5,13},{6,2},{7,15},{8,12},{9,1},{1... | collective-permute-start | bytes 479240 | tf_op jit(solution)/shard_map/ppermute | solution.py:501
  16.3 6.7 %collective-permute-start.3 = (bf16[128,384]{1,0:T(8,128)(2,1)S(1)}, bf16[128,384]{1,0:T(8,128)(2,1)S(1)}, u32[]{:S(2)}, u32[]{:S(2)}) collective-permute-start(bf16[128,384]{1,0:T(8,128)(2,1)S(1)} %get-tuple-element.41), channel_id=1, source_target_pairs={{0,4},{1,9},{2,6},{3,11},{4,0},{5,13},{6,2},{7,15},{8,12},{9,1},{1... | collective-permute-start | bytes 294920 | tf_op jit(solution)/shard_map/ppermute | solution.py:501
  20.4 6.4 %collective-permute-start.6 = (bf16[112,768]{1,0:T(8,128)(2,1)S(1)}, bf16[112,768]{1,0:T(8,128)(2,1)S(1)}, u32[]{:S(2)}, u32[]{:S(2)}) collective-permute-start(bf16[112,768]{1,0:T(8,128)(2,1)S(1)} %get-tuple-element.48.kept_ref), channel_id=1, source_target_pairs={{0,8},{1,3},{2,10},{3,1},{4,12},{5,7},{6,14},{7,5},{8,0},{9,11},{1... | collective-permute-start | bytes 516104 | tf_op jit(solution)/shard_map/ppermute | solution.py:501
  23.5 6.1 %collective-permute-start.5 = (bf16[128,384]{1,0:T(8,128)(2,1)S(1)}, bf16[128,384]{1,0:T(8,128)(2,1)S(1)}, u32[]{:S(2)}, u32[]{:S(2)}) collective-permute-start(bf16[128,384]{1,0:T(8,128)(2,1)S(1)} %get-tuple-element.46.kept_ref), channel_id=1, source_target_pairs={{0,8},{1,3},{2,10},{3,1},{4,12},{5,7},{6,14},{7,5},{8,0},{9,11},{1... | collective-permute-start | bytes 294920 | tf_op jit(solution)/shard_map/ppermute | solution.py:501
  31.2 4.8 %collective-permute-start.9 = (f16[97,512]{1,0:T(8,128)(2,1)S(1)}, f16[97,512]{1,0:T(8,128)(2,1)S(1)}, u32[]{:S(2)}, u32[]{:S(2)}) collective-permute-start(f16[97,512]{1,0:T(8,128)(2,1)S(1)} %slice.23), channel_id=1, source_target_pairs={{0,2},{1,9},{2,0},{3,11},{4,6},{5,13},{6,4},{7,15},{8,10},{9,1},{1... | collective-permute-start | bytes 297992 | tf_op jit(solution)/shard_map/ppermute | solution.py:501
  32.8 5.3 %collective-permute-start.7 = (f16[97,640]{1,0:T(8,128)(2,1)S(1)}, f16[97,640]{1,0:T(8,128)(2,1)S(1)}, u32[]{:S(2)}, u32[]{:S(2)}) collective-permute-start(f16[97,640]{1,0:T(8,128)(2,1)S(1)} %slice.22), channel_id=1, source_target_pairs={{0,2},{1,9},{2,0},{3,11},{4,6},{5,13},{6,4},{7,15},{8,10},{9,1},{1... | collective-permute-start | bytes 372488 | tf_op jit(solution)/shard_map/ppermute | solution.py:501
  36.0 5.9 %collective-permute-start.10 = (f16[97,512]{1,0:T(8,128)(2,1)S(1)}, f16[97,512]{1,0:T(8,128)(2,1)S(1)}, u32[]{:S(2)}, u32[]{:S(2)}) collective-permute-start(f16[97,512]{1,0:T(8,128)(2,1)S(1)} %add_convert_fusion.1), channel_id=1, source_target_pairs={{0,4},{1,5},{2,6},{3,7},{4,0},{5,1},{6,2},{7,3},{8,12},{9,13},{10,... | collective-permute-start | bytes 297992 | tf_op jit(solution)/shard_map/ppermute | solution.py:501
  38.2 5.3 %collective-permute-start.8 = (f16[97,640]{1,0:T(8,128)(2,1)S(1)}, f16[97,640]{1,0:T(8,128)(2,1)S(1)}, u32[]{:S(2)}, u32[]{:S(2)}) collective-permute-start(f16[97,640]{1,0:T(8,128)(2,1)S(1)} %add_convert_fusion), channel_id=1, source_target_pairs={{0,4},{1,5},{2,6},{3,7},{4,0},{5,1},{6,2},{7,3},{8,12},{9,13},{10,... | collective-permute-start | bytes 372488 | tf_op jit(solution)/shard_map/ppermute | solution.py:501
  42.0 2.5 %collective-permute-start.11 = (f32[97,384]{1,0:T(8,128)S(1)}, f32[97,384]{1,0:T(8,128)S(1)}, u32[]{:S(2)}, u32[]{:S(2)}) collective-permute-start(f32[97,384]{1,0:T(8,128)S(1)} %slice.26), channel_id=1, source_target_pairs={{0,1},{1,0},{2,3},{3,2},{4,5},{5,4},{6,7},{7,6},{8,9},{9,8},{10,11... | collective-permute-start | bytes 446984 | tf_op jit(solution)/shard_map/ppermute | solution.py:504
  44.5 1.4 %collective-permute-start.12 = (f32[200,97]{1,0:T(8,128)S(1)}, f32[200,97]{1,0:T(8,128)S(1)}, u32[]{:S(2)}, u32[]{:S(2)}) collective-permute-start(f32[200,97]{1,0:T(8,128)S(1)} %shard_map.77), channel_id=1, source_target_pairs={{0,1},{1,0},{2,3},{3,2},{4,5},{5,4},{6,7},{7,6},{8,9},{9,8},{10,11... | collective-permute-start | bytes 232808 | tf_op jit(solution)/shard_map/ppermute | solution.py:504

commit v7 on v6

--- a/solution.py
+++ b/solution.py
@@ -13,7 +13,7 @@
 F32 = jnp.float32
 BF16 = jnp.bfloat16
 ORDERS = [[0, 1, 2], [1, 2, 0]]
-ROUNDS = [[0, 1], [2, 1]]
+ROUNDS = [[0, 1], [1, 2]]
 VMEM_LIMIT = 20 * 1024 * 1024
 
 

time: 46.7 us -> 46.5 us (level)
  no operation moved by 1% of the time
where the time goes in v7:
time: 46.5 us; the launch traced here: 46.3 us
  starting transfers between devices  20 us (43%)
  Pallas kernels  12 us (26%)
  waiting for transfers between devices  10.3 us (22%)
  other arithmetic  1.63 us (4%)
  local copies, waits for them, and re-layouts  1.58 us (3%)
  between operations  0.82 us (2%)
    ppermute x10, starting transfers between devices, exchange(): return lax.ppermute(x, ('samples', 'genome'), route)  19.3 us
    pallas_call x10, Pallas kernels, call(): pl.pallas_call(kernel, out_shape=outputs, in_specs=[smem] + [vmem] * (len...  12 us
    ppermute x10, waiting for transfers between devices, exchange(): return lax.ppermute(x, ('samples', 'genome'), route)  9.78 us
    unnamed x10, local copies, waits for them, and re-layouts  1.44 us
  transfers between devices with their start and end apart: 13, of which 9 were waited for; matrix products, arithmetic and copies ran while one was open for 2% of the time, Pallas kernels for 17%

profile of v7, /device:TPU:0, one launch (start us, length us, event | category | flops | bytes accessed | tf_op | source)
XLA Modules:
  0.0 46.3 jit_solution(9328274375348328615)
XLA Ops:
  0.6 0.1 stack.27.pos_ref
  0.7 1.4 %copy-done.4 = bf16[1024,768]{1,0:T(8,128)(2,1)S(1)} copy-done((bf16[1024,768]{1,0:T(8,128)(2,1)S(1)}, bf16[1024,768]{1,0:T(8,128)(2,1)}, u32[]{:S(2)}) %copy-start.4) | copy-done | bytes 1572888
  2.1 2.4 %shard_map.68 = (f32[192,768]{1,0:T(8,128)S(1)}, bf16[200,768]{1,0:T(8,128)(2,1)S(1)}, f32[16,768]{1,0:T(8,128)S(1)}, bf16[768,1024]{1,0:T(8,128)(2,1)S(1)}, bf16[1024,384]{1,0:T(8,128)(2,1)S(1)}) custom-call(s32[6]{0:T(128)S(1)} %stack.27.pos_ref, bf16[1024,768]{1,0:T(8,128)(2,1)S(1)} %copy-done.4), custom_call_target="tpu_custom_call" | custom-call | flops 905969664 | bytes 1572864 | tf_op jit(solution)/shard_map/pallas_call | solution.py:472
  4.6 0.5 %collective-permute-start = (bf16[1024,384]{1,0:T(8,128)(2,1)S(1)}, bf16[1024,384]{1,0:T(8,128)(2,1)S(1)}, u32[]{:S(2)}, u32[]{:S(2)}) collective-permute-start(bf16[1024,384]{1,0:T(8,128)(2,1)S(1)} %get-tuple-element.31), channel_id=1, source_target_pairs={{0,1},{1,0},{2,3},{3,2},{4,5},{5,4},{6,7},{7,6},{8,9},{9,8},{10,11... | collective-permute-start | bytes 2359304 | tf_op jit(solution)/shard_map/ppermute | solution.py:504
  5.1 2.6 %collective-permute-start.2 = (bf16[200,768]{1,0:T(8,128)(2,1)S(1)}, bf16[200,768]{1,0:T(8,128)(2,1)S(1)}, u32[]{:S(2)}, u32[]{:S(2)}) collective-permute-start(bf16[200,768]{1,0:T(8,128)(2,1)S(1)} %get-tuple-element.37), channel_id=1, source_target_pairs={{0,2},{1,5},{2,0},{3,7},{4,6},{5,1},{6,4},{7,3},{8,10},{9,13},{10,... | collective-permute-start | bytes 921608 | tf_op jit(solution)/shard_map/ppermute | solution.py:501
  7.7 0.0 collective-permute-done.there_ref
  7.7 2.3 %shard_map.69 = (f32[192,384]{1,0:T(8,128)S(1)}, bf16[224,384]{1,0:T(8,128)(2,1)S(1)}, f32[16,384]{1,0:T(8,128)S(1)}) custom-call(s32[6]{0:T(128)S(1)} %stack.27.pos_ref, bf16[768,1024]{1,0:T(8,128)(2,1)S(1)} %get-tuple-element.30.turned_ref, bf16[1024,384]{1,0:T(8,128)(2,1)S(1)} %collective-permute-done.there_ref, ...), custom_call_target="tpu_custom_call" | custom-call | flops 905969664 | bytes 1572864 | tf_op jit(solution)/shard_map/pallas_call | solution.py:472
  10.0 0.0 copy-start
  10.0 0.0 copy-start.1
  10.0 0.0 copy-start.2
  10.0 0.0 copy-start.3
  10.0 2.3 %collective-permute-start.1 = (bf16[224,384]{1,0:T(8,128)(2,1)S(1)}, bf16[224,384]{1,0:T(8,128)(2,1)S(1)}, u32[]{:S(2)}, u32[]{:S(2)}) collective-permute-start(bf16[224,384]{1,0:T(8,128)(2,1)S(1)} %get-tuple-element.34), channel_id=1, source_target_pairs={{0,2},{1,5},{2,0},{3,7},{4,6},{5,1},{6,4},{7,3},{8,10},{9,13},{10,... | collective-permute-start | bytes 516104 | tf_op jit(solution)/shard_map/ppermute | solution.py:501
  12.3 0.2 collective-permute-done.2.msg_ref
  12.5 0.6 %shard_map.70 = (f32[96,768]{1,0:T(8,128)S(1)}, bf16[104,768]{1,0:T(8,128)(2,1)S(1)}, f32[16,768]{1,0:T(8,128)S(1)}) custom-call(s32[6]{0:T(128)S(1)} %stack.27.pos_ref, f32[192,768]{1,0:T(8,128)S(1)} %get-tuple-element.36.kept_ref, bf16[200,768]{1,0:T(8,128)(2,1)S(1)} %collective-permute-done.2.msg_ref, f32[16,768]{1,0:T(8,128)S(1)} %get-tuple-element.32.own_stats_ref.stats_ref), custom_call_target="tpu_custom_call" | custom-call | flops 589824 | bytes 1474560 | tf_op jit(solution)/shard_map/pallas_call | solution.py:472
  13.1 2.2 %collective-permute-start.4 = (bf16[104,768]{1,0:T(8,128)(2,1)S(1)}, bf16[104,768]{1,0:T(8,128)(2,1)S(1)}, u32[]{:S(2)}, u32[]{:S(2)}) collective-permute-start(bf16[104,768]{1,0:T(8,128)(2,1)S(1)} %get-tuple-element.44), channel_id=1, source_target_pairs={{0,4},{1,9},{2,6},{3,11},{4,0},{5,13},{6,2},{7,15},{8,12},{9,1},{1... | collective-permute-start | bytes 479240 | tf_op jit(solution)/shard_map/ppermute | solution.py:501
  15.3 0.4 collective-permute-done.1.msg_ref
  15.7 0.6 %shard_map.71 = (f32[96,384]{1,0:T(8,128)S(1)}, bf16[128,384]{1,0:T(8,128)(2,1)S(1)}, f32[16,384]{1,0:T(8,128)S(1)}) custom-call(s32[6]{0:T(128)S(1)} %stack.27.pos_ref, f32[192,384]{1,0:T(8,128)S(1)} %get-tuple-element.33.kept_ref, bf16[224,384]{1,0:T(8,128)(2,1)S(1)} %collective-permute-done.1.msg_ref, f32[16,384]{1,0:T(8,128)S(1)} %get-tuple-element.35.stats_ref, ...), custom_call_target="tpu_custom_call" | custom-call | flops 294912 | bytes 737280 | tf_op jit(solution)/shard_map/pallas_call | solution.py:472
  16.3 2.2 %collective-permute-start.3 = (bf16[128,384]{1,0:T(8,128)(2,1)S(1)}, bf16[128,384]{1,0:T(8,128)(2,1)S(1)}, u32[]{:S(2)}, u32[]{:S(2)}) collective-permute-start(bf16[128,384]{1,0:T(8,128)(2,1)S(1)} %get-tuple-element.41), channel_id=1, source_target_pairs={{0,4},{1,9},{2,6},{3,11},{4,0},{5,13},{6,2},{7,15},{8,12},{9,1},{1... | collective-permute-start | bytes 294920 | tf_op jit(solution)/shard_map/ppermute | solution.py:501
  18.4 1.3 %collective-permute-done.4.msg_ref = bf16[104,768]{1,0:T(8,128)(2,1)S(1)} collective-permute-done((bf16[104,768]{1,0:T(8,128)(2,1)S(1)}, bf16[104,768]{1,0:T(8,128)(2,1)S(1)}, u32[]{:S(2)}, u32[]{:S(2)}) %collective-permute-start.4) | collective-permute-done | bytes 159776 | tf_op jit(solution)/shard_map/ppermute | solution.py:501
  19.8 0.6 %shard_map.72 = (bf16[112,768]{1,0:T(8,128)(2,1)S(1)}, f32[16,768]{1,0:T(8,128)S(1)}) custom-call(s32[6]{0:T(128)S(1)} %stack.27.pos_ref, f32[96,768]{1,0:T(8,128)S(1)} %get-tuple-element.43.kept_ref, bf16[104,768]{1,0:T(8,128)(2,1)S(1)} %collective-permute-done.4.msg_ref, f32[16,768]{1,0:T(8,128)S(1)} %get-tuple-element.39.refs_0_.stats_ref), custom_call_target="tpu_custom_call" | custom-call | flops 589824 | bytes 1474560 | tf_op jit(solution)/shard_map/pallas_call | solution.py:472
  20.4 2.6 %collective-permute-start.6 = (bf16[112,768]{1,0:T(8,128)(2,1)S(1)}, bf16[112,768]{1,0:T(8,128)(2,1)S(1)}, u32[]{:S(2)}, u32[]{:S(2)}) collective-permute-start(bf16[112,768]{1,0:T(8,128)(2,1)S(1)} %get-tuple-element.48.kept_ref), channel_id=1, source_target_pairs={{0,8},{1,3},{2,10},{3,1},{4,12},{5,7},{6,14},{7,5},{8,0},{9,11},{1... | collective-permute-start | bytes 516104 | tf_op jit(solution)/shard_map/ppermute | solution.py:501
  23.0 0.0 collective-permute-done.3.msg_ref
  23.0 0.6 %shard_map.73 = (bf16[128,384]{1,0:T(8,128)(2,1)S(1)}, f32[16,384]{1,0:T(8,128)S(1)}) custom-call(s32[6]{0:T(128)S(1)} %stack.27.pos_ref, f32[96,384]{1,0:T(8,128)S(1)} %get-tuple-element.40.kept_ref, bf16[128,384]{1,0:T(8,128)(2,1)S(1)} %collective-permute-done.3.msg_ref, f32[16,384]{1,0:T(8,128)S(1)} %get-tuple-element.42.stats_ref, ...), custom_call_target="tpu_custom_call" | custom-call | flops 294912 | bytes 737280 | tf_op jit(solution)/shard_map/pallas_call | solution.py:472
  23.5 1.5 %collective-permute-start.5 = (bf16[128,384]{1,0:T(8,128)(2,1)S(1)}, bf16[128,384]{1,0:T(8,128)(2,1)S(1)}, u32[]{:S(2)}, u32[]{:S(2)}) collective-permute-start(bf16[128,384]{1,0:T(8,128)(2,1)S(1)} %get-tuple-element.46.kept_ref), channel_id=1, source_target_pairs={{0,8},{1,3},{2,10},{3,1},{4,12},{5,7},{6,14},{7,5},{8,0},{9,11},{1... | collective-permute-start | bytes 294920 | tf_op jit(solution)/shard_map/ppermute | solution.py:501
  25.0 0.0 copy-done
  25.0 0.0 copy-done.1
  25.0 0.0 copy-done.2
  25.0 0.0 copy-done.3
  25.0 1.0 %shard_map.74 = (bf16[97,1152]{1,0:T(8,128)(2,1)S(1)}, bf16[97,1536]{1,0:T(8,128)(2,1)S(1)}, bf16[97,640]{1,0:T(8,128)(2,1)S(1)}, f32[8,1152]{1,0:T(8,128)S(1)}, bf16[200,1152]{1,0:T(8,128)(2,1)S(1)}) custom-call(s32[6]{0:T(128)S(1)} %stack.27.pos_ref, s32[97,1536]{1,0:T(8,128)S(1)} %copy-done, s32[12,128]{1,0:T(8,128)S(1)} %bitcast.11, ...), custom_call_target="tpu_custom_call" | custom-call | flops 1489920 | bytes 1191936 | tf_op jit(solution)/shard_map/pallas_call | solution.py:472
  26.0 0.7 %collective-permute-done.6.msg_ref = bf16[112,768]{1,0:T(8,128)(2,1)S(1)} collective-permute-done((bf16[112,768]{1,0:T(8,128)(2,1)S(1)}, bf16[112,768]{1,0:T(8,128)(2,1)S(1)}, u32[]{:S(2)}, u32[]{:S(2)}) %collective-permute-start.6) | collective-permute-done | bytes 172064 | tf_op jit(solution)/shard_map/ppermute | solution.py:501
  26.7 1.4 %shard_map.75 = (f32[97,768]{1,0:T(8,128)S(1)}, f32[16,768]{1,0:T(8,128)S(1)}) custom-call(s32[6]{0:T(128)S(1)} %stack.27.pos_ref, bf16[112,768]{1,0:T(8,128)(2,1)S(1)} %get-tuple-element.48.kept_ref, bf16[112,768]{1,0:T(8,128)(2,1)S(1)} %collective-permute-done.6.msg_ref, f32[16,768]{1,0:T(8,128)S(1)} %get-tuple-element.45.refs_0_.stats_ref, ...), custom_call_target="tpu_custom_call" | custom-call | flops 57212928 | bytes 1474560 | tf_op jit(solution)/shard_map/pallas_call | solution.py:472
  28.2 1.5 %collective-permute-done.5.msg_ref = bf16[128,384]{1,0:T(8,128)(2,1)S(1)} collective-permute-done((bf16[128,384]{1,0:T(8,128)(2,1)S(1)}, bf16[128,384]{1,0:T(8,128)(2,1)S(1)}, u32[]{:S(2)}, u32[]{:S(2)}) %collective-permute-start.5) | collective-permute-done | bytes 98336 | tf_op jit(solution)/shard_map/ppermute | solution.py:501
  29.7 1.5 %shard_map.76 = f32[97,1152]{1,0:T(8,128)S(1)} custom-call(s32[6]{0:T(128)S(1)} %stack.27.pos_ref, bf16[128,384]{1,0:T(8,128)(2,1)S(1)} %get-tuple-element.46.kept_ref, bf16[128,384]{1,0:T(8,128)(2,1)S(1)} %collective-permute-done.5.msg_ref, f32[16,384]{1,0:T(8,128)S(1)} %get-tuple-element.47.stats_ref, f32[16,768]{1,0:T(8,128)S(1)} %get-tuple-element.52.vec_ref, ...), custom_call_target="tpu_custom_call" | custom-call | flops 57212928 | bytes 1474560 | tf_op jit(solution)/shard_map/pallas_call | solution.py:472
  31.2 1.6 %collective-permute-start.9 = (f16[97,512]{1,0:T(8,128)(2,1)S(1)}, f16[97,512]{1,0:T(8,128)(2,1)S(1)}, u32[]{:S(2)}, u32[]{:S(2)}) collective-permute-start(f16[97,512]{1,0:T(8,128)(2,1)S(1)} %slice.23), channel_id=1, source_target_pairs={{0,2},{1,5},{2,0},{3,7},{4,6},{5,1},{6,4},{7,3},{8,10},{9,13},{10,... | collective-permute-start | bytes 297992 | tf_op jit(solution)/shard_map/ppermute | solution.py:501
  32.8 0.6 %collective-permute-start.7 = (f16[97,640]{1,0:T(8,128)(2,1)S(1)}, f16[97,640]{1,0:T(8,128)(2,1)S(1)}, u32[]{:S(2)}, u32[]{:S(2)}) collective-permute-start(f16[97,640]{1,0:T(8,128)(2,1)S(1)} %slice.22), channel_id=1, source_target_pairs={{0,2},{1,5},{2,0},{3,7},{4,6},{5,1},{6,4},{7,3},{8,10},{9,13},{10,... | collective-permute-start | bytes 372488 | tf_op jit(solution)/shard_map/ppermute | solution.py:501
  33.4 2.6 %collective-permute-done.9 = f16[97,512]{1,0:T(8,128)(2,1)S(1)} collective-permute-done((f16[97,512]{1,0:T(8,128)(2,1)S(1)}, f16[97,512]{1,0:T(8,128)(2,1)S(1)}, u32[]{:S(2)}, u32[]{:S(2)}) %collective-permute-start.9) | collective-permute-done | bytes 99360 | tf_op jit(solution)/shard_map/ppermute | solution.py:501
  36.0 2.1 %collective-permute-start.10 = (f16[97,512]{1,0:T(8,128)(2,1)S(1)}, f16[97,512]{1,0:T(8,128)(2,1)S(1)}, u32[]{:S(2)}, u32[]{:S(2)}) collective-permute-start(f16[97,512]{1,0:T(8,128)(2,1)S(1)} %add_convert_fusion.1), channel_id=1, source_target_pairs={{0,4},{1,9},{2,6},{3,11},{4,0},{5,13},{6,2},{7,15},{8,12},{9,1},{1... | collective-permute-start | bytes 297992 | tf_op jit(solution)/shard_map/ppermute | solution.py:501
  38.2 0.0 collective-permute-done.7
  38.2 1.8 %collective-permute-start.8 = (f16[97,640]{1,0:T(8,128)(2,1)S(1)}, f16[97,640]{1,0:T(8,128)(2,1)S(1)}, u32[]{:S(2)}, u32[]{:S(2)}) collective-permute-start(f16[97,640]{1,0:T(8,128)(2,1)S(1)} %add_convert_fusion), channel_id=1, source_target_pairs={{0,4},{1,9},{2,6},{3,11},{4,0},{5,13},{6,2},{7,15},{8,12},{9,1},{1... | collective-permute-start | bytes 372488 | tf_op jit(solution)/shard_map/ppermute | solution.py:501
  40.0 1.1 %collective-permute-done.10 = f16[97,512]{1,0:T(8,128)(2,1)S(1)} collective-permute-done((f16[97,512]{1,0:T(8,128)(2,1)S(1)}, f16[97,512]{1,0:T(8,128)(2,1)S(1)}, u32[]{:S(2)}, u32[]{:S(2)}) %collective-permute-start.10) | collective-permute-done | bytes 99360 | tf_op jit(solution)/shard_map/ppermute | solution.py:501
  41.2 0.1 collective-permute-start.11
  41.2 2.0 %collective-permute-done.8 = f16[97,640]{1,0:T(8,128)(2,1)S(1)} collective-permute-done((f16[97,640]{1,0:T(8,128)(2,1)S(1)}, f16[97,640]{1,0:T(8,128)(2,1)S(1)}, u32[]{:S(2)}, u32[]{:S(2)}) %collective-permute-start.8) | collective-permute-done | bytes 124192 | tf_op jit(solution)/shard_map/ppermute | solution.py:501
  43.4 0.9 %shard_map.77 = f32[200,97]{1,0:T(8,128)S(1)} custom-call(s32[6]{0:T(128)S(1)} %stack.27.pos_ref, f32[97,1152]{1,0:T(8,128)S(1)} %pad_maximum_fusion.score_ref, bf16[97,1152]{1,0:T(8,128)(2,1)S(1)} %get-tuple-element.50.flag_ref, bf16[200,1152]{1,0:T(8,128)(2,1)S(1)} %get-tuple-element.55.hot_ref), custom_call_target="tpu_custom_call" | custom-call | flops 89395200 | bytes 893952 | tf_op jit(solution)/shard_map/pallas_call | solution.py:472
  44.3 0.1 collective-permute-start.12
  44.4 0.0 collective-permute-done.11
  44.4 0.8 %fusion.2 = f32[97,768]{1,0:T(8,128)} fusion(f32[97,640]{1,0:T(8,128)S(1)} %convert_add_fusion, f32[97,512]{1,0:T(8,128)S(1)} %convert_add_fusion.1, f32[97,384]{1,0:T(8,128)S(1)} %collective-permute-done.11, bf16[97,1152]{1,0:T(8,128)(2,1)S(1)} %get-tuple-element.50.flag_ref, pred[]{:T(512)S(6)} %eq.2), kind=kLoop, calls=%fused_computation.5 | loop fusion | flops 372480 | bytes 1042945 | tf_op jit(solution)/shard_map/add | solution.py:615
  45.1 0.5 %collective-permute-done.12 = f32[200,97]{1,0:T(8,128)S(1)} collective-permute-done((f32[200,97]{1,0:T(8,128)S(1)}, f32[200,97]{1,0:T(8,128)S(1)}, u32[]{:S(2)}, u32[]{:S(2)}) %collective-permute-start.12) | collective-permute-done | bytes 77632 | tf_op jit(solution)/shard_map/ppermute | solution.py:504
  45.6 0.7 %add_bitcast_fusion = f32[97,200]{0,1:T(8,128)} fusion(f32[200,97]{1,0:T(8,128)S(1)} %shard_map.77, f32[200,97]{1,0:T(8,128)S(1)} %collective-permute-done.12), kind=kLoop, calls=%fused_computation.10 | loop fusion | flops 19400 | bytes 232800 | tf_op jit(solution)/shard_map/transpose | solution.py:622
  (10 shorter events, 0.3 us)
Async XLA Ops:
  0.7 1.4 %copy-start.4 = (bf16[1024,768]{1,0:T(8,128)(2,1)S(1)}, bf16[1024,768]{1,0:T(8,128)(2,1)}, u32[]{:S(2)}) copy-start(bf16[1024,768]{1,0:T(8,128)(2,1)} %own_ref.1) | copy-start | bytes 4718596
  4.6 3.1 %collective-permute-start = (bf16[1024,384]{1,0:T(8,128)(2,1)S(1)}, bf16[1024,384]{1,0:T(8,128)(2,1)S(1)}, u32[]{:S(2)}, u32[]{:S(2)}) collective-permute-start(bf16[1024,384]{1,0:T(8,128)(2,1)S(1)} %get-tuple-element.31), channel_id=1, source_target_pairs={{0,1},{1,0},{2,3},{3,2},{4,5},{5,4},{6,7},{7,6},{8,9},{9,8},{10,11... | collective-permute-start | bytes 2359304 | tf_op jit(solution)/shard_map/ppermute | solution.py:504
  5.1 7.4 %collective-permute-start.2 = (bf16[200,768]{1,0:T(8,128)(2,1)S(1)}, bf16[200,768]{1,0:T(8,128)(2,1)S(1)}, u32[]{:S(2)}, u32[]{:S(2)}) collective-permute-start(bf16[200,768]{1,0:T(8,128)(2,1)S(1)} %get-tuple-element.37), channel_id=1, source_target_pairs={{0,2},{1,5},{2,0},{3,7},{4,6},{5,1},{6,4},{7,3},{8,10},{9,13},{10,... | collective-permute-start | bytes 921608 | tf_op jit(solution)/shard_map/ppermute | solution.py:501
  10.0 15.1 %copy-start = (s32[97,1536]{1,0:T(8,128)S(1)}, s32[97,1536]{1,0:T(8,128)}, u32[]{:S(2)}) copy-start(s32[97,1536]{1,0:T(8,128)} %annot_ref.1) | copy-start | bytes 1787908
  10.0 15.0 %copy-start.1 = (s32[1536]{0:T(1024)S(1)}, s32[1536]{0:T(1024)}, u32[]{:S(2)}) copy-start(s32[1536]{0:T(1024)} %param.6) | copy-start | bytes 18436
  10.0 15.0 %copy-start.2 = (s32[1536]{0:T(1024)S(1)}, s32[1536]{0:T(1024)}, u32[]{:S(2)}) copy-start(s32[1536]{0:T(1024)} %param.9) | copy-start | bytes 18436
  10.0 15.0 %copy-start.3 = (s32[1536]{0:T(1024)S(1)}, s32[1536]{0:T(1024)}, u32[]{:S(2)}) copy-start(s32[1536]{0:T(1024)} %param.7) | copy-start | bytes 18436
  10.0 5.7 %collective-permute-start.1 = (bf16[224,384]{1,0:T(8,128)(2,1)S(1)}, bf16[224,384]{1,0:T(8,128)(2,1)S(1)}, u32[]{:S(2)}, u32[]{:S(2)}) collective-permute-start(bf16[224,384]{1,0:T(8,128)(2,1)S(1)} %get-tuple-element.34), channel_id=1, source_target_pairs={{0,2},{1,5},{2,0},{3,7},{4,6},{5,1},{6,4},{7,3},{8,10},{9,13},{10,... | collective-permute-start | bytes 516104 | tf_op jit(solution)/shard_map/ppermute | solution.py:501
  13.1 6.6 %collective-permute-start.4 = (bf16[104,768]{1,0:T(8,128)(2,1)S(1)}, bf16[104,768]{1,0:T(8,128)(2,1)S(1)}, u32[]{:S(2)}, u32[]{:S(2)}) collective-permute-start(bf16[104,768]{1,0:T(8,128)(2,1)S(1)} %get-tuple-element.44), channel_id=1, source_target_pairs={{0,4},{1,9},{2,6},{3,11},{4,0},{5,13},{6,2},{7,15},{8,12},{9,1},{1... | collective-permute-start | bytes 479240 | tf_op jit(solution)/shard_map/ppermute | solution.py:501
  16.3 6.7 %collective-permute-start.3 = (bf16[128,384]{1,0:T(8,128)(2,1)S(1)}, bf16[128,384]{1,0:T(8,128)(2,1)S(1)}, u32[]{:S(2)}, u32[]{:S(2)}) collective-permute-start(bf16[128,384]{1,0:T(8,128)(2,1)S(1)} %get-tuple-element.41), channel_id=1, source_target_pairs={{0,4},{1,9},{2,6},{3,11},{4,0},{5,13},{6,2},{7,15},{8,12},{9,1},{1... | collective-permute-start | bytes 294920 | tf_op jit(solution)/shard_map/ppermute | solution.py:501
  20.4 6.4 %collective-permute-start.6 = (bf16[112,768]{1,0:T(8,128)(2,1)S(1)}, bf16[112,768]{1,0:T(8,128)(2,1)S(1)}, u32[]{:S(2)}, u32[]{:S(2)}) collective-permute-start(bf16[112,768]{1,0:T(8,128)(2,1)S(1)} %get-tuple-element.48.kept_ref), channel_id=1, source_target_pairs={{0,8},{1,3},{2,10},{3,1},{4,12},{5,7},{6,14},{7,5},{8,0},{9,11},{1... | collective-permute-start | bytes 516104 | tf_op jit(solution)/shard_map/ppermute | solution.py:501
  23.5 6.1 %collective-permute-start.5 = (bf16[128,384]{1,0:T(8,128)(2,1)S(1)}, bf16[128,384]{1,0:T(8,128)(2,1)S(1)}, u32[]{:S(2)}, u32[]{:S(2)}) collective-permute-start(bf16[128,384]{1,0:T(8,128)(2,1)S(1)} %get-tuple-element.46.kept_ref), channel_id=1, source_target_pairs={{0,8},{1,3},{2,10},{3,1},{4,12},{5,7},{6,14},{7,5},{8,0},{9,11},{1... | collective-permute-start | bytes 294920 | tf_op jit(solution)/shard_map/ppermute | solution.py:501
  31.2 4.8 %collective-permute-start.9 = (f16[97,512]{1,0:T(8,128)(2,1)S(1)}, f16[97,512]{1,0:T(8,128)(2,1)S(1)}, u32[]{:S(2)}, u32[]{:S(2)}) collective-permute-start(f16[97,512]{1,0:T(8,128)(2,1)S(1)} %slice.23), channel_id=1, source_target_pairs={{0,2},{1,5},{2,0},{3,7},{4,6},{5,1},{6,4},{7,3},{8,10},{9,13},{10,... | collective-permute-start | bytes 297992 | tf_op jit(solution)/shard_map/ppermute | solution.py:501
  32.8 5.3 %collective-permute-start.7 = (f16[97,640]{1,0:T(8,128)(2,1)S(1)}, f16[97,640]{1,0:T(8,128)(2,1)S(1)}, u32[]{:S(2)}, u32[]{:S(2)}) collective-permute-start(f16[97,640]{1,0:T(8,128)(2,1)S(1)} %slice.22), channel_id=1, source_target_pairs={{0,2},{1,5},{2,0},{3,7},{4,6},{5,1},{6,4},{7,3},{8,10},{9,13},{10,... | collective-permute-start | bytes 372488 | tf_op jit(solution)/shard_map/ppermute | solution.py:501
  36.0 5.0 %collective-permute-start.10 = (f16[97,512]{1,0:T(8,128)(2,1)S(1)}, f16[97,512]{1,0:T(8,128)(2,1)S(1)}, u32[]{:S(2)}, u32[]{:S(2)}) collective-permute-start(f16[97,512]{1,0:T(8,128)(2,1)S(1)} %add_convert_fusion.1), channel_id=1, source_target_pairs={{0,4},{1,9},{2,6},{3,11},{4,0},{5,13},{6,2},{7,15},{8,12},{9,1},{1... | collective-permute-start | bytes 297992 | tf_op jit(solution)/shard_map/ppermute | solution.py:501
  38.2 5.1 %collective-permute-start.8 = (f16[97,640]{1,0:T(8,128)(2,1)S(1)}, f16[97,640]{1,0:T(8,128)(2,1)S(1)}, u32[]{:S(2)}, u32[]{:S(2)}) collective-permute-start(f16[97,640]{1,0:T(8,128)(2,1)S(1)} %add_convert_fusion), channel_id=1, source_target_pairs={{0,4},{1,9},{2,6},{3,11},{4,0},{5,13},{6,2},{7,15},{8,12},{9,1},{1... | collective-permute-start | bytes 372488 | tf_op jit(solution)/shard_map/ppermute | solution.py:501
  41.2 3.2 %collective-permute-start.11 = (f32[97,384]{1,0:T(8,128)S(1)}, f32[97,384]{1,0:T(8,128)S(1)}, u32[]{:S(2)}, u32[]{:S(2)}) collective-permute-start(f32[97,384]{1,0:T(8,128)S(1)} %slice.26), channel_id=1, source_target_pairs={{0,1},{1,0},{2,3},{3,2},{4,5},{5,4},{6,7},{7,6},{8,9},{9,8},{10,11... | collective-permute-start | bytes 446984 | tf_op jit(solution)/shard_map/ppermute | solution.py:504
  44.3 1.4 %collective-permute-start.12 = (f32[200,97]{1,0:T(8,128)S(1)}, f32[200,97]{1,0:T(8,128)S(1)}, u32[]{:S(2)}, u32[]{:S(2)}) collective-permute-start(f32[200,97]{1,0:T(8,128)S(1)} %shard_map.77), channel_id=1, source_target_pairs={{0,1},{1,0},{2,3},{3,2},{4,5},{5,4},{6,7},{7,6},{8,9},{9,8},{10,11... | collective-permute-start | bytes 232808 | tf_op jit(solution)/shard_map/ppermute | solution.py:504

commit v8 on v7

--- a/solution.py
+++ b/solution.py
@@ -617,7 +617,8 @@
         jnp.concatenate([nothing, arrived], axis=1),
         jnp.concatenate([arrived, nothing], axis=1),
     )
-    sums_there = across(sums)
+    sums = sums.astype(jnp.float16)
+    sums, sums_there = sums.astype(F32), across(sums).astype(F32)
     sums, ld_scores = lax.optimization_barrier((sums, ld_scores))
     return (ld_scores, (sums + sums_there)[:NBLK].T)
 

time: 46.5 us -> 46.4 us (level)
  no operation moved by 1% of the time
where the time goes in v8:
time: 46.4 us; the launch traced here: 46.3 us
  starting transfers between devices  20 us (43%)
  Pallas kernels  12 us (26%)
  waiting for transfers between devices  10.2 us (22%)
  other arithmetic  1.65 us (4%)
  local copies, waits for them, and re-layouts  1.58 us (3%)
  between operations  0.83 us (2%)
    ppermute x10, starting transfers between devices, exchange(): return lax.ppermute(x, ('samples', 'genome'), route)  19.3 us
    pallas_call x10, Pallas kernels, call(): pl.pallas_call(kernel, out_shape=outputs, in_specs=[smem] + [vmem] * (len...  12 us
    ppermute x10, waiting for transfers between devices, exchange(): return lax.ppermute(x, ('samples', 'genome'), route)  9.78 us
    unnamed x10, local copies, waits for them, and re-layouts  1.44 us
  transfers between devices with their start and end apart: 13, of which 9 were waited for; matrix products, arithmetic and copies ran while one was open for 2% of the time, Pallas kernels for 17%

profile of v8, /device:TPU:0, one launch (start us, length us, event | category | flops | bytes accessed | tf_op | source)
XLA Modules:
  0.0 46.3 jit_solution(551850407103596130)
XLA Ops:
  0.6 0.1 stack.27.pos_ref
  0.7 1.4 %copy-done.4 = bf16[1024,768]{1,0:T(8,128)(2,1)S(1)} copy-done((bf16[1024,768]{1,0:T(8,128)(2,1)S(1)}, bf16[1024,768]{1,0:T(8,128)(2,1)}, u32[]{:S(2)}) %copy-start.4) | copy-done | bytes 1572888
  2.1 2.4 %shard_map.68 = (f32[192,768]{1,0:T(8,128)S(1)}, bf16[200,768]{1,0:T(8,128)(2,1)S(1)}, f32[16,768]{1,0:T(8,128)S(1)}, bf16[768,1024]{1,0:T(8,128)(2,1)S(1)}, bf16[1024,384]{1,0:T(8,128)(2,1)S(1)}) custom-call(s32[6]{0:T(128)S(1)} %stack.27.pos_ref, bf16[1024,768]{1,0:T(8,128)(2,1)S(1)} %copy-done.4), custom_call_target="tpu_custom_call" | custom-call | flops 905969664 | bytes 1572864 | tf_op jit(solution)/shard_map/pallas_call | solution.py:472
  4.6 0.5 %collective-permute-start = (bf16[1024,384]{1,0:T(8,128)(2,1)S(1)}, bf16[1024,384]{1,0:T(8,128)(2,1)S(1)}, u32[]{:S(2)}, u32[]{:S(2)}) collective-permute-start(bf16[1024,384]{1,0:T(8,128)(2,1)S(1)} %get-tuple-element.31), channel_id=1, source_target_pairs={{0,1},{1,0},{2,3},{3,2},{4,5},{5,4},{6,7},{7,6},{8,9},{9,8},{10,11... | collective-permute-start | bytes 2359304 | tf_op jit(solution)/shard_map/ppermute | solution.py:504
  5.1 2.6 %collective-permute-start.2 = (bf16[200,768]{1,0:T(8,128)(2,1)S(1)}, bf16[200,768]{1,0:T(8,128)(2,1)S(1)}, u32[]{:S(2)}, u32[]{:S(2)}) collective-permute-start(bf16[200,768]{1,0:T(8,128)(2,1)S(1)} %get-tuple-element.37), channel_id=1, source_target_pairs={{0,2},{1,5},{2,0},{3,7},{4,6},{5,1},{6,4},{7,3},{8,10},{9,13},{10,... | collective-permute-start | bytes 921608 | tf_op jit(solution)/shard_map/ppermute | solution.py:501
  7.7 0.0 collective-permute-done.there_ref
  7.7 2.3 %shard_map.69 = (f32[192,384]{1,0:T(8,128)S(1)}, bf16[224,384]{1,0:T(8,128)(2,1)S(1)}, f32[16,384]{1,0:T(8,128)S(1)}) custom-call(s32[6]{0:T(128)S(1)} %stack.27.pos_ref, bf16[768,1024]{1,0:T(8,128)(2,1)S(1)} %get-tuple-element.30.turned_ref, bf16[1024,384]{1,0:T(8,128)(2,1)S(1)} %collective-permute-done.there_ref, ...), custom_call_target="tpu_custom_call" | custom-call | flops 905969664 | bytes 1572864 | tf_op jit(solution)/shard_map/pallas_call | solution.py:472
  10.0 0.0 copy-start
  10.0 0.0 copy-start.1
  10.0 0.0 copy-start.2
  10.0 0.0 copy-start.3
  10.0 2.3 %collective-permute-start.1 = (bf16[224,384]{1,0:T(8,128)(2,1)S(1)}, bf16[224,384]{1,0:T(8,128)(2,1)S(1)}, u32[]{:S(2)}, u32[]{:S(2)}) collective-permute-start(bf16[224,384]{1,0:T(8,128)(2,1)S(1)} %get-tuple-element.34), channel_id=1, source_target_pairs={{0,2},{1,5},{2,0},{3,7},{4,6},{5,1},{6,4},{7,3},{8,10},{9,13},{10,... | collective-permute-start | bytes 516104 | tf_op jit(solution)/shard_map/ppermute | solution.py:501
  12.3 0.2 collective-permute-done.2.msg_ref
  12.5 0.6 %shard_map.70 = (f32[96,768]{1,0:T(8,128)S(1)}, bf16[104,768]{1,0:T(8,128)(2,1)S(1)}, f32[16,768]{1,0:T(8,128)S(1)}) custom-call(s32[6]{0:T(128)S(1)} %stack.27.pos_ref, f32[192,768]{1,0:T(8,128)S(1)} %get-tuple-element.36.kept_ref, bf16[200,768]{1,0:T(8,128)(2,1)S(1)} %collective-permute-done.2.msg_ref, f32[16,768]{1,0:T(8,128)S(1)} %get-tuple-element.32.own_stats_ref.stats_ref), custom_call_target="tpu_custom_call" | custom-call | flops 589824 | bytes 1474560 | tf_op jit(solution)/shard_map/pallas_call | solution.py:472
  13.1 2.2 %collective-permute-start.4 = (bf16[104,768]{1,0:T(8,128)(2,1)S(1)}, bf16[104,768]{1,0:T(8,128)(2,1)S(1)}, u32[]{:S(2)}, u32[]{:S(2)}) collective-permute-start(bf16[104,768]{1,0:T(8,128)(2,1)S(1)} %get-tuple-element.44), channel_id=1, source_target_pairs={{0,4},{1,9},{2,6},{3,11},{4,0},{5,13},{6,2},{7,15},{8,12},{9,1},{1... | collective-permute-start | bytes 479240 | tf_op jit(solution)/shard_map/ppermute | solution.py:501
  15.3 0.4 collective-permute-done.1.msg_ref
  15.7 0.6 %shard_map.71 = (f32[96,384]{1,0:T(8,128)S(1)}, bf16[128,384]{1,0:T(8,128)(2,1)S(1)}, f32[16,384]{1,0:T(8,128)S(1)}) custom-call(s32[6]{0:T(128)S(1)} %stack.27.pos_ref, f32[192,384]{1,0:T(8,128)S(1)} %get-tuple-element.33.kept_ref, bf16[224,384]{1,0:T(8,128)(2,1)S(1)} %collective-permute-done.1.msg_ref, f32[16,384]{1,0:T(8,128)S(1)} %get-tuple-element.35.stats_ref, ...), custom_call_target="tpu_custom_call" | custom-call | flops 294912 | bytes 737280 | tf_op jit(solution)/shard_map/pallas_call | solution.py:472
  16.3 2.2 %collective-permute-start.3 = (bf16[128,384]{1,0:T(8,128)(2,1)S(1)}, bf16[128,384]{1,0:T(8,128)(2,1)S(1)}, u32[]{:S(2)}, u32[]{:S(2)}) collective-permute-start(bf16[128,384]{1,0:T(8,128)(2,1)S(1)} %get-tuple-element.41), channel_id=1, source_target_pairs={{0,4},{1,9},{2,6},{3,11},{4,0},{5,13},{6,2},{7,15},{8,12},{9,1},{1... | collective-permute-start | bytes 294920 | tf_op jit(solution)/shard_map/ppermute | solution.py:501
  18.4 1.3 %collective-permute-done.4.msg_ref = bf16[104,768]{1,0:T(8,128)(2,1)S(1)} collective-permute-done((bf16[104,768]{1,0:T(8,128)(2,1)S(1)}, bf16[104,768]{1,0:T(8,128)(2,1)S(1)}, u32[]{:S(2)}, u32[]{:S(2)}) %collective-permute-start.4) | collective-permute-done | bytes 159776 | tf_op jit(solution)/shard_map/ppermute | solution.py:501
  19.8 0.6 %shard_map.72 = (bf16[112,768]{1,0:T(8,128)(2,1)S(1)}, f32[16,768]{1,0:T(8,128)S(1)}) custom-call(s32[6]{0:T(128)S(1)} %stack.27.pos_ref, f32[96,768]{1,0:T(8,128)S(1)} %get-tuple-element.43.kept_ref, bf16[104,768]{1,0:T(8,128)(2,1)S(1)} %collective-permute-done.4.msg_ref, f32[16,768]{1,0:T(8,128)S(1)} %get-tuple-element.39.refs_0_.stats_ref), custom_call_target="tpu_custom_call" | custom-call | flops 589824 | bytes 1474560 | tf_op jit(solution)/shard_map/pallas_call | solution.py:472
  20.4 2.6 %collective-permute-start.6 = (bf16[112,768]{1,0:T(8,128)(2,1)S(1)}, bf16[112,768]{1,0:T(8,128)(2,1)S(1)}, u32[]{:S(2)}, u32[]{:S(2)}) collective-permute-start(bf16[112,768]{1,0:T(8,128)(2,1)S(1)} %get-tuple-element.48.kept_ref), channel_id=1, source_target_pairs={{0,8},{1,3},{2,10},{3,1},{4,12},{5,7},{6,14},{7,5},{8,0},{9,11},{1... | collective-permute-start | bytes 516104 | tf_op jit(solution)/shard_map/ppermute | solution.py:501
  23.0 0.0 collective-permute-done.3.msg_ref
  23.0 0.6 %shard_map.73 = (bf16[128,384]{1,0:T(8,128)(2,1)S(1)}, f32[16,384]{1,0:T(8,128)S(1)}) custom-call(s32[6]{0:T(128)S(1)} %stack.27.pos_ref, f32[96,384]{1,0:T(8,128)S(1)} %get-tuple-element.40.kept_ref, bf16[128,384]{1,0:T(8,128)(2,1)S(1)} %collective-permute-done.3.msg_ref, f32[16,384]{1,0:T(8,128)S(1)} %get-tuple-element.42.stats_ref, ...), custom_call_target="tpu_custom_call" | custom-call | flops 294912 | bytes 737280 | tf_op jit(solution)/shard_map/pallas_call | solution.py:472
  23.5 1.5 %collective-permute-start.5 = (bf16[128,384]{1,0:T(8,128)(2,1)S(1)}, bf16[128,384]{1,0:T(8,128)(2,1)S(1)}, u32[]{:S(2)}, u32[]{:S(2)}) collective-permute-start(bf16[128,384]{1,0:T(8,128)(2,1)S(1)} %get-tuple-element.46.kept_ref), channel_id=1, source_target_pairs={{0,8},{1,3},{2,10},{3,1},{4,12},{5,7},{6,14},{7,5},{8,0},{9,11},{1... | collective-permute-start | bytes 294920 | tf_op jit(solution)/shard_map/ppermute | solution.py:501
  25.0 0.0 copy-done
  25.0 0.0 copy-done.1
  25.0 0.0 copy-done.2
  25.0 0.0 copy-done.3
  25.0 1.0 %shard_map.74 = (bf16[97,1152]{1,0:T(8,128)(2,1)S(1)}, bf16[97,1536]{1,0:T(8,128)(2,1)S(1)}, bf16[97,640]{1,0:T(8,128)(2,1)S(1)}, f32[8,1152]{1,0:T(8,128)S(1)}, bf16[200,1152]{1,0:T(8,128)(2,1)S(1)}) custom-call(s32[6]{0:T(128)S(1)} %stack.27.pos_ref, s32[97,1536]{1,0:T(8,128)S(1)} %copy-done, s32[12,128]{1,0:T(8,128)S(1)} %bitcast.11, ...), custom_call_target="tpu_custom_call" | custom-call | flops 1489920 | bytes 1191936 | tf_op jit(solution)/shard_map/pallas_call | solution.py:472
  26.0 0.7 %collective-permute-done.6.msg_ref = bf16[112,768]{1,0:T(8,128)(2,1)S(1)} collective-permute-done((bf16[112,768]{1,0:T(8,128)(2,1)S(1)}, bf16[112,768]{1,0:T(8,128)(2,1)S(1)}, u32[]{:S(2)}, u32[]{:S(2)}) %collective-permute-start.6) | collective-permute-done | bytes 172064 | tf_op jit(solution)/shard_map/ppermute | solution.py:501
  26.7 1.4 %shard_map.75 = (f32[97,768]{1,0:T(8,128)S(1)}, f32[16,768]{1,0:T(8,128)S(1)}) custom-call(s32[6]{0:T(128)S(1)} %stack.27.pos_ref, bf16[112,768]{1,0:T(8,128)(2,1)S(1)} %get-tuple-element.48.kept_ref, bf16[112,768]{1,0:T(8,128)(2,1)S(1)} %collective-permute-done.6.msg_ref, f32[16,768]{1,0:T(8,128)S(1)} %get-tuple-element.45.refs_0_.stats_ref, ...), custom_call_target="tpu_custom_call" | custom-call | flops 57212928 | bytes 1474560 | tf_op jit(solution)/shard_map/pallas_call | solution.py:472
  28.2 1.5 %collective-permute-done.5.msg_ref = bf16[128,384]{1,0:T(8,128)(2,1)S(1)} collective-permute-done((bf16[128,384]{1,0:T(8,128)(2,1)S(1)}, bf16[128,384]{1,0:T(8,128)(2,1)S(1)}, u32[]{:S(2)}, u32[]{:S(2)}) %collective-permute-start.5) | collective-permute-done | bytes 98336 | tf_op jit(solution)/shard_map/ppermute | solution.py:501
  29.7 1.5 %shard_map.76 = f32[97,1152]{1,0:T(8,128)S(1)} custom-call(s32[6]{0:T(128)S(1)} %stack.27.pos_ref, bf16[128,384]{1,0:T(8,128)(2,1)S(1)} %get-tuple-element.46.kept_ref, bf16[128,384]{1,0:T(8,128)(2,1)S(1)} %collective-permute-done.5.msg_ref, f32[16,384]{1,0:T(8,128)S(1)} %get-tuple-element.47.stats_ref, f32[16,768]{1,0:T(8,128)S(1)} %get-tuple-element.52.vec_ref, ...), custom_call_target="tpu_custom_call" | custom-call | flops 57212928 | bytes 1474560 | tf_op jit(solution)/shard_map/pallas_call | solution.py:472
  31.2 1.6 %collective-permute-start.9 = (f16[97,512]{1,0:T(8,128)(2,1)S(1)}, f16[97,512]{1,0:T(8,128)(2,1)S(1)}, u32[]{:S(2)}, u32[]{:S(2)}) collective-permute-start(f16[97,512]{1,0:T(8,128)(2,1)S(1)} %slice.23), channel_id=1, source_target_pairs={{0,2},{1,5},{2,0},{3,7},{4,6},{5,1},{6,4},{7,3},{8,10},{9,13},{10,... | collective-permute-start | bytes 297992 | tf_op jit(solution)/shard_map/ppermute | solution.py:501
  32.8 0.6 %collective-permute-start.7 = (f16[97,640]{1,0:T(8,128)(2,1)S(1)}, f16[97,640]{1,0:T(8,128)(2,1)S(1)}, u32[]{:S(2)}, u32[]{:S(2)}) collective-permute-start(f16[97,640]{1,0:T(8,128)(2,1)S(1)} %slice.22), channel_id=1, source_target_pairs={{0,2},{1,5},{2,0},{3,7},{4,6},{5,1},{6,4},{7,3},{8,10},{9,13},{10,... | collective-permute-start | bytes 372488 | tf_op jit(solution)/shard_map/ppermute | solution.py:501
  33.4 2.6 %collective-permute-done.9 = f16[97,512]{1,0:T(8,128)(2,1)S(1)} collective-permute-done((f16[97,512]{1,0:T(8,128)(2,1)S(1)}, f16[97,512]{1,0:T(8,128)(2,1)S(1)}, u32[]{:S(2)}, u32[]{:S(2)}) %collective-permute-start.9) | collective-permute-done | bytes 99360 | tf_op jit(solution)/shard_map/ppermute | solution.py:501
  36.0 2.1 %collective-permute-start.10 = (f16[97,512]{1,0:T(8,128)(2,1)S(1)}, f16[97,512]{1,0:T(8,128)(2,1)S(1)}, u32[]{:S(2)}, u32[]{:S(2)}) collective-permute-start(f16[97,512]{1,0:T(8,128)(2,1)S(1)} %add_convert_fusion.1), channel_id=1, source_target_pairs={{0,4},{1,9},{2,6},{3,11},{4,0},{5,13},{6,2},{7,15},{8,12},{9,1},{1... | collective-permute-start | bytes 297992 | tf_op jit(solution)/shard_map/ppermute | solution.py:501
  38.2 0.0 collective-permute-done.7
  38.2 1.8 %collective-permute-start.8 = (f16[97,640]{1,0:T(8,128)(2,1)S(1)}, f16[97,640]{1,0:T(8,128)(2,1)S(1)}, u32[]{:S(2)}, u32[]{:S(2)}) collective-permute-start(f16[97,640]{1,0:T(8,128)(2,1)S(1)} %add_convert_fusion), channel_id=1, source_target_pairs={{0,4},{1,9},{2,6},{3,11},{4,0},{5,13},{6,2},{7,15},{8,12},{9,1},{1... | collective-permute-start | bytes 372488 | tf_op jit(solution)/shard_map/ppermute | solution.py:501
  40.0 1.1 %collective-permute-done.10 = f16[97,512]{1,0:T(8,128)(2,1)S(1)} collective-permute-done((f16[97,512]{1,0:T(8,128)(2,1)S(1)}, f16[97,512]{1,0:T(8,128)(2,1)S(1)}, u32[]{:S(2)}, u32[]{:S(2)}) %collective-permute-start.10) | collective-permute-done | bytes 99360 | tf_op jit(solution)/shard_map/ppermute | solution.py:501
  41.2 0.1 collective-permute-start.11
  41.2 2.0 %collective-permute-done.8 = f16[97,640]{1,0:T(8,128)(2,1)S(1)} collective-permute-done((f16[97,640]{1,0:T(8,128)(2,1)S(1)}, f16[97,640]{1,0:T(8,128)(2,1)S(1)}, u32[]{:S(2)}, u32[]{:S(2)}) %collective-permute-start.8) | collective-permute-done | bytes 124192 | tf_op jit(solution)/shard_map/ppermute | solution.py:501
  43.4 0.9 %shard_map.77 = f32[200,97]{1,0:T(8,128)S(1)} custom-call(s32[6]{0:T(128)S(1)} %stack.27.pos_ref, f32[97,1152]{1,0:T(8,128)S(1)} %pad_maximum_fusion.score_ref, bf16[97,1152]{1,0:T(8,128)(2,1)S(1)} %get-tuple-element.50.flag_ref, bf16[200,1152]{1,0:T(8,128)(2,1)S(1)} %get-tuple-element.55.hot_ref), custom_call_target="tpu_custom_call" | custom-call | flops 89395200 | bytes 893952 | tf_op jit(solution)/shard_map/pallas_call | solution.py:472
  44.3 0.1 collective-permute-start.12
  44.4 0.0 collective-permute-done.11
  44.4 0.8 %fusion.2 = f32[97,768]{1,0:T(8,128)} fusion(f32[97,640]{1,0:T(8,128)S(1)} %convert_add_fusion, f32[97,512]{1,0:T(8,128)S(1)} %convert_add_fusion.1, f32[97,384]{1,0:T(8,128)S(1)} %collective-permute-done.11, bf16[97,1152]{1,0:T(8,128)(2,1)S(1)} %get-tuple-element.50.flag_ref, pred[]{:T(512)S(6)} %eq.2), kind=kLoop, calls=%fused_computation.5 | loop fusion | flops 372480 | bytes 1042945 | tf_op jit(solution)/shard_map/add | solution.py:615
  45.2 0.4 collective-permute-done.12
  45.6 0.7 %add_bitcast_fusion = f32[97,200]{0,1:T(8,128)} fusion(f32[200,97]{1,0:T(8,128)S(1)} %get-tuple-element.57, f16[200,97]{1,0:T(8,128)(2,1)S(1)} %collective-permute-done.12), kind=kLoop, calls=%fused_computation.10 | loop fusion | flops 38800 | bytes 194000 | tf_op jit(solution)/shard_map/transpose | solution.py:623
  (11 shorter events, 0.3 us)
Async XLA Ops:
  0.7 1.4 %copy-start.4 = (bf16[1024,768]{1,0:T(8,128)(2,1)S(1)}, bf16[1024,768]{1,0:T(8,128)(2,1)}, u32[]{:S(2)}) copy-start(bf16[1024,768]{1,0:T(8,128)(2,1)} %own_ref.1) | copy-start | bytes 4718596
  4.6 3.1 %collective-permute-start = (bf16[1024,384]{1,0:T(8,128)(2,1)S(1)}, bf16[1024,384]{1,0:T(8,128)(2,1)S(1)}, u32[]{:S(2)}, u32[]{:S(2)}) collective-permute-start(bf16[1024,384]{1,0:T(8,128)(2,1)S(1)} %get-tuple-element.31), channel_id=1, source_target_pairs={{0,1},{1,0},{2,3},{3,2},{4,5},{5,4},{6,7},{7,6},{8,9},{9,8},{10,11... | collective-permute-start | bytes 2359304 | tf_op jit(solution)/shard_map/ppermute | solution.py:504
  5.1 7.4 %collective-permute-start.2 = (bf16[200,768]{1,0:T(8,128)(2,1)S(1)}, bf16[200,768]{1,0:T(8,128)(2,1)S(1)}, u32[]{:S(2)}, u32[]{:S(2)}) collective-permute-start(bf16[200,768]{1,0:T(8,128)(2,1)S(1)} %get-tuple-element.37), channel_id=1, source_target_pairs={{0,2},{1,5},{2,0},{3,7},{4,6},{5,1},{6,4},{7,3},{8,10},{9,13},{10,... | collective-permute-start | bytes 921608 | tf_op jit(solution)/shard_map/ppermute | solution.py:501
  10.0 15.1 %copy-start = (s32[97,1536]{1,0:T(8,128)S(1)}, s32[97,1536]{1,0:T(8,128)}, u32[]{:S(2)}) copy-start(s32[97,1536]{1,0:T(8,128)} %annot_ref.1) | copy-start | bytes 1787908
  10.0 15.0 %copy-start.1 = (s32[1536]{0:T(1024)S(1)}, s32[1536]{0:T(1024)}, u32[]{:S(2)}) copy-start(s32[1536]{0:T(1024)} %param.6) | copy-start | bytes 18436
  10.0 15.0 %copy-start.2 = (s32[1536]{0:T(1024)S(1)}, s32[1536]{0:T(1024)}, u32[]{:S(2)}) copy-start(s32[1536]{0:T(1024)} %param.9) | copy-start | bytes 18436
  10.0 15.0 %copy-start.3 = (s32[1536]{0:T(1024)S(1)}, s32[1536]{0:T(1024)}, u32[]{:S(2)}) copy-start(s32[1536]{0:T(1024)} %param.7) | copy-start | bytes 18436
  10.0 5.7 %collective-permute-start.1 = (bf16[224,384]{1,0:T(8,128)(2,1)S(1)}, bf16[224,384]{1,0:T(8,128)(2,1)S(1)}, u32[]{:S(2)}, u32[]{:S(2)}) collective-permute-start(bf16[224,384]{1,0:T(8,128)(2,1)S(1)} %get-tuple-element.34), channel_id=1, source_target_pairs={{0,2},{1,5},{2,0},{3,7},{4,6},{5,1},{6,4},{7,3},{8,10},{9,13},{10,... | collective-permute-start | bytes 516104 | tf_op jit(solution)/shard_map/ppermute | solution.py:501
  13.1 6.6 %collective-permute-start.4 = (bf16[104,768]{1,0:T(8,128)(2,1)S(1)}, bf16[104,768]{1,0:T(8,128)(2,1)S(1)}, u32[]{:S(2)}, u32[]{:S(2)}) collective-permute-start(bf16[104,768]{1,0:T(8,128)(2,1)S(1)} %get-tuple-element.44), channel_id=1, source_target_pairs={{0,4},{1,9},{2,6},{3,11},{4,0},{5,13},{6,2},{7,15},{8,12},{9,1},{1... | collective-permute-start | bytes 479240 | tf_op jit(solution)/shard_map/ppermute | solution.py:501
  16.3 6.7 %collective-permute-start.3 = (bf16[128,384]{1,0:T(8,128)(2,1)S(1)}, bf16[128,384]{1,0:T(8,128)(2,1)S(1)}, u32[]{:S(2)}, u32[]{:S(2)}) collective-permute-start(bf16[128,384]{1,0:T(8,128)(2,1)S(1)} %get-tuple-element.41), channel_id=1, source_target_pairs={{0,4},{1,9},{2,6},{3,11},{4,0},{5,13},{6,2},{7,15},{8,12},{9,1},{1... | collective-permute-start | bytes 294920 | tf_op jit(solution)/shard_map/ppermute | solution.py:501
  20.4 6.4 %collective-permute-start.6 = (bf16[112,768]{1,0:T(8,128)(2,1)S(1)}, bf16[112,768]{1,0:T(8,128)(2,1)S(1)}, u32[]{:S(2)}, u32[]{:S(2)}) collective-permute-start(bf16[112,768]{1,0:T(8,128)(2,1)S(1)} %get-tuple-element.48.kept_ref), channel_id=1, source_target_pairs={{0,8},{1,3},{2,10},{3,1},{4,12},{5,7},{6,14},{7,5},{8,0},{9,11},{1... | collective-permute-start | bytes 516104 | tf_op jit(solution)/shard_map/ppermute | solution.py:501
  23.5 6.1 %collective-permute-start.5 = (bf16[128,384]{1,0:T(8,128)(2,1)S(1)}, bf16[128,384]{1,0:T(8,128)(2,1)S(1)}, u32[]{:S(2)}, u32[]{:S(2)}) collective-permute-start(bf16[128,384]{1,0:T(8,128)(2,1)S(1)} %get-tuple-element.46.kept_ref), channel_id=1, source_target_pairs={{0,8},{1,3},{2,10},{3,1},{4,12},{5,7},{6,14},{7,5},{8,0},{9,11},{1... | collective-permute-start | bytes 294920 | tf_op jit(solution)/shard_map/ppermute | solution.py:501
  31.2 4.8 %collective-permute-start.9 = (f16[97,512]{1,0:T(8,128)(2,1)S(1)}, f16[97,512]{1,0:T(8,128)(2,1)S(1)}, u32[]{:S(2)}, u32[]{:S(2)}) collective-permute-start(f16[97,512]{1,0:T(8,128)(2,1)S(1)} %slice.23), channel_id=1, source_target_pairs={{0,2},{1,5},{2,0},{3,7},{4,6},{5,1},{6,4},{7,3},{8,10},{9,13},{10,... | collective-permute-start | bytes 297992 | tf_op jit(solution)/shard_map/ppermute | solution.py:501
  32.8 5.3 %collective-permute-start.7 = (f16[97,640]{1,0:T(8,128)(2,1)S(1)}, f16[97,640]{1,0:T(8,128)(2,1)S(1)}, u32[]{:S(2)}, u32[]{:S(2)}) collective-permute-start(f16[97,640]{1,0:T(8,128)(2,1)S(1)} %slice.22), channel_id=1, source_target_pairs={{0,2},{1,5},{2,0},{3,7},{4,6},{5,1},{6,4},{7,3},{8,10},{9,13},{10,... | collective-permute-start | bytes 372488 | tf_op jit(solution)/shard_map/ppermute | solution.py:501
  36.0 5.0 %collective-permute-start.10 = (f16[97,512]{1,0:T(8,128)(2,1)S(1)}, f16[97,512]{1,0:T(8,128)(2,1)S(1)}, u32[]{:S(2)}, u32[]{:S(2)}) collective-permute-start(f16[97,512]{1,0:T(8,128)(2,1)S(1)} %add_convert_fusion.1), channel_id=1, source_target_pairs={{0,4},{1,9},{2,6},{3,11},{4,0},{5,13},{6,2},{7,15},{8,12},{9,1},{1... | collective-permute-start | bytes 297992 | tf_op jit(solution)/shard_map/ppermute | solution.py:501
  38.2 5.1 %collective-permute-start.8 = (f16[97,640]{1,0:T(8,128)(2,1)S(1)}, f16[97,640]{1,0:T(8,128)(2,1)S(1)}, u32[]{:S(2)}, u32[]{:S(2)}) collective-permute-start(f16[97,640]{1,0:T(8,128)(2,1)S(1)} %add_convert_fusion), channel_id=1, source_target_pairs={{0,4},{1,9},{2,6},{3,11},{4,0},{5,13},{6,2},{7,15},{8,12},{9,1},{1... | collective-permute-start | bytes 372488 | tf_op jit(solution)/shard_map/ppermute | solution.py:501
  41.2 3.2 %collective-permute-start.11 = (f32[97,384]{1,0:T(8,128)S(1)}, f32[97,384]{1,0:T(8,128)S(1)}, u32[]{:S(2)}, u32[]{:S(2)}) collective-permute-start(f32[97,384]{1,0:T(8,128)S(1)} %slice.26), channel_id=1, source_target_pairs={{0,1},{1,0},{2,3},{3,2},{4,5},{5,4},{6,7},{7,6},{8,9},{9,8},{10,11... | collective-permute-start | bytes 446984 | tf_op jit(solution)/shard_map/ppermute | solution.py:504
  44.3 1.3 %collective-permute-start.12 = (f16[200,97]{1,0:T(8,128)(2,1)S(1)}, f16[200,97]{1,0:T(8,128)(2,1)S(1)}, u32[]{:S(2)}, u32[]{:S(2)}) collective-permute-start(f16[200,97]{1,0:T(8,128)(2,1)S(1)} %get-tuple-element.59), channel_id=1, source_target_pairs={{0,1},{1,0},{2,3},{3,2},{4,5},{5,4},{6,7},{7,6},{8,9},{9,8},{10,11... | collective-permute-start | bytes 116408 | tf_op jit(solution)/shard_map/ppermute | solution.py:504

commit v9 on v8

--- a/solution.py
+++ b/solution.py
@@ -597,11 +597,11 @@
         rows * slab * 20,
     )
     cut = -(-width // 256) * 128
-    pieces = [partial[:, :cut], partial[:, cut:]]
+    pieces = [partial[:, cut:], partial[:, :cut]]
     for t in range(2):
         rounded = [x.astype(jnp.float16) for x in pieces]
         pieces = [x.astype(F32) + exchange(x, t, ROUNDS).astype(F32) for x in rounded]
-    partial = jnp.concatenate(pieces, axis=1)
+    partial = jnp.concatenate(pieces[::-1], axis=1)
     arrived = across(partial[:, slab:])
     sums = call(
         block_kernel,

time: 46.4 us -> 46.4 us (level)
  no operation moved by 1% of the time
where the time goes in v9:
time: 46.4 us; the launch traced here: 46.3 us
  starting transfers between devices  20 us (43%)
  Pallas kernels  12 us (26%)
  waiting for transfers between devices  10.2 us (22%)
  other arithmetic  1.65 us (4%)
  local copies, waits for them, and re-layouts  1.58 us (3%)
  between operations  0.83 us (2%)
    ppermute x10, starting transfers between devices, exchange(): return lax.ppermute(x, ('samples', 'genome'), route)  19.3 us
    pallas_call x10, Pallas kernels, call(): pl.pallas_call(kernel, out_shape=outputs, in_specs=[smem] + [vmem] * (len...  12 us
    ppermute x10, waiting for transfers between devices, exchange(): return lax.ppermute(x, ('samples', 'genome'), route)  9.78 us
    unnamed x10, local copies, waits for them, and re-layouts  1.44 us
  transfers between devices with their start and end apart: 13, of which 9 were waited for; matrix products, arithmetic and copies ran while one was open for 2% of the time, Pallas kernels for 17%

profile of v9, /device:TPU:0, one launch (start us, length us, event | category | flops | bytes accessed | tf_op | source)
XLA Modules:
  0.0 46.3 jit_solution(551850407103596130)
XLA Ops:
  0.6 0.1 stack.27.pos_ref
  0.7 1.4 %copy-done.4 = bf16[1024,768]{1,0:T(8,128)(2,1)S(1)} copy-done((bf16[1024,768]{1,0:T(8,128)(2,1)S(1)}, bf16[1024,768]{1,0:T(8,128)(2,1)}, u32[]{:S(2)}) %copy-start.4) | copy-done | bytes 1572888
  2.1 2.4 %shard_map.68 = (f32[192,768]{1,0:T(8,128)S(1)}, bf16[200,768]{1,0:T(8,128)(2,1)S(1)}, f32[16,768]{1,0:T(8,128)S(1)}, bf16[768,1024]{1,0:T(8,128)(2,1)S(1)}, bf16[1024,384]{1,0:T(8,128)(2,1)S(1)}) custom-call(s32[6]{0:T(128)S(1)} %stack.27.pos_ref, bf16[1024,768]{1,0:T(8,128)(2,1)S(1)} %copy-done.4), custom_call_target="tpu_custom_call" | custom-call | flops 905969664 | bytes 1572864 | tf_op jit(solution)/shard_map/pallas_call | solution.py:472
  4.6 0.5 %collective-permute-start = (bf16[1024,384]{1,0:T(8,128)(2,1)S(1)}, bf16[1024,384]{1,0:T(8,128)(2,1)S(1)}, u32[]{:S(2)}, u32[]{:S(2)}) collective-permute-start(bf16[1024,384]{1,0:T(8,128)(2,1)S(1)} %get-tuple-element.31), channel_id=1, source_target_pairs={{0,1},{1,0},{2,3},{3,2},{4,5},{5,4},{6,7},{7,6},{8,9},{9,8},{10,11... | collective-permute-start | bytes 2359304 | tf_op jit(solution)/shard_map/ppermute | solution.py:504
  5.1 2.6 %collective-permute-start.2 = (bf16[200,768]{1,0:T(8,128)(2,1)S(1)}, bf16[200,768]{1,0:T(8,128)(2,1)S(1)}, u32[]{:S(2)}, u32[]{:S(2)}) collective-permute-start(bf16[200,768]{1,0:T(8,128)(2,1)S(1)} %get-tuple-element.37), channel_id=1, source_target_pairs={{0,2},{1,5},{2,0},{3,7},{4,6},{5,1},{6,4},{7,3},{8,10},{9,13},{10,... | collective-permute-start | bytes 921608 | tf_op jit(solution)/shard_map/ppermute | solution.py:501
  7.7 0.0 collective-permute-done.there_ref
  7.7 2.3 %shard_map.69 = (f32[192,384]{1,0:T(8,128)S(1)}, bf16[224,384]{1,0:T(8,128)(2,1)S(1)}, f32[16,384]{1,0:T(8,128)S(1)}) custom-call(s32[6]{0:T(128)S(1)} %stack.27.pos_ref, bf16[768,1024]{1,0:T(8,128)(2,1)S(1)} %get-tuple-element.30.turned_ref, bf16[1024,384]{1,0:T(8,128)(2,1)S(1)} %collective-permute-done.there_ref, ...), custom_call_target="tpu_custom_call" | custom-call | flops 905969664 | bytes 1572864 | tf_op jit(solution)/shard_map/pallas_call | solution.py:472
  10.0 0.0 copy-start
  10.0 0.0 copy-start.1
  10.0 0.0 copy-start.2
  10.0 0.0 copy-start.3
  10.0 2.3 %collective-permute-start.1 = (bf16[224,384]{1,0:T(8,128)(2,1)S(1)}, bf16[224,384]{1,0:T(8,128)(2,1)S(1)}, u32[]{:S(2)}, u32[]{:S(2)}) collective-permute-start(bf16[224,384]{1,0:T(8,128)(2,1)S(1)} %get-tuple-element.34), channel_id=1, source_target_pairs={{0,2},{1,5},{2,0},{3,7},{4,6},{5,1},{6,4},{7,3},{8,10},{9,13},{10,... | collective-permute-start | bytes 516104 | tf_op jit(solution)/shard_map/ppermute | solution.py:501
  12.3 0.2 collective-permute-done.2.msg_ref
  12.5 0.6 %shard_map.70 = (f32[96,768]{1,0:T(8,128)S(1)}, bf16[104,768]{1,0:T(8,128)(2,1)S(1)}, f32[16,768]{1,0:T(8,128)S(1)}) custom-call(s32[6]{0:T(128)S(1)} %stack.27.pos_ref, f32[192,768]{1,0:T(8,128)S(1)} %get-tuple-element.36.kept_ref, bf16[200,768]{1,0:T(8,128)(2,1)S(1)} %collective-permute-done.2.msg_ref, f32[16,768]{1,0:T(8,128)S(1)} %get-tuple-element.32.own_stats_ref.stats_ref), custom_call_target="tpu_custom_call" | custom-call | flops 589824 | bytes 1474560 | tf_op jit(solution)/shard_map/pallas_call | solution.py:472
  13.1 2.2 %collective-permute-start.4 = (bf16[104,768]{1,0:T(8,128)(2,1)S(1)}, bf16[104,768]{1,0:T(8,128)(2,1)S(1)}, u32[]{:S(2)}, u32[]{:S(2)}) collective-permute-start(bf16[104,768]{1,0:T(8,128)(2,1)S(1)} %get-tuple-element.44), channel_id=1, source_target_pairs={{0,4},{1,9},{2,6},{3,11},{4,0},{5,13},{6,2},{7,15},{8,12},{9,1},{1... | collective-permute-start | bytes 479240 | tf_op jit(solution)/shard_map/ppermute | solution.py:501
  15.3 0.4 collective-permute-done.1.msg_ref
  15.7 0.6 %shard_map.71 = (f32[96,384]{1,0:T(8,128)S(1)}, bf16[128,384]{1,0:T(8,128)(2,1)S(1)}, f32[16,384]{1,0:T(8,128)S(1)}) custom-call(s32[6]{0:T(128)S(1)} %stack.27.pos_ref, f32[192,384]{1,0:T(8,128)S(1)} %get-tuple-element.33.kept_ref, bf16[224,384]{1,0:T(8,128)(2,1)S(1)} %collective-permute-done.1.msg_ref, f32[16,384]{1,0:T(8,128)S(1)} %get-tuple-element.35.stats_ref, ...), custom_call_target="tpu_custom_call" | custom-call | flops 294912 | bytes 737280 | tf_op jit(solution)/shard_map/pallas_call | solution.py:472
  16.3 2.2 %collective-permute-start.3 = (bf16[128,384]{1,0:T(8,128)(2,1)S(1)}, bf16[128,384]{1,0:T(8,128)(2,1)S(1)}, u32[]{:S(2)}, u32[]{:S(2)}) collective-permute-start(bf16[128,384]{1,0:T(8,128)(2,1)S(1)} %get-tuple-element.41), channel_id=1, source_target_pairs={{0,4},{1,9},{2,6},{3,11},{4,0},{5,13},{6,2},{7,15},{8,12},{9,1},{1... | collective-permute-start | bytes 294920 | tf_op jit(solution)/shard_map/ppermute | solution.py:501
  18.4 1.3 %collective-permute-done.4.msg_ref = bf16[104,768]{1,0:T(8,128)(2,1)S(1)} collective-permute-done((bf16[104,768]{1,0:T(8,128)(2,1)S(1)}, bf16[104,768]{1,0:T(8,128)(2,1)S(1)}, u32[]{:S(2)}, u32[]{:S(2)}) %collective-permute-start.4) | collective-permute-done | bytes 159776 | tf_op jit(solution)/shard_map/ppermute | solution.py:501
  19.8 0.6 %shard_map.72 = (bf16[112,768]{1,0:T(8,128)(2,1)S(1)}, f32[16,768]{1,0:T(8,128)S(1)}) custom-call(s32[6]{0:T(128)S(1)} %stack.27.pos_ref, f32[96,768]{1,0:T(8,128)S(1)} %get-tuple-element.43.kept_ref, bf16[104,768]{1,0:T(8,128)(2,1)S(1)} %collective-permute-done.4.msg_ref, f32[16,768]{1,0:T(8,128)S(1)} %get-tuple-element.39.refs_0_.stats_ref), custom_call_target="tpu_custom_call" | custom-call | flops 589824 | bytes 1474560 | tf_op jit(solution)/shard_map/pallas_call | solution.py:472
  20.4 2.6 %collective-permute-start.6 = (bf16[112,768]{1,0:T(8,128)(2,1)S(1)}, bf16[112,768]{1,0:T(8,128)(2,1)S(1)}, u32[]{:S(2)}, u32[]{:S(2)}) collective-permute-start(bf16[112,768]{1,0:T(8,128)(2,1)S(1)} %get-tuple-element.48.kept_ref), channel_id=1, source_target_pairs={{0,8},{1,3},{2,10},{3,1},{4,12},{5,7},{6,14},{7,5},{8,0},{9,11},{1... | collective-permute-start | bytes 516104 | tf_op jit(solution)/shard_map/ppermute | solution.py:501
  23.0 0.0 collective-permute-done.3.msg_ref
  23.0 0.6 %shard_map.73 = (bf16[128,384]{1,0:T(8,128)(2,1)S(1)}, f32[16,384]{1,0:T(8,128)S(1)}) custom-call(s32[6]{0:T(128)S(1)} %stack.27.pos_ref, f32[96,384]{1,0:T(8,128)S(1)} %get-tuple-element.40.kept_ref, bf16[128,384]{1,0:T(8,128)(2,1)S(1)} %collective-permute-done.3.msg_ref, f32[16,384]{1,0:T(8,128)S(1)} %get-tuple-element.42.stats_ref, ...), custom_call_target="tpu_custom_call" | custom-call | flops 294912 | bytes 737280 | tf_op jit(solution)/shard_map/pallas_call | solution.py:472
  23.5 1.5 %collective-permute-start.5 = (bf16[128,384]{1,0:T(8,128)(2,1)S(1)}, bf16[128,384]{1,0:T(8,128)(2,1)S(1)}, u32[]{:S(2)}, u32[]{:S(2)}) collective-permute-start(bf16[128,384]{1,0:T(8,128)(2,1)S(1)} %get-tuple-element.46.kept_ref), channel_id=1, source_target_pairs={{0,8},{1,3},{2,10},{3,1},{4,12},{5,7},{6,14},{7,5},{8,0},{9,11},{1... | collective-permute-start | bytes 294920 | tf_op jit(solution)/shard_map/ppermute | solution.py:501
  25.0 0.0 copy-done
  25.0 0.0 copy-done.1
  25.0 0.0 copy-done.2
  25.0 0.0 copy-done.3
  25.0 1.0 %shard_map.74 = (bf16[97,1152]{1,0:T(8,128)(2,1)S(1)}, bf16[97,1536]{1,0:T(8,128)(2,1)S(1)}, bf16[97,640]{1,0:T(8,128)(2,1)S(1)}, f32[8,1152]{1,0:T(8,128)S(1)}, bf16[200,1152]{1,0:T(8,128)(2,1)S(1)}) custom-call(s32[6]{0:T(128)S(1)} %stack.27.pos_ref, s32[97,1536]{1,0:T(8,128)S(1)} %copy-done, s32[12,128]{1,0:T(8,128)S(1)} %bitcast.11, ...), custom_call_target="tpu_custom_call" | custom-call | flops 1489920 | bytes 1191936 | tf_op jit(solution)/shard_map/pallas_call | solution.py:472
  26.0 0.7 %collective-permute-done.6.msg_ref = bf16[112,768]{1,0:T(8,128)(2,1)S(1)} collective-permute-done((bf16[112,768]{1,0:T(8,128)(2,1)S(1)}, bf16[112,768]{1,0:T(8,128)(2,1)S(1)}, u32[]{:S(2)}, u32[]{:S(2)}) %collective-permute-start.6) | collective-permute-done | bytes 172064 | tf_op jit(solution)/shard_map/ppermute | solution.py:501
  26.7 1.4 %shard_map.75 = (f32[97,768]{1,0:T(8,128)S(1)}, f32[16,768]{1,0:T(8,128)S(1)}) custom-call(s32[6]{0:T(128)S(1)} %stack.27.pos_ref, bf16[112,768]{1,0:T(8,128)(2,1)S(1)} %get-tuple-element.48.kept_ref, bf16[112,768]{1,0:T(8,128)(2,1)S(1)} %collective-permute-done.6.msg_ref, f32[16,768]{1,0:T(8,128)S(1)} %get-tuple-element.45.refs_0_.stats_ref, ...), custom_call_target="tpu_custom_call" | custom-call | flops 57212928 | bytes 1474560 | tf_op jit(solution)/shard_map/pallas_call | solution.py:472
  28.2 1.5 %collective-permute-done.5.msg_ref = bf16[128,384]{1,0:T(8,128)(2,1)S(1)} collective-permute-done((bf16[128,384]{1,0:T(8,128)(2,1)S(1)}, bf16[128,384]{1,0:T(8,128)(2,1)S(1)}, u32[]{:S(2)}, u32[]{:S(2)}) %collective-permute-start.5) | collective-permute-done | bytes 98336 | tf_op jit(solution)/shard_map/ppermute | solution.py:501
  29.7 1.5 %shard_map.76 = f32[97,1152]{1,0:T(8,128)S(1)} custom-call(s32[6]{0:T(128)S(1)} %stack.27.pos_ref, bf16[128,384]{1,0:T(8,128)(2,1)S(1)} %get-tuple-element.46.kept_ref, bf16[128,384]{1,0:T(8,128)(2,1)S(1)} %collective-permute-done.5.msg_ref, f32[16,384]{1,0:T(8,128)S(1)} %get-tuple-element.47.stats_ref, f32[16,768]{1,0:T(8,128)S(1)} %get-tuple-element.52.vec_ref, ...), custom_call_target="tpu_custom_call" | custom-call | flops 57212928 | bytes 1474560 | tf_op jit(solution)/shard_map/pallas_call | solution.py:472
  31.2 1.6 %collective-permute-start.9 = (f16[97,512]{1,0:T(8,128)(2,1)S(1)}, f16[97,512]{1,0:T(8,128)(2,1)S(1)}, u32[]{:S(2)}, u32[]{:S(2)}) collective-permute-start(f16[97,512]{1,0:T(8,128)(2,1)S(1)} %slice.23), channel_id=1, source_target_pairs={{0,2},{1,5},{2,0},{3,7},{4,6},{5,1},{6,4},{7,3},{8,10},{9,13},{10,... | collective-permute-start | bytes 297992 | tf_op jit(solution)/shard_map/ppermute | solution.py:501
  32.8 0.6 %collective-permute-start.7 = (f16[97,640]{1,0:T(8,128)(2,1)S(1)}, f16[97,640]{1,0:T(8,128)(2,1)S(1)}, u32[]{:S(2)}, u32[]{:S(2)}) collective-permute-start(f16[97,640]{1,0:T(8,128)(2,1)S(1)} %slice.22), channel_id=1, source_target_pairs={{0,2},{1,5},{2,0},{3,7},{4,6},{5,1},{6,4},{7,3},{8,10},{9,13},{10,... | collective-permute-start | bytes 372488 | tf_op jit(solution)/shard_map/ppermute | solution.py:501
  33.4 2.6 %collective-permute-done.9 = f16[97,512]{1,0:T(8,128)(2,1)S(1)} collective-permute-done((f16[97,512]{1,0:T(8,128)(2,1)S(1)}, f16[97,512]{1,0:T(8,128)(2,1)S(1)}, u32[]{:S(2)}, u32[]{:S(2)}) %collective-permute-start.9) | collective-permute-done | bytes 99360 | tf_op jit(solution)/shard_map/ppermute | solution.py:501
  36.0 2.1 %collective-permute-start.10 = (f16[97,512]{1,0:T(8,128)(2,1)S(1)}, f16[97,512]{1,0:T(8,128)(2,1)S(1)}, u32[]{:S(2)}, u32[]{:S(2)}) collective-permute-start(f16[97,512]{1,0:T(8,128)(2,1)S(1)} %add_convert_fusion.1), channel_id=1, source_target_pairs={{0,4},{1,9},{2,6},{3,11},{4,0},{5,13},{6,2},{7,15},{8,12},{9,1},{1... | collective-permute-start | bytes 297992 | tf_op jit(solution)/shard_map/ppermute | solution.py:501
  38.2 0.0 collective-permute-done.7
  38.2 1.8 %collective-permute-start.8 = (f16[97,640]{1,0:T(8,128)(2,1)S(1)}, f16[97,640]{1,0:T(8,128)(2,1)S(1)}, u32[]{:S(2)}, u32[]{:S(2)}) collective-permute-start(f16[97,640]{1,0:T(8,128)(2,1)S(1)} %add_convert_fusion), channel_id=1, source_target_pairs={{0,4},{1,9},{2,6},{3,11},{4,0},{5,13},{6,2},{7,15},{8,12},{9,1},{1... | collective-permute-start | bytes 372488 | tf_op jit(solution)/shard_map/ppermute | solution.py:501
  40.0 1.1 %collective-permute-done.10 = f16[97,512]{1,0:T(8,128)(2,1)S(1)} collective-permute-done((f16[97,512]{1,0:T(8,128)(2,1)S(1)}, f16[97,512]{1,0:T(8,128)(2,1)S(1)}, u32[]{:S(2)}, u32[]{:S(2)}) %collective-permute-start.10) | collective-permute-done | bytes 99360 | tf_op jit(solution)/shard_map/ppermute | solution.py:501
  41.2 0.1 collective-permute-start.11
  41.2 2.0 %collective-permute-done.8 = f16[97,640]{1,0:T(8,128)(2,1)S(1)} collective-permute-done((f16[97,640]{1,0:T(8,128)(2,1)S(1)}, f16[97,640]{1,0:T(8,128)(2,1)S(1)}, u32[]{:S(2)}, u32[]{:S(2)}) %collective-permute-start.8) | collective-permute-done | bytes 124192 | tf_op jit(solution)/shard_map/ppermute | solution.py:501
  43.4 0.9 %shard_map.77 = f32[200,97]{1,0:T(8,128)S(1)} custom-call(s32[6]{0:T(128)S(1)} %stack.27.pos_ref, f32[97,1152]{1,0:T(8,128)S(1)} %pad_maximum_fusion.score_ref, bf16[97,1152]{1,0:T(8,128)(2,1)S(1)} %get-tuple-element.50.flag_ref, bf16[200,1152]{1,0:T(8,128)(2,1)S(1)} %get-tuple-element.55.hot_ref), custom_call_target="tpu_custom_call" | custom-call | flops 89395200 | bytes 893952 | tf_op jit(solution)/shard_map/pallas_call | solution.py:472
  44.3 0.1 collective-permute-start.12
  44.4 0.0 collective-permute-done.11
  44.4 0.8 %fusion.2 = f32[97,768]{1,0:T(8,128)} fusion(f32[97,640]{1,0:T(8,128)S(1)} %convert_add_fusion, f32[97,512]{1,0:T(8,128)S(1)} %convert_add_fusion.1, f32[97,384]{1,0:T(8,128)S(1)} %collective-permute-done.11, bf16[97,1152]{1,0:T(8,128)(2,1)S(1)} %get-tuple-element.50.flag_ref, pred[]{:T(512)S(6)} %eq.2), kind=kLoop, calls=%fused_computation.5 | loop fusion | flops 372480 | bytes 1042945 | tf_op jit(solution)/shard_map/add | solution.py:615
  45.2 0.4 collective-permute-done.12
  45.6 0.7 %add_bitcast_fusion = f32[97,200]{0,1:T(8,128)} fusion(f32[200,97]{1,0:T(8,128)S(1)} %get-tuple-element.57, f16[200,97]{1,0:T(8,128)(2,1)S(1)} %collective-permute-done.12), kind=kLoop, calls=%fused_computation.10 | loop fusion | flops 38800 | bytes 194000 | tf_op jit(solution)/shard_map/transpose | solution.py:623
  (11 shorter events, 0.3 us)
Async XLA Ops:
  0.7 1.4 %copy-start.4 = (bf16[1024,768]{1,0:T(8,128)(2,1)S(1)}, bf16[1024,768]{1,0:T(8,128)(2,1)}, u32[]{:S(2)}) copy-start(bf16[1024,768]{1,0:T(8,128)(2,1)} %own_ref.1) | copy-start | bytes 4718596
  4.6 3.1 %collective-permute-start = (bf16[1024,384]{1,0:T(8,128)(2,1)S(1)}, bf16[1024,384]{1,0:T(8,128)(2,1)S(1)}, u32[]{:S(2)}, u32[]{:S(2)}) collective-permute-start(bf16[1024,384]{1,0:T(8,128)(2,1)S(1)} %get-tuple-element.31), channel_id=1, source_target_pairs={{0,1},{1,0},{2,3},{3,2},{4,5},{5,4},{6,7},{7,6},{8,9},{9,8},{10,11... | collective-permute-start | bytes 2359304 | tf_op jit(solution)/shard_map/ppermute | solution.py:504
  5.1 7.4 %collective-permute-start.2 = (bf16[200,768]{1,0:T(8,128)(2,1)S(1)}, bf16[200,768]{1,0:T(8,128)(2,1)S(1)}, u32[]{:S(2)}, u32[]{:S(2)}) collective-permute-start(bf16[200,768]{1,0:T(8,128)(2,1)S(1)} %get-tuple-element.37), channel_id=1, source_target_pairs={{0,2},{1,5},{2,0},{3,7},{4,6},{5,1},{6,4},{7,3},{8,10},{9,13},{10,... | collective-permute-start | bytes 921608 | tf_op jit(solution)/shard_map/ppermute | solution.py:501
  10.0 15.1 %copy-start = (s32[97,1536]{1,0:T(8,128)S(1)}, s32[97,1536]{1,0:T(8,128)}, u32[]{:S(2)}) copy-start(s32[97,1536]{1,0:T(8,128)} %annot_ref.1) | copy-start | bytes 1787908
  10.0 15.0 %copy-start.1 = (s32[1536]{0:T(1024)S(1)}, s32[1536]{0:T(1024)}, u32[]{:S(2)}) copy-start(s32[1536]{0:T(1024)} %param.6) | copy-start | bytes 18436
  10.0 15.0 %copy-start.2 = (s32[1536]{0:T(1024)S(1)}, s32[1536]{0:T(1024)}, u32[]{:S(2)}) copy-start(s32[1536]{0:T(1024)} %param.9) | copy-start | bytes 18436
  10.0 15.0 %copy-start.3 = (s32[1536]{0:T(1024)S(1)}, s32[1536]{0:T(1024)}, u32[]{:S(2)}) copy-start(s32[1536]{0:T(1024)} %param.7) | copy-start | bytes 18436
  10.0 5.7 %collective-permute-start.1 = (bf16[224,384]{1,0:T(8,128)(2,1)S(1)}, bf16[224,384]{1,0:T(8,128)(2,1)S(1)}, u32[]{:S(2)}, u32[]{:S(2)}) collective-permute-start(bf16[224,384]{1,0:T(8,128)(2,1)S(1)} %get-tuple-element.34), channel_id=1, source_target_pairs={{0,2},{1,5},{2,0},{3,7},{4,6},{5,1},{6,4},{7,3},{8,10},{9,13},{10,... | collective-permute-start | bytes 516104 | tf_op jit(solution)/shard_map/ppermute | solution.py:501
  13.1 6.6 %collective-permute-start.4 = (bf16[104,768]{1,0:T(8,128)(2,1)S(1)}, bf16[104,768]{1,0:T(8,128)(2,1)S(1)}, u32[]{:S(2)}, u32[]{:S(2)}) collective-permute-start(bf16[104,768]{1,0:T(8,128)(2,1)S(1)} %get-tuple-element.44), channel_id=1, source_target_pairs={{0,4},{1,9},{2,6},{3,11},{4,0},{5,13},{6,2},{7,15},{8,12},{9,1},{1... | collective-permute-start | bytes 479240 | tf_op jit(solution)/shard_map/ppermute | solution.py:501
  16.3 6.7 %collective-permute-start.3 = (bf16[128,384]{1,0:T(8,128)(2,1)S(1)}, bf16[128,384]{1,0:T(8,128)(2,1)S(1)}, u32[]{:S(2)}, u32[]{:S(2)}) collective-permute-start(bf16[128,384]{1,0:T(8,128)(2,1)S(1)} %get-tuple-element.41), channel_id=1, source_target_pairs={{0,4},{1,9},{2,6},{3,11},{4,0},{5,13},{6,2},{7,15},{8,12},{9,1},{1... | collective-permute-start | bytes 294920 | tf_op jit(solution)/shard_map/ppermute | solution.py:501
  20.4 6.4 %collective-permute-start.6 = (bf16[112,768]{1,0:T(8,128)(2,1)S(1)}, bf16[112,768]{1,0:T(8,128)(2,1)S(1)}, u32[]{:S(2)}, u32[]{:S(2)}) collective-permute-start(bf16[112,768]{1,0:T(8,128)(2,1)S(1)} %get-tuple-element.48.kept_ref), channel_id=1, source_target_pairs={{0,8},{1,3},{2,10},{3,1},{4,12},{5,7},{6,14},{7,5},{8,0},{9,11},{1... | collective-permute-start | bytes 516104 | tf_op jit(solution)/shard_map/ppermute | solution.py:501
  23.5 6.1 %collective-permute-start.5 = (bf16[128,384]{1,0:T(8,128)(2,1)S(1)}, bf16[128,384]{1,0:T(8,128)(2,1)S(1)}, u32[]{:S(2)}, u32[]{:S(2)}) collective-permute-start(bf16[128,384]{1,0:T(8,128)(2,1)S(1)} %get-tuple-element.46.kept_ref), channel_id=1, source_target_pairs={{0,8},{1,3},{2,10},{3,1},{4,12},{5,7},{6,14},{7,5},{8,0},{9,11},{1... | collective-permute-start | bytes 294920 | tf_op jit(solution)/shard_map/ppermute | solution.py:501
  31.2 4.8 %collective-permute-start.9 = (f16[97,512]{1,0:T(8,128)(2,1)S(1)}, f16[97,512]{1,0:T(8,128)(2,1)S(1)}, u32[]{:S(2)}, u32[]{:S(2)}) collective-permute-start(f16[97,512]{1,0:T(8,128)(2,1)S(1)} %slice.23), channel_id=1, source_target_pairs={{0,2},{1,5},{2,0},{3,7},{4,6},{5,1},{6,4},{7,3},{8,10},{9,13},{10,... | collective-permute-start | bytes 297992 | tf_op jit(solution)/shard_map/ppermute | solution.py:501
  32.8 5.3 %collective-permute-start.7 = (f16[97,640]{1,0:T(8,128)(2,1)S(1)}, f16[97,640]{1,0:T(8,128)(2,1)S(1)}, u32[]{:S(2)}, u32[]{:S(2)}) collective-permute-start(f16[97,640]{1,0:T(8,128)(2,1)S(1)} %slice.22), channel_id=1, source_target_pairs={{0,2},{1,5},{2,0},{3,7},{4,6},{5,1},{6,4},{7,3},{8,10},{9,13},{10,... | collective-permute-start | bytes 372488 | tf_op jit(solution)/shard_map/ppermute | solution.py:501
  36.0 5.0 %collective-permute-start.10 = (f16[97,512]{1,0:T(8,128)(2,1)S(1)}, f16[97,512]{1,0:T(8,128)(2,1)S(1)}, u32[]{:S(2)}, u32[]{:S(2)}) collective-permute-start(f16[97,512]{1,0:T(8,128)(2,1)S(1)} %add_convert_fusion.1), channel_id=1, source_target_pairs={{0,4},{1,9},{2,6},{3,11},{4,0},{5,13},{6,2},{7,15},{8,12},{9,1},{1... | collective-permute-start | bytes 297992 | tf_op jit(solution)/shard_map/ppermute | solution.py:501
  38.2 5.1 %collective-permute-start.8 = (f16[97,640]{1,0:T(8,128)(2,1)S(1)}, f16[97,640]{1,0:T(8,128)(2,1)S(1)}, u32[]{:S(2)}, u32[]{:S(2)}) collective-permute-start(f16[97,640]{1,0:T(8,128)(2,1)S(1)} %add_convert_fusion), channel_id=1, source_target_pairs={{0,4},{1,9},{2,6},{3,11},{4,0},{5,13},{6,2},{7,15},{8,12},{9,1},{1... | collective-permute-start | bytes 372488 | tf_op jit(solution)/shard_map/ppermute | solution.py:501
  41.2 3.2 %collective-permute-start.11 = (f32[97,384]{1,0:T(8,128)S(1)}, f32[97,384]{1,0:T(8,128)S(1)}, u32[]{:S(2)}, u32[]{:S(2)}) collective-permute-start(f32[97,384]{1,0:T(8,128)S(1)} %slice.26), channel_id=1, source_target_pairs={{0,1},{1,0},{2,3},{3,2},{4,5},{5,4},{6,7},{7,6},{8,9},{9,8},{10,11... | collective-permute-start | bytes 446984 | tf_op jit(solution)/shard_map/ppermute | solution.py:504
  44.3 1.3 %collective-permute-start.12 = (f16[200,97]{1,0:T(8,128)(2,1)S(1)}, f16[200,97]{1,0:T(8,128)(2,1)S(1)}, u32[]{:S(2)}, u32[]{:S(2)}) collective-permute-start(f16[200,97]{1,0:T(8,128)(2,1)S(1)} %get-tuple-element.59), channel_id=1, source_target_pairs={{0,1},{1,0},{2,3},{3,2},{4,5},{5,4},{6,7},{7,6},{8,9},{9,8},{10,11... | collective-permute-start | bytes 116408 | tf_op jit(solution)/shard_map/ppermute | solution.py:504
